TPU v7x, 32 devices: a whole 2x2x4 slice. The times are simulated.
32 devices in a mesh: dp: 4 (over x, core), tensor: 8 (over z, y).
Axes of the slice: x: 2, y: 2, z: 4, core: 2. Of those that a mesh axis runs over, the one named last changes fastest.
Arguments:
- hidden_in: bfloat16 [8192, 2048], P('dp'), may hold values from -6 to 6
- seq_lengths: int32 [4], P('dp'), may hold values from 1024 to 2048, as said below
- out_grad: bfloat16 [8192, 2048], P('dp'), may hold values from -6 to 6
- attn_gain: float32 [2048], replicated, may hold values from 0.5 to 1.5
- mlp_gain: float32 [2048], replicated, may hold values from 0.5 to 1.5
- w_query: bfloat16 [2048, 2048], P(None, 'tensor'), may hold values from -0.5 to 0.5
- w_key: bfloat16 [2048, 512], P('tensor'), may hold values from -0.5 to 0.5
- w_value: bfloat16 [2048, 512], P('tensor'), may hold values from -0.125 to 0.125
- w_out: bfloat16 [2048, 2048], P('tensor'), may hold values from -2 to 2
- w_gate: bfloat16 [2048, 8192], P(None, 'tensor'), may hold values from -0.125 to 0.125
- w_up: bfloat16 [2048, 8192], P(None, 'tensor'), may hold values from -0.125 to 0.125
- w_down: bfloat16 [8192, 2048], P('tensor'), may hold values from -0.5 to 0.5
Outputs:
- layer_out: bfloat16 [8192, 2048], P(('dp', 'tensor'))
- in_grad: float32 [8192, 2048], P(('dp', 'tensor'))
- attn_gain_grad: float32 [2048], P(('dp', 'tensor'))
- mlp_gain_grad: float32 [2048], P(('dp', 'tensor'))
- w_query_grad: float32 [2048, 2048], P('dp', 'tensor')
- w_key_grad: float32 [2048, 512], P(('dp', 'tensor'))
- w_value_grad: float32 [2048, 512], P(('dp', 'tensor'))
- w_out_grad: float32 [2048, 2048], P('tensor', 'dp')
- w_gate_grad: float32 [2048, 8192], P('dp', 'tensor')
- w_up_grad: float32 [2048, 8192], P('dp', 'tensor')
- w_down_grad: float32 [8192, 2048], P('tensor', 'dp')
Inputs may be any that keep to these rules, and one draw needn't show every extreme that they name: `seq_lengths`: each sequence has between half of its 2048 slots and all of them valid; some sequence is full and some is exactly half full.
All inputs are finite; a program needn't handle non-finite values.
Results may differ from a plain program's by a relative error of at most 0.02.
Values may be sent and summed in bfloat16 or wider, within the bound.
No kernel may reach another device: no remote copies, remote signals or barrier semaphores. Data moves between devices by JAX's collectives and lax.ppermute only.
A program may use at most 256 MiB of HBM per device.

v0:
```python
import math

import jax
import jax.numpy as jnp
from jax import lax
from jax.sharding import PartitionSpec as P

H = 32
KVH = 8
HD = 64
SEQ_LEN = 2048
QB = 512


RESID = 0.22
ATTN_SCALE = 0.015625
EPSILON = 1e-05
THETA_LOG = math.log(10000000.0)
MASKED = -1e30


def rope_tables(count):
    positions = (jnp.arange(count, dtype=jnp.int32) % SEQ_LEN).astype(jnp.float32)[:, None]
    freqs = jnp.exp(-THETA_LOG * jnp.arange(0, HD, 2, dtype=jnp.int32).astype(jnp.float32) / HD)[
        None, :
    ]
    angle_rows = positions * freqs
    angle_rows = jnp.concatenate([angle_rows, angle_rows], 1)
    return (jnp.cos(angle_rows), jnp.sin(angle_rows))


def turn_half(values):
    half = HD // 2
    return jnp.concatenate([-values[..., half:], values[..., :half]], -1)


def rotate(values, cosines, sines):
    return values * cosines[:, None, :] + turn_half(values) * sines[:, None, :]


def unrotate(grads, cosines, sines):
    return grads * cosines[:, None, :] - turn_half(grads * sines[:, None, :])


def norm_rows(rows, gain):
    row_scale = lax.rsqrt(jnp.mean(rows * rows, axis=-1, keepdims=True) + EPSILON)
    return (rows * row_scale * gain, row_scale)


def norm_back(rows, row_scale, gain, incoming):
    normed = rows * row_scale
    scaled = incoming * gain
    return row_scale * (scaled - normed * jnp.mean(scaled * normed, axis=-1, keepdims=True))


def local(
    hidden_in,
    seq_lengths,
    out_grad,
    attn_gain,
    mlp_gain,
    w_query,
    w_key,
    w_value,
    w_out,
    w_gate,
    w_up,
    w_down,
):
    rows_total = hidden_in.shape[0]
    heads_here = w_query.shape[1] // HD
    groups = lax.axis_size("tensor")
    member = lax.axis_index("tensor")
    share = rows_total // groups
    share_start = member * share
    blocks = rows_total // QB
    bf16 = jnp.bfloat16
    f32 = jnp.float32
    over_rows = (((0,), (0,)), ((), ()))
    over_cols = (((1,), (1,)), ((), ()))
    cosines, sines = rope_tables(rows_total)
    inputs = hidden_in.astype(f32)
    normed_one, scale_one = norm_rows(inputs, attn_gain)
    normed_low = normed_one.astype(bf16)
    key_all, value_all = (
        lax.all_gather(w_key, "tensor", axis=0, tiled=True),
        lax.all_gather(w_value, "tensor", axis=0, tiled=True),
    )
    kv_head = member * heads_here // (H // KVH)
    key_cols = lax.dynamic_slice_in_dim(key_all, kv_head * HD, HD, 1)
    value_cols = lax.dynamic_slice_in_dim(value_all, kv_head * HD, HD, 1)
    query_raw = jnp.dot(normed_low, w_query, preferred_element_type=f32).reshape(
        rows_total, heads_here, HD
    )
    key_raw = jnp.dot(normed_low, key_cols, preferred_element_type=f32)
    value_raw = jnp.dot(normed_low, value_cols, preferred_element_type=f32)
    queries = rotate(query_raw, cosines, sines).astype(bf16)
    keys = rotate(key_raw[:, None, :], cosines, sines)[:, 0, :].astype(bf16)
    values = value_raw.astype(bf16)
    seq_slots = jnp.arange(seq_lengths.shape[0], dtype=jnp.int32)

    def block_inputs(index):
        start = index * QB
        seq_index = start // SEQ_LEN
        key_start = seq_index * SEQ_LEN
        length = jnp.sum(jnp.where(seq_slots == seq_index, seq_lengths, 0))
        query_rows = lax.dynamic_slice_in_dim(queries, start, QB, 0)
        raw = jnp.einsum("qhd,kd->hqk", query_rows, keys, preferred_element_type=f32) * ATTN_SCALE
        query_pos = start - key_start + jnp.arange(QB, dtype=jnp.int32)
        key_pos = jnp.arange(SEQ_LEN, dtype=jnp.int32)
        allowed = (key_pos[None, :] <= query_pos[:, None]) & (key_pos[None, :] < length)
        scores = jnp.where(allowed[None], raw, MASKED)
        return (start, key_start, query_rows, keys, values, scores)

    def forward_block(index):
        start, key_start, query_rows, key_rows, value_rows, scores = block_inputs(index)
        highest = jnp.max(scores, axis=-1, keepdims=True)
        expos = jnp.exp(scores - highest)
        totals = jnp.sum(expos, axis=-1, keepdims=True)
        probs = (expos / totals).astype(bf16)
        block_out = jnp.einsum("hqk,kd->qhd", probs, value_rows, preferred_element_type=f32)
        return (block_out, (highest + jnp.log(totals))[..., 0])

    attn_blocks, lse_blocks = lax.map(forward_block, jnp.arange(blocks, dtype=jnp.int32))
    attended = attn_blocks.reshape(rows_total, heads_here * HD).astype(bf16)
    attn_part = jnp.dot(attended, w_out, preferred_element_type=f32)
    attn_share = lax.psum_scatter(attn_part, "tensor", scatter_dimension=0, tiled=True)
    inputs_share = lax.dynamic_slice_in_dim(inputs, share_start, share, 0)
    scale_one_share = lax.dynamic_slice_in_dim(scale_one, share_start, share, 0)
    attn_full = lax.all_gather(attn_share, "tensor", axis=0, tiled=True)
    middle = inputs + RESID * attn_full
    normed_two, scale_two = norm_rows(middle, mlp_gain)
    normed_two_low = normed_two.astype(bf16)
    middle_share = lax.dynamic_slice_in_dim(middle, share_start, share, 0)
    scale_two_share = lax.dynamic_slice_in_dim(scale_two, share_start, share, 0)
    gate_rows = jnp.dot(normed_two_low, w_gate, preferred_element_type=f32)
    up_rows = jnp.dot(normed_two_low, w_up, preferred_element_type=f32)
    sigmoid_gate = jax.nn.sigmoid(gate_rows)
    silu_gate = gate_rows * sigmoid_gate
    activ = (silu_gate * up_rows).astype(bf16)
    mlp_part = jnp.dot(activ, w_down, preferred_element_type=f32)
    mlp_share = lax.psum_scatter(
        mlp_part.astype(jnp.bfloat16), "tensor", scatter_dimension=0, tiled=True
    ).astype(jnp.float32)
    layer_out = (middle_share + RESID * mlp_share).astype(bf16)
    row_ids = jnp.arange(rows_total, dtype=jnp.int32)
    length_rows = jnp.sum(
        jnp.where((row_ids // SEQ_LEN)[:, None] == seq_slots[None, :], seq_lengths[None, :], 0),
        axis=1,
    )
    valid_rows = (row_ids % SEQ_LEN < length_rows).astype(f32)[:, None]
    cotangent = out_grad.astype(f32) * valid_rows
    down_in = (RESID * cotangent).astype(bf16)
    down_wgrad = lax.dot_general(activ, down_in, over_rows, preferred_element_type=f32)
    activ_grad = lax.dot_general(down_in, w_down, over_cols, preferred_element_type=f32)
    gate_grad = (
        activ_grad * up_rows * sigmoid_gate * (1.0 + gate_rows * (1.0 - sigmoid_gate))
    ).astype(bf16)
    up_grad = (activ_grad * silu_gate).astype(bf16)
    gate_wgrad = lax.dot_general(normed_two_low, gate_grad, over_rows, preferred_element_type=f32)
    up_wgrad = lax.dot_general(normed_two_low, up_grad, over_rows, preferred_element_type=f32)
    norm_two_part = lax.dot_general(gate_grad, w_gate, over_cols, preferred_element_type=f32)
    norm_two_part = norm_two_part + lax.dot_general(
        up_grad, w_up, over_cols, preferred_element_type=f32
    )
    norm_two_share = lax.psum_scatter(norm_two_part, "tensor", scatter_dimension=0, tiled=True)
    norm_two_full = lax.all_gather(norm_two_share, "tensor", axis=0, tiled=True)
    middle_grad = cotangent + norm_back(middle, scale_two, mlp_gain, norm_two_full)
    branch_grad = (RESID * middle_grad).astype(bf16)
    middle_grad_share = lax.dynamic_slice_in_dim(middle_grad, share_start, share, 0)
    mlp_gain_part = jnp.sum(norm_two_share * middle_share * scale_two_share, axis=0)
    out_wgrad = lax.dot_general(attended, branch_grad, over_rows, preferred_element_type=f32)
    attended_grad = lax.dot_general(branch_grad, w_out, over_cols, preferred_element_type=f32)
    attended_grad = attended_grad.reshape(rows_total, heads_here, HD).astype(bf16)

    def backward_block(carry, index):
        key_grad, value_grad = carry
        start, key_start, query_rows, key_rows, value_rows, scores = block_inputs(index)
        lse_rows = lax.dynamic_index_in_dim(lse_blocks, index, 0, keepdims=False)
        probs = jnp.exp(scores - lse_rows[:, :, None])
        probs_low = probs.astype(bf16)
        grad_rows = lax.dynamic_slice_in_dim(attended_grad, start, QB, 0)
        value_part = jnp.einsum("hqk,qhd->khd", probs_low, grad_rows, preferred_element_type=f32)
        prob_grad = jnp.einsum("qhd,kd->hqk", grad_rows, value_rows, preferred_element_type=f32)
        row_delta = jnp.sum(prob_grad * probs, axis=-1, keepdims=True)
        score_grad = (probs * (prob_grad - row_delta)).astype(bf16)
        query_part = (
            jnp.einsum("hqk,kd->qhd", score_grad, key_rows, preferred_element_type=f32) * ATTN_SCALE
        )
        key_part = (
            jnp.einsum("hqk,qhd->khd", score_grad, query_rows, preferred_element_type=f32)
            * ATTN_SCALE
        )
        key_grad = key_grad + key_part
        value_grad = value_grad + value_part
        return ((key_grad, value_grad), query_part)

    empty_grad = jnp.zeros((rows_total, heads_here, HD), f32)
    (key_grad, value_grad), query_blocks = lax.scan(
        backward_block, (empty_grad, empty_grad), jnp.arange(blocks, dtype=jnp.int32)
    )
    query_grad = query_blocks.reshape(rows_total, heads_here, HD)
    query_low = (
        unrotate(query_grad, cosines, sines).reshape(rows_total, heads_here * HD).astype(bf16)
    )
    key_low = unrotate(key_grad, cosines, sines).reshape(rows_total, heads_here * HD).astype(bf16)
    value_low = value_grad.reshape(rows_total, heads_here * HD).astype(bf16)
    width = normed_low.shape[1]
    query_wgrad = lax.dot_general(normed_low, query_low, over_rows, preferred_element_type=f32)
    key_head_grad = (
        lax.dot_general(normed_low, key_low, over_rows, preferred_element_type=f32)
        .reshape(width, heads_here, HD)
        .sum(axis=1)
    )
    value_head_grad = (
        lax.dot_general(normed_low, value_low, over_rows, preferred_element_type=f32)
        .reshape(width, heads_here, HD)
        .sum(axis=1)
    )
    key_tiled = jnp.tile(key_cols, (1, heads_here))
    value_tiled = jnp.tile(value_cols, (1, heads_here))
    norm_one_part = lax.dot_general(query_low, w_query, over_cols, preferred_element_type=f32)
    norm_one_part = norm_one_part + lax.dot_general(
        key_low, key_tiled, over_cols, preferred_element_type=f32
    )
    norm_one_part = norm_one_part + lax.dot_general(
        value_low, value_tiled, over_cols, preferred_element_type=f32
    )
    norm_one_share = lax.psum_scatter(
        norm_one_part.astype(jnp.bfloat16), "tensor", scatter_dimension=0, tiled=True
    ).astype(jnp.float32)
    in_grad = middle_grad_share + norm_back(
        inputs_share, scale_one_share, attn_gain, norm_one_share
    )
    attn_gain_part = jnp.sum(norm_one_share * inputs_share * scale_one_share, axis=0)
    key_full = lax.dynamic_update_slice_in_dim(
        jnp.zeros(key_all.shape, f32), key_head_grad, kv_head * HD, 1
    )
    value_full = lax.dynamic_update_slice_in_dim(
        jnp.zeros(value_all.shape, f32), value_head_grad, kv_head * HD, 1
    )
    dense = (
        lax.psum_scatter(
            query_wgrad.astype(jnp.bfloat16), "dp", scatter_dimension=0, tiled=True
        ).astype(jnp.float32),
        lax.psum_scatter(
            gate_wgrad.astype(jnp.bfloat16), "dp", scatter_dimension=0, tiled=True
        ).astype(jnp.float32),
        lax.psum_scatter(
            up_wgrad.astype(jnp.bfloat16), "dp", scatter_dimension=0, tiled=True
        ).astype(jnp.float32),
        lax.psum_scatter(
            out_wgrad.astype(jnp.bfloat16), "dp", scatter_dimension=1, tiled=True
        ).astype(jnp.float32),
        lax.psum_scatter(
            down_wgrad.astype(jnp.bfloat16), "dp", scatter_dimension=1, tiled=True
        ).astype(jnp.float32),
    )
    shared = (
        lax.psum_scatter(key_full, ("dp", "tensor"), scatter_dimension=0, tiled=True),
        lax.psum_scatter(value_full, ("dp", "tensor"), scatter_dimension=0, tiled=True),
        lax.psum_scatter(attn_gain_part, ("dp", "tensor"), scatter_dimension=0, tiled=True),
        lax.psum_scatter(mlp_gain_part, ("dp", "tensor"), scatter_dimension=0, tiled=True),
    )
    return (
        layer_out,
        in_grad,
        shared[2],
        shared[3],
        dense[0],
        shared[0],
        shared[1],
        dense[3],
        dense[1],
        dense[2],
        dense[4],
    )


def solution(mesh):
    placed = (
        P("dp", None),
        P("dp"),
        P("dp", None),
        P(),
        P(),
        P(None, "tensor"),
        P("tensor", None),
        P("tensor", None),
        P("tensor", None),
        P(None, "tensor"),
        P(None, "tensor"),
        P("tensor", None),
    )
    return jax.shard_map(
        local,
        mesh=mesh,
        in_specs=placed,
        out_specs=(
            P(("dp", "tensor"), None),
            P(("dp", "tensor"), None),
            P(("dp", "tensor")),
            P(("dp", "tensor")),
            P("dp", "tensor"),
            P(("dp", "tensor"), None),
            P(("dp", "tensor"), None),
            P("tensor", "dp"),
            P("dp", "tensor"),
            P("dp", "tensor"),
            P("tensor", "dp"),
        ),
        check_vma=False,
    )
```

profile of v0, /device:TPU:0, one launch (start us, length us, event | category | flops | bytes accessed | tf_op | source)
XLA Modules:
  0.0 2184.7 jit_solution(15121321370525812363)
XLA Ops:
  14.7 8.7 multiply_convert_fusion.3
  23.5 5.8 fusion.99
  30.8 31.4 %all-gather.7.cloned.1.call-done = bf16[2048,512]{1,0:T(8,128)(2,1)} async-done(((bf16[256,512]{1,0:T(8,128)(2,1)}), bf16[2048,512]{1,0:T(8,128)(2,1)}) %all-gather.7.cloned.1.call-update) | async-done | bytes 2097168 | tf_op jit(solution)/shard_map/all_gather | solution.py:87
  62.2 49.9 %all-gather.5.cloned.1.call-done = bf16[2048,512]{1,0:T(8,128)(2,1)} async-done(((bf16[256,512]{1,0:T(8,128)(2,1)}), bf16[2048,512]{1,0:T(8,128)(2,1)}) %all-gather.5.cloned.1.call-update) | async-done | bytes 2097168 | tf_op jit(solution)/shard_map/all_gather | solution.py:86
  113.7 6.4 fusion.100
  120.2 6.2 convolution_convert_fusion.5
  131.2 70.8 %while.31 = (s32[]{:T(128)}, bf16[4,512,4,64]{1,3,2,0:T(8,128)(2,1)}, f32[4,4,512]{2,1,0:T(4,128)}, s32[4]{0:T(128)S(1)}, s32[1]{0:T(128)}, /*index=5*/bf16[2048...) while((s32[]{:T(128)}, ...), condition=%wide.region_4.5_spmd, body=%wide.region_1.4_spmd.sunk | while | flops 1126171136 | bytes 64299484 | solution.py:124
  142.7 5.2 fusion.160
  160.4 5.2 fusion.160
  205.4 8.2 fusion.101
  213.7 281.2 %reduce-scatter.12.cloned.1.call-done = f32[256,2048]{1,0:T(8,128)} async-done(((f32[2048,2048]{1,0:T(8,128)}), f32[256,2048]{1,0:T(8,128)}) %reduce-scatter.12.cloned.1.call-update) | async-done | bytes 2097168 | tf_op jit(solution)/shard_map/reduce_scatter | solution.py:127
  495.6 228.2 %all-gather.9.cloned.1.call-done = f32[2048,2048]{1,0:T(8,128)} async-done(((f32[256,2048]{1,0:T(8,128)}), f32[2048,2048]{1,0:T(8,128)}) %all-gather.9.cloned.1.call-update) | async-done | bytes 16777232 | tf_op jit(solution)/shard_map/all_gather | solution.py:130
  723.8 10.1 multiply_reduce_fusion.1
  733.9 5.8 copy-done.1
  741.9 11.0 fusion.102
  753.0 11.0 fusion.103
  764.0 23.2 %multiply_convert_fusion.4 = (bf16[2048,1024]{1,0:T(8,128)(2,1)}, bf16[2048,1024]{1,0:T(8,128)(2,1)}, bf16[2048,1024]{1,0:T(8,128)(2,1)}) fusion(f32[2048,1024]{1,0:T(8,128)} %fusion.102, f32[2048,1024]{1,0:T(8,128)} %fusion.103, bf16[1024,2048]{1,0:T(8,128)(2,1)} %param.27, bf16[2048,2048]{1,0:T(8,128)(2,1)} %param.18, f32[2048]{0:T(1024)S(1)} %fusion.94), kind=kOutput, calls=%fused_computation.75 | convolution fusion | flops 8638169088 | bytes 41951232 | tf_op jit(solution)/shard_map/dot_general | solution.py:155
  787.1 15.3 fusion.104
  802.4 17.3 convolution_add_fusion
  819.8 281.0 %reduce-scatter.16.cloned.1.call-done = f32[256,2048]{1,0:T(8,128)} async-done(((f32[2048,2048]{1,0:T(8,128)}), f32[256,2048]{1,0:T(8,128)}) %reduce-scatter.16.cloned.1.call-update) | async-done | bytes 2097168 | tf_op jit(solution)/shard_map/reduce_scatter | solution.py:166
  1100.9 14.1 convolution_convert_fusion.3
  1115.1 14.5 convolution_convert_fusion.2
  1129.7 14.7 convolution_convert_fusion.1
  1146.3 14.2 convolution_convert_fusion
  1160.6 168.9 %all-gather.11.cloned.1.call-done = f32[2048,2048]{1,0:T(8,128)} async-done(((f32[256,2048]{1,0:T(8,128)}), f32[2048,2048]{1,0:T(8,128)}) %all-gather.11.cloned.1.call-update) | async-done | bytes 16777232 | tf_op jit(solution)/shard_map/all_gather | solution.py:167
  1329.5 13.7 multiply_reduce_fusion
  1343.2 15.7 multiply_add_fusion
  1365.0 302.3 %while.32 = (s32[]{:T(128)}, f32[2048,4,64]{0,2,1:T(8,128)}, f32[2048,4,64]{0,2,1:T(8,128)}, f32[4,512,4,64]{1,0,3,2:T(4,128)}, s32[4]{0:T(128)S(1)}, /*index=5*...) while((s32[]{:T(128)}, f32[2048,4,64]{0,2,1:T(8,128)}, ...), condition=%wide.region_12.13_spmd.clone, body=%wide.region_10.12_spmd.clone.sunk | while | flops 2752119296 | bytes 239403760 | solution.py:199
  1366.4 9.2 fusion.169
  1380.7 16.7 fusion.171
  1399.9 11.1 fusion.172
  1411.0 6.5 fusion.173
  1417.5 8.5 fusion.174
  1430.4 11.2 dynamic_update_slice.36
  1442.9 9.3 fusion.169
  1457.3 15.2 fusion.171
  1474.4 11.3 fusion.172
  1485.7 7.2 fusion.173
  1492.9 8.5 fusion.174
  1505.8 11.2 dynamic_update_slice.36
  1518.2 9.3 fusion.169
  1532.5 15.3 fusion.171
  1549.7 11.1 fusion.172
  1560.8 7.4 fusion.173
  1568.2 8.5 fusion.174
  1581.1 11.1 dynamic_update_slice.36
  1593.4 9.2 fusion.169
  1607.7 15.2 fusion.171
  1624.8 11.0 fusion.172
  1635.8 7.1 fusion.173
  1642.9 8.5 fusion.174
  1655.8 11.1 dynamic_update_slice.36
  1687.4 10.8 fusion.80
  1701.9 9.5 fusion.84
  1711.3 16.1 fusion.46
  1728.6 5.8 fusion.68
  1737.4 5.9 dynamic_update_slice.26
  1743.6 7.1 fusion.71
  1753.5 5.9 dynamic_update_slice.27
  1759.4 11.3 convert_element_type.153
  1788.3 99.4 %reduce-scatter.18.cloned.1.call-done = bf16[256,2048]{1,0:T(8,128)(2,1)} async-done(((bf16[2048,2048]{1,0:T(8,128)(2,1)}), bf16[256,2048]{1,0:T(8,128)(2,1)}) %reduce-scatter.18.cloned.1.call-update) | async-done | bytes 1048592 | tf_op jit(solution)/shard_map/reduce_scatter | solution.py:229
  1890.3 41.4 %all-reduce.2 = (f32[2048]{0:T(1024)S(1)}, f32[2048]{0:T(1024)S(1)}) all-reduce(f32[2048]{0:T(1024)S(1)} %get-tuple-element.295, f32[2048]{0:T(1024)S(1)} %get-tuple-element.343), channel_id=6, replica_groups=mesh['dp'=4,'tensor'=8] {'dp','tensor'}, use_global_device_ids=true, to_apply=%region_16.17.clone | all-reduce | flops 4096 | bytes 32768
  1937.3 96.4 %reduce-scatter.22.cloned.1.call-done = f32[64,512]{1,0:T(8,128)} async-done(((f32[2048,512]{1,0:T(8,128)}), f32[64,512]{1,0:T(8,128)}) %reduce-scatter.22.cloned.1.call-update) | async-done | bytes 131088 | tf_op jit(solution)/shard_map/reduce_scatter | solution.py:260
  2033.7 144.2 %reduce-scatter.24.cloned.1.call-done = f32[64,512]{1,0:T(8,128)} async-done(((f32[2048,512]{1,0:T(8,128)}), f32[64,512]{1,0:T(8,128)}) %reduce-scatter.24.cloned.1.call-update) | async-done | bytes 131088 | tf_op jit(solution)/shard_map/reduce_scatter | solution.py:261
  (328 shorter events, 178.5 us)
Async XLA Ops:
  7.2 198.3 %copy-start = (bf16[256,2048]{1,0:T(8,128)(2,1)S(1)}, bf16[256,2048]{1,0:T(8,128)(2,1)}, u32[]{:S(2)}) copy-start(bf16[256,2048]{1,0:T(8,128)(2,1)} %param.24) | copy-start | bytes 3145732
  7.2 7.5 copy-start.31
  7.2 55.0 %all-gather.7.cloned.1.call-start = ((), (), s32[]{:S(2)}) async-start(), calls=%async_computation.12 | async-start | bytes 2359296 | tf_op jit(solution)/shard_map/all_gather | solution.py:87
  7.9 104.2 %all-gather.5.cloned.1.call-start = ((), (), s32[]{:S(2)}) async-start(), calls=%async_computation.11 | async-start | bytes 2359296 | tf_op jit(solution)/shard_map/all_gather | solution.py:86
  8.7 486.2 %reduce-scatter.12.cloned.1.call-start = ((), (), s32[]{:S(2)}) async-start(), calls=%async_computation.13 | async-start | bytes 18874368 | tf_op jit(solution)/shard_map/reduce_scatter | solution.py:127
  13.9 9.6 copy-start.35
  14.7 8.8 copy-start.21
  113.7 12.7 copy-start.15
  120.2 9.5 copy-start.9
  202.0 11.6 copy-start.5
  213.6 510.1 %all-gather.9.cloned.1.call-start = ((), (), s32[]{:S(2)}) async-start(), calls=%async_computation.14 | async-start | bytes 18874368 | tf_op jit(solution)/shard_map/all_gather | solution.py:130
  494.9 606.0 %reduce-scatter.16.cloned.1.call-start = ((), (), s32[]{:S(2)}) async-start(), calls=%async_computation.16 | async-start | bytes 18874368 | tf_op jit(solution)/shard_map/reduce_scatter | solution.py:166
  495.6 244.1 %copy-start.33 = (f32[2048]{0:T(1024)S(1)}, f32[2048]{0:T(1024)}, u32[]{:S(2)}) copy-start(f32[2048]{0:T(1024)} %param.20) | copy-start | bytes 24580
  741.9 11.0 copy-start.11
  741.9 11.0 copy-start.37
  787.1 15.3 copy-start.38
  819.7 509.7 %all-gather.11.cloned.1.call-start = ((), (), s32[]{:S(2)}) async-start(), calls=%async_computation.17 | async-start | bytes 18874368 | tf_op jit(solution)/shard_map/all_gather | solution.py:167
  1100.9 671.6 %reduce-scatter.28.cloned.1.call-start = ((), (), s32[]{:S(2)}) async-start(), calls=%async_computation.23 | async-start | bytes 5242880 | tf_op jit(solution)/shard_map/reduce_scatter | solution.py:246
  1115.1 660.2 %reduce-scatter.30.cloned.1.call-start = ((), (), s32[]{:S(2)}) async-start(), calls=%async_computation.24 | async-start | bytes 5242880 | tf_op jit(solution)/shard_map/reduce_scatter | solution.py:249
  1129.6 648.6 %reduce-scatter.32.cloned.1.call-start = ((), (), s32[]{:S(2)}) async-start(), calls=%async_computation.25 | async-start | bytes 5242880 | tf_op jit(solution)/shard_map/reduce_scatter | solution.py:255
  1129.6 14.8 copy-start.16
  1129.6 15.7 copy-start.18
  1144.4 636.7 %reduce-scatter.14.cloned.1.call-start = ((), (), s32[]{:S(2)}) async-start(), calls=%async_computation.15 | async-start | bytes 9437184 | tf_op jit(solution)/shard_map/reduce_scatter | solution.py:142
  1160.5 169.0 %copy-start.30 = (f32[2048]{0:T(1024)S(1)}, f32[2048]{0:T(1024)}, u32[]{:S(2)}) copy-start(f32[2048]{0:T(1024)} %copy-done.29) | copy-start | bytes 24580
  1160.5 169.0 %copy-start.34 = (f32[2048]{0:T(1024)S(1)}, f32[2048]{0:T(1024)}, u32[]{:S(2)}) copy-start(f32[2048]{0:T(1024)} %param.20) | copy-start | bytes 24580
  1160.5 624.2 %reduce-scatter.20.cloned.1.call-start = ((), (), s32[]{:S(2)}) async-start(), calls=%async_computation.19 | async-start | bytes 1310720 | tf_op jit(solution)/shard_map/reduce_scatter | solution.py:243
  1380.6 16.7 slice-start
  1380.6 16.7 slice-start.1
  1380.6 18.1 slice-start.2
  1380.7 19.2 slice-start.3
  1411.0 15.1 slice-start.4
  1417.5 8.6 slice-start.5
  1457.3 15.2 slice-start
  1457.3 15.2 slice-start.1
  1457.3 15.9 slice-start.2
  1457.3 17.1 slice-start.3
  1485.7 15.8 slice-start.4
  1492.8 8.6 slice-start.5
  1532.5 15.4 slice-start
  1532.5 15.4 slice-start.1
  1532.5 16.0 slice-start.2
  1532.5 17.2 slice-start.3
  1560.8 7.4 copy-start.39
  1560.8 15.9 slice-start.4
  1568.2 8.5 slice-start.5
  1607.7 15.3 slice-start
  1607.7 15.3 slice-start.1
  1607.7 15.9 slice-start.2
  1607.7 17.1 slice-start.3
  1635.8 15.6 slice-start.4
  1642.9 8.5 slice-start.5
  1684.0 102.4 %reduce-scatter.26.cloned.1.call-start = ((), (), s32[]{:S(2)}) async-start(), calls=%async_computation.22 | async-start | bytes 1310720 | tf_op jit(solution)/shard_map/reduce_scatter | solution.py:252
  1684.1 14.1 slice-start.6
  1687.4 10.8 slice-start.7
  1687.4 10.8 slice-start.8
  1687.4 10.8 slice-start.9
  1687.4 10.8 copy-start.7
  1701.6 9.7 copy-start.20
  1701.6 9.7 copy-start.22
  1701.6 186.0 %reduce-scatter.18.cloned.1.call-start = ((), (), s32[]{:S(2)}) async-start(), calls=%async_computation.18 | async-start | bytes 9437184 | tf_op jit(solution)/shard_map/reduce_scatter | solution.py:229
  1727.4 306.3 %reduce-scatter.22.cloned.1.call-start = ((), (), s32[]{:S(2)}) async-start(), calls=%async_computation.20 | async-start | bytes 4325376 | tf_op jit(solution)/shard_map/reduce_scatter | solution.py:260
  1743.3 434.7 %reduce-scatter.24.cloned.1.call-start = ((), (), s32[]{:S(2)}) async-start(), calls=%async_computation.21 | async-start | bytes 4325376 | tf_op jit(solution)/shard_map/reduce_scatter | solution.py:261
  1770.8 10.3 copy-start.10
  1772.4 115.2 %copy-start.32 = (f32[2048]{0:T(1024)S(1)}, f32[2048]{0:T(1024)}, u32[]{:S(2)}) copy-start(f32[2048]{0:T(1024)} %param.19) | copy-start | bytes 24580
  (37 other events, 153.5 us)
Sparse Core Ops, SparseCore 0:
  10.2 51.9 all-gather.6
  64.3 47.7 all-gather.4
  213.8 281.0 reduce-scatter.11
  497.0 226.6 all-gather.8
  819.9 280.9 reduce-scatter.15
  1102.8 226.6 all-gather.10
  1332.0 42.6 reduce-scatter.27
  1377.4 44.5 reduce-scatter.29
  1424.5 44.4 reduce-scatter.31
  1472.9 149.0 reduce-scatter.13
  1684.2 23.2 reduce-scatter.19
  1710.0 24.8 reduce-scatter.25
  1738.6 149.0 reduce-scatter.17
  1890.5 143.2 reduce-scatter.21
  2036.5 141.3 reduce-scatter.23
where the time goes:
time: 2200 us; the launch traced here: 2180 us
  waiting for transfers between devices  1380 us (63%)
  matrix products  437 us (20%)
  other arithmetic  178 us (8%)
  local copies, waits for them, and re-layouts  110 us (5%)
  blocking collectives  41.4 us (2%)
    reduce_scatter x1, waiting for transfers between devices, local(): lax.psum_scatter(attn_part, 'tensor', scatter_dimension=0, tiled=True)  281 us
    reduce_scatter x1, waiting for transfers between devices, local(): lax.psum_scatter(norm_two_part, 'tensor', scatter_dimension=0, tiled=True)  281 us
    all_gather x1, waiting for transfers between devices, local(): attn_full = lax.all_gather(attn_share, 'tensor', axis=0, tiled=True)  228 us
    all_gather x1, waiting for transfers between devices, local(): norm_two_full = lax.all_gather(norm_two_share, 'tensor', axis=0, tiled=True)  169 us
    reduce_scatter x1, waiting for transfers between devices, local(): lax.psum_scatter(value_full, ('dp', 'tensor'), scatter_dimension=0, tiled...  144 us
    reduce_scatter x1, waiting for transfers between devices, local(): lax.psum_scatter(norm_one_part.astype(jnp.bfloat16), 'tensor', scatter_di...  99.4 us
    reduce_scatter x1, waiting for transfers between devices, local(): lax.psum_scatter(key_full, ('dp', 'tensor'), scatter_dimension=0, tiled=T...  96.4 us
    dot_general x4, matrix products, backward_block(): jnp.einsum('qhd,kd->hqk', grad_rows, value_rows, preferred_element_type=f32)  62.5 us
  transfers between devices with their start and end apart: 15, of which 9 were waited for; matrix products, arithmetic and copies ran while one was open for 24% of the time, Pallas kernels for 0%

commit v1 on v0

v1 whole, which is shorter than its diff:
```python
import functools
import math

import jax
import jax.numpy as jnp
from jax import lax
from jax.experimental import pallas as pl
from jax.experimental.pallas import tpu as pltpu
from jax.sharding import PartitionSpec as P

H = 32
KVH = 8
HD = 64
SEQ_LEN = 2048
QB = 256
WIDE = 512

RESID = 0.22
ATTN_SCALE = 0.015625
EPSILON = 1e-05
THETA_LOG = math.log(10000000.0)
MASKED = -1e30

f32 = jnp.float32
bf16 = jnp.bfloat16
NN = (((1,), (0,)), ((), ()))
NT = (((1,), (1,)), ((), ()))
TN = (((0,), (0,)), ((), ()))


def mm(left, right, dims):
    return lax.dot_general(left, right, dims, preferred_element_type=f32)


def grant(mib):
    return pltpu.CompilerParams(vmem_limit_bytes=mib * 1024 * 1024)


def cost(flops, nbytes):
    return pl.CostEstimate(flops=int(flops), bytes_accessed=int(nbytes), transcendentals=0)


def rope_tables(count):
    positions = jnp.arange(count, dtype=jnp.int32).astype(f32)[:, None]
    lane = jnp.arange(128, dtype=jnp.int32) % (HD // 2)
    freqs = jnp.exp(-THETA_LOG * (2 * lane).astype(f32) / HD)[None, :]
    angle_rows = positions * freqs
    return (jnp.cos(angle_rows), jnp.sin(angle_rows))


def widen(table, count):
    return table if count == 128 else jnp.concatenate([table] * (count // 128), 1)


def swap_halves(rows):
    count = rows.shape[1]
    lane = lax.broadcasted_iota(jnp.int32, rows.shape, 1)
    ahead = pltpu.roll(rows, count - HD // 2, 1)
    behind = pltpu.roll(rows, HD // 2, 1)
    return jnp.where(lane % HD < HD // 2, ahead, behind)


def half_sign(shape):
    lane = lax.broadcasted_iota(jnp.int32, shape, 1)
    return jnp.where(lane % HD < HD // 2, -1.0, 1.0)


def rotate(rows, cosines, sines):
    count = rows.shape[1]
    turned = swap_halves(rows) * half_sign(rows.shape)
    return rows * widen(cosines, count) + turned * widen(sines, count)


def unrotate(rows, cosines, sines):
    count = rows.shape[1]
    turned = swap_halves(rows * widen(sines, count)) * half_sign(rows.shape)
    return rows * widen(cosines, count) - turned


def front_kernel(
    length_ref,
    rows_ref,
    gain_ref,
    wq_ref,
    wkv_ref,
    cos_ref,
    sin_ref,
    normed_ref,
    q_ref,
    k_ref,
    kt_ref,
    v_ref,
    vt_ref,
):
    rows = rows_ref[...].astype(f32)
    row_scale = lax.rsqrt(jnp.mean(rows * rows, axis=-1, keepdims=True) + EPSILON)
    normed_ref[...] = (rows * row_scale * gain_ref[...]).astype(bf16)
    normed = normed_ref[...]
    cosines = cos_ref[...]
    sines = sin_ref[...]
    q_raw = mm(normed, wq_ref[...], NN)
    q_ref[...] = (rotate(q_raw, cosines, sines).astype(bf16).astype(f32) * ATTN_SCALE).astype(bf16)
    kv_raw = mm(normed, wkv_ref[...], NN)
    lane = lax.broadcasted_iota(jnp.int32, kv_raw.shape, 1)
    position = pl.program_id(0) * QB + lax.broadcasted_iota(jnp.int32, kv_raw.shape, 0)
    turned = rotate(kv_raw, cosines, sines)
    keys = jnp.where(lane < HD, turned, 0.0)
    blocked = jnp.where((lane == HD) & (position >= length_ref[0]), MASKED, 0.0)
    k_ref[...] = (keys + blocked).astype(bf16)
    kt_ref[...] = keys.T.astype(bf16)
    values = jnp.concatenate([kv_raw[:, HD:], kv_raw[:, :HD]], 1)
    values = jnp.where(lane < HD, values, 1.0)
    v_ref[...] = values.astype(bf16)
    vt_ref[...] = values.T.astype(bf16)


def front(length, hidden, gain, w_query, w_kv, cosines, sines):
    count, width = hidden.shape
    q_cols = w_query.shape[1]
    row = lambda i, s: (i, 0)
    col = lambda i, s: (0, i)
    whole = lambda i, s: (0, 0)
    return pl.pallas_call(
        front_kernel,
        grid_spec=pltpu.PrefetchScalarGridSpec(
            num_scalar_prefetch=1,
            grid=(count // QB,),
            in_specs=[
                pl.BlockSpec((QB, width), row),
                pl.BlockSpec((1, width), whole),
                pl.BlockSpec((width, q_cols), whole),
                pl.BlockSpec((width, 128), whole),
                pl.BlockSpec((QB, 128), row),
                pl.BlockSpec((QB, 128), row),
            ],
            out_specs=[
                pl.BlockSpec((QB, width), row),
                pl.BlockSpec((QB, q_cols), row),
                pl.BlockSpec((QB, 128), row),
                pl.BlockSpec((128, QB), col),
                pl.BlockSpec((QB, 128), row),
                pl.BlockSpec((128, QB), col),
            ],
        ),
        out_shape=[
            jax.ShapeDtypeStruct((count, width), bf16),
            jax.ShapeDtypeStruct((count, q_cols), bf16),
            jax.ShapeDtypeStruct((count, 128), bf16),
            jax.ShapeDtypeStruct((128, count), bf16),
            jax.ShapeDtypeStruct((count, 128), bf16),
            jax.ShapeDtypeStruct((128, count), bf16),
        ],
        cost_estimate=cost(2 * count * width * (q_cols + 128), 5 * count * width),
        name="norm_and_project",
    )(length, hidden, gain, w_query, w_kv, cosines, sines)


def head_slab(rows, head, fill):
    pair = rows[:, 128 * (head // 2) : 128 * (head // 2) + 128]
    if head % 2:
        pair = jnp.concatenate([pair[:, HD:], pair[:, :HD]], 1)
    lane = lax.broadcasted_iota(jnp.int32, pair.shape, 1)
    other = jnp.where(lane == HD, jnp.full(pair.shape, fill, f32), 0.0).astype(pair.dtype)
    return jnp.where(lane < HD, pair, other)


def causal(keys_count, rows_count):
    key = lax.broadcasted_iota(jnp.int32, (keys_count, rows_count), 0)
    return key <= lax.broadcasted_iota(jnp.int32, (keys_count, rows_count), 1)


def attend_kernel(heads, q_ref, k_ref, vt_ref, o_ref, lse_ref, slab_ref, high_ref, total_ref):
    block = pl.program_id(0)
    rows = q_ref[...]
    for head in range(heads):
        slab_ref[head] = head_slab(rows, head, 1.0)
    high_ref[...] = jnp.full(high_ref.shape, MASKED, f32)
    total_ref[...] = jnp.zeros(total_ref.shape, f32)

    def step(start, width, diagonal):
        keys = k_ref[pl.ds(start, width), :]
        values = vt_ref[:, pl.ds(start, width)]
        scores = [mm(keys, slab_ref[head], NT) for head in range(heads)]
        for head in range(heads):
            score = scores[head]
            if diagonal:
                score = jnp.where(causal(width, QB), score, MASKED)
            old = high_ref[head : head + 1, :]
            new = jnp.maximum(old, jnp.max(score, axis=0, keepdims=True))
            probs = jnp.exp(score - new).astype(bf16)
            high_ref[head : head + 1, :] = new
            total_ref[head] = total_ref[head] * jnp.exp(old - new) + mm(values, probs, NN)

    def body(index, carry):
        step(pl.multiple_of(index * WIDE, WIDE), WIDE, False)
        return carry

    lax.fori_loop(0, block // 2, body, 0)

    @pl.when(block % 2 == 1)
    def _():
        step(pl.multiple_of((block - 1) * QB, QB), QB, False)

    step(pl.multiple_of(block * QB, QB), QB, True)
    outs = []
    for head in range(heads):
        total = total_ref[head]
        mass = total[HD : HD + 1, :]
        lse_ref[head : head + 1, :] = high_ref[head : head + 1, :] + jnp.log(mass)
        outs.append(total[:HD, :] * (1.0 / mass))
    o_ref[...] = jnp.concatenate(outs, 0).T.astype(bf16)


def attend(queries, keys, values_t):
    count, q_cols = queries.shape
    heads = q_cols // HD
    return pl.pallas_call(
        functools.partial(attend_kernel, heads),
        grid=(count // QB,),
        in_specs=[
            pl.BlockSpec((QB, q_cols), lambda i: (i, 0)),
            pl.BlockSpec((count, 128), lambda i: (0, 0)),
            pl.BlockSpec((128, count), lambda i: (0, 0)),
        ],
        out_specs=[
            pl.BlockSpec((QB, q_cols), lambda i: (i, 0)),
            pl.BlockSpec((8, QB), lambda i: (0, i)),
        ],
        out_shape=[
            jax.ShapeDtypeStruct((count, q_cols), bf16),
            jax.ShapeDtypeStruct((8, count), f32),
        ],
        scratch_shapes=[
            pltpu.VMEM((heads, QB, 128), bf16),
            pltpu.VMEM((8, QB), f32),
            pltpu.VMEM((heads, 128, QB), f32),
        ],
        cost_estimate=cost(heads * count * count * 512, 4 * count * q_cols),
        name="attend",
    )(queries, keys, values_t)


def attend_back_kernel(
    heads,
    q_ref,
    do_ref,
    o_ref,
    lse_ref,
    k_ref,
    kt_ref,
    v_ref,
    cos_ref,
    sin_ref,
    out_ref,
    qs_ref,
    ds_ref,
    delta_ref,
    dq_ref,
    dk_ref,
    dv_ref,
):
    block = pl.program_id(0)
    blocks = pl.num_programs(0)
    q_cols = heads * HD

    @pl.when(block == 0)
    def _():
        dk_ref[...] = jnp.zeros(dk_ref.shape, f32)
        dv_ref[...] = jnp.zeros(dv_ref.shape, f32)

    rows = q_ref[...]
    grads = do_ref[...]
    product = (grads.astype(f32) * o_ref[...].astype(f32)).T
    for head in range(heads):
        qs_ref[head] = head_slab(rows, head, 1.0)
        ds_ref[head] = head_slab(grads, head, 0.0)
        delta_ref[head : head + 1, :] = jnp.sum(
            product[head * HD : (head + 1) * HD, :], axis=0, keepdims=True
        )
    dq_ref[...] = jnp.zeros(dq_ref.shape, f32)

    def step(start, diagonal):
        here = pl.ds(start, QB)
        keys = k_ref[here, :]
        keys_t = kt_ref[:, here]
        values = v_ref[here, :]
        dk = dk_ref[here, :]
        dv = dv_ref[here, :]

        def products(head):
            return (mm(keys, qs_ref[head], NT), mm(values, ds_ref[head], NT))

        ready = products(0)
        for head in range(heads):
            score, prob_grad = ready
            if head + 1 < heads:
                ready = products(head + 1)
            probs = jnp.exp(score - lse_ref[head : head + 1, :])
            if diagonal:
                probs = jnp.where(causal(QB, QB), probs, 0.0)
            dv = dv + mm(probs.astype(bf16), ds_ref[head], NN)
            score_grad = (probs * (prob_grad - delta_ref[head : head + 1, :])).astype(bf16)
            dk = dk + mm(score_grad, qs_ref[head], NN)
            dq_ref[head] = dq_ref[head] + mm(keys_t, score_grad, NN)
        dk_ref[here, :] = dk
        dv_ref[here, :] = dv

    def body(index, carry):
        step(pl.multiple_of(index * QB, QB), False)
        return carry

    lax.fori_loop(0, block, body, 0)
    step(pl.multiple_of(block * QB, QB), True)
    dq = jnp.concatenate([dq_ref[head, :HD, :] for head in range(heads)], 0).T * ATTN_SCALE
    here = pl.ds(pl.multiple_of(block * QB, QB), QB)
    out_ref[here, :q_cols] = unrotate(dq, cos_ref[here, :], sin_ref[here, :]).astype(bf16)

    @pl.when(block == blocks - 1)
    def _():
        def finish(index, carry):
            there = pl.ds(pl.multiple_of(index * QB, QB), QB)
            dk = dk_ref[there, :]
            lane = lax.broadcasted_iota(jnp.int32, dk.shape, 1)
            dk = unrotate(jnp.where(lane < HD, dk, 0.0), cos_ref[there, :], sin_ref[there, :])
            dv = dv_ref[there, :]
            out_ref[there, q_cols:] = jnp.concatenate([dk[:, :HD], dv[:, :HD]], 1).astype(bf16)
            return carry

        lax.fori_loop(0, blocks, finish, 0)


def attend_back(queries, out_grads, attended, lse, keys, keys_t, values, cosines, sines):
    count, q_cols = queries.shape
    heads = q_cols // HD
    row = lambda i: (i, 0)
    whole = lambda i: (0, 0)
    return pl.pallas_call(
        functools.partial(attend_back_kernel, heads),
        grid=(count // QB,),
        in_specs=[
            pl.BlockSpec((QB, q_cols), row),
            pl.BlockSpec((QB, q_cols), row),
            pl.BlockSpec((QB, q_cols), row),
            pl.BlockSpec((8, QB), lambda i: (0, i)),
            pl.BlockSpec((count, 128), whole),
            pl.BlockSpec((128, count), whole),
            pl.BlockSpec((count, 128), whole),
            pl.BlockSpec((count, 128), whole),
            pl.BlockSpec((count, 128), whole),
        ],
        out_specs=pl.BlockSpec((count, q_cols + 128), whole),
        out_shape=jax.ShapeDtypeStruct((count, q_cols + 128), bf16),
        scratch_shapes=[
            pltpu.VMEM((heads, QB, 128), bf16),
            pltpu.VMEM((heads, QB, 128), bf16),
            pltpu.VMEM((8, QB), f32),
            pltpu.VMEM((heads, 128, QB), f32),
            pltpu.VMEM((count, 128), f32),
            pltpu.VMEM((count, 128), f32),
        ],
        cost_estimate=cost(heads * count * count * 1280, 10 * count * q_cols),
        name="attend_back",
    )(queries, out_grads, attended, lse, keys, keys_t, values, cosines, sines)


def out_norm_kernel(ids_ref, o_ref, w_ref, rows_ref, gain_ref, middle_ref, normed_ref, sum_ref):
    step = pl.program_id(0)

    @pl.when(step == 0)
    def _():
        sum_ref[...] = jnp.zeros(sum_ref.shape, f32)

    sum_ref[...] += mm(o_ref[0], w_ref[...], NN)

    @pl.when(step == pl.num_programs(0) - 1)
    def _():
        middle = rows_ref[...].astype(f32) + RESID * sum_ref[...]
        middle_ref[...] = middle
        row_scale = lax.rsqrt(jnp.mean(middle * middle, axis=-1, keepdims=True) + EPSILON)
        normed_ref[...] = (middle * row_scale * gain_ref[...]).astype(bf16)


def out_norm(ids, attended, w_out, hidden, gain):
    groups, share, q_cols = attended.shape
    width = hidden.shape[1]
    return pl.pallas_call(
        out_norm_kernel,
        grid_spec=pltpu.PrefetchScalarGridSpec(
            num_scalar_prefetch=1,
            grid=(groups,),
            in_specs=[
                pl.BlockSpec((1, share, q_cols), lambda t, s: (t, 0, 0)),
                pl.BlockSpec((q_cols, width), lambda t, s: (t, 0)),
                pl.BlockSpec((share, width), lambda t, s: (s[0], 0)),
                pl.BlockSpec((1, width), lambda t, s: (0, 0)),
            ],
            out_specs=[
                pl.BlockSpec((share, width), lambda t, s: (0, 0)),
                pl.BlockSpec((share, width), lambda t, s: (0, 0)),
            ],
            scratch_shapes=[pltpu.VMEM((share, width), f32)],
        ),
        out_shape=[
            jax.ShapeDtypeStruct((share, width), f32),
            jax.ShapeDtypeStruct((share, width), bf16),
        ],
        cost_estimate=cost(2 * groups * share * q_cols * width, 2 * groups * q_cols * width),
        name="out_project_and_norm",
    )(ids, attended, w_out, hidden, gain)


def back_norm_kernel(
    parts,
    ids_ref,
    *refs,
):
    part_refs = refs[:parts]
    (
        middle_ref,
        gain_ref,
        cotangent_ref,
        w_ref,
        dh_ref,
        da_ref,
        gain_grad_ref,
        do_ref,
    ) = refs[parts:]

    @pl.when(pl.program_id(0) == 0)
    def _():
        incoming = part_refs[0][...].astype(f32)
        for ref in part_refs[1:]:
            incoming = incoming + ref[...].astype(f32)
        middle = middle_ref[...]
        row_scale = lax.rsqrt(jnp.mean(middle * middle, axis=-1, keepdims=True) + EPSILON)
        normed = middle * row_scale
        gain_grad_ref[...] = jnp.sum(incoming * normed, axis=0, keepdims=True)
        scaled = incoming * gain_ref[...]
        branch = row_scale * (scaled - normed * jnp.mean(scaled * normed, axis=-1, keepdims=True))
        share = middle.shape[0]
        position = ids_ref[0] * share + lax.broadcasted_iota(jnp.int32, (share, 1), 0)
        direct = jnp.where(position < ids_ref[1], cotangent_ref[...].astype(f32), 0.0)
        dh = direct + branch
        dh_ref[...] = dh
        da_ref[...] = (RESID * dh).astype(bf16)

    do_ref[0] = mm(da_ref[...], w_ref[...], NT).astype(bf16)


def back_norm(ids, parts, middle, gain, cotangent, w_out, q_cols):
    share, width = middle.shape
    groups = w_out.shape[0] // q_cols
    whole = lambda t, s: (0, 0)
    return pl.pallas_call(
        functools.partial(back_norm_kernel, len(parts)),
        grid_spec=pltpu.PrefetchScalarGridSpec(
            num_scalar_prefetch=1,
            grid=(groups,),
            in_specs=[pl.BlockSpec((share, width), whole)] * len(parts)
            + [
                pl.BlockSpec((share, width), whole),
                pl.BlockSpec((1, width), whole),
                pl.BlockSpec((share, width), lambda t, s: (s[0], 0)),
                pl.BlockSpec((q_cols, width), lambda t, s: (t, 0)),
            ],
            out_specs=[
                pl.BlockSpec((share, width), whole),
                pl.BlockSpec((share, width), whole),
                pl.BlockSpec((1, width), whole),
                pl.BlockSpec((1, share, q_cols), lambda t, s: (t, 0, 0)),
            ],
        ),
        out_shape=[
            jax.ShapeDtypeStruct((share, width), f32),
            jax.ShapeDtypeStruct((share, width), bf16),
            jax.ShapeDtypeStruct((1, width), f32),
            jax.ShapeDtypeStruct((groups, share, q_cols), bf16),
        ],
        cost_estimate=cost(2 * groups * share * q_cols * width, 2 * groups * q_cols * width),
        name="norm_back_and_project",
    )(ids, *parts, middle, gain, cotangent, w_out)


def in_grad_kernel(ids_ref, d_ref, w_ref, rows_ref, gain_ref, dh_ref, out_ref, sum_ref):
    step = pl.program_id(0)

    @pl.when(step == 0)
    def _():
        sum_ref[...] = jnp.zeros(sum_ref.shape, f32)

    sum_ref[...] += mm(d_ref[0], w_ref[0], NT)

    @pl.when(step == pl.num_programs(0) - 1)
    def _():
        rows = rows_ref[...].astype(f32)
        row_scale = lax.rsqrt(jnp.mean(rows * rows, axis=-1, keepdims=True) + EPSILON)
        normed = rows * row_scale
        scaled = sum_ref[...] * gain_ref[...]
        branch = row_scale * (scaled - normed * jnp.mean(scaled * normed, axis=-1, keepdims=True))
        out_ref[...] = dh_ref[...] + branch


def in_grad(ids, grads, w_qkv, hidden, gain, dh):
    groups, share, cols = grads.shape
    width = hidden.shape[1]
    whole = lambda t, s: (0, 0)
    return pl.pallas_call(
        in_grad_kernel,
        grid_spec=pltpu.PrefetchScalarGridSpec(
            num_scalar_prefetch=1,
            grid=(groups,),
            in_specs=[
                pl.BlockSpec((1, share, cols), lambda t, s: (t, 0, 0)),
                pl.BlockSpec((1, width, cols), lambda t, s: (t, 0, 0)),
                pl.BlockSpec((share, width), lambda t, s: (s[0], 0)),
                pl.BlockSpec((1, width), whole),
                pl.BlockSpec((share, width), whole),
            ],
            out_specs=pl.BlockSpec((share, width), whole),
            scratch_shapes=[pltpu.VMEM((share, width), f32)],
        ),
        out_shape=jax.ShapeDtypeStruct((share, width), f32),
        cost_estimate=cost(2 * groups * share * cols * width, 2 * groups * cols * width),
        name="input_grad",
    )(ids, grads, w_qkv, hidden, gain, dh)


def units_kernel(pieces, shares, ids_ref, *refs):
    piece_refs = refs[:pieces]
    cot_refs = refs[pieces : pieces + shares]
    gate_w_ref, up_w_ref, down_w_ref = refs[pieces + shares : pieces + shares + 3]
    outs = refs[-9:]
    normed_ref, down_ref, act_ref, dgate_ref, dup_ref, dn_ref, mlp_ref, dn_sum, mlp_sum = outs
    step = pl.program_id(0)

    @pl.when(step == 0)
    def _():
        at = 0
        for ref in piece_refs:
            normed_ref[at : at + ref.shape[0], :] = ref[...]
            at += ref.shape[0]
        share = cot_refs[0].shape[0]
        for index, ref in enumerate(cot_refs):
            position = ids_ref[1 + index] * share + lax.broadcasted_iota(jnp.int32, (share, 1), 0)
            masked = jnp.where(position < ids_ref[0], ref[...].astype(f32) * RESID, 0.0)
            down_ref[index * share : (index + 1) * share, :] = masked.astype(bf16)
        dn_sum[...] = jnp.zeros(dn_sum.shape, f32)
        mlp_sum[...] = jnp.zeros(mlp_sum.shape, f32)

    normed = normed_ref[...]
    gate = mm(normed, gate_w_ref[...], NN)
    up = mm(normed, up_w_ref[...], NN)
    dact = mm(down_ref[...], down_w_ref[...], NT)
    sg = jax.nn.sigmoid(gate)
    silu = gate * sg
    act_ref[...] = (silu * up).astype(bf16)
    dgate_ref[...] = (dact * up * sg * (1.0 + gate * (1.0 - sg))).astype(bf16)
    dup_ref[...] = (dact * silu).astype(bf16)
    dn_sum[...] += mm(dgate_ref[...], gate_w_ref[...], NT) + mm(dup_ref[...], up_w_ref[...], NT)
    mlp_sum[...] += mm(act_ref[...], down_w_ref[...], NN)

    @pl.when(step == pl.num_programs(0) - 1)
    def _():
        dn_ref[...] = dn_sum[...].astype(bf16)
        mlp_ref[...] = mlp_sum[...].astype(bf16)


def units(ids, pieces, cotangent, weights, slot, buffers, total_rows):
    w_gate, w_up, w_down = weights
    width, unit_count = w_gate.shape
    rows = sum(piece.shape[0] for piece in pieces)
    shares = ids.shape[0] - 1
    share = rows // shares
    block = min(256, unit_count)
    whole = lambda u, s: (0, 0)
    place = slot * share // rows
    in_specs = [pl.BlockSpec(piece.shape, whole) for piece in pieces]
    for index in range(shares):
        in_specs.append(
            pl.BlockSpec((share, width), functools.partial(lambda k, u, s: (s[1 + k], 0), index))
        )
    in_specs += [
        pl.BlockSpec((width, block), lambda u, s: (0, u)),
        pl.BlockSpec((width, block), lambda u, s: (0, u)),
        pl.BlockSpec((block, width), lambda u, s: (u, 0)),
    ]
    operands = [*pieces, *([cotangent] * shares), w_gate, w_up, w_down]
    aliases = {}
    if buffers is not None:
        for index, buffer in enumerate(buffers):
            aliases[1 + len(operands)] = index
            operands.append(buffer)
            in_specs.append(pl.BlockSpec(memory_space=pl.ANY))
    full = lambda u, s: (place, 0)
    part = lambda u, s: (place, u)
    return pl.pallas_call(
        functools.partial(units_kernel, len(pieces), shares),
        grid_spec=pltpu.PrefetchScalarGridSpec(
            num_scalar_prefetch=1,
            grid=(unit_count // block,),
            in_specs=in_specs,
            out_specs=[
                pl.BlockSpec((rows, width), full),
                pl.BlockSpec((rows, width), full),
                pl.BlockSpec((rows, block), part),
                pl.BlockSpec((rows, block), part),
                pl.BlockSpec((rows, block), part),
                pl.BlockSpec((rows, width), whole),
                pl.BlockSpec((rows, width), whole),
            ],
            scratch_shapes=[pltpu.VMEM((rows, width), f32), pltpu.VMEM((rows, width), f32)],
        ),
        out_shape=[
            jax.ShapeDtypeStruct((total_rows, width), bf16),
            jax.ShapeDtypeStruct((total_rows, width), bf16),
            jax.ShapeDtypeStruct((total_rows, unit_count), bf16),
            jax.ShapeDtypeStruct((total_rows, unit_count), bf16),
            jax.ShapeDtypeStruct((total_rows, unit_count), bf16),
            jax.ShapeDtypeStruct((rows, width), bf16),
            jax.ShapeDtypeStruct((rows, width), bf16),
        ],
        input_output_aliases=aliases,
        compiler_params=grant(58),
        cost_estimate=cost(14 * rows * width * unit_count, 6 * width * unit_count + 20 * rows * width),
        name="swiglu_rows",
    )(ids, *operands)


def ring_order(count):
    inner = 2 if count <= 8 else 4
    outer = count // inner
    cells = [(0, 0)]
    for row in range(outer):
        cells += [(row, c) for c in (range(1, inner) if row % 2 == 0 else range(inner - 1, 0, -1))]
    cells += [(row, 0) for row in range(outer - 1, 0, -1)]
    return [row * inner + c for row, c in cells]


def add_low(left, right):
    return (left.astype(f32) + right.astype(f32)).astype(bf16)


def ring_reduce(parts_up, parts_down, far, ahead, behind):
    half = far.shape[0] // 2
    got_up = lax.ppermute(far[:half], "tensor", ahead)
    got_down = lax.ppermute(far[half:], "tensor", behind)
    first = True
    for up, down in zip(reversed(parts_up), reversed(parts_down)):
        if first:
            up = jnp.concatenate([add_low(up[:half], got_up), up[half:]], 0)
            down = jnp.concatenate([down[:half], add_low(down[half:], got_down)], 0)
            first = False
        else:
            up = add_low(up, got_up)
            down = add_low(down, got_down)
        got_up = lax.ppermute(up, "tensor", ahead)
        got_down = lax.ppermute(down, "tensor", behind)
    return got_up, got_down


def local(
    hidden_in,
    seq_lengths,
    out_grad,
    attn_gain,
    mlp_gain,
    w_query,
    w_key,
    w_value,
    w_out,
    w_gate,
    w_up,
    w_down,
):
    rows_total, width = hidden_in.shape
    q_cols = w_query.shape[1]
    heads_here = q_cols // HD
    groups = lax.axis_size("tensor")
    replicas = lax.axis_size("dp")
    member = lax.axis_index("tensor")
    replica = lax.axis_index("dp")
    share = rows_total // groups
    order = ring_order(groups)
    place = [order.index(i) for i in range(groups)]
    ahead = [(order[i], order[(i + 1) % groups]) for i in range(groups)]
    behind = [(b, a) for a, b in ahead]
    half_way = groups // 2
    table = [
        [order[(place[i] + d) % groups] for d in range(-half_way + 1, half_way + 1)]
        for i in range(groups)
    ]
    near = jnp.asarray(table, jnp.int32)[member]
    at = lambda d: near[d + half_way - 1]
    length = seq_lengths[0]
    cosines, sines = rope_tables(rows_total)
    gain_one = attn_gain[None, :]
    gain_two = mlp_gain[None, :]

    def quarter(array):
        count = array.shape[0] // replicas
        return lax.dynamic_slice_in_dim(array, replica * count, count, 0)

    w_out_all = lax.all_gather(quarter(w_out), ("tensor", "dp"), axis=0, tiled=True)
    kv_of = [i * heads_here // (H // KVH) for i in range(groups)]
    pick = lambda w: jnp.stack([w[:, h * HD : (h + 1) * HD] for h in kv_of], 0)
    kv_send = jnp.concatenate([pick(w_key), pick(w_value)], 2)
    w_kv = lax.all_to_all(kv_send, "tensor", 0, 0, tiled=True).reshape(width, 2 * HD)
    w_qkv = jnp.concatenate([w_query, w_kv], 1)
    w_qkv_all = lax.all_gather(quarter(w_qkv), ("tensor", "dp"), axis=0, tiled=True)
    w_qkv_all = w_qkv_all.reshape(groups, width, q_cols + 2 * HD)

    normed_one, queries, keys, keys_t, values, values_t = front(
        seq_lengths, hidden_in, gain_one, w_query, w_kv, cosines, sines
    )
    attended, lse = attend(queries, keys, values_t)
    attended_rows = lax.all_to_all(
        attended.reshape(groups, share, q_cols), "tensor", 0, 0, tiled=True
    )
    own_id = jnp.stack([member, length])
    middle, normed_two = out_norm(own_id, attended_rows, w_out_all, hidden_in, gain_two)

    weights = (w_gate, w_up, w_down)
    buffers = None
    dn_up, dn_down, mlp_up, mlp_down = [], [], [], []
    *buffers, dn_own, mlp_own = units(
        jnp.stack([length, member]), [normed_two], out_grad, weights, groups - 2, None, rows_total
    )
    from_behind = from_ahead = normed_two
    for distance in range(1, half_way):
        from_behind = lax.ppermute(from_behind, "tensor", ahead)
        from_ahead = lax.ppermute(from_ahead, "tensor", behind)
        ids = jnp.stack([length, at(-distance), at(distance)])
        *buffers, dn, mlp = units(
            ids,
            [from_behind, from_ahead],
            out_grad,
            weights,
            2 * (distance - 1),
            buffers,
            rows_total,
        )
        dn_down.append(dn[:share])
        dn_up.append(dn[share:])
        mlp_down.append(mlp[:share])
        mlp_up.append(mlp[share:])
    top = lax.ppermute(from_behind[: share // 2], "tensor", ahead)
    bottom = lax.ppermute(from_ahead[share // 2 :], "tensor", behind)
    *buffers, dn_far, mlp_far = units(
        jnp.stack([length, at(half_way)]),
        [top, bottom],
        out_grad,
        weights,
        groups - 1,
        buffers,
        rows_total,
    )
    normed_ring, down_ring, act, dgate, dup = buffers

    dn_a, dn_b = ring_reduce(dn_up, dn_down, dn_far, ahead, behind)
    middle_grad, branch_grad, mlp_gain_part, do_send = back_norm(
        own_id, [dn_own, dn_a, dn_b], middle, gain_two, out_grad, w_out_all, q_cols
    )
    attended_grad = lax.all_to_all(do_send, "tensor", 0, 0, tiled=True).reshape(rows_total, q_cols)

    mlp_far, _ = lax.optimization_barrier((mlp_far, dn_a))
    mlp_a, mlp_b = ring_reduce(mlp_up, mlp_down, mlp_far, ahead, behind)
    layer_out = (
        middle + RESID * (mlp_own.astype(f32) + mlp_a.astype(f32) + mlp_b.astype(f32))
    ).astype(bf16)

    down_wgrad = mm(act, down_ring, TN).astype(bf16)
    gate_wgrad = mm(normed_ring, dgate, TN).astype(bf16)
    up_wgrad = mm(normed_ring, dup, TN).astype(bf16)
    attended_cols = jnp.swapaxes(attended_rows, 0, 1).reshape(share, groups * q_cols)
    out_wgrad = mm(attended_cols, branch_grad, TN).astype(bf16)

    qkv_grad = attend_back(
        queries, attended_grad, attended, lse, keys, keys_t, values, cosines, sines
    )
    qkv_rows = lax.all_to_all(
        qkv_grad.reshape(groups, share, q_cols + 2 * HD), "tensor", 0, 0, tiled=True
    )
    input_grad = in_grad(own_id, qkv_rows, w_qkv_all, hidden_in, gain_one, middle_grad)

    qkv_wgrad = mm(normed_one, qkv_grad, TN)
    attn_gain_part = jnp.sum(qkv_wgrad * w_qkv.astype(f32), axis=1) / attn_gain
    small = jnp.concatenate(
        [
            qkv_wgrad[:, q_cols:],
            attn_gain_part[:, None],
            mlp_gain_part[0][:, None],
            jnp.zeros((width, 126), f32),
        ],
        1,
    )
    over_dp = lambda a, d: lax.psum_scatter(a, "dp", scatter_dimension=d, tiled=True)
    small = over_dp(small, 0)
    pieces = lax.all_to_all(
        small.reshape(groups, small.shape[0] // groups, 256), "tensor", 0, 0, tiled=True
    )
    gains = jnp.sum(pieces[:, :, 128:130], axis=0)
    kv = pieces[:, :, :128].reshape(KVH, groups // KVH, -1, 128).sum(axis=1)
    kv = jnp.swapaxes(kv, 0, 1)
    key_wgrad = kv[:, :, :HD].reshape(-1, KVH * HD)
    value_wgrad = kv[:, :, HD:].reshape(-1, KVH * HD)
    query_wgrad = over_dp(qkv_wgrad[:, :q_cols].astype(bf16), 0).astype(f32)
    gate_wgrad = over_dp(gate_wgrad, 0).astype(f32)
    up_wgrad = over_dp(up_wgrad, 0).astype(f32)
    down_wgrad = over_dp(down_wgrad, 1).astype(f32)
    out_wgrad = over_dp(out_wgrad, 1)
    out_wgrad = lax.psum_scatter(out_wgrad, "tensor", scatter_dimension=0, tiled=True).astype(f32)
    return (
        layer_out,
        input_grad,
        gains[:, 0],
        gains[:, 1],
        query_wgrad,
        key_wgrad,
        value_wgrad,
        out_wgrad,
        gate_wgrad,
        up_wgrad,
        down_wgrad,
    )


def solution(mesh):
    placed = (
        P("dp", None),
        P("dp"),
        P("dp", None),
        P(),
        P(),
        P(None, "tensor"),
        P("tensor", None),
        P("tensor", None),
        P("tensor", None),
        P(None, "tensor"),
        P(None, "tensor"),
        P("tensor", None),
    )
    return jax.shard_map(
        local,
        mesh=mesh,
        in_specs=placed,
        out_specs=(
            P(("dp", "tensor"), None),
            P(("dp", "tensor"), None),
            P(("dp", "tensor")),
            P(("dp", "tensor")),
            P("dp", "tensor"),
            P(("dp", "tensor"), None),
            P(("dp", "tensor"), None),
            P("tensor", "dp"),
            P("dp", "tensor"),
            P("dp", "tensor"),
            P("tensor", "dp"),
        ),
        check_vma=False,
    )
```

time: 2200 us -> 892 us (0.41)
  waiting for transfers between devices: 1380 us -> 425 us
  matrix products: 437 us -> 55.6 us
  Pallas kernels: 0 us -> 229 us
  other arithmetic: 178 us -> 47 us
  local copies, waits for them, and re-layouts: 110 us -> 51.9 us
  starting transfers between devices: 0.99 us -> 57.9 us
  blocking collectives: 41.4 us -> 0 us
    reduce_scatter x11 -> x7, waiting for transfers between devices: 902 us -> 173 us  [the longest x6 109 us: local(): lax.psum_scatter(a, 'dp', scatter_dimension=d, tiled=True)]
    all_gather x4 -> x2, waiting for transfers between devices: 478 us -> 0.02 us  [the longest x1 0.02 us: local(): lax.all_gather(quarter(w_qkv), ('tensor', 'dp'), axis=0, tiled=True)]
    dot_general x49 -> x5, matrix products: 437 us -> 55.6 us  [mm(): return lax.dot_general(left, right, dims, preferred_element_type=f32)]
    pallas_call x0 -> x11, Pallas kernels: none -> 229 us  [the longest x5 116 us: units(): pl.pallas_call(functools.partial(units_kernel, len(pieces), shares), grid...]
    ppermute x0 -> x24, waiting for transfers between devices: none -> 195 us  [the longest x6 131 us: ring_reduce(): got_up = lax.ppermute(up, 'tensor', ahead)]
    convert_element_type x18 -> x12, other arithmetic: 87.5 us -> 26.6 us  [the longest x6 12.6 us: add_low(): return (left.astype(f32) + right.astype(f32)).astype(bf16)]
    dynamic_update_slice x10 -> x0, local copies, waits for them, and re-layouts: 58.6 us -> none  [the longest x8 46.8 us: local(): lax.map(forward_block, jnp.arange(blocks, dtype=jnp.int32))]
    all_to_all x0 -> x5, waiting for transfers between devices: none -> 57.7 us  [the longest x1 27.1 us: local(): lax.all_to_all(attended.reshape(groups, share, q_cols), 'tensor', 0, 0, t...]
  transfers between devices with their start and end apart: 15 -> 38, of which waited for: 9 -> 20; matrix products, arithmetic and copies ran while one was open for 24% -> 15% of each run, Pallas kernels for 0% -> 21%
where the time goes in v1:
time: 892 us; the launch traced here: 882 us
  waiting for transfers between devices  425 us (48%)
  Pallas kernels  229 us (26%)
  starting transfers between devices  57.9 us (6%)
  matrix products  55.6 us (6%)
  local copies, waits for them, and re-layouts  51.9 us (6%)
  other arithmetic  47 us (5%)
  between operations  15.5 us (2%)
    ppermute x6, waiting for transfers between devices, ring_reduce(): got_up = lax.ppermute(up, 'tensor', ahead)  131 us
    pallas_call x5, Pallas kernels, units(): pl.pallas_call(functools.partial(units_kernel, len(pieces), shares), grid...  116 us
    reduce_scatter x6, waiting for transfers between devices, local(): lax.psum_scatter(a, 'dp', scatter_dimension=d, tiled=True)  109 us
    reduce_scatter x1, waiting for transfers between devices, local(): lax.psum_scatter(out_wgrad, 'tensor', scatter_dimension=0, tiled=True)  63.9 us
    dot_general x5, matrix products, mm(): return lax.dot_general(left, right, dims, preferred_element_type=f32)  55.6 us
    ppermute x6, waiting for transfers between devices, ring_reduce(): got_down = lax.ppermute(down, 'tensor', behind)  38.1 us
    pallas_call x1, Pallas kernels, attend_back(): pl.pallas_call(functools.partial(attend_back_kernel, heads), grid=(count...  37.1 us
    all_to_all x1, waiting for transfers between devices, local(): lax.all_to_all(attended.reshape(groups, share, q_cols), 'tensor', 0, 0, t...  27.1 us
  transfers between devices with their start and end apart: 38, of which 20 were waited for; matrix products, arithmetic and copies ran while one was open for 15% of the time, Pallas kernels for 21%

profile of v1, /device:TPU:0, one launch (start us, length us, event | category | flops | bytes accessed | tf_op | source)
XLA Modules:
  0.0 882.5 jit_solution(1653632463483653007)
XLA Ops:
  20.4 7.3 all-to-all-start
  28.3 5.5 multiply_sine_fusion
  33.8 11.4 %all-to-all-done = bf16[8,256,128]{2,1,0:T(8,128)(2,1)S(1)} async-done(((bf16[8,256,128]{2,1,0:T(8,128)(2,1)}), bf16[8,256,128]{2,1,0:T(8,128)(2,1)S(1)}, u32[]{:S(2)}, u32[]{:S(2)}) %all-to-all-start) | async-done | bytes 524320 | tf_op jit(solution)/shard_map/all_to_all | solution.py:707
  46.1 14.6 %norm_and_project.1 = (bf16[2048,2048]{1,0:T(8,128)(2,1)}, bf16[2048,256]{1,0:T(8,128)(2,1)}, bf16[2048,128]{1,0:T(8,128)(2,1)}, bf16[128,2048]{1,0:T(8,128)(2,1...) custom-call(s32[1]{0:T(128)S(6)} %copy.114.length_ref, bf16[2048,2048]{1,0:T(8,128)(2,1)} %rows_ref.5, ...), custom_call_target="tpu_custom_call" | custom-call | flops 3221225472 | bytes 20971520 | tf_op jit(solution)/shard_map/norm_and_project/pallas_call | solution.py:123
  60.7 22.7 %attend.1 = (bf16[2048,256]{1,0:T(8,128)(2,1)}, f32[8,2048]{1,0:T(8,128)}) custom-call(bf16[2048,256]{1,0:T(8,128)(2,1)} %get-tuple-element.61.q_ref, bf16[2048,128]{1,0:T(8,128)(2,1)} %get-tuple-element.62.k_ref, bf16[128,2048]{1,0:T(8,128)(2,1)} %get-tuple-element.63.vt_ref), custom_call_target="tpu_custom_call" | custom-call | flops 8589934592 | bytes 2097152 | tf_op jit(solution)/shard_map/attend/pallas_call | solution.py:217
  83.3 3.8 all-to-all-start.1
  89.8 27.1 %all-to-all-done.1.o_ref = bf16[8,256,256]{2,1,0:T(8,128)(2,1)S(1)} async-done(((bf16[8,256,256]{2,1,0:T(8,128)(2,1)}), bf16[8,256,256]{2,1,0:T(8,128)(2,1)S(1)}, u32[]{:S(2)}, u32[]{:S(2)}) %all-to-all-start.1) | async-done | bytes 1048608 | tf_op jit(solution)/shard_map/all_to_all | solution.py:716
  117.9 11.2 %out_project_and_norm.1 = (f32[256,2048]{1,0:T(8,128)}, bf16[256,2048]{1,0:T(8,128)(2,1)}) custom-call(s32[2]{0:T(128)} %pad_add_fusion.ids_ref, bf16[8,256,256]{2,1,0:T(8,128)(2,1)} %copy-done.2, bf16[2048,2048]{1,0:T(8,128)(2,1)} %all-gather.3.cloned.1.call-done.w_ref.refs_6_, bf16[2048,2048]{1,0:T(8,128)(2,1)} %rows_ref.5, f32[1,2048]{1,0:T(1,128)} %bitcast.73), custom_call_target="tpu_custom_call" | custom-call | flops 2147483648 | bytes 8388608 | tf_op jit(solution)/shard_map/out_project_and_norm/pallas_call | solution.py:386
  129.0 1.5 collective-permute-start
  132.3 1.9 pad_add_fusion.2.ids_ref
  134.2 1.8 pad_add_fusion.3.ids_ref
  136.0 1.9 pad_add_fusion.4.ids_ref
  137.9 16.3 %swiglu_rows.5 = (bf16[2048,2048]{1,0:T(8,128)(2,1)}, bf16[2048,2048]{1,0:T(8,128)(2,1)}, bf16[2048,1024]{1,0:T(8,128)(2,1)}, bf16[2048,1024]{1,0:T(8,128)(2,1)}...) custom-call(s32[2]{0:T(128)} %pad_add_fusion.1.ids_ref, ...), custom_call_target="tpu_custom_call" | custom-call | flops 7516192768 | bytes 23068672 | tf_op jit(solution)/shard_map/swiglu_rows/pallas_call | solution.py:596
  154.3 1.5 collective-permute-start.2
  156.8 27.7 %swiglu_rows.6 = (bf16[2048,2048]{1,0:T(8,128)(2,1)}, bf16[2048,2048]{1,0:T(8,128)(2,1)}, bf16[2048,1024]{1,0:T(8,128)(2,1)}, bf16[2048,1024]{1,0:T(8,128)(2,1)}...) custom-call(s32[3]{0:T(128)} %pad_add_fusion.2.ids_ref, ...), custom_call_target="tpu_custom_call", output_to_operand_aliasing={{0}: (8, {}), {1}: (9, {}), {2}: (10, {}), {3}: (11, {}), {... | custom-call | flops 15032385536 | bytes 33554432 | tf_op jit(solution)/shard_map/swiglu_rows/pallas_call | solution.py:596
  186.8 27.7 %swiglu_rows.7 = (bf16[2048,2048]{1,0:T(8,128)(2,1)}, bf16[2048,2048]{1,0:T(8,128)(2,1)}, bf16[2048,1024]{1,0:T(8,128)(2,1)}, bf16[2048,1024]{1,0:T(8,128)(2,1)}...) custom-call(s32[3]{0:T(128)} %pad_add_fusion.3.ids_ref, ...), custom_call_target="tpu_custom_call", output_to_operand_aliasing={{0}: (8, {}), {1}: (9, {}), {2}: (10, {}), {3}: (11, {}), {... | custom-call | flops 15032385536 | bytes 33554432 | tf_op jit(solution)/shard_map/swiglu_rows/pallas_call | solution.py:596
  215.7 1.5 collective-permute-start.7
  217.1 27.6 %swiglu_rows.8 = (bf16[2048,2048]{1,0:T(8,128)(2,1)}, bf16[2048,2048]{1,0:T(8,128)(2,1)}, bf16[2048,1024]{1,0:T(8,128)(2,1)}, bf16[2048,1024]{1,0:T(8,128)(2,1)}...) custom-call(s32[3]{0:T(128)} %pad_add_fusion.4.ids_ref, ...), custom_call_target="tpu_custom_call", output_to_operand_aliasing={{0}: (8, {}), {1}: (9, {}), {2}: (10, {}), {3}: (11, {}), {... | custom-call | flops 15032385536 | bytes 33554432 | tf_op jit(solution)/shard_map/swiglu_rows/pallas_call | solution.py:596
  245.8 16.3 %swiglu_rows.9 = (bf16[2048,2048]{1,0:T(8,128)(2,1)}, bf16[2048,2048]{1,0:T(8,128)(2,1)}, bf16[2048,1024]{1,0:T(8,128)(2,1)}, bf16[2048,1024]{1,0:T(8,128)(2,1)}...) custom-call(s32[2]{0:T(128)} %pad_add_fusion.5.ids_ref, ...), custom_call_target="tpu_custom_call", output_to_operand_aliasing={{0}: (7, {}), {1}: (8, {}), {2}: (9, {}), {3}: (10, {}), {4... | custom-call | flops 7516192768 | bytes 23068672 | tf_op jit(solution)/shard_map/swiglu_rows/pallas_call | solution.py:596
  262.1 1.4 fusion.7
  265.8 9.6 %collective-permute-done.20 = bf16[128,2048]{1,0:T(8,128)(2,1)S(1)} collective-permute-done((bf16[128,2048]{1,0:T(8,128)(2,1)S(1)}, bf16[128,2048]{1,0:T(8,128)(2,1)S(1)}, u32[]{:S(2)}, u32[]{:S(2)}) %collective-permute-start.20) | collective-permute-done | bytes 524320 | tf_op jit(solution)/shard_map/ppermute | solution.py:646
  279.0 20.3 %collective-permute-done.9 = bf16[256,2048]{1,0:T(8,128)(2,1)S(1)} collective-permute-done((bf16[256,2048]{1,0:T(8,128)(2,1)S(1)}, bf16[256,2048]{1,0:T(8,128)(2,1)S(1)}, u32[]{:S(2)}, u32[]{:S(2)}) %collective-permute-start.9) | collective-permute-done | bytes 1048608 | tf_op jit(solution)/shard_map/ppermute | solution.py:656
  301.1 1.9 collective-permute-start.22
  303.0 18.4 %collective-permute-done.10 = bf16[256,2048]{1,0:T(8,128)(2,1)S(1)} collective-permute-done((bf16[256,2048]{1,0:T(8,128)(2,1)S(1)}, bf16[256,2048]{1,0:T(8,128)(2,1)S(1)}, u32[]{:S(2)}, u32[]{:S(2)}) %collective-permute-start.10) | collective-permute-done | bytes 1048608 | tf_op jit(solution)/shard_map/ppermute | solution.py:656
  321.9 2.1 add_convert_fusion
  324.8 1.5 collective-permute-start.23
  326.8 17.4 %collective-permute-done.11.refs_1_ = bf16[256,2048]{1,0:T(8,128)(2,1)S(1)} collective-permute-done((bf16[256,2048]{1,0:T(8,128)(2,1)}, bf16[256,2048]{1,0:T(8,128)(2,1)S(1)}, u32[]{:S(2)}, u32[]{:S(2)}) %collective-permute-start.11) | collective-permute-done | bytes 1048608 | tf_op jit(solution)/shard_map/ppermute | solution.py:656
  345.1 13.9 %norm_back_and_project.1 = (f32[256,2048]{1,0:T(8,128)}, bf16[256,2048]{1,0:T(8,128)(2,1)}, f32[1,2048]{1,0:T(1,128)}, bf16[8,256,256]{2,1,0:T(8,128)(2,1)}) custom-call(s32[2]{0:T(128)} %pad_add_fusion.ids_ref, bf16[256,2048]{1,0:T(8,128)(2,1)} %get-tuple-element.97.refs_0_, bf16[256,2048]{1,0:T(8,128)(2,1)} %copy-done.20, ...), custom_call_target="tpu_custom_call" | custom-call | flops 2147483648 | bytes 8388608 | tf_op jit(solution)/shard_map/norm_back_and_project/pallas_call | solution.py:454
  359.0 6.8 convolution_convert_fusion
  365.8 4.6 all-to-all-start.2
  371.5 19.1 %all-to-all-done.2 = bf16[8,256,256]{2,1,0:T(8,128)(2,1)} async-done(((bf16[8,256,256]{2,1,0:T(8,128)(2,1)}), bf16[8,256,256]{2,1,0:T(8,128)(2,1)}, u32[]{:S(2)}, u32[]{:S(2)}) %all-to-all-start.2) | async-done | bytes 1048608 | tf_op jit(solution)/shard_map/all_to_all | solution.py:763
  390.6 37.1 %attend_back.1 = bf16[2048,384]{1,0:T(8,128)(2,1)} custom-call(bf16[2048,256]{1,0:T(8,128)(2,1)} %get-tuple-element.61.q_ref, bf16[2048,256]{1,0:T(8,128)(2,1)} %bitcast.28.do_ref, bf16[2048,256]{1,0:T(8,128)(2,1)} %get-tuple-element.64.o_ref, f32[8,2048]{1,0:T(8,128)} %get-tuple-element.99.lse_ref, bf16[2048,128]{1,0:T(8,128)(2,1)} %get-tuple-element.62.k_ref, ...), custom_call_target="tpu_custom_call" | custom-call | flops 21474836480 | bytes 5242880 | tf_op jit(solution)/shard_map/attend_back/pallas_call | solution.py:337
  427.7 6.4 multiply_reduce_fusion
  434.2 1.6 copy-done.15
  435.9 1.5 maximum_maximum_fusion
  438.4 2.8 slice.296
  441.4 14.0 %convolution_convert_fusion.1 = bf16[1024,2048]{1,0:T(8,128)(2,1)} fusion(bf16[2048,1024]{1,0:T(8,128)(2,1)} %get-tuple-element.109, bf16[2048,2048]{1,0:T(8,128)(2,1)} %get-tuple-element.110), kind=kOutput, calls=%fused_computation.1 | convolution fusion | flops 8592031744 | bytes 16777216 | tf_op jit(solution)/shard_map/dot_general | solution.py:32
  455.5 14.3 %convolution_convert_fusion.2 = bf16[2048,1024]{1,0:T(8,128)(2,1)} fusion(bf16[2048,2048]{1,0:T(8,128)(2,1)} %get-tuple-element.106, bf16[2048,1024]{1,0:T(8,128)(2,1)} %get-tuple-element.108), kind=kOutput, calls=%fused_computation.2 | convolution fusion | flops 8592031744 | bytes 16777216 | tf_op jit(solution)/shard_map/dot_general | solution.py:32
  470.2 14.1 %convolution_convert_fusion.3 = bf16[2048,1024]{1,0:T(8,128)(2,1)} fusion(bf16[2048,2048]{1,0:T(8,128)(2,1)} %get-tuple-element.106, bf16[2048,1024]{1,0:T(8,128)(2,1)} %get-tuple-element.107), kind=kOutput, calls=%fused_computation.3 | convolution fusion | flops 8592031744 | bytes 16777216 | tf_op jit(solution)/shard_map/dot_general | solution.py:32
  487.8 11.9 %collective-permute-done.12 = bf16[128,2048]{1,0:T(8,128)(2,1)S(1)} collective-permute-done((bf16[128,2048]{1,0:T(8,128)(2,1)S(1)}, bf16[128,2048]{1,0:T(8,128)(2,1)S(1)}, u32[]{:S(2)}, u32[]{:S(2)}) %collective-permute-start.12) | collective-permute-done | bytes 524320 | tf_op jit(solution)/shard_map/ppermute | solution.py:645
  499.6 2.9 collective-permute-done.16
  504.0 2.5 collective-permute-start.17
  507.6 4.5 all-to-all-start.3
  512.1 36.4 %collective-permute-done.17 = bf16[256,2048]{1,0:T(8,128)(2,1)} collective-permute-done((bf16[256,2048]{1,0:T(8,128)(2,1)}, bf16[256,2048]{1,0:T(8,128)(2,1)}, u32[]{:S(2)}, u32[]{:S(2)}) %collective-permute-start.17) | collective-permute-done | bytes 1048608 | tf_op jit(solution)/shard_map/ppermute | solution.py:657
  548.5 12.0 %collective-permute-done.13 = bf16[256,2048]{1,0:T(8,128)(2,1)S(1)} collective-permute-done((bf16[256,2048]{1,0:T(8,128)(2,1)}, bf16[256,2048]{1,0:T(8,128)(2,1)S(1)}, u32[]{:S(2)}, u32[]{:S(2)}) %collective-permute-start.13) | collective-permute-done | bytes 1048608 | tf_op jit(solution)/shard_map/ppermute | solution.py:656
  560.5 4.1 add_convert_fusion.6
  564.6 2.0 collective-permute-start.18
  566.6 63.2 %collective-permute-done.14 = bf16[256,2048]{1,0:T(8,128)(2,1)S(1)} collective-permute-done((bf16[256,2048]{1,0:T(8,128)(2,1)}, bf16[256,2048]{1,0:T(8,128)(2,1)S(1)}, u32[]{:S(2)}, u32[]{:S(2)}) %collective-permute-start.14) | collective-permute-done | bytes 1048608 | tf_op jit(solution)/shard_map/ppermute | solution.py:656
  629.8 4.8 add_convert_fusion.5
  634.6 8.9 %collective-permute-start.19 = (bf16[256,2048]{1,0:T(8,128)(2,1)}, bf16[256,2048]{1,0:T(8,128)(2,1)}, u32[]{:S(2)}, u32[]{:S(2)}) collective-permute-start(bf16[256,2048]{1,0:T(8,128)(2,1)} %get-tuple-element.177), channel_id=1, source_target_pairs={{1,0},{3,1},{5,3},{7,5},{6,7},{4,6},{2,4},{0,2},{9,8},{11,9},{13,1... | collective-permute-start | bytes 3145736 | tf_op jit(solution)/shard_map/ppermute | solution.py:657
  643.5 2.0 copy.75
  646.7 4.2 all-to-all-start.4
  650.9 16.9 %copy.74 = bf16[16384,384]{1,0:T(8,128)(2,1)} copy(bf16[16384,384]{0,1:T(8,128)(2,1)} %all-gather.5.cloned.1.call-done) | data formatting | bytes 25165824 | tf_op jit(solution)/shard_map/all_gather | solution.py:709
  667.8 3.7 add_convert_fusion.2
  671.5 1.9 copy.79
  673.5 14.4 %input_grad.1 = f32[256,2048]{1,0:T(8,128)} custom-call(s32[2]{0:T(128)} %pad_add_fusion.ids_ref, bf16[8,256,384]{2,1,0:T(8,128)(2,1)} %copy-done.5, bf16[8,2048,384]{2,1,0:T(8,128)(2,1)} %bitcast.64, bf16[2048,2048]{1,0:T(8,128)(2,1)} %rows_ref.5, f32[1,2048]{1,0:T(1,128)} %bitcast.72, f32[256,2048]{1,0:T(8,128)} %get-tuple-element.102.dh_ref), custom_call_target="tpu_custom_call" | custom-call | flops 3221225472 | bytes 12582912 | tf_op jit(solution)/shard_map/input_grad/pallas_call | solution.py:507
  687.8 20.2 %reduce-scatter.20.cloned.1.call-done = bf16[1024,512]{1,0:T(8,128)(2,1)} async-done(((bf16[1024,2048]{1,0:T(8,128)(2,1)}), bf16[1024,512]{1,0:T(8,128)(2,1)}) %reduce-scatter.20.cloned.1.call-update) | async-done | bytes 1048592 | tf_op jit(solution)/shard_map/reduce_scatter | solution.py:796
  708.0 2.8 convert_element_type.228
  710.8 44.2 %reduce-scatter.18.cloned.1.call-done = bf16[512,1024]{1,0:T(8,128)(2,1)} async-done(((bf16[2048,1024]{1,0:T(8,128)(2,1)}), bf16[512,1024]{1,0:T(8,128)(2,1)}) %reduce-scatter.18.cloned.1.call-update) | async-done | bytes 1048592 | tf_op jit(solution)/shard_map/reduce_scatter | solution.py:796
  755.0 2.8 convert_element_type.226
  757.8 44.4 %reduce-scatter.16.cloned.1.call-done = bf16[512,1024]{1,0:T(8,128)(2,1)} async-done(((bf16[2048,1024]{1,0:T(8,128)(2,1)}), bf16[512,1024]{1,0:T(8,128)(2,1)}) %reduce-scatter.16.cloned.1.call-update) | async-done | bytes 1048592 | tf_op jit(solution)/shard_map/reduce_scatter | solution.py:796
  802.3 2.8 convert_element_type.224
  809.8 63.9 %reduce-scatter.14.cloned.1.call-done = bf16[256,512]{1,0:T(8,128)(2,1)} async-done(((bf16[2048,512]{1,0:T(8,128)(2,1)}), bf16[256,512]{1,0:T(8,128)(2,1)}) %reduce-scatter.14.cloned.1.call-update) | async-done | bytes 262160 | tf_op jit(solution)/shard_map/reduce_scatter | solution.py:811
  873.7 1.8 convert_element_type.222
  (163 shorter events, 49.8 us)
Async XLA Ops:
  7.2 1.2 copy-start
  7.2 10.9 %copy-start.22 = (bf16[256,512]{1,0:T(8,128)(2,1)S(1)}, bf16[256,512]{1,0:T(8,128)(2,1)}, u32[]{:S(2)}) copy-start(bf16[256,512]{1,0:T(8,128)(2,1)} %param.19) | copy-start | bytes 786436
  7.2 109.7 %all-gather.3.cloned.1.call-start = ((), (), s32[]{:S(2)}) async-start(), calls=%async_computation.12 | async-start | bytes 8650752 | tf_op jit(solution)/shard_map/all_gather | solution.py:703
  20.4 24.9 %all-to-all-start = ((bf16[8,256,128]{2,1,0:T(8,128)(2,1)}), bf16[8,256,128]{2,1,0:T(8,128)(2,1)S(1)}, u32[]{:S(2)}, u32[]{:S(2)}) async-start(bf16[8,256,128]{2,1,0:T(8,128)(2,1)} %pad_maximum_fusion.5), calls=%async_computation | async-start | bytes 1048576 | tf_op jit(solution)/shard_map/all_to_all | solution.py:707
  83.3 33.5 %all-to-all-start.1 = ((bf16[8,256,256]{2,1,0:T(8,128)(2,1)}), bf16[8,256,256]{2,1,0:T(8,128)(2,1)S(1)}, u32[]{:S(2)}, u32[]{:S(2)}) async-start(bf16[8,256,256]{2,1,0:T(8,128)(2,1)} %bitcast.70), calls=%async_computation.1 | async-start | bytes 2097152 | tf_op jit(solution)/shard_map/all_to_all | solution.py:716
  87.1 479.5 %reduce-scatter.12.cloned.1.call-start = ((), (), s32[]{:S(2)}) async-start(), calls=%async_computation.16 | async-start | bytes 10485760 | tf_op jit(solution)/shard_map/reduce_scatter | solution.py:796
  116.9 1.0 copy-start.2
  129.0 25.2 %collective-permute-start = (bf16[256,2048]{1,0:T(8,128)(2,1)}, bf16[256,2048]{1,0:T(8,128)(2,1)S(1)}, u32[]{:S(2)}, u32[]{:S(2)}) collective-permute-start(bf16[256,2048]{1,0:T(8,128)(2,1)} %get-tuple-element.66.refs_0_), channel_id=1, source_target_pairs={{0,1},{1,3},{3,5},{5,7},{7,6},{6,4},{4,2},{2,0},{8,9},{9,11},{11,1... | collective-permute-start | bytes 3145736 | tf_op jit(solution)/shard_map/ppermute | solution.py:730
  130.5 25.3 %collective-permute-start.1 = (bf16[256,2048]{1,0:T(8,128)(2,1)}, bf16[256,2048]{1,0:T(8,128)(2,1)S(1)}, u32[]{:S(2)}, u32[]{:S(2)}) collective-permute-start(bf16[256,2048]{1,0:T(8,128)(2,1)} %get-tuple-element.66.refs_0_), channel_id=1, source_target_pairs={{1,0},{3,1},{5,3},{7,5},{6,7},{4,6},{2,4},{0,2},{9,8},{11,9},{13,1... | collective-permute-start | bytes 3145736 | tf_op jit(solution)/shard_map/ppermute | solution.py:731
  154.3 2.3 copy-start.17
  154.3 30.2 %collective-permute-start.2 = (bf16[256,2048]{1,0:T(8,128)(2,1)S(1)}, bf16[256,2048]{1,0:T(8,128)(2,1)S(1)}, u32[]{:S(2)}, u32[]{:S(2)}) collective-permute-start(bf16[256,2048]{1,0:T(8,128)(2,1)S(1)} %collective-permute-done.refs_0_), channel_id=1, source_target_pairs={{0,1},{1,3},{3,5},{5,7},{7,6},{6,4},{4,2},{2,0},{8,9},{9,11},{11,1... | collective-permute-start | bytes 3145736 | tf_op jit(solution)/shard_map/ppermute | solution.py:730
  155.8 1.0 copy-start.16
  155.8 30.0 %collective-permute-start.3 = (bf16[256,2048]{1,0:T(8,128)(2,1)S(1)}, bf16[256,2048]{1,0:T(8,128)(2,1)S(1)}, u32[]{:S(2)}, u32[]{:S(2)}) collective-permute-start(bf16[256,2048]{1,0:T(8,128)(2,1)S(1)} %collective-permute-done.1.refs_1_), channel_id=1, source_target_pairs={{1,0},{3,1},{5,3},{7,5},{6,7},{4,6},{2,4},{0,2},{9,8},{11,9},{13,1... | collective-permute-start | bytes 3145736 | tf_op jit(solution)/shard_map/ppermute | solution.py:731
  184.5 2.1 copy-start.19
  184.5 30.0 %collective-permute-start.4 = (bf16[256,2048]{1,0:T(8,128)(2,1)S(1)}, bf16[256,2048]{1,0:T(8,128)(2,1)S(1)}, u32[]{:S(2)}, u32[]{:S(2)}) collective-permute-start(bf16[256,2048]{1,0:T(8,128)(2,1)S(1)} %collective-permute-done.2.refs_0_), channel_id=1, source_target_pairs={{0,1},{1,3},{3,5},{5,7},{7,6},{6,4},{4,2},{2,0},{8,9},{9,11},{11,1... | collective-permute-start | bytes 3145736 | tf_op jit(solution)/shard_map/ppermute | solution.py:730
  185.8 1.0 copy-start.18
  185.8 29.8 %collective-permute-start.5 = (bf16[256,2048]{1,0:T(8,128)(2,1)S(1)}, bf16[256,2048]{1,0:T(8,128)(2,1)S(1)}, u32[]{:S(2)}, u32[]{:S(2)}) collective-permute-start(bf16[256,2048]{1,0:T(8,128)(2,1)S(1)} %collective-permute-done.3.refs_1_), channel_id=1, source_target_pairs={{1,0},{3,1},{5,3},{7,5},{6,7},{4,6},{2,4},{0,2},{9,8},{11,9},{13,1... | collective-permute-start | bytes 3145736 | tf_op jit(solution)/shard_map/ppermute | solution.py:731
  214.5 2.7 copy-start.9
  214.5 30.2 %collective-permute-start.6 = (bf16[128,2048]{1,0:T(8,128)(2,1)S(1)}, bf16[128,2048]{1,0:T(8,128)(2,1)S(1)}, u32[]{:S(2)}, u32[]{:S(2)}) collective-permute-start(bf16[128,2048]{1,0:T(8,128)(2,1)S(1)} %slice.253), channel_id=1, source_target_pairs={{0,1},{1,3},{3,5},{5,7},{7,6},{6,4},{4,2},{2,0},{8,9},{9,11},{11,1... | collective-permute-start | bytes 1572872 | tf_op jit(solution)/shard_map/ppermute | solution.py:746
  215.6 1.5 copy-start.10
  215.7 29.1 %collective-permute-start.7 = (bf16[128,2048]{1,0:T(8,128)(2,1)S(1)}, bf16[128,2048]{1,0:T(8,128)(2,1)S(1)}, u32[]{:S(2)}, u32[]{:S(2)}) collective-permute-start(bf16[128,2048]{1,0:T(8,128)(2,1)S(1)} %slice.254), channel_id=1, source_target_pairs={{1,0},{3,1},{5,3},{7,5},{6,7},{4,6},{2,4},{0,2},{9,8},{11,9},{13,1... | collective-permute-start | bytes 1572872 | tf_op jit(solution)/shard_map/ppermute | solution.py:747
  244.8 1.0 copy-start.25
  262.1 3.5 copy-start.14
  263.6 11.8 %collective-permute-start.20 = (bf16[128,2048]{1,0:T(8,128)(2,1)S(1)}, bf16[128,2048]{1,0:T(8,128)(2,1)S(1)}, u32[]{:S(2)}, u32[]{:S(2)}) collective-permute-start(bf16[128,2048]{1,0:T(8,128)(2,1)S(1)} %get-tuple-element.184), channel_id=1, source_target_pairs={{1,0},{3,1},{5,3},{7,5},{6,7},{4,6},{2,4},{0,2},{9,8},{11,9},{13,1... | collective-permute-start | bytes 1572872 | tf_op jit(solution)/shard_map/ppermute | solution.py:646
  264.4 11.8 %collective-permute-start.8 = (bf16[128,2048]{1,0:T(8,128)(2,1)S(1)}, bf16[128,2048]{1,0:T(8,128)(2,1)S(1)}, u32[]{:S(2)}, u32[]{:S(2)}) collective-permute-start(bf16[128,2048]{1,0:T(8,128)(2,1)S(1)} %get-tuple-element.185), channel_id=1, source_target_pairs={{0,1},{1,3},{3,5},{5,7},{7,6},{6,4},{4,2},{2,0},{8,9},{9,11},{11,1... | collective-permute-start | bytes 1572872 | tf_op jit(solution)/shard_map/ppermute | solution.py:645
  276.6 23.5 %copy-start.12 = (bf16[512,2048]{1,0:T(8,128)(2,1)S(1)}, bf16[512,2048]{1,0:T(8,128)(2,1)}, u32[]{:S(2)}) copy-start(bf16[512,2048]{1,0:T(8,128)(2,1)} %get-tuple-element.93) | copy-start | bytes 6291460
  276.7 22.5 %collective-permute-start.9 = (bf16[256,2048]{1,0:T(8,128)(2,1)S(1)}, bf16[256,2048]{1,0:T(8,128)(2,1)S(1)}, u32[]{:S(2)}, u32[]{:S(2)}) collective-permute-start(bf16[256,2048]{1,0:T(8,128)(2,1)S(1)} %pad_maximum_fusion.1), channel_id=1, source_target_pairs={{0,1},{1,3},{3,5},{5,7},{7,6},{6,4},{4,2},{2,0},{8,9},{9,11},{11,1... | collective-permute-start | bytes 3145736 | tf_op jit(solution)/shard_map/ppermute | solution.py:656
  277.9 22.2 %collective-permute-start.21 = (bf16[256,2048]{1,0:T(8,128)(2,1)S(1)}, bf16[256,2048]{1,0:T(8,128)(2,1)S(1)}, u32[]{:S(2)}, u32[]{:S(2)}) collective-permute-start(bf16[256,2048]{1,0:T(8,128)(2,1)S(1)} %pad_maximum_fusion.4), channel_id=1, source_target_pairs={{1,0},{3,1},{5,3},{7,5},{6,7},{4,6},{2,4},{0,2},{9,8},{11,9},{13,1... | collective-permute-start | bytes 3145736 | tf_op jit(solution)/shard_map/ppermute | solution.py:657
  300.1 21.8 %copy-start.11 = (bf16[512,2048]{1,0:T(8,128)(2,1)S(1)}, bf16[512,2048]{1,0:T(8,128)(2,1)}, u32[]{:S(2)}) copy-start(bf16[512,2048]{1,0:T(8,128)(2,1)} %get-tuple-element.92) | copy-start | bytes 6291460
  300.9 20.5 %collective-permute-start.10 = (bf16[256,2048]{1,0:T(8,128)(2,1)S(1)}, bf16[256,2048]{1,0:T(8,128)(2,1)S(1)}, u32[]{:S(2)}, u32[]{:S(2)}) collective-permute-start(bf16[256,2048]{1,0:T(8,128)(2,1)S(1)} %get-tuple-element.171), channel_id=1, source_target_pairs={{0,1},{1,3},{3,5},{5,7},{7,6},{6,4},{4,2},{2,0},{8,9},{9,11},{11,1... | collective-permute-start | bytes 3145736 | tf_op jit(solution)/shard_map/ppermute | solution.py:656
  301.1 20.8 %collective-permute-start.22 = (bf16[256,2048]{1,0:T(8,128)(2,1)S(1)}, bf16[256,2048]{1,0:T(8,128)(2,1)S(1)}, u32[]{:S(2)}, u32[]{:S(2)}) collective-permute-start(bf16[256,2048]{1,0:T(8,128)(2,1)S(1)} %get-tuple-element.170), channel_id=1, source_target_pairs={{1,0},{3,1},{5,3},{7,5},{6,7},{4,6},{2,4},{0,2},{9,8},{11,9},{13,1... | collective-permute-start | bytes 3145736 | tf_op jit(solution)/shard_map/ppermute | solution.py:657
  321.9 4.3 copy-start.3
  324.1 20.1 %collective-permute-start.11 = (bf16[256,2048]{1,0:T(8,128)(2,1)}, bf16[256,2048]{1,0:T(8,128)(2,1)S(1)}, u32[]{:S(2)}, u32[]{:S(2)}) collective-permute-start(bf16[256,2048]{1,0:T(8,128)(2,1)} %get-tuple-element.169), channel_id=1, source_target_pairs={{0,1},{1,3},{3,5},{5,7},{7,6},{6,4},{4,2},{2,0},{8,9},{9,11},{11,1... | collective-permute-start | bytes 3145736 | tf_op jit(solution)/shard_map/ppermute | solution.py:656
  324.8 19.8 %collective-permute-start.23 = (bf16[256,2048]{1,0:T(8,128)(2,1)}, bf16[256,2048]{1,0:T(8,128)(2,1)}, u32[]{:S(2)}, u32[]{:S(2)}) collective-permute-start(bf16[256,2048]{1,0:T(8,128)(2,1)} %get-tuple-element.168), channel_id=1, source_target_pairs={{1,0},{3,1},{5,3},{7,5},{6,7},{4,6},{2,4},{0,2},{9,8},{11,9},{13,1... | collective-permute-start | bytes 3145736 | tf_op jit(solution)/shard_map/ppermute | solution.py:657
  344.2 1.0 copy-start.20
  365.8 4.7 copy-start.8
  365.8 5.4 copy-start.7
  365.8 24.8 %all-to-all-start.2 = ((bf16[8,256,256]{2,1,0:T(8,128)(2,1)}), bf16[8,256,256]{2,1,0:T(8,128)(2,1)}, u32[]{:S(2)}, u32[]{:S(2)}) async-start(bf16[8,256,256]{2,1,0:T(8,128)(2,1)} %get-tuple-element.98), calls=%async_computation.2 | async-start | bytes 2097152 | tf_op jit(solution)/shard_map/all_to_all | solution.py:763
  370.5 273.0 %reduce-scatter.8.cloned.1.call-start = ((), (), s32[]{:S(2)}) async-start(), calls=%async_computation.14 | async-start | bytes 2621440 | tf_op jit(solution)/shard_map/reduce_scatter | solution.py:796
  434.1 1.7 copy-start.15
  434.1 1.7 copy-start.26
  434.1 1.8 copy-start.27
  437.5 213.4 %all-gather.5.cloned.1.call-start = ((), (), s32[]{:S(2)}) async-start(), calls=%async_computation.13 | async-start | bytes 12976128 | tf_op jit(solution)/shard_map/all_gather | solution.py:709
  438.3 233.2 %reduce-scatter.10.cloned.1.call-start = ((), (), s32[]{:S(2)}) async-start(), calls=%async_computation.15 | async-start | bytes 1310720 | tf_op jit(solution)/shard_map/reduce_scatter | solution.py:796
  441.1 266.8 %reduce-scatter.20.cloned.1.call-start = ((), (), s32[]{:S(2)}) async-start(), calls=%async_computation.20 | async-start | bytes 5242880 | tf_op jit(solution)/shard_map/reduce_scatter | solution.py:796
  455.5 299.6 %reduce-scatter.18.cloned.1.call-start = ((), (), s32[]{:S(2)}) async-start(), calls=%async_computation.19 | async-start | bytes 5242880 | tf_op jit(solution)/shard_map/reduce_scatter | solution.py:796
  469.9 332.4 %reduce-scatter.16.cloned.1.call-start = ((), (), s32[]{:S(2)}) async-start(), calls=%async_computation.18 | async-start | bytes 5242880 | tf_op jit(solution)/shard_map/reduce_scatter | solution.py:796
  484.2 1.2 copy-start.21
  484.3 3.4 copy-start.13
  485.6 14.0 %collective-permute-start.12 = (bf16[128,2048]{1,0:T(8,128)(2,1)S(1)}, bf16[128,2048]{1,0:T(8,128)(2,1)S(1)}, u32[]{:S(2)}, u32[]{:S(2)}) collective-permute-start(bf16[128,2048]{1,0:T(8,128)(2,1)S(1)} %get-tuple-element.186), channel_id=1, source_target_pairs={{0,1},{1,3},{3,5},{5,7},{7,6},{6,4},{4,2},{2,0},{8,9},{9,11},{11,1... | collective-permute-start | bytes 1572872 | tf_op jit(solution)/shard_map/ppermute | solution.py:645
  486.9 15.6 %collective-permute-start.16 = (bf16[128,2048]{1,0:T(8,128)(2,1)S(1)}, bf16[128,2048]{1,0:T(8,128)(2,1)S(1)}, u32[]{:S(2)}, u32[]{:S(2)}) collective-permute-start(bf16[128,2048]{1,0:T(8,128)(2,1)S(1)} %get-tuple-element.187), channel_id=1, source_target_pairs={{1,0},{3,1},{5,3},{7,5},{6,7},{4,6},{2,4},{0,2},{9,8},{11,9},{13,1... | collective-permute-start | bytes 1572872 | tf_op jit(solution)/shard_map/ppermute | solution.py:646
  504.0 44.5 %collective-permute-start.17 = (bf16[256,2048]{1,0:T(8,128)(2,1)}, bf16[256,2048]{1,0:T(8,128)(2,1)}, u32[]{:S(2)}, u32[]{:S(2)}) collective-permute-start(bf16[256,2048]{1,0:T(8,128)(2,1)} %pad_maximum_fusion.3), channel_id=1, source_target_pairs={{1,0},{3,1},{5,3},{7,5},{6,7},{4,6},{2,4},{0,2},{9,8},{11,9},{13,1... | collective-permute-start | bytes 3145736 | tf_op jit(solution)/shard_map/ppermute | solution.py:657
  507.6 52.9 %collective-permute-start.13 = (bf16[256,2048]{1,0:T(8,128)(2,1)}, bf16[256,2048]{1,0:T(8,128)(2,1)S(1)}, u32[]{:S(2)}, u32[]{:S(2)}) collective-permute-start(bf16[256,2048]{1,0:T(8,128)(2,1)} %pad_maximum_fusion.2), channel_id=1, source_target_pairs={{0,1},{1,3},{3,5},{5,7},{7,6},{6,4},{4,2},{2,0},{8,9},{9,11},{11,1... | collective-permute-start | bytes 3145736 | tf_op jit(solution)/shard_map/ppermute | solution.py:656
  507.6 137.9 %all-to-all-start.3 = ((bf16[8,256,384]{2,1,0:T(8,128)(2,1)}), bf16[8,256,384]{2,1,0:T(8,128)(2,1)S(1)}, u32[]{:S(2)}, u32[]{:S(2)}) async-start(bf16[8,256,384]{2,1,0:T(8,128)(2,1)} %bitcast.69), calls=%async_computation.3 | async-start | bytes 3145728 | tf_op jit(solution)/shard_map/all_to_all | solution.py:780
  512.1 361.6 %reduce-scatter.14.cloned.1.call-start = ((), (), s32[]{:S(2)}) async-start(), calls=%async_computation.17 | async-start | bytes 2359296 | tf_op jit(solution)/shard_map/reduce_scatter | solution.py:811
  564.6 65.2 %collective-permute-start.14 = (bf16[256,2048]{1,0:T(8,128)(2,1)}, bf16[256,2048]{1,0:T(8,128)(2,1)S(1)}, u32[]{:S(2)}, u32[]{:S(2)}) collective-permute-start(bf16[256,2048]{1,0:T(8,128)(2,1)} %get-tuple-element.178), channel_id=1, source_target_pairs={{0,1},{1,3},{3,5},{5,7},{7,6},{6,4},{4,2},{2,0},{8,9},{9,11},{11,1... | collective-permute-start | bytes 3145736 | tf_op jit(solution)/shard_map/ppermute | solution.py:656
  564.6 65.2 %collective-permute-start.18 = (bf16[256,2048]{1,0:T(8,128)(2,1)}, bf16[256,2048]{1,0:T(8,128)(2,1)}, u32[]{:S(2)}, u32[]{:S(2)}) collective-permute-start(bf16[256,2048]{1,0:T(8,128)(2,1)} %get-tuple-element.179), channel_id=1, source_target_pairs={{1,0},{3,1},{5,3},{7,5},{6,7},{4,6},{2,4},{0,2},{9,8},{11,9},{13,1... | collective-permute-start | bytes 3145736 | tf_op jit(solution)/shard_map/ppermute | solution.py:657
  634.6 33.2 %collective-permute-start.15 = (bf16[256,2048]{1,0:T(8,128)(2,1)}, bf16[256,2048]{1,0:T(8,128)(2,1)}, u32[]{:S(2)}, u32[]{:S(2)}) collective-permute-start(bf16[256,2048]{1,0:T(8,128)(2,1)} %get-tuple-element.176), channel_id=1, source_target_pairs={{0,1},{1,3},{3,5},{5,7},{7,6},{6,4},{4,2},{2,0},{8,9},{9,11},{11,1... | collective-permute-start | bytes 3145736 | tf_op jit(solution)/shard_map/ppermute | solution.py:656
  634.6 33.2 %collective-permute-start.19 = (bf16[256,2048]{1,0:T(8,128)(2,1)}, bf16[256,2048]{1,0:T(8,128)(2,1)}, u32[]{:S(2)}, u32[]{:S(2)}) collective-permute-start(bf16[256,2048]{1,0:T(8,128)(2,1)} %get-tuple-element.177), channel_id=1, source_target_pairs={{1,0},{3,1},{5,3},{7,5},{6,7},{4,6},{2,4},{0,2},{9,8},{11,9},{13,1... | collective-permute-start | bytes 3145736 | tf_op jit(solution)/shard_map/ppermute | solution.py:657
  645.5 1.1 copy-start.5
  646.7 158.4 %all-to-all-start.4 = ((f32[8,64,256]{2,1,0:T(8,128)}), f32[8,64,256]{2,1,0:T(8,128)}, u32[]{:S(2)}, u32[]{:S(2)}) async-start(f32[8,64,256]{2,1,0:T(8,128)} %bitcast.33), calls=%async_computation.5 | async-start | bytes 1048576 | tf_op jit(solution)/shard_map/all_to_all | solution.py:798
  650.9 16.9 %copy-start.4 = (f32[256,2048]{1,0:T(8,128)S(1)}, f32[256,2048]{1,0:T(8,128)}, u32[]{:S(2)}) copy-start(f32[256,2048]{1,0:T(8,128)} %get-tuple-element.65.refs_3_) | copy-start | bytes 6291460
  650.9 16.9 %copy-start.23 = (bf16[256,2048]{1,0:T(8,128)(2,1)S(1)}, bf16[256,2048]{1,0:T(8,128)(2,1)}, u32[]{:S(2)}) copy-start(bf16[256,2048]{1,0:T(8,128)(2,1)} %get-tuple-element.67) | copy-start | bytes 3145732
  805.1 70.4 %copy-start.1 = (bf16[256,2048]{1,0:T(8,128)(2,1)S(1)}, bf16[256,2048]{1,0:T(8,128)(2,1)}, u32[]{:S(2)}) copy-start(bf16[256,2048]{1,0:T(8,128)(2,1)} %param.21) | copy-start | bytes 3145732
  (2 other events, 1.6 us)
Sparse Core Ops, SparseCore 0:
  11.5 86.5 all-gather.2
  365.9 70.7 reduce-scatter.11
  440.0 31.3 reduce-scatter.7
  474.7 159.5 all-gather.4
  636.7 24.2 reduce-scatter.9
  663.5 44.4 reduce-scatter.19
  710.5 44.4 reduce-scatter.17
  757.7 44.4 reduce-scatter.15
  805.8 67.8 reduce-scatter.13

commit v2 on v1

v2 whole, which is shorter than its diff:
```python
import functools
import math

import jax
import jax.numpy as jnp
from jax import lax
from jax.experimental import pallas as pl
from jax.experimental.pallas import tpu as pltpu
from jax.sharding import PartitionSpec as P

H = 32
KVH = 8
HD = 64
SEQ_LEN = 2048
QB = 256
WIDE = 512

RESID = 0.22
ATTN_SCALE = 0.015625
EPSILON = 1e-05
THETA_LOG = math.log(10000000.0)
MASKED = -1e30

f32 = jnp.float32
bf16 = jnp.bfloat16
NN = (((1,), (0,)), ((), ()))
NT = (((1,), (1,)), ((), ()))
TN = (((0,), (0,)), ((), ()))


def mm(left, right, dims):
    return lax.dot_general(left, right, dims, preferred_element_type=f32)


def grant(mib):
    return pltpu.CompilerParams(vmem_limit_bytes=mib * 1024 * 1024)


def cost(flops, nbytes):
    return pl.CostEstimate(flops=int(flops), bytes_accessed=int(nbytes), transcendentals=0)


def rope_tables(count):
    lane = jnp.arange(128, dtype=jnp.int32) % (HD // 2)
    freqs = jnp.exp(-THETA_LOG * (2 * lane).astype(f32) / HD)[None, :]
    fine = jnp.arange(QB, dtype=jnp.int32)
    coarse = jnp.arange(count // QB * 8, dtype=jnp.int32) // 8 * QB
    angle_rows = jnp.concatenate([fine, coarse]).astype(f32)[:, None] * freqs
    return jnp.concatenate([jnp.cos(angle_rows), jnp.sin(angle_rows)], 1)


def turn_at(table_ref, block):
    fine = table_ref[:QB, :]
    start = pl.multiple_of(QB + block * 8, 8)
    coarse = table_ref[pl.ds(start, 8), :][:1, :]
    cos_f, sin_f, cos_c, sin_c = fine[:, :128], fine[:, 128:], coarse[:, :128], coarse[:, 128:]
    return cos_f * cos_c - sin_f * sin_c, sin_f * cos_c + cos_f * sin_c


def widen(table, count):
    return table if count == 128 else jnp.concatenate([table] * (count // 128), 1)


def swap_halves(rows):
    count = rows.shape[1]
    lane = lax.broadcasted_iota(jnp.int32, rows.shape, 1)
    ahead = pltpu.roll(rows, count - HD // 2, 1)
    behind = pltpu.roll(rows, HD // 2, 1)
    return jnp.where(lane % HD < HD // 2, ahead, behind)


def half_sign(shape):
    lane = lax.broadcasted_iota(jnp.int32, shape, 1)
    return jnp.where(lane % HD < HD // 2, -1.0, 1.0)


def rotate(rows, cosines, sines):
    count = rows.shape[1]
    turned = swap_halves(rows) * half_sign(rows.shape)
    return rows * widen(cosines, count) + turned * widen(sines, count)


def unrotate(rows, cosines, sines):
    count = rows.shape[1]
    turned = swap_halves(rows * widen(sines, count)) * half_sign(rows.shape)
    return rows * widen(cosines, count) - turned


def front_kernel(rows_ref, gain_ref, wq_ref, table_ref, normed_ref, q_ref):
    rows = rows_ref[...].astype(f32)
    row_scale = lax.rsqrt(jnp.mean(rows * rows, axis=-1, keepdims=True) + EPSILON)
    normed_ref[...] = (rows * row_scale * gain_ref[...]).astype(bf16)
    q_raw = mm(normed_ref[...], wq_ref[...], NN)
    turned = rotate(q_raw, *turn_at(table_ref, pl.program_id(0)))
    q_ref[...] = (turned.astype(bf16).astype(f32) * ATTN_SCALE).astype(bf16)


def front(hidden, gain, w_query, table):
    count, width = hidden.shape
    q_cols = w_query.shape[1]
    row = lambda i: (i, 0)
    whole = lambda i: (0, 0)
    return pl.pallas_call(
        front_kernel,
        grid=(count // QB,),
        in_specs=[
            pl.BlockSpec((QB, width), row),
            pl.BlockSpec((1, width), whole),
            pl.BlockSpec((width, q_cols), whole),
            pl.BlockSpec(table.shape, whole),
        ],
        out_specs=[pl.BlockSpec((QB, width), row), pl.BlockSpec((QB, q_cols), row)],
        out_shape=[
            jax.ShapeDtypeStruct((count, width), bf16),
            jax.ShapeDtypeStruct((count, q_cols), bf16),
        ],
        cost_estimate=cost(2 * count * width * q_cols, 5 * count * width),
        name="norm_and_query",
    )(hidden, gain, w_query, table)


def keys_kernel(length_ref, normed_ref, wkv_ref, table_ref, k_ref, kt_ref, v_ref, vt_ref):
    kv_raw = mm(normed_ref[...], wkv_ref[...], NN)
    lane = lax.broadcasted_iota(jnp.int32, kv_raw.shape, 1)
    position = pl.program_id(0) * WIDE + lax.broadcasted_iota(jnp.int32, kv_raw.shape, 0)
    blocks = [turn_at(table_ref, pl.program_id(0) * (WIDE // QB) + i) for i in range(WIDE // QB)]
    cosines, sines = (jnp.concatenate([b[i] for b in blocks], 0) for i in range(2))
    turned = rotate(kv_raw, cosines, sines)
    keys = jnp.where(lane < HD, turned, 0.0)
    blocked = jnp.where((lane == HD) & (position >= length_ref[0]), MASKED, 0.0)
    k_ref[...] = (keys + blocked).astype(bf16)
    kt_ref[...] = keys.T.astype(bf16)
    values = jnp.concatenate([kv_raw[:, HD:], kv_raw[:, :HD]], 1)
    values = jnp.where(lane < HD, values, 1.0)
    v_ref[...] = values.astype(bf16)
    vt_ref[...] = values.T.astype(bf16)


def keys_values(length, normed, w_kv, table):
    count, width = normed.shape
    row = lambda i, s: (i, 0)
    col = lambda i, s: (0, i)
    return pl.pallas_call(
        keys_kernel,
        grid_spec=pltpu.PrefetchScalarGridSpec(
            num_scalar_prefetch=1,
            grid=(count // WIDE,),
            in_specs=[
                pl.BlockSpec((WIDE, width), row),
                pl.BlockSpec((width, 128), lambda i, s: (0, 0)),
                pl.BlockSpec(table.shape, lambda i, s: (0, 0)),
            ],
            out_specs=[
                pl.BlockSpec((WIDE, 128), row),
                pl.BlockSpec((128, WIDE), col),
                pl.BlockSpec((WIDE, 128), row),
                pl.BlockSpec((128, WIDE), col),
            ],
        ),
        out_shape=[
            jax.ShapeDtypeStruct((count, 128), bf16),
            jax.ShapeDtypeStruct((128, count), bf16),
            jax.ShapeDtypeStruct((count, 128), bf16),
            jax.ShapeDtypeStruct((128, count), bf16),
        ],
        cost_estimate=cost(2 * count * width * 128, 2 * count * width),
        name="keys_and_values",
    )(length, normed, w_kv, table)


def pick_kernel(picks, k_ref, v_ref, out_ref):
    for index, head in enumerate(picks):
        both = [ref[:, 128 * (head // 2) : 128 * (head // 2) + 128] for ref in (k_ref, v_ref)]
        at = head % 2 * HD
        out_ref[index] = jnp.concatenate([b[:, at : at + HD] for b in both], 1)


def pick_heads(w_key, w_value, picks):
    return pl.pallas_call(
        functools.partial(pick_kernel, picks),
        out_shape=jax.ShapeDtypeStruct((len(picks), w_key.shape[0], 2 * HD), bf16),
        name="pick_heads",
    )(w_key, w_value)


def head_slab(rows, head, fill):
    pair = rows[:, 128 * (head // 2) : 128 * (head // 2) + 128]
    if head % 2:
        pair = jnp.concatenate([pair[:, HD:], pair[:, :HD]], 1)
    lane = lax.broadcasted_iota(jnp.int32, pair.shape, 1)
    other = jnp.where(lane == HD, jnp.full(pair.shape, fill, f32), 0.0).astype(pair.dtype)
    return jnp.where(lane < HD, pair, other)


def causal(keys_count, rows_count):
    key = lax.broadcasted_iota(jnp.int32, (keys_count, rows_count), 0)
    return key <= lax.broadcasted_iota(jnp.int32, (keys_count, rows_count), 1)


def attend_kernel(heads, q_ref, k_ref, vt_ref, o_ref, lse_ref, slab_ref, high_ref, total_ref):
    block = pl.program_id(0)
    rows = q_ref[...]
    for head in range(heads):
        slab_ref[head] = head_slab(rows, head, 1.0)
    high_ref[...] = jnp.full(high_ref.shape, MASKED, f32)
    total_ref[...] = jnp.zeros(total_ref.shape, f32)

    def step(start, width, diagonal):
        keys = k_ref[pl.ds(start, width), :]
        values = vt_ref[:, pl.ds(start, width)]
        scores = [mm(keys, slab_ref[head], NT) for head in range(heads)]
        for head in range(heads):
            score = scores[head]
            if diagonal:
                score = jnp.where(causal(width, QB), score, MASKED)
            old = high_ref[head : head + 1, :]
            new = jnp.maximum(old, jnp.max(score, axis=0, keepdims=True))
            probs = jnp.exp(score - new).astype(bf16)
            high_ref[head : head + 1, :] = new
            total_ref[head] = total_ref[head] * jnp.exp(old - new) + mm(values, probs, NN)

    def body(index, carry):
        step(pl.multiple_of(index * WIDE, WIDE), WIDE, False)
        return carry

    lax.fori_loop(0, block // 2, body, 0)

    @pl.when(block % 2 == 1)
    def _():
        step(pl.multiple_of((block - 1) * QB, QB), QB, False)

    step(pl.multiple_of(block * QB, QB), QB, True)
    outs = []
    for head in range(heads):
        total = total_ref[head]
        mass = total[HD : HD + 1, :]
        lse_ref[head : head + 1, :] = high_ref[head : head + 1, :] + jnp.log(mass)
        outs.append(total[:HD, :] * (1.0 / mass))
    o_ref[...] = jnp.concatenate(outs, 0).T.astype(bf16)


def attend(queries, keys, values_t):
    count, q_cols = queries.shape
    heads = q_cols // HD
    return pl.pallas_call(
        functools.partial(attend_kernel, heads),
        grid=(count // QB,),
        in_specs=[
            pl.BlockSpec((QB, q_cols), lambda i: (i, 0)),
            pl.BlockSpec((count, 128), lambda i: (0, 0)),
            pl.BlockSpec((128, count), lambda i: (0, 0)),
        ],
        out_specs=[
            pl.BlockSpec((QB, q_cols), lambda i: (i, 0)),
            pl.BlockSpec((8, QB), lambda i: (0, i)),
        ],
        out_shape=[
            jax.ShapeDtypeStruct((count, q_cols), bf16),
            jax.ShapeDtypeStruct((8, count), f32),
        ],
        scratch_shapes=[
            pltpu.VMEM((heads, QB, 128), bf16),
            pltpu.VMEM((8, QB), f32),
            pltpu.VMEM((heads, 128, QB), f32),
        ],
        cost_estimate=cost(heads * count * count * 512, 4 * count * q_cols),
        name="attend",
    )(queries, keys, values_t)


def attend_back_kernel(
    heads,
    q_ref,
    do_ref,
    o_ref,
    lse_ref,
    k_ref,
    kt_ref,
    v_ref,
    table_ref,
    out_ref,
    qs_ref,
    ds_ref,
    delta_ref,
    dq_ref,
    dk_ref,
    dv_ref,
):
    block = pl.program_id(0)
    blocks = pl.num_programs(0)
    q_cols = heads * HD

    @pl.when(block == 0)
    def _():
        dk_ref[...] = jnp.zeros(dk_ref.shape, f32)
        dv_ref[...] = jnp.zeros(dv_ref.shape, f32)

    rows = q_ref[...]
    grads = do_ref[...]
    product = (grads.astype(f32) * o_ref[...].astype(f32)).T
    for head in range(heads):
        qs_ref[head] = head_slab(rows, head, 1.0)
        ds_ref[head] = head_slab(grads, head, 0.0)
        delta_ref[head : head + 1, :] = jnp.sum(
            product[head * HD : (head + 1) * HD, :], axis=0, keepdims=True
        )
    dq_ref[...] = jnp.zeros(dq_ref.shape, f32)

    def step(start, diagonal):
        here = pl.ds(start, QB)
        keys = k_ref[here, :]
        keys_t = kt_ref[:, here]
        values = v_ref[here, :]
        dk = dk_ref[here, :]
        dv = dv_ref[here, :]

        def products(head):
            return (mm(keys, qs_ref[head], NT), mm(values, ds_ref[head], NT))

        ready = products(0)
        for head in range(heads):
            score, prob_grad = ready
            if head + 1 < heads:
                ready = products(head + 1)
            probs = jnp.exp(score - lse_ref[head : head + 1, :])
            if diagonal:
                probs = jnp.where(causal(QB, QB), probs, 0.0)
            dv = dv + mm(probs.astype(bf16), ds_ref[head], NN)
            score_grad = (probs * (prob_grad - delta_ref[head : head + 1, :])).astype(bf16)
            dk = dk + mm(score_grad, qs_ref[head], NN)
            dq_ref[head] = dq_ref[head] + mm(keys_t, score_grad, NN)
        dk_ref[here, :] = dk
        dv_ref[here, :] = dv

    def body(index, carry):
        step(pl.multiple_of(index * QB, QB), False)
        return carry

    lax.fori_loop(0, block, body, 0)
    step(pl.multiple_of(block * QB, QB), True)
    dq = jnp.concatenate([dq_ref[head, :HD, :] for head in range(heads)], 0).T * ATTN_SCALE
    here = pl.ds(pl.multiple_of(block * QB, QB), QB)
    out_ref[here, :q_cols] = unrotate(dq, *turn_at(table_ref, block)).astype(bf16)

    @pl.when(block == blocks - 1)
    def _():
        def finish(index, carry):
            there = pl.ds(pl.multiple_of(index * QB, QB), QB)
            dk = dk_ref[there, :]
            lane = lax.broadcasted_iota(jnp.int32, dk.shape, 1)
            dk = unrotate(jnp.where(lane < HD, dk, 0.0), *turn_at(table_ref, index))
            dv = dv_ref[there, :]
            out_ref[there, q_cols:] = jnp.concatenate([dk[:, :HD], dv[:, :HD]], 1).astype(bf16)
            return carry

        lax.fori_loop(0, blocks, finish, 0)


def attend_back(queries, out_grads, attended, lse, keys, keys_t, values, table):
    count, q_cols = queries.shape
    heads = q_cols // HD
    row = lambda i: (i, 0)
    whole = lambda i: (0, 0)
    return pl.pallas_call(
        functools.partial(attend_back_kernel, heads),
        grid=(count // QB,),
        in_specs=[
            pl.BlockSpec((QB, q_cols), row),
            pl.BlockSpec((QB, q_cols), row),
            pl.BlockSpec((QB, q_cols), row),
            pl.BlockSpec((8, QB), lambda i: (0, i)),
            pl.BlockSpec((count, 128), whole),
            pl.BlockSpec((128, count), whole),
            pl.BlockSpec((count, 128), whole),
            pl.BlockSpec(table.shape, whole),
        ],
        out_specs=pl.BlockSpec((count, q_cols + 128), whole),
        out_shape=jax.ShapeDtypeStruct((count, q_cols + 128), bf16),
        scratch_shapes=[
            pltpu.VMEM((heads, QB, 128), bf16),
            pltpu.VMEM((heads, QB, 128), bf16),
            pltpu.VMEM((8, QB), f32),
            pltpu.VMEM((heads, 128, QB), f32),
            pltpu.VMEM((count, 128), f32),
            pltpu.VMEM((count, 128), f32),
        ],
        cost_estimate=cost(heads * count * count * 1280, 10 * count * q_cols),
        name="attend_back",
    )(queries, out_grads, attended, lse, keys, keys_t, values, table)


def column_block(ref, width):
    return pl.ds(pl.multiple_of(pl.program_id(0) * width, width), width)


def out_norm_kernel(ids_ref, o_ref, w_ref, rows_ref, gain_ref, middle_ref, normed_ref):
    here = column_block(middle_ref, w_ref.shape[1])
    groups, _, q_cols = o_ref.shape
    total = mm(o_ref[0], w_ref[:q_cols, :], NN)
    for group in range(1, groups):
        total += mm(o_ref[group], w_ref[group * q_cols : (group + 1) * q_cols, :], NN)
    middle_ref[:, here] = rows_ref[:, here].astype(f32) + RESID * total

    @pl.when(pl.program_id(0) == pl.num_programs(0) - 1)
    def _():
        middle = middle_ref[...]
        row_scale = lax.rsqrt(jnp.mean(middle * middle, axis=-1, keepdims=True) + EPSILON)
        normed_ref[...] = (middle * row_scale * gain_ref[...]).astype(bf16)


def out_norm(ids, attended, w_out, hidden, gain):
    groups, share, q_cols = attended.shape
    width = hidden.shape[1]
    whole = lambda j, s: (0, 0)
    return pl.pallas_call(
        out_norm_kernel,
        grid_spec=pltpu.PrefetchScalarGridSpec(
            num_scalar_prefetch=1,
            grid=(width // WIDE,),
            in_specs=[
                pl.BlockSpec((groups, share, q_cols), lambda j, s: (0, 0, 0)),
                pl.BlockSpec((groups * q_cols, WIDE), lambda j, s: (0, j)),
                pl.BlockSpec((share, width), lambda j, s: (s[0], 0)),
                pl.BlockSpec((1, width), whole),
            ],
            out_specs=[pl.BlockSpec((share, width), whole), pl.BlockSpec((share, width), whole)],
        ),
        out_shape=[
            jax.ShapeDtypeStruct((share, width), f32),
            jax.ShapeDtypeStruct((share, width), bf16),
        ],
        cost_estimate=cost(2 * groups * share * q_cols * width, 2 * groups * q_cols * width),
        name="out_project_and_norm",
    )(ids, attended, w_out, hidden, gain)


def norm_back_kernel(
    parts,
    ids_ref,
    *refs,
):
    part_refs = refs[:parts]
    middle_ref, gain_ref, cotangent_ref, w_ref, dh_ref, da_ref, gain_grad_ref, do_ref = refs[parts:]

    @pl.when(pl.program_id(0) == 0)
    def _():
        incoming = part_refs[0][...].astype(f32)
        for ref in part_refs[1:]:
            incoming = incoming + ref[...].astype(f32)
        middle = middle_ref[...]
        row_scale = lax.rsqrt(jnp.mean(middle * middle, axis=-1, keepdims=True) + EPSILON)
        normed = middle * row_scale
        gain_grad_ref[...] = jnp.sum(incoming * normed, axis=0, keepdims=True)
        scaled = incoming * gain_ref[...]
        branch = row_scale * (scaled - normed * jnp.mean(scaled * normed, axis=-1, keepdims=True))
        share = middle.shape[0]
        position = ids_ref[0] * share + lax.broadcasted_iota(jnp.int32, (share, 1), 0)
        direct = jnp.where(position < ids_ref[1], cotangent_ref[...].astype(f32), 0.0)
        dh = direct + branch
        dh_ref[...] = dh
        da_ref[...] = (RESID * dh).astype(bf16)

    per_step, _, q_cols = do_ref.shape
    for index in range(per_step):
        rows = w_ref[index * q_cols : (index + 1) * q_cols, :]
        do_ref[index] = mm(da_ref[...], rows, NT).astype(bf16)


def norm_back(ids, parts, middle, gain, cotangent, w_out, q_cols):
    share, width = middle.shape
    groups = w_out.shape[0] // q_cols
    per_step = WIDE // q_cols
    whole = lambda t, s: (0, 0)
    return pl.pallas_call(
        functools.partial(norm_back_kernel, len(parts)),
        grid_spec=pltpu.PrefetchScalarGridSpec(
            num_scalar_prefetch=1,
            grid=(groups // per_step,),
            in_specs=[pl.BlockSpec((share, width), whole)] * len(parts)
            + [
                pl.BlockSpec((share, width), whole),
                pl.BlockSpec((1, width), whole),
                pl.BlockSpec((share, width), lambda t, s: (s[0], 0)),
                pl.BlockSpec((WIDE, width), lambda t, s: (t, 0)),
            ],
            out_specs=[
                pl.BlockSpec((share, width), whole),
                pl.BlockSpec((share, width), whole),
                pl.BlockSpec((1, width), whole),
                pl.BlockSpec((per_step, share, q_cols), lambda t, s: (t, 0, 0)),
            ],
        ),
        out_shape=[
            jax.ShapeDtypeStruct((share, width), f32),
            jax.ShapeDtypeStruct((share, width), bf16),
            jax.ShapeDtypeStruct((1, width), f32),
            jax.ShapeDtypeStruct((groups, share, q_cols), bf16),
        ],
        cost_estimate=cost(2 * groups * share * q_cols * width, 2 * groups * q_cols * width),
        name="norm_back_and_project",
    )(ids, *parts, middle, gain, cotangent, w_out)


def in_grad_kernel(ids_ref, d_ref, w_ref, rows_ref, gain_ref, dh_ref, out_ref):
    here = column_block(out_ref, w_ref.shape[1])
    total = mm(d_ref[0], w_ref[0], NT)
    for group in range(1, d_ref.shape[0]):
        total += mm(d_ref[group], w_ref[group], NT)
    out_ref[:, here] = total

    @pl.when(pl.program_id(0) == pl.num_programs(0) - 1)
    def _():
        rows = rows_ref[...].astype(f32)
        row_scale = lax.rsqrt(jnp.mean(rows * rows, axis=-1, keepdims=True) + EPSILON)
        normed = rows * row_scale
        scaled = out_ref[...] * gain_ref[...]
        branch = row_scale * (scaled - normed * jnp.mean(scaled * normed, axis=-1, keepdims=True))
        out_ref[...] = dh_ref[...] + branch


def in_grad(ids, grads, w_qkv, hidden, gain, dh):
    groups, share, cols = grads.shape
    width = hidden.shape[1]
    whole = lambda j, s: (0, 0)
    return pl.pallas_call(
        in_grad_kernel,
        grid_spec=pltpu.PrefetchScalarGridSpec(
            num_scalar_prefetch=1,
            grid=(width // WIDE,),
            in_specs=[
                pl.BlockSpec((groups, share, cols), lambda j, s: (0, 0, 0)),
                pl.BlockSpec((groups, WIDE, cols), lambda j, s: (0, j, 0)),
                pl.BlockSpec((share, width), lambda j, s: (s[0], 0)),
                pl.BlockSpec((1, width), whole),
                pl.BlockSpec((share, width), whole),
            ],
            out_specs=pl.BlockSpec((share, width), whole),
        ),
        out_shape=jax.ShapeDtypeStruct((share, width), f32),
        cost_estimate=cost(2 * groups * share * cols * width, 2 * groups * cols * width),
        name="input_grad",
    )(ids, grads, w_qkv, hidden, gain, dh)


def out_wgrad_kernel(core_ref, o_ref, da_ref, send_ref, keep_ref):
    step = pl.program_id(0)
    groups, _, q_cols = o_ref.shape

    def store(ref):
        for group in range(groups):
            part = mm(o_ref[group], da_ref[...], TN)
            ref[0, group * q_cols : (group + 1) * q_cols, :] = part.astype(bf16)

    half = pl.num_programs(0) // 2
    pl.when(step < half)(lambda: store(send_ref))
    pl.when(step >= half)(lambda: store(keep_ref))


def out_wgrad_parts(core, attended, branch_grad, replicas):
    groups, share, q_cols = attended.shape
    width = branch_grad.shape[1]
    cols = width // replicas
    chips = replicas // 2
    column = lambda i, s: jnp.where(i < chips, 2 * i + 1 - s[0], 2 * (i - chips) + s[0])
    out = jax.ShapeDtypeStruct((chips, groups * q_cols, cols), bf16)
    block = (1, groups * q_cols, cols)
    return pl.pallas_call(
        out_wgrad_kernel,
        grid_spec=pltpu.PrefetchScalarGridSpec(
            num_scalar_prefetch=1,
            grid=(replicas,),
            in_specs=[
                pl.BlockSpec((groups, share, q_cols), lambda i, s: (0, 0, 0)),
                pl.BlockSpec((share, cols), lambda i, s: (0, column(i, s))),
            ],
            out_specs=[
                pl.BlockSpec(block, lambda i, s: (jnp.minimum(i, chips - 1), 0, 0)),
                pl.BlockSpec(block, lambda i, s: (jnp.maximum(i - chips, 0), 0, 0)),
            ],
        ),
        out_shape=[out, out],
        cost_estimate=cost(2 * groups * share * q_cols * width, 2 * groups * q_cols * width),
        name="out_weight_grad",
    )(core, attended, branch_grad)


def swiglu(normed, down_in, w_gate, w_up, w_down):
    gate = mm(normed, w_gate, NN)
    up = mm(normed, w_up, NN)
    act_grad = mm(down_in, w_down, NT)
    sg = jax.nn.sigmoid(gate)
    silu = gate * sg
    act = (silu * up).astype(bf16)
    gate_grad = (act_grad * up * sg * (1.0 + gate * (1.0 - sg))).astype(bf16)
    up_grad = (act_grad * silu).astype(bf16)
    normed_grad = (mm(gate_grad, w_gate, NT) + mm(up_grad, w_up, NT)).astype(bf16)
    return act, gate_grad, up_grad, normed_grad


def ring_order(count):
    inner = 2 if count <= 8 else 4
    outer = count // inner
    cells = [(0, 0)]
    for row in range(outer):
        cells += [(row, c) for c in (range(1, inner) if row % 2 == 0 else range(inner - 1, 0, -1))]
    cells += [(row, 0) for row in range(outer - 1, 0, -1)]
    return [row * inner + c for row, c in cells]


def add_low(left, right):
    return (left.astype(f32) + right.astype(f32)).astype(bf16)


def tie(*values):
    return lax.optimization_barrier(values)


def split_by_core(parts):
    replicas = parts.shape[0]
    core = lax.axis_index("dp") % 2
    by_core = parts.reshape((replicas // 2, 2) + parts.shape[1:])
    take = lambda i: lax.dynamic_index_in_dim(by_core, i, 1, keepdims=False)
    return take(1 - core), take(core)


def over_dp(send, keep):
    chips = send.shape[0]
    replicas = 2 * chips
    chip = lax.axis_index("dp") // 2
    take = lambda a, i: lax.dynamic_index_in_dim(a, i, 0, keepdims=False)
    got = lax.ppermute(send, "dp", [(i, i ^ 1) for i in range(replicas)])
    total = take(keep, chip).astype(f32) + take(got, chip).astype(f32)
    for step in range(1, chips):
        there = (chip + step) % chips
        term = take(keep, there).astype(f32) + take(got, there).astype(f32)
        moved = lax.ppermute(
            term.astype(send.dtype),
            "dp",
            [(i, ((i // 2 + step) % chips) * 2 + i % 2) for i in range(replicas)],
        )
        total = total + moved.astype(f32)
    return total


def local(
    hidden_in,
    seq_lengths,
    out_grad,
    attn_gain,
    mlp_gain,
    w_query,
    w_key,
    w_value,
    w_out,
    w_gate,
    w_up,
    w_down,
):
    rows_total, width = hidden_in.shape
    q_cols = w_query.shape[1]
    heads_here = q_cols // HD
    groups = lax.axis_size("tensor")
    replicas = lax.axis_size("dp")
    member = lax.axis_index("tensor")
    replica = lax.axis_index("dp")
    share = rows_total // groups
    order = ring_order(groups)
    place = [order.index(i) for i in range(groups)]
    ahead = [(order[i], order[(i + 1) % groups]) for i in range(groups)]
    behind = [(b, a) for a, b in ahead]
    half_way = groups // 2
    chunks = [
        [order[(place[i] + d) % groups] for d in range(-half_way + 1, half_way + 1)]
        for i in range(groups)
    ]
    near = jnp.asarray(chunks, jnp.int32)[member]
    at = lambda d: near[d + half_way - 1]
    length = seq_lengths[0]
    own_id = jnp.stack([member, length])
    table = rope_tables(rows_total)
    gain_one = attn_gain[None, :]
    gain_two = mlp_gain[None, :]
    half = share // 2

    def quarter(array):
        count = array.shape[0] // replicas
        return lax.dynamic_slice_in_dim(array, replica * count, count, 0)

    def exchange(array):
        return lax.all_to_all(array, "tensor", 0, 0, tiled=True)

    w_out_all = lax.all_gather(quarter(w_out), ("tensor", "dp"), axis=0, tiled=True)
    kv_of = [i * heads_here // (H // KVH) for i in range(groups)]
    w_kv = exchange(pick_heads(w_key, w_value, kv_of)).reshape(width, 2 * HD)
    normed_one, queries = front(hidden_in, gain_one, w_query, table)
    w_kv, normed_one = tie(w_kv, normed_one)
    w_qkv = jnp.concatenate([w_query, w_kv], 1)
    w_qkv_all = lax.all_gather(quarter(w_qkv), ("tensor", "dp"), axis=0, tiled=True)
    w_qkv_all = w_qkv_all.reshape(groups, width, q_cols + 2 * HD)
    keys, keys_t, values, values_t = keys_values(seq_lengths, normed_one, w_kv, table)
    attended, lse = attend(queries, keys, values_t)
    attended_rows = exchange(attended.reshape(groups, share, q_cols))
    positions = jnp.arange(rows_total, dtype=jnp.int32)[:, None]
    down_in = (jnp.where(positions < length, out_grad.astype(f32), 0.0) * RESID).astype(bf16)
    attended_rows, down_in = tie(attended_rows, down_in)
    middle, normed_two = out_norm(own_id, attended_rows, w_out_all, hidden_in, gain_two)
    normed_two, down_in = tie(normed_two, down_in)

    weights = (w_gate, w_up, w_down)
    chunk = lambda i: lax.dynamic_slice_in_dim(down_in, i * share, share, 0)
    ring_rows, ring_down, done = [normed_two], [chunk(member)], []
    from_behind = from_ahead = normed_two
    for distance in range(1, half_way + 1):
        if distance < half_way:
            from_behind = lax.ppermute(from_behind, "tensor", ahead)
            from_ahead = lax.ppermute(from_ahead, "tensor", behind)
        else:
            from_behind = lax.ppermute(from_behind[:half], "tensor", ahead)
            from_ahead = lax.ppermute(from_ahead[half:], "tensor", behind)
        units = swiglu(ring_rows[-1], ring_down[-1], *weights)
        from_behind, from_ahead, *units = tie(from_behind, from_ahead, *units)
        done.append(units)
        ring_rows.append(jnp.concatenate([from_behind, from_ahead], 0))
        if distance < half_way:
            ring_down.append(jnp.concatenate([chunk(at(-distance)), chunk(at(distance))], 0))
        else:
            ring_down.append(chunk(at(half_way)))
    done.append(swiglu(ring_rows[-1], ring_down[-1], *weights))
    act, gate_grad, up_grad = (jnp.concatenate([d[i] for d in done], 0) for i in range(3))
    normed_ring = jnp.concatenate(ring_rows, 0)
    down_ring = jnp.concatenate(ring_down, 0)

    def first_hop(far):
        return (
            lax.ppermute(far[:half], "tensor", ahead),
            lax.ppermute(far[half:], "tensor", behind),
        )

    def next_hop(pair, got, first):
        down, up = pair[:share], pair[share:]
        if first:
            up = jnp.concatenate([add_low(up[:half], got[0]), up[half:]], 0)
            down = jnp.concatenate([down[:half], add_low(down[half:], got[1])], 0)
        else:
            up, down = add_low(up, got[0]), add_low(down, got[1])
        return lax.ppermute(up, "tensor", ahead), lax.ppermute(down, "tensor", behind)

    grads = [d[3] for d in done]
    got = first_hop(grads[-1])
    mlp = mm(act, w_down, NN).astype(bf16)
    got, mlp = tie(got, mlp)
    fillers = [
        lambda: mm(act, down_ring, TN).astype(bf16),
        lambda: mm(normed_ring, gate_grad, TN).astype(bf16),
        lambda: mm(normed_ring, up_grad, TN).astype(bf16),
    ]
    filled = []
    for hop, pair in enumerate(reversed(grads[1:-1])):
        got = next_hop(pair, got, hop == 0)
        if hop < len(fillers):
            got, value = tie(got, fillers[hop]())
            filled.append(value)
    down_wgrad, gate_wgrad, up_wgrad = filled
    scatter = lambda a, d: lax.psum_scatter(a, "dp", scatter_dimension=d, tiled=True)
    down_wgrad = scatter(down_wgrad, 1)
    gate_wgrad = scatter(gate_wgrad, 0)
    up_wgrad = scatter(up_wgrad, 0)

    bounds = [0, share] + [share + 2 * share * d for d in range(1, half_way)] + [rows_total]
    mlp = [mlp[a:b] for a, b in zip(bounds[:-1], bounds[1:])]
    mlp_own, mlp_far, mlp_pairs = mlp[0], mlp[-1], list(reversed(mlp[1:-1]))
    got, mlp_far = tie(got, mlp_far)
    mlp_got = first_hop(mlp_far)
    middle_grad, branch_grad, mlp_gain_part, do_send = norm_back(
        own_id, [grads[0], *got], middle, gain_two, out_grad, w_out_all, q_cols
    )
    mlp_got, do_send, branch_grad = tie(mlp_got, do_send, branch_grad)
    attended_grad = exchange(do_send).reshape(rows_total, q_cols)
    core_id = (replica % 2)[None]
    out_parts = out_wgrad_parts(core_id, attended_rows, branch_grad, replicas)
    mlp_got = next_hop(mlp_pairs[0], mlp_got, True)
    attended_grad, mlp_got, *out_parts = tie(attended_grad, mlp_got, *out_parts)
    out_wgrad = over_dp(*out_parts).astype(bf16)
    mlp_got = next_hop(mlp_pairs[1], mlp_got, False)
    qkv_grad = attend_back(
        queries, attended_grad, attended, lse, keys, keys_t, values, table
    )
    mlp_got, qkv_grad, down_wgrad = tie(mlp_got, qkv_grad, down_wgrad)
    qkv_rows = exchange(qkv_grad.reshape(groups, share, q_cols + 2 * HD))

    qkv_wgrad = mm(normed_one, qkv_grad, TN)
    qkv_rows, qkv_wgrad, gate_wgrad = tie(qkv_rows, qkv_wgrad, gate_wgrad)
    attn_gain_part = jnp.sum(qkv_wgrad * w_qkv.astype(f32), axis=1) / attn_gain
    small = jnp.concatenate(
        [
            qkv_wgrad[:, q_cols:],
            attn_gain_part[:, None],
            mlp_gain_part[0][:, None],
            jnp.zeros((width, 126), f32),
        ],
        1,
    )
    small = over_dp(*split_by_core(small.reshape(replicas, -1, 256)))
    query_wgrad = qkv_wgrad[:, :q_cols].astype(bf16).reshape(replicas, -1, q_cols)
    query_wgrad = over_dp(*split_by_core(query_wgrad))
    pieces = exchange(small.reshape(groups, small.shape[0] // groups, 256))
    input_grad = in_grad(own_id, qkv_rows, w_qkv_all, hidden_in, gain_one, middle_grad)
    for pair in mlp_pairs[2:]:
        mlp_got = next_hop(pair, mlp_got, False)
    layer_out = (
        middle
        + RESID * (mlp_own.astype(f32) + mlp_got[0].astype(f32) + mlp_got[1].astype(f32))
    ).astype(bf16)
    gains = jnp.sum(pieces[:, :, 128:130], axis=0)
    kv = pieces[:, :, :128].reshape(KVH, groups // KVH, -1, 128).sum(axis=1)
    kv = jnp.swapaxes(kv, 0, 1)
    key_wgrad = kv[:, :, :HD].reshape(-1, KVH * HD)
    value_wgrad = kv[:, :, HD:].reshape(-1, KVH * HD)
    out_wgrad = lax.psum_scatter(out_wgrad, "tensor", scatter_dimension=0, tiled=True).astype(f32)
    return (
        layer_out,
        input_grad,
        gains[:, 0],
        gains[:, 1],
        query_wgrad,
        key_wgrad,
        value_wgrad,
        out_wgrad,
        gate_wgrad.astype(f32),
        up_wgrad.astype(f32),
        down_wgrad.astype(f32),
    )


def solution(mesh):
    placed = (
        P("dp", None),
        P("dp"),
        P("dp", None),
        P(),
        P(),
        P(None, "tensor"),
        P("tensor", None),
        P("tensor", None),
        P("tensor", None),
        P(None, "tensor"),
        P(None, "tensor"),
        P("tensor", None),
    )
    return jax.shard_map(
        local,
        mesh=mesh,
        in_specs=placed,
        out_specs=(
            P(("dp", "tensor"), None),
            P(("dp", "tensor"), None),
            P(("dp", "tensor")),
            P(("dp", "tensor")),
            P("dp", "tensor"),
            P(("dp", "tensor"), None),
            P(("dp", "tensor"), None),
            P("tensor", "dp"),
            P("dp", "tensor"),
            P("dp", "tensor"),
            P("tensor", "dp"),
        ),
        check_vma=False,
    )
```

time: 892 us -> 663 us (0.74)
  waiting for transfers between devices: 425 us -> 181 us
  Pallas kernels: 229 us -> 120 us
  matrix products: 55.6 us -> 157 us
  other arithmetic: 47 us -> 66.7 us
    reduce_scatter x6 -> x3, waiting for transfers between devices: 109 us -> 0.04 us  [local(): lax.psum_scatter(a, 'dp', scatter_dimension=d, tiled=True)]
    pallas_call x7 -> x5, Pallas kernels: 144 us -> 39.4 us  [the longest x1 12.2 us: norm_back(): pl.pallas_call(functools.partial(norm_back_kernel, len(parts)), grid_spec...]
    dot_general x5 -> x30, matrix products: 55.6 us -> 157 us  [mm(): return lax.dot_general(left, right, dims, preferred_element_type=f32)]
    ppermute x18 -> x24, waiting for transfers between devices: 195 us -> 103 us  [the longest x3 54.6 us: over_dp(): lax.ppermute(term.astype(send.dtype), 'dp', [(i, (i // 2 + step) % chips...]
    reduce_scatter x1, waiting for transfers between devices: 63.9 us -> 39 us  [local(): lax.psum_scatter(out_wgrad, 'tensor', scatter_dimension=0, tiled=True)]
    all_to_all x5, waiting for transfers between devices: 57.7 us -> 33.2 us  [exchange(): return lax.all_to_all(array, 'tensor', 0, 0, tiled=True)]
    all_gather x1 -> x0, local copies, waits for them, and re-layouts: 16.9 us -> none  [local(): lax.all_gather(quarter(w_qkv), ('tensor', 'dp'), axis=0, tiled=True)]
    convert_element_type x5 -> x9, other arithmetic: 12.1 us -> 28.5 us  [the longest x1 8.11 us: local(): (jnp.where(positions < length, out_grad.astype(f32), 0.0) * RESID).astype...]
  transfers between devices with their start and end apart: 38 -> 41, of which waited for: 20 -> 20; matrix products, arithmetic and copies ran while one was open for 15% -> 32% of each run, Pallas kernels for 21% -> 17%
where the time goes in v2:
time: 663 us; the launch traced here: 656 us
  waiting for transfers between devices  181 us (27%)
  matrix products  157 us (24%)
  Pallas kernels  120 us (18%)
  other arithmetic  66.7 us (10%)
  starting transfers between devices  61.2 us (9%)
  local copies, waits for them, and re-layouts  49.9 us (8%)
  between operations  20.3 us (3%)
    dot_general x30, matrix products, mm(): return lax.dot_general(left, right, dims, preferred_element_type=f32)  157 us
    ppermute x3, waiting for transfers between devices, over_dp(): lax.ppermute(term.astype(send.dtype), 'dp', [(i, (i // 2 + step) % chips...  54.6 us
    reduce_scatter x1, waiting for transfers between devices, local(): lax.psum_scatter(out_wgrad, 'tensor', scatter_dimension=0, tiled=True)  39 us
    pallas_call x1, Pallas kernels, attend_back(): pl.pallas_call(functools.partial(attend_back_kernel, heads), grid=(count...  36.9 us
    all_to_all x5, waiting for transfers between devices, exchange(): return lax.all_to_all(array, 'tensor', 0, 0, tiled=True)  33.2 us
    unnamed x106, local copies, waits for them, and re-layouts  31.1 us
    ppermute x6, waiting for transfers between devices, next_hop(): lax.ppermute(down, 'tensor', behind)  25 us
    all_to_all x5, starting transfers between devices, exchange(): return lax.all_to_all(array, 'tensor', 0, 0, tiled=True)  24 us
  transfers between devices with their start and end apart: 41, of which 20 were waited for; matrix products, arithmetic and copies ran while one was open for 32% of the time, Pallas kernels for 17%

profile of v2, /device:TPU:0, one launch (start us, length us, event | category | flops | bytes accessed | tf_op | source)
XLA Modules:
  0.0 656.4 jit_solution(18418273940083615162)
XLA Ops:
  11.2 7.3 %all-to-all-start = ((bf16[8,256,128]{2,1,0:T(8,128)(2,1)}), bf16[8,256,128]{2,1,0:T(8,128)(2,1)S(1)}, u32[]{:S(2)}, u32[]{:S(2)}) async-start(bf16[8,256,128]{2,1,0:T(8,128)(2,1)} %pick_heads.1), calls=%async_computation | async-start | bytes 1048576 | tf_op jit(solution)/shard_map/all_to_all | solution.py:690
  20.6 10.8 %norm_and_query.1 = (bf16[2048,2048]{1,0:T(8,128)(2,1)}, bf16[2048,256]{1,0:T(8,128)(2,1)}) custom-call(bf16[2048,2048]{1,0:T(8,128)(2,1)} %rows_ref.5, f32[1,2048]{1,0:T(1,128)} %bitcast.121, bf16[2048,256]{1,0:T(8,128)(2,1)} %wq_ref.1, f32[320,256]{1,0:T(8,128)} %pad_maximum_fusion.4.table_ref), custom_call_target="tpu_custom_call" | custom-call | flops 2147483648 | bytes 20971520 | tf_op jit(solution)/shard_map/norm_and_query/pallas_call | solution.py:103
  31.4 7.1 %all-to-all-done = bf16[8,256,128]{2,1,0:T(8,128)(2,1)S(1)} async-done(((bf16[8,256,128]{2,1,0:T(8,128)(2,1)}), bf16[8,256,128]{2,1,0:T(8,128)(2,1)S(1)}, u32[]{:S(2)}, u32[]{:S(2)}) %all-to-all-start) | async-done | bytes 524320 | tf_op jit(solution)/shard_map/all_to_all | solution.py:690
  39.2 7.2 %keys_and_values.1 = (bf16[2048,128]{1,0:T(8,128)(2,1)}, bf16[128,2048]{1,0:T(8,128)(2,1)}, bf16[2048,128]{1,0:T(8,128)(2,1)}, bf16[128,2048]{1,0:T(8,128)(2,1)}) custom-call(s32[1]{0:T(128)} %copy.71.length_ref, bf16[2048,2048]{1,0:T(8,128)(2,1)} %get-tuple-element.90.normed_ref, bf16[2048,128]{1,0:T(8,128)(2,1)} %bitcast.112, ...), custom_call_target="tpu_custom_call" | custom-call | flops 1073741824 | bytes 8388608 | tf_op jit(solution)/shard_map/keys_and_values/pallas_call | solution.py:143
  46.4 22.7 %attend.1 = (bf16[2048,256]{1,0:T(8,128)(2,1)}, f32[8,2048]{1,0:T(8,128)}) custom-call(bf16[2048,256]{1,0:T(8,128)(2,1)} %get-tuple-element.88.q_ref, bf16[2048,128]{1,0:T(8,128)(2,1)} %get-tuple-element.92.k_ref, bf16[128,2048]{1,0:T(8,128)(2,1)} %get-tuple-element.93.vt_ref), custom_call_target="tpu_custom_call" | custom-call | flops 8589934592 | bytes 2097152 | tf_op jit(solution)/shard_map/attend/pallas_call | solution.py:245
  69.1 3.6 all-to-all-start.1
  79.3 8.1 %multiply_convert_fusion = bf16[2048,2048]{1,0:T(8,128)(2,1)} fusion(bf16[2048,2048]{1,0:T(8,128)(2,1)} %refs_5_.1, pred[2048]{0:T(1024)(128)(4,1)S(1)} %iota_compare_fusion), kind=kLoop, calls=%fused_computation | loop fusion | flops 16777216 | bytes 16779264 | tf_op jit(solution)/shard_map/convert_element_type | solution.py:704
  87.4 26.1 %all-to-all-done.1.o_ref = bf16[8,256,256]{2,1,0:T(8,128)(2,1)S(1)} async-done(((bf16[8,256,256]{2,1,0:T(8,128)(2,1)}), bf16[8,256,256]{2,1,0:T(8,128)(2,1)S(1)}, u32[]{:S(2)}, u32[]{:S(2)}) %all-to-all-start.1) | async-done | bytes 1048608 | tf_op jit(solution)/shard_map/all_to_all | solution.py:690
  114.5 8.8 %out_project_and_norm.1 = (f32[256,2048]{1,0:T(8,128)}, bf16[256,2048]{1,0:T(8,128)(2,1)}) custom-call(s32[2]{0:T(128)} %pad_add_fusion.ids_ref, bf16[8,256,256]{2,1,0:T(8,128)(2,1)} %copy-done.9, bf16[2048,2048]{1,0:T(8,128)(2,1)} %all-gather.3.cloned.1.call-done.w_ref.refs_6_, bf16[2048,2048]{1,0:T(8,128)(2,1)} %rows_ref.5, f32[1,2048]{1,0:T(1,128)} %bitcast.123), custom_call_target="tpu_custom_call" | custom-call | flops 2147483648 | bytes 8388608 | tf_op jit(solution)/shard_map/out_project_and_norm/pallas_call | solution.py:415
  125.8 3.9 fusion.45
  136.8 2.3 fusion.23
  146.3 2.3 fusion.1.refs_0_
  150.7 3.7 fusion.48
  154.4 3.7 fusion.49
  160.2 6.5 multiply_convert_fusion.7
  166.7 4.3 fusion.50
  172.9 5.8 add_convert_fusion.3
  178.8 3.0 collective-permute-done.2
  182.9 2.4 fusion.51
  185.3 3.7 fusion.52
  191.0 6.5 multiply_convert_fusion.4
  197.5 6.5 fusion.53
  207.2 7.2 %add_convert_fusion.2 = bf16[512,2048]{1,0:T(8,128)(2,1)} fusion(f32[512,2048]{1,0:T(8,128)} %fusion.53, bf16[512,1024]{1,0:T(8,128)(2,1)S(1)} %get-tuple-element.129, bf16[2048,1024]{1,0:T(8,128)(2,1)} %param.23), kind=kOutput, calls=%fused_computation.6 | convolution fusion | flops 2149580800 | bytes 11534336 | tf_op jit(solution)/shard_map/dot_general | solution.py:32
  216.5 2.4 fusion.54
  218.9 2.4 fusion.55
  221.4 5.3 multiply_convert_fusion.1
  226.7 6.9 %fusion.56 = f32[512,2048]{1,0:T(8,128)} fusion(bf16[512,1024]{1,0:T(8,128)(2,1)S(1)} %get-tuple-element.124, bf16[2048,1024]{1,0:T(8,128)(2,1)} %param.22), kind=kOutput, calls=%fused_computation.179 | convolution fusion | flops 2147483648 | bytes 9437184 | tf_op jit(solution)/shard_map/dot_general | solution.py:32
  239.7 4.6 add_convert_fusion.1
  245.2 6.5 fusion.57
  255.0 2.7 constant_dynamic-update-slice_fusion.27
  263.4 10.9 %convolution_convert_fusion = bf16[2048,2048]{1,0:T(8,128)(2,1)} fusion(bf16[2048,1024]{1,0:T(8,128)(2,1)S(1)} %get-tuple-element.208, bf16[1024,2048]{1,0:T(8,128)(2,1)S(1)} %copy-done.37), kind=kOutput, calls=%fused_computation.1 | convolution fusion | flops 8594128896 | bytes 16777216 | tf_op jit(solution)/shard_map/dot_general | solution.py:32
  279.0 13.2 %convolution_convert_fusion.1 = bf16[1024,2048]{1,0:T(8,128)(2,1)} fusion(bf16[2048,1024]{1,0:T(8,128)(2,1)S(1)} %get-tuple-element.208, bf16[2048,2048]{1,0:T(8,128)(2,1)} %dynamic-slice_dynamic-update-slice_fusion.1), kind=kOutput, calls=%fused_computation.8 | convolution fusion | flops 8592031744 | bytes 16777216 | tf_op jit(solution)/shard_map/dot_general | solution.py:32
  292.2 4.7 collective-permute-done.11
  298.9 4.2 add_convert_fusion.11
  305.2 13.5 %convolution_convert_fusion.3 = bf16[2048,1024]{1,0:T(8,128)(2,1)} fusion(bf16[2048,2048]{1,0:T(8,128)(2,1)} %copy-done.21, bf16[2048,1024]{1,0:T(8,128)(2,1)S(1)} %copy-done.24), kind=kOutput, calls=%fused_computation.10 | convolution fusion | flops 8592031744 | bytes 16777216 | tf_op jit(solution)/shard_map/dot_general | solution.py:32
  318.7 4.1 collective-permute-done.12
  323.5 3.5 add_convert_fusion.9
  329.0 13.1 %convolution_convert_fusion.2 = bf16[2048,1024]{1,0:T(8,128)(2,1)} fusion(bf16[2048,2048]{1,0:T(8,128)(2,1)} %copy-done.21, bf16[2048,1024]{1,0:T(8,128)(2,1)S(1)} %copy-done.23), kind=kOutput, calls=%fused_computation.9 | convolution fusion | flops 8592031744 | bytes 16777216 | tf_op jit(solution)/shard_map/dot_general | solution.py:32
  342.1 3.8 collective-permute-done.14.refs_1_
  353.8 12.2 %norm_back_and_project.1 = (f32[256,2048]{1,0:T(8,128)}, bf16[256,2048]{1,0:T(8,128)(2,1)}, f32[1,2048]{1,0:T(1,128)}, bf16[8,256,256]{2,1,0:T(8,128)(2,1)}) custom-call(s32[2]{0:T(128)} %pad_add_fusion.ids_ref, bf16[256,2048]{1,0:T(8,128)(2,1)} %fusion.1.refs_0_, bf16[256,2048]{1,0:T(8,128)(2,1)} %copy-done.14, ...), custom_call_target="tpu_custom_call" | custom-call | flops 2147483648 | bytes 8388608 | tf_op jit(solution)/shard_map/norm_back_and_project/pallas_call | solution.py:474
  366.0 3.6 all-to-all-start.2
  374.4 7.1 %out_weight_grad.1 = (bf16[2,2048,512]{2,1,0:T(8,128)(2,1)}, bf16[2,2048,512]{2,1,0:T(8,128)(2,1)}) custom-call(s32[1]{0:T(128)} %bitcast.14.core_ref, bf16[8,256,256]{2,1,0:T(8,128)(2,1)} %copy-done.9, bf16[256,2048]{1,0:T(8,128)(2,1)} %get-tuple-element.142.da_ref), custom_call_target="tpu_custom_call" | custom-call | flops 2147483648 | bytes 8388608 | tf_op jit(solution)/shard_map/out_weight_grad/pallas_call | solution.py:567
  381.6 19.5 %collective-permute-done.19 = bf16[256,2048]{1,0:T(8,128)(2,1)} collective-permute-done((bf16[256,2048]{1,0:T(8,128)(2,1)S(1)}, bf16[256,2048]{1,0:T(8,128)(2,1)}, u32[]{:S(2)}, u32[]{:S(2)}) %collective-permute-start.19) | collective-permute-done | bytes 1048608 | tf_op jit(solution)/shard_map/ppermute | solution.py:746
  403.4 4.4 add_convert_fusion.7
  408.7 6.2 collective-permute-start.21
  414.9 36.9 %attend_back.1 = bf16[2048,384]{1,0:T(8,128)(2,1)} custom-call(bf16[2048,256]{1,0:T(8,128)(2,1)} %get-tuple-element.88.q_ref, bf16[2048,256]{1,0:T(8,128)(2,1)} %bitcast.120, bf16[2048,256]{1,0:T(8,128)(2,1)} %get-tuple-element.94.o_ref, f32[8,2048]{1,0:T(8,128)} %get-tuple-element.148.lse_ref, bf16[2048,128]{1,0:T(8,128)(2,1)} %get-tuple-element.92.k_ref, ...), custom_call_target="tpu_custom_call" | custom-call | flops 21474836480 | bytes 5242880 | tf_op jit(solution)/shard_map/attend_back/pallas_call | solution.py:364
  452.9 4.0 all-to-all-start.3
  457.0 4.2 fusion.3
  466.0 10.2 %fusion.59 = f32[2048,384]{1,0:T(8,128)} fusion(bf16[2048,2048]{1,0:T(8,128)(2,1)} %get-tuple-element.90.normed_ref, bf16[2048,384]{1,0:T(8,128)(2,1)} %attend_back.1), kind=kOutput, calls=%fused_computation.182 | convolution fusion | flops 3221225472 | bytes 13107200 | tf_op jit(solution)/shard_map/dot_general | solution.py:32
  476.2 46.3 %collective-permute-done.29 = bf16[2048,512]{1,0:T(8,128)(2,1)} collective-permute-done((bf16[2048,512]{1,0:T(8,128)(2,1)}, bf16[2048,512]{1,0:T(8,128)(2,1)}, u32[]{:S(2)}, u32[]{:S(2)}) %collective-permute-start.29) | collective-permute-done | bytes 2097184 | tf_op jit(solution)/shard_map/ppermute | solution.py:636
  522.5 4.5 fusion
  527.1 3.3 multiply_reduce_fusion
  535.6 3.7 add_convert_fusion.6
  543.4 2.5 collective-permute-start.25
  550.1 8.3 %collective-permute-done.25 = f32[512,256]{1,0:T(8,128)} collective-permute-done((f32[512,256]{1,0:T(8,128)}, f32[512,256]{1,0:T(8,128)}, u32[]{:S(2)}, u32[]{:S(2)}) %collective-permute-start.25) | collective-permute-done | bytes 524320 | tf_op jit(solution)/shard_map/ppermute | solution.py:636
  558.4 2.3 fusion.28
  560.7 5.5 all-to-all-start.4
  566.2 10.8 %collective-permute-done.22 = bf16[256,2048]{1,0:T(8,128)(2,1)} collective-permute-done((bf16[256,2048]{1,0:T(8,128)(2,1)}, bf16[256,2048]{1,0:T(8,128)(2,1)}, u32[]{:S(2)}, u32[]{:S(2)}) %collective-permute-start.22) | collective-permute-done | bytes 1048608 | tf_op jit(solution)/shard_map/ppermute | solution.py:746
  577.0 3.5 add_convert_fusion.4
  580.5 2.9 convert_element_type.375
  583.4 2.8 convert_element_type.374
  587.2 2.3 collective-permute-start.27
  589.5 12.4 %input_grad.1 = f32[256,2048]{1,0:T(8,128)} custom-call(s32[2]{0:T(128)} %pad_add_fusion.ids_ref, bf16[8,256,384]{2,1,0:T(8,128)(2,1)} %copy-done.5, bf16[8,2048,384]{2,1,0:T(8,128)(2,1)} %bitcast.110, bf16[2048,2048]{1,0:T(8,128)(2,1)} %rows_ref.5, f32[1,2048]{1,0:T(1,128)} %bitcast.122, f32[256,2048]{1,0:T(8,128)} %get-tuple-element.157.dh_ref), custom_call_target="tpu_custom_call" | custom-call | flops 3221225472 | bytes 12582912 | tf_op jit(solution)/shard_map/input_grad/pallas_call | solution.py:525
  608.5 39.0 %reduce-scatter.9.cloned.1.call-done = bf16[256,512]{1,0:T(8,128)(2,1)} async-done(((bf16[2048,512]{1,0:T(8,128)(2,1)}), bf16[256,512]{1,0:T(8,128)(2,1)}) %reduce-scatter.9.cloned.1.call-update) | async-done | bytes 262160 | tf_op jit(solution)/shard_map/reduce_scatter | solution.py:819
  (236 shorter events, 112.5 us)
Async XLA Ops:
  7.2 106.5 %all-gather.3.cloned.1.call-start = ((), (), s32[]{:S(2)}) async-start(), calls=%async_computation.9 | async-start | bytes 8650752 | tf_op jit(solution)/shard_map/all_gather | solution.py:692
  11.2 27.2 %all-to-all-start = ((bf16[8,256,128]{2,1,0:T(8,128)(2,1)}), bf16[8,256,128]{2,1,0:T(8,128)(2,1)S(1)}, u32[]{:S(2)}, u32[]{:S(2)}) async-start(bf16[8,256,128]{2,1,0:T(8,128)(2,1)} %pick_heads.1), calls=%async_computation | async-start | bytes 1048576 | tf_op jit(solution)/shard_map/all_to_all | solution.py:690
  69.1 44.4 %all-to-all-start.1 = ((bf16[8,256,256]{2,1,0:T(8,128)(2,1)}), bf16[8,256,256]{2,1,0:T(8,128)(2,1)S(1)}, u32[]{:S(2)}, u32[]{:S(2)}) async-start(bf16[8,256,256]{2,1,0:T(8,128)(2,1)} %bitcast.119), calls=%async_computation.1 | async-start | bytes 2097152 | tf_op jit(solution)/shard_map/all_to_all | solution.py:690
  72.7 379.2 %reduce-scatter.5.cloned.1.call-start = ((), (), s32[]{:S(2)}) async-start(), calls=%async_computation.10 | async-start | bytes 5242880 | tf_op jit(solution)/shard_map/reduce_scatter | solution.py:764
  123.3 6.4 copy-start.15
  123.3 6.4 copy-start.31
  123.3 25.3 %collective-permute-start = (bf16[256,2048]{1,0:T(8,128)(2,1)}, bf16[256,2048]{1,0:T(8,128)(2,1)S(1)}, u32[]{:S(2)}, u32[]{:S(2)}) collective-permute-start(bf16[256,2048]{1,0:T(8,128)(2,1)} %get-tuple-element.100), channel_id=1, source_target_pairs={{0,1},{1,3},{3,5},{5,7},{7,6},{6,4},{4,2},{2,0},{8,9},{9,11},{11,1... | collective-permute-start | bytes 3145736 | tf_op jit(solution)/shard_map/ppermute | solution.py:715
  124.8 25.4 %collective-permute-start.1 = (bf16[256,2048]{1,0:T(8,128)(2,1)}, bf16[256,2048]{1,0:T(8,128)(2,1)S(1)}, u32[]{:S(2)}, u32[]{:S(2)}) collective-permute-start(bf16[256,2048]{1,0:T(8,128)(2,1)} %get-tuple-element.100), channel_id=1, source_target_pairs={{1,0},{3,1},{5,3},{7,5},{6,7},{4,6},{2,4},{0,2},{9,8},{11,9},{13,1... | collective-permute-start | bytes 3145736 | tf_op jit(solution)/shard_map/ppermute | solution.py:716
  125.8 5.2 copy-start.2
  158.0 23.7 %collective-permute-start.2 = (bf16[256,2048]{1,0:T(8,128)(2,1)S(1)}, bf16[256,2048]{1,0:T(8,128)(2,1)S(1)}, u32[]{:S(2)}, u32[]{:S(2)}) collective-permute-start(bf16[256,2048]{1,0:T(8,128)(2,1)S(1)} %collective-permute-done), channel_id=1, source_target_pairs={{0,1},{1,3},{3,5},{5,7},{7,6},{6,4},{4,2},{2,0},{8,9},{9,11},{11,1... | collective-permute-start | bytes 3145736 | tf_op jit(solution)/shard_map/ppermute | solution.py:715
  158.4 23.9 %collective-permute-start.3 = (bf16[256,2048]{1,0:T(8,128)(2,1)S(1)}, bf16[256,2048]{1,0:T(8,128)(2,1)S(1)}, u32[]{:S(2)}, u32[]{:S(2)}) collective-permute-start(bf16[256,2048]{1,0:T(8,128)(2,1)S(1)} %collective-permute-done.1), channel_id=1, source_target_pairs={{1,0},{3,1},{5,3},{7,5},{6,7},{4,6},{2,4},{0,2},{9,8},{11,9},{13,1... | collective-permute-start | bytes 3145736 | tf_op jit(solution)/shard_map/ppermute | solution.py:716
  178.8 4.1 copy-start.28
  189.0 25.4 %collective-permute-start.4 = (bf16[256,2048]{1,0:T(8,128)(2,1)S(1)}, bf16[256,2048]{1,0:T(8,128)(2,1)S(1)}, u32[]{:S(2)}, u32[]{:S(2)}) collective-permute-start(bf16[256,2048]{1,0:T(8,128)(2,1)S(1)} %collective-permute-done.2), channel_id=1, source_target_pairs={{0,1},{1,3},{3,5},{5,7},{7,6},{6,4},{4,2},{2,0},{8,9},{9,11},{11,1... | collective-permute-start | bytes 3145736 | tf_op jit(solution)/shard_map/ppermute | solution.py:715
  189.5 24.8 %collective-permute-start.5 = (bf16[256,2048]{1,0:T(8,128)(2,1)S(1)}, bf16[256,2048]{1,0:T(8,128)(2,1)S(1)}, u32[]{:S(2)}, u32[]{:S(2)}) collective-permute-start(bf16[256,2048]{1,0:T(8,128)(2,1)S(1)} %collective-permute-done.3), channel_id=1, source_target_pairs={{1,0},{3,1},{5,3},{7,5},{6,7},{4,6},{2,4},{0,2},{9,8},{11,9},{13,1... | collective-permute-start | bytes 3145736 | tf_op jit(solution)/shard_map/ppermute | solution.py:716
  233.7 11.1 %collective-permute-start.6 = (bf16[128,2048]{1,0:T(8,128)(2,1)S(1)}, bf16[128,2048]{1,0:T(8,128)(2,1)S(1)}, u32[]{:S(2)}, u32[]{:S(2)}) collective-permute-start(bf16[128,2048]{1,0:T(8,128)(2,1)S(1)} %slice.151), channel_id=1, source_target_pairs={{0,1},{1,3},{3,5},{5,7},{7,6},{6,4},{4,2},{2,0},{8,9},{9,11},{11,1... | collective-permute-start | bytes 1572872 | tf_op jit(solution)/shard_map/ppermute | solution.py:718
  234.2 10.9 %collective-permute-start.7 = (bf16[128,2048]{1,0:T(8,128)(2,1)S(1)}, bf16[128,2048]{1,0:T(8,128)(2,1)S(1)}, u32[]{:S(2)}, u32[]{:S(2)}) collective-permute-start(bf16[128,2048]{1,0:T(8,128)(2,1)S(1)} %slice.152), channel_id=1, source_target_pairs={{1,0},{3,1},{5,3},{7,5},{6,7},{4,6},{2,4},{0,2},{9,8},{11,9},{13,1... | collective-permute-start | bytes 1572872 | tf_op jit(solution)/shard_map/ppermute | solution.py:719
  245.2 7.6 %copy-start.21 = (bf16[2048,2048]{1,0:T(8,128)(2,1)}, bf16[2048,2048]{1,0:T(8,128)(2,1)S(1)}, u32[]{:S(2)}) copy-start(bf16[2048,2048]{1,0:T(8,128)(2,1)S(1)} %get-tuple-element.230) | copy-start | bytes 25165828
  245.2 7.6 %copy-start.25 = (bf16[2048,1024]{1,0:T(8,128)(2,1)S(1)}, bf16[2048,1024]{1,0:T(8,128)(2,1)}, u32[]{:S(2)}) copy-start(bf16[2048,1024]{1,0:T(8,128)(2,1)} %constant_dynamic-update-slice_fusion.9) | copy-start | bytes 12582916
  259.9 3.5 copy-start.37
  261.3 13.1 %collective-permute-start.8 = (bf16[128,2048]{1,0:T(8,128)(2,1)S(1)}, bf16[128,2048]{1,0:T(8,128)(2,1)S(1)}, u32[]{:S(2)}, u32[]{:S(2)}) collective-permute-start(bf16[128,2048]{1,0:T(8,128)(2,1)S(1)} %get-tuple-element.229), channel_id=1, source_target_pairs={{0,1},{1,3},{3,5},{5,7},{7,6},{6,4},{4,2},{2,0},{8,9},{9,11},{11,1... | collective-permute-start | bytes 1572872 | tf_op jit(solution)/shard_map/ppermute | solution.py:735
  262.5 11.9 %collective-permute-start.9 = (bf16[128,2048]{1,0:T(8,128)(2,1)S(1)}, bf16[128,2048]{1,0:T(8,128)(2,1)S(1)}, u32[]{:S(2)}, u32[]{:S(2)}) collective-permute-start(bf16[128,2048]{1,0:T(8,128)(2,1)S(1)} %get-tuple-element.228), channel_id=1, source_target_pairs={{1,0},{3,1},{5,3},{7,5},{6,7},{4,6},{2,4},{0,2},{9,8},{11,9},{13,1... | collective-permute-start | bytes 1572872 | tf_op jit(solution)/shard_map/ppermute | solution.py:736
  275.9 20.9 %collective-permute-start.11 = (bf16[256,2048]{1,0:T(8,128)(2,1)}, bf16[256,2048]{1,0:T(8,128)(2,1)}, u32[]{:S(2)}, u32[]{:S(2)}) collective-permute-start(bf16[256,2048]{1,0:T(8,128)(2,1)} %pad_maximum_fusion.1), channel_id=1, source_target_pairs={{1,0},{3,1},{5,3},{7,5},{6,7},{4,6},{2,4},{0,2},{9,8},{11,9},{13,1... | collective-permute-start | bytes 3145736 | tf_op jit(solution)/shard_map/ppermute | solution.py:746
  278.4 20.5 %collective-permute-start.10 = (bf16[256,2048]{1,0:T(8,128)(2,1)}, bf16[256,2048]{1,0:T(8,128)(2,1)S(1)}, u32[]{:S(2)}, u32[]{:S(2)}) collective-permute-start(bf16[256,2048]{1,0:T(8,128)(2,1)} %pad_maximum_fusion), channel_id=1, source_target_pairs={{0,1},{1,3},{3,5},{5,7},{7,6},{6,4},{4,2},{2,0},{8,9},{9,11},{11,1... | collective-permute-start | bytes 3145736 | tf_op jit(solution)/shard_map/ppermute | solution.py:746
  298.9 228.2 %reduce-scatter.7.cloned.1.call-start = ((), (), s32[]{:S(2)}) async-start(), calls=%async_computation.11 | async-start | bytes 5242880 | tf_op jit(solution)/shard_map/reduce_scatter | solution.py:764
  298.9 6.3 copy-start.24
  303.2 19.6 %collective-permute-start.12 = (bf16[256,2048]{1,0:T(8,128)(2,1)}, bf16[256,2048]{1,0:T(8,128)(2,1)S(1)}, u32[]{:S(2)}, u32[]{:S(2)}) collective-permute-start(bf16[256,2048]{1,0:T(8,128)(2,1)} %get-tuple-element.203), channel_id=1, source_target_pairs={{0,1},{1,3},{3,5},{5,7},{7,6},{6,4},{4,2},{2,0},{8,9},{9,11},{11,1... | collective-permute-start | bytes 3145736 | tf_op jit(solution)/shard_map/ppermute | solution.py:746
  303.9 19.5 %collective-permute-start.13 = (bf16[256,2048]{1,0:T(8,128)(2,1)}, bf16[256,2048]{1,0:T(8,128)(2,1)}, u32[]{:S(2)}, u32[]{:S(2)}) collective-permute-start(bf16[256,2048]{1,0:T(8,128)(2,1)} %get-tuple-element.202), channel_id=1, source_target_pairs={{1,0},{3,1},{5,3},{7,5},{6,7},{4,6},{2,4},{0,2},{9,8},{11,9},{13,1... | collective-permute-start | bytes 3145736 | tf_op jit(solution)/shard_map/ppermute | solution.py:746
  323.4 257.1 %reduce-scatter.11.cloned.1.call-start = ((), (), s32[]{:S(2)}) async-start(), calls=%async_computation.14 | async-start | bytes 5242880 | tf_op jit(solution)/shard_map/reduce_scatter | solution.py:764
  323.5 5.5 copy-start.23
  327.0 18.9 %collective-permute-start.14 = (bf16[256,2048]{1,0:T(8,128)(2,1)}, bf16[256,2048]{1,0:T(8,128)(2,1)S(1)}, u32[]{:S(2)}, u32[]{:S(2)}) collective-permute-start(bf16[256,2048]{1,0:T(8,128)(2,1)} %get-tuple-element.201), channel_id=1, source_target_pairs={{0,1},{1,3},{3,5},{5,7},{7,6},{6,4},{4,2},{2,0},{8,9},{9,11},{11,1... | collective-permute-start | bytes 3145736 | tf_op jit(solution)/shard_map/ppermute | solution.py:746
  327.4 18.8 %collective-permute-start.15 = (bf16[256,2048]{1,0:T(8,128)(2,1)}, bf16[256,2048]{1,0:T(8,128)(2,1)}, u32[]{:S(2)}, u32[]{:S(2)}) collective-permute-start(bf16[256,2048]{1,0:T(8,128)(2,1)} %get-tuple-element.200), channel_id=1, source_target_pairs={{1,0},{3,1},{5,3},{7,5},{6,7},{4,6},{2,4},{0,2},{9,8},{11,9},{13,1... | collective-permute-start | bytes 3145736 | tf_op jit(solution)/shard_map/ppermute | solution.py:746
  342.1 4.8 copy-start.12
  342.1 4.9 copy-start.8
  346.9 242.6 %all-gather.5.cloned.1.call-start = ((), (), s32[]{:S(2)}) async-start(), calls=%async_computation.12 | async-start | bytes 12976128 | tf_op jit(solution)/shard_map/all_gather | solution.py:698
  350.2 15.8 %collective-permute-start.16 = (bf16[128,2048]{1,0:T(8,128)(2,1)}, bf16[128,2048]{1,0:T(8,128)(2,1)S(1)}, u32[]{:S(2)}, u32[]{:S(2)}) collective-permute-start(bf16[128,2048]{1,0:T(8,128)(2,1)} %get-tuple-element.215), channel_id=1, source_target_pairs={{0,1},{1,3},{3,5},{5,7},{7,6},{6,4},{4,2},{2,0},{8,9},{9,11},{11,1... | collective-permute-start | bytes 1572872 | tf_op jit(solution)/shard_map/ppermute | solution.py:735
  350.6 15.4 %collective-permute-start.17 = (bf16[128,2048]{1,0:T(8,128)(2,1)}, bf16[128,2048]{1,0:T(8,128)(2,1)S(1)}, u32[]{:S(2)}, u32[]{:S(2)}) collective-permute-start(bf16[128,2048]{1,0:T(8,128)(2,1)} %get-tuple-element.214), channel_id=1, source_target_pairs={{1,0},{3,1},{5,3},{7,5},{6,7},{4,6},{2,4},{0,2},{9,8},{11,9},{13,1... | collective-permute-start | bytes 1572872 | tf_op jit(solution)/shard_map/ppermute | solution.py:736
  366.0 37.3 %all-to-all-start.2 = ((bf16[8,256,256]{2,1,0:T(8,128)(2,1)}), bf16[8,256,256]{2,1,0:T(8,128)(2,1)S(1)}, u32[]{:S(2)}, u32[]{:S(2)}) async-start(bf16[8,256,256]{2,1,0:T(8,128)(2,1)} %get-tuple-element.139), calls=%async_computation.2 | async-start | bytes 2097152 | tf_op jit(solution)/shard_map/all_to_all | solution.py:690
  371.3 29.8 %collective-permute-start.19 = (bf16[256,2048]{1,0:T(8,128)(2,1)S(1)}, bf16[256,2048]{1,0:T(8,128)(2,1)}, u32[]{:S(2)}, u32[]{:S(2)}) collective-permute-start(bf16[256,2048]{1,0:T(8,128)(2,1)S(1)} %pad_maximum_fusion.3), channel_id=1, source_target_pairs={{1,0},{3,1},{5,3},{7,5},{6,7},{4,6},{2,4},{0,2},{9,8},{11,9},{13,1... | collective-permute-start | bytes 3145736 | tf_op jit(solution)/shard_map/ppermute | solution.py:746
  374.3 29.0 %collective-permute-start.18 = (bf16[256,2048]{1,0:T(8,128)(2,1)}, bf16[256,2048]{1,0:T(8,128)(2,1)S(1)}, u32[]{:S(2)}, u32[]{:S(2)}) collective-permute-start(bf16[256,2048]{1,0:T(8,128)(2,1)} %pad_maximum_fusion.2), channel_id=1, source_target_pairs={{0,1},{1,3},{3,5},{5,7},{7,6},{6,4},{4,2},{2,0},{8,9},{9,11},{11,1... | collective-permute-start | bytes 3145736 | tf_op jit(solution)/shard_map/ppermute | solution.py:746
  403.3 11.6 %copy-start.16 = (bf16[8,256,256]{2,1,0:T(8,128)(2,1)}, bf16[8,256,256]{2,1,0:T(8,128)(2,1)S(1)}, u32[]{:S(2)}) copy-start(bf16[8,256,256]{2,1,0:T(8,128)(2,1)S(1)} %all-to-all-done.2) | copy-start | bytes 3145732
  403.3 53.6 %collective-permute-start.28 = (bf16[2,2048,512]{2,1,0:T(8,128)(2,1)}, bf16[2,2048,512]{2,1,0:T(8,128)(2,1)}, u32[]{:S(2)}, u32[]{:S(2)}) collective-permute-start(bf16[2,2048,512]{2,1,0:T(8,128)(2,1)} %get-tuple-element.161), channel_id=1, source_target_pairs={{0,8},{8,0},{16,24},{24,16},{1,9},{9,1},{17,25},{25,17},{2,10},{10... | collective-permute-start | bytes 12582920 | tf_op jit(solution)/shard_map/ppermute | solution.py:631
  407.8 44.0 %collective-permute-start.20 = (bf16[256,2048]{1,0:T(8,128)(2,1)}, bf16[256,2048]{1,0:T(8,128)(2,1)S(1)}, u32[]{:S(2)}, u32[]{:S(2)}) collective-permute-start(bf16[256,2048]{1,0:T(8,128)(2,1)} %get-tuple-element.186), channel_id=1, source_target_pairs={{0,1},{1,3},{3,5},{5,7},{7,6},{6,4},{4,2},{2,0},{8,9},{9,11},{11,1... | collective-permute-start | bytes 3145736 | tf_op jit(solution)/shard_map/ppermute | solution.py:746
  408.7 43.1 %collective-permute-start.21 = (bf16[256,2048]{1,0:T(8,128)(2,1)}, bf16[256,2048]{1,0:T(8,128)(2,1)S(1)}, u32[]{:S(2)}, u32[]{:S(2)}) collective-permute-start(bf16[256,2048]{1,0:T(8,128)(2,1)} %get-tuple-element.185), channel_id=1, source_target_pairs={{1,0},{3,1},{5,3},{7,5},{6,7},{4,6},{2,4},{0,2},{9,8},{11,9},{13,1... | collective-permute-start | bytes 3145736 | tf_op jit(solution)/shard_map/ppermute | solution.py:746
  451.8 9.3 %copy-start.17 = (bf16[256,2048]{1,0:T(8,128)(2,1)}, bf16[256,2048]{1,0:T(8,128)(2,1)S(1)}, u32[]{:S(2)}) copy-start(bf16[256,2048]{1,0:T(8,128)(2,1)S(1)} %collective-permute-done.20) | copy-start | bytes 3145732
  451.9 11.6 %copy-start.26 = (f32[1,2048]{1,0:T(1,128)S(1)}, f32[1,2048]{1,0:T(1,128)}, u32[]{:S(2)}) copy-start(f32[1,2048]{1,0:T(1,128)} %get-tuple-element.159) | copy-start | bytes 24580
  452.9 74.2 %all-to-all-start.3 = ((bf16[8,256,384]{2,1,0:T(8,128)(2,1)}), bf16[8,256,384]{2,1,0:T(8,128)(2,1)S(1)}, u32[]{:S(2)}, u32[]{:S(2)}) async-start(bf16[8,256,384]{2,1,0:T(8,128)(2,1)} %bitcast.118), calls=%async_computation.4 | async-start | bytes 3145728 | tf_op jit(solution)/shard_map/all_to_all | solution.py:690
  456.9 190.7 %reduce-scatter.9.cloned.1.call-start = ((), (), s32[]{:S(2)}) async-start(), calls=%async_computation.13 | async-start | bytes 2359296 | tf_op jit(solution)/shard_map/reduce_scatter | solution.py:819
  461.1 61.4 %collective-permute-start.29 = (bf16[2048,512]{1,0:T(8,128)(2,1)}, bf16[2048,512]{1,0:T(8,128)(2,1)}, u32[]{:S(2)}, u32[]{:S(2)}) collective-permute-start(bf16[2048,512]{1,0:T(8,128)(2,1)} %fusion.3), channel_id=1, source_target_pairs={{0,16},{8,24},{16,0},{24,8},{1,17},{9,25},{17,1},{25,9},{2,18},{10... | collective-permute-start | bytes 6291464 | tf_op jit(solution)/shard_map/ppermute | solution.py:636
  466.0 56.5 %copy-start.10 = (bf16[2,2048,512]{2,1,0:T(8,128)(2,1)S(1)}, bf16[2,2048,512]{2,1,0:T(8,128)(2,1)}, u32[]{:S(2)}) copy-start(bf16[2,2048,512]{2,1,0:T(8,128)(2,1)} %get-tuple-element.160) | copy-start | bytes 12582916
  527.0 3.4 copy-start.22
  527.0 5.3 slice-start
  527.1 5.2 copy-start.5
  534.4 7.1 %copy-start.4 = (f32[2,2,512,256]{3,2,1,0:T(8,128)}, f32[2,2,512,256]{3,2,1,0:T(8,128)S(1)}, u32[]{:S(2)}) copy-start(f32[2,2,512,256]{3,2,1,0:T(8,128)S(1)} %maximum_maximum_fusion) | copy-start | bytes 6291460
  535.5 10.3 %copy-start.13 = (bf16[1024,512]{1,0:T(8,128)(2,1)S(1)}, bf16[1024,512]{1,0:T(8,128)(2,1)}, u32[]{:S(2)}) copy-start(bf16[1024,512]{1,0:T(8,128)(2,1)} %reduce-scatter.5.cloned.1.call-done) | copy-start | bytes 3145732
  535.5 5.9 collective-permute-start.24
  539.3 37.7 %collective-permute-start.22 = (bf16[256,2048]{1,0:T(8,128)(2,1)}, bf16[256,2048]{1,0:T(8,128)(2,1)}, u32[]{:S(2)}, u32[]{:S(2)}) collective-permute-start(bf16[256,2048]{1,0:T(8,128)(2,1)} %get-tuple-element.183), channel_id=1, source_target_pairs={{0,1},{1,3},{3,5},{5,7},{7,6},{6,4},{4,2},{2,0},{8,9},{9,11},{11,1... | collective-permute-start | bytes 3145736 | tf_op jit(solution)/shard_map/ppermute | solution.py:746
  541.2 35.8 %collective-permute-start.23 = (bf16[256,2048]{1,0:T(8,128)(2,1)}, bf16[256,2048]{1,0:T(8,128)(2,1)}, u32[]{:S(2)}, u32[]{:S(2)}) collective-permute-start(bf16[256,2048]{1,0:T(8,128)(2,1)} %get-tuple-element.184), channel_id=1, source_target_pairs={{1,0},{3,1},{5,3},{7,5},{6,7},{4,6},{2,4},{0,2},{9,8},{11,9},{13,1... | collective-permute-start | bytes 3145736 | tf_op jit(solution)/shard_map/ppermute | solution.py:746
  543.4 15.0 %collective-permute-start.25 = (f32[512,256]{1,0:T(8,128)}, f32[512,256]{1,0:T(8,128)}, u32[]{:S(2)}, u32[]{:S(2)}) collective-permute-start(f32[512,256]{1,0:T(8,128)} %bitcast_add_fusion.1), channel_id=1, source_target_pairs={{0,16},{8,24},{16,0},{24,8},{1,17},{9,25},{17,1},{25,9},{2,18},{10... | collective-permute-start | bytes 1572872 | tf_op jit(solution)/shard_map/ppermute | solution.py:636
  545.9 31.1 %copy-start.3 = (f32[256,2048]{1,0:T(8,128)S(1)}, f32[256,2048]{1,0:T(8,128)}, u32[]{:S(2)}) copy-start(f32[256,2048]{1,0:T(8,128)} %get-tuple-element.96.refs_3_) | copy-start | bytes 6291460
  549.2 37.0 %copy-start.11 = (bf16[2048,256]{1,0:T(8,128)(2,1)}, bf16[2048,256]{1,0:T(8,128)(2,1)S(1)}, u32[]{:S(2)}) copy-start(bf16[2048,256]{1,0:T(8,128)(2,1)S(1)} %slice.212) | copy-start | bytes 3145732
  550.1 36.0 %collective-permute-start.26 = (bf16[2,512,256]{2,1,0:T(8,128)(2,1)}, bf16[2,512,256]{2,1,0:T(8,128)(2,1)}, u32[]{:S(2)}, u32[]{:S(2)}) collective-permute-start(bf16[2,512,256]{2,1,0:T(8,128)(2,1)} %dynamic-slice_bitcast_fusion.1), channel_id=1, source_target_pairs={{0,8},{8,0},{16,24},{24,16},{1,9},{9,1},{17,25},{25,17},{2,10},{10... | collective-permute-start | bytes 1572872 | tf_op jit(solution)/shard_map/ppermute | solution.py:631
  560.7 43.2 %all-to-all-start.4 = ((f32[8,64,256]{2,1,0:T(8,128)}), f32[8,64,256]{2,1,0:T(8,128)}, u32[]{:S(2)}, u32[]{:S(2)}) async-start(f32[8,64,256]{2,1,0:T(8,128)} %bitcast.117), calls=%async_computation.6 | async-start | bytes 1048576 | tf_op jit(solution)/shard_map/all_to_all | solution.py:690
  587.2 14.7 %collective-permute-start.27 = (bf16[512,256]{1,0:T(8,128)(2,1)S(1)}, bf16[512,256]{1,0:T(8,128)(2,1)S(1)}, u32[]{:S(2)}, u32[]{:S(2)}) collective-permute-start(bf16[512,256]{1,0:T(8,128)(2,1)S(1)} %fusion.26), channel_id=1, source_target_pairs={{0,16},{8,24},{16,0},{24,8},{1,17},{9,25},{17,1},{25,9},{2,18},{10... | collective-permute-start | bytes 786440 | tf_op jit(solution)/shard_map/ppermute | solution.py:636
  589.5 59.8 %copy-start.1 = (bf16[256,2048]{1,0:T(8,128)(2,1)S(1)}, bf16[256,2048]{1,0:T(8,128)(2,1)}, u32[]{:S(2)}) copy-start(bf16[256,2048]{1,0:T(8,128)(2,1)} %param.21) | copy-start | bytes 3145732
  (19 other events, 42.2 us)
Sparse Core Ops, SparseCore 0:
  11.5 102.2 all-gather.2
  299.0 42.6 reduce-scatter.4
  344.4 44.4 reduce-scatter.6
  391.3 44.4 reduce-scatter.10
  439.0 126.6 all-gather.4
  569.4 78.0 reduce-scatter.8

commit v3 on v2

v3 whole, which is shorter than its diff:
```python
import functools
import math

import jax
import jax.numpy as jnp
from jax import lax
from jax.experimental import pallas as pl
from jax.experimental.pallas import tpu as pltpu
from jax.sharding import PartitionSpec as P

H = 32
KVH = 8
HD = 64
SEQ_LEN = 2048
QB = 256
WIDE = 512

RESID = 0.22
ATTN_SCALE = 0.015625
EPSILON = 1e-05
THETA_LOG = math.log(10000000.0)
MASKED = -1e30

f32 = jnp.float32
bf16 = jnp.bfloat16
NN = (((1,), (0,)), ((), ()))
NT = (((1,), (1,)), ((), ()))
TN = (((0,), (0,)), ((), ()))


def mm(left, right, dims):
    return lax.dot_general(left, right, dims, preferred_element_type=f32)


def grant(mib):
    return pltpu.CompilerParams(vmem_limit_bytes=mib * 1024 * 1024)


def cost(flops, nbytes):
    return pl.CostEstimate(flops=int(flops), bytes_accessed=int(nbytes), transcendentals=0)


def rope_tables(count):
    lane = jnp.arange(128, dtype=jnp.int32) % (HD // 2)
    freqs = jnp.exp(-THETA_LOG * (2 * lane).astype(f32) / HD)[None, :]
    fine = jnp.arange(QB, dtype=jnp.int32)
    coarse = jnp.arange(count // QB * 8, dtype=jnp.int32) // 8 * QB
    angle_rows = jnp.concatenate([fine, coarse]).astype(f32)[:, None] * freqs
    return jnp.concatenate([jnp.cos(angle_rows), jnp.sin(angle_rows)], 1)


def turn_at(table_ref, block):
    fine = table_ref[:QB, :]
    coarse = table_ref[pl.ds(pl.multiple_of(QB + block * 8, 8), 8), :][:1, :]
    cos_f, sin_f, cos_c, sin_c = fine[:, :128], fine[:, 128:], coarse[:, :128], coarse[:, 128:]
    return cos_f * cos_c - sin_f * sin_c, sin_f * cos_c + cos_f * sin_c


def widen(table, count):
    return table if count == 128 else jnp.concatenate([table] * (count // 128), 1)


def swap_halves(rows):
    count = rows.shape[1]
    lane = lax.broadcasted_iota(jnp.int32, rows.shape, 1)
    ahead = pltpu.roll(rows, count - HD // 2, 1)
    behind = pltpu.roll(rows, HD // 2, 1)
    return jnp.where(lane % HD < HD // 2, ahead, behind)


def half_sign(shape):
    lane = lax.broadcasted_iota(jnp.int32, shape, 1)
    return jnp.where(lane % HD < HD // 2, -1.0, 1.0)


def rotate(rows, cosines, sines):
    count = rows.shape[1]
    turned = swap_halves(rows) * half_sign(rows.shape)
    return rows * widen(cosines, count) + turned * widen(sines, count)


def unrotate(rows, cosines, sines):
    count = rows.shape[1]
    turned = swap_halves(rows * widen(sines, count)) * half_sign(rows.shape)
    return rows * widen(cosines, count) - turned


def front_kernel(rows_ref, gain_ref, wq_ref, table_ref, normed_ref, q_ref):
    rows = rows_ref[...].astype(f32)
    row_scale = lax.rsqrt(jnp.mean(rows * rows, axis=-1, keepdims=True) + EPSILON)
    normed_ref[...] = (rows * row_scale * gain_ref[...]).astype(bf16)
    q_raw = mm(normed_ref[...], wq_ref[...], NN)
    turned = rotate(q_raw, *turn_at(table_ref, pl.program_id(0)))
    q_ref[...] = (turned.astype(bf16).astype(f32) * ATTN_SCALE).astype(bf16)


def front(hidden, gain, w_query, table):
    count, width = hidden.shape
    q_cols = w_query.shape[1]
    row = lambda i: (i, 0)
    whole = lambda i: (0, 0)
    return pl.pallas_call(
        front_kernel,
        grid=(count // QB,),
        in_specs=[
            pl.BlockSpec((QB, width), row),
            pl.BlockSpec((1, width), whole),
            pl.BlockSpec((width, q_cols), whole),
            pl.BlockSpec(table.shape, whole),
        ],
        out_specs=[pl.BlockSpec((QB, width), row), pl.BlockSpec((QB, q_cols), row)],
        out_shape=[
            jax.ShapeDtypeStruct((count, width), bf16),
            jax.ShapeDtypeStruct((count, q_cols), bf16),
        ],
        cost_estimate=cost(2 * count * width * q_cols, 5 * count * width),
        name="norm_and_query",
    )(hidden, gain, w_query, table)


def keys_kernel(length_ref, normed_ref, wkv_ref, table_ref, k_ref, kt_ref, v_ref, vt_ref):
    kv_raw = mm(normed_ref[...], wkv_ref[...], NN)
    lane = lax.broadcasted_iota(jnp.int32, kv_raw.shape, 1)
    position = pl.program_id(0) * WIDE + lax.broadcasted_iota(jnp.int32, kv_raw.shape, 0)
    blocks = [turn_at(table_ref, pl.program_id(0) * (WIDE // QB) + i) for i in range(WIDE // QB)]
    cosines, sines = (jnp.concatenate([b[i] for b in blocks], 0) for i in range(2))
    turned = rotate(kv_raw, cosines, sines)
    keys = jnp.where(lane < HD, turned, 0.0)
    blocked = jnp.where((lane == HD) & (position >= length_ref[0]), MASKED, 0.0)
    k_ref[...] = (keys + blocked).astype(bf16)
    kt_ref[...] = keys.T.astype(bf16)
    values = jnp.concatenate([kv_raw[:, HD:], kv_raw[:, :HD]], 1)
    values = jnp.where(lane < HD, values, 1.0)
    v_ref[...] = values.astype(bf16)
    vt_ref[...] = values.T.astype(bf16)


def keys_values(length, normed, w_kv, table):
    count, width = normed.shape
    row = lambda i, s: (i, 0)
    col = lambda i, s: (0, i)
    return pl.pallas_call(
        keys_kernel,
        grid_spec=pltpu.PrefetchScalarGridSpec(
            num_scalar_prefetch=1,
            grid=(count // WIDE,),
            in_specs=[
                pl.BlockSpec((WIDE, width), row),
                pl.BlockSpec((width, 128), lambda i, s: (0, 0)),
                pl.BlockSpec(table.shape, lambda i, s: (0, 0)),
            ],
            out_specs=[
                pl.BlockSpec((WIDE, 128), row),
                pl.BlockSpec((128, WIDE), col),
                pl.BlockSpec((WIDE, 128), row),
                pl.BlockSpec((128, WIDE), col),
            ],
        ),
        out_shape=[
            jax.ShapeDtypeStruct((count, 128), bf16),
            jax.ShapeDtypeStruct((128, count), bf16),
            jax.ShapeDtypeStruct((count, 128), bf16),
            jax.ShapeDtypeStruct((128, count), bf16),
        ],
        cost_estimate=cost(2 * count * width * 128, 2 * count * width),
        name="keys_and_values",
    )(length, normed, w_kv, table)


def pick_kernel(picks, k_ref, v_ref, out_ref):
    for index, head in enumerate(picks):
        both = [ref[:, 128 * (head // 2) : 128 * (head // 2) + 128] for ref in (k_ref, v_ref)]
        at = head % 2 * HD
        out_ref[index] = jnp.concatenate([b[:, at : at + HD] for b in both], 1)


def pick_heads(w_key, w_value, picks):
    return pl.pallas_call(
        functools.partial(pick_kernel, picks),
        out_shape=jax.ShapeDtypeStruct((len(picks), w_key.shape[0], 2 * HD), bf16),
        name="pick_heads",
    )(w_key, w_value)


def head_slab(rows, head, fill):
    pair = rows[:, 128 * (head // 2) : 128 * (head // 2) + 128]
    if head % 2:
        pair = jnp.concatenate([pair[:, HD:], pair[:, :HD]], 1)
    lane = lax.broadcasted_iota(jnp.int32, pair.shape, 1)
    other = jnp.where(lane == HD, jnp.full(pair.shape, fill, f32), 0.0).astype(pair.dtype)
    return jnp.where(lane < HD, pair, other)


def causal(keys_count, rows_count):
    key = lax.broadcasted_iota(jnp.int32, (keys_count, rows_count), 0)
    return key <= lax.broadcasted_iota(jnp.int32, (keys_count, rows_count), 1)


def attend_kernel(heads, q_ref, k_ref, vt_ref, o_ref, lse_ref, slab_ref, high_ref, total_ref):
    block = pl.program_id(0)
    rows = q_ref[...]
    for head in range(heads):
        slab_ref[head] = head_slab(rows, head, 1.0)
    high_ref[...] = jnp.full(high_ref.shape, MASKED, f32)
    total_ref[...] = jnp.zeros(total_ref.shape, f32)

    def step(start, width, diagonal):
        keys = k_ref[pl.ds(start, width), :]
        values = vt_ref[:, pl.ds(start, width)]
        scores = [mm(keys, slab_ref[head], NT) for head in range(heads)]
        for head in range(heads):
            score = scores[head]
            if diagonal:
                score = jnp.where(causal(width, QB), score, MASKED)
            old = high_ref[head : head + 1, :]
            new = jnp.maximum(old, jnp.max(score, axis=0, keepdims=True))
            probs = jnp.exp(score - new).astype(bf16)
            high_ref[head : head + 1, :] = new
            total_ref[head] = total_ref[head] * jnp.exp(old - new) + mm(values, probs, NN)

    def body(index, carry):
        step(pl.multiple_of(index * WIDE, WIDE), WIDE, False)
        return carry

    lax.fori_loop(0, block // 2, body, 0)

    @pl.when(block % 2 == 1)
    def _():
        step(pl.multiple_of((block - 1) * QB, QB), QB, False)

    step(pl.multiple_of(block * QB, QB), QB, True)
    outs = []
    for head in range(heads):
        total = total_ref[head]
        mass = total[HD : HD + 1, :]
        lse_ref[head : head + 1, :] = high_ref[head : head + 1, :] + jnp.log(mass)
        outs.append(total[:HD, :] * (1.0 / mass))
    o_ref[...] = jnp.concatenate(outs, 0).T.astype(bf16)


def attend(queries, keys, values_t):
    count, q_cols = queries.shape
    heads = q_cols // HD
    return pl.pallas_call(
        functools.partial(attend_kernel, heads),
        grid=(count // QB,),
        in_specs=[
            pl.BlockSpec((QB, q_cols), lambda i: (i, 0)),
            pl.BlockSpec((count, 128), lambda i: (0, 0)),
            pl.BlockSpec((128, count), lambda i: (0, 0)),
        ],
        out_specs=[
            pl.BlockSpec((QB, q_cols), lambda i: (i, 0)),
            pl.BlockSpec((8, QB), lambda i: (0, i)),
        ],
        out_shape=[
            jax.ShapeDtypeStruct((count, q_cols), bf16),
            jax.ShapeDtypeStruct((8, count), f32),
        ],
        scratch_shapes=[
            pltpu.VMEM((heads, QB, 128), bf16),
            pltpu.VMEM((8, QB), f32),
            pltpu.VMEM((heads, 128, QB), f32),
        ],
        cost_estimate=cost(heads * count * count * 512, 4 * count * q_cols),
        name="attend",
    )(queries, keys, values_t)


def attend_back_kernel(
    heads,
    first,
    q_ref,
    do_ref,
    o_ref,
    lse_ref,
    k_ref,
    kt_ref,
    v_ref,
    table_ref,
    *refs,
):
    carried = refs[:3] if first else ()
    outs = refs[len(carried) : -6]
    qs_ref, ds_ref, delta_ref, dq_ref, dk_ref, dv_ref = refs[-6:]
    step_id = pl.program_id(0)
    block = first + step_id
    last = pl.num_programs(0) - 1
    q_cols = heads * HD

    @pl.when(step_id == 0)
    def _():
        dk_ref[...] = carried[1][...] if first else jnp.zeros(dk_ref.shape, f32)
        dv_ref[...] = carried[2][...] if first else jnp.zeros(dv_ref.shape, f32)
        if first:
            outs[0][: first * QB, :q_cols] = carried[0][...]

    rows = q_ref[...]
    grads = do_ref[...]
    product = (grads.astype(f32) * o_ref[...].astype(f32)).T
    for head in range(heads):
        qs_ref[head] = head_slab(rows, head, 1.0)
        ds_ref[head] = head_slab(grads, head, 0.0)
        delta_ref[head : head + 1, :] = jnp.sum(
            product[head * HD : (head + 1) * HD, :], axis=0, keepdims=True
        )
    dq_ref[...] = jnp.zeros(dq_ref.shape, f32)

    def step(start, diagonal):
        here = pl.ds(start, QB)
        keys = k_ref[here, :]
        keys_t = kt_ref[:, here]
        values = v_ref[here, :]
        dk = dk_ref[here, :]
        dv = dv_ref[here, :]

        def products(head):
            return (mm(keys, qs_ref[head], NT), mm(values, ds_ref[head], NT))

        ready = products(0)
        for head in range(heads):
            score, prob_grad = ready
            if head + 1 < heads:
                ready = products(head + 1)
            probs = jnp.exp(score - lse_ref[head : head + 1, :])
            if diagonal:
                probs = jnp.where(causal(QB, QB), probs, 0.0)
            dv = dv + mm(probs.astype(bf16), ds_ref[head], NN)
            score_grad = (probs * (prob_grad - delta_ref[head : head + 1, :])).astype(bf16)
            dk = dk + mm(score_grad, qs_ref[head], NN)
            dq_ref[head] = dq_ref[head] + mm(keys_t, score_grad, NN)
        dk_ref[here, :] = dk
        dv_ref[here, :] = dv

    def body(index, carry):
        step(pl.multiple_of(index * QB, QB), False)
        return carry

    lax.fori_loop(0, block, body, 0)
    step(pl.multiple_of(block * QB, QB), True)
    dq = jnp.concatenate([dq_ref[head, :HD, :] for head in range(heads)], 0).T * ATTN_SCALE
    here = pl.ds(pl.multiple_of(block * QB, QB), QB)
    dq = unrotate(dq, *turn_at(table_ref, block)).astype(bf16)
    if first:
        outs[0][here, :q_cols] = dq
    else:
        outs[0][...] = dq

    @pl.when(step_id == last)
    def _():
        if not first:
            outs[1][...] = dk_ref[...]
            outs[2][...] = dv_ref[...]
            return

        def finish(index, carry):
            there = pl.ds(pl.multiple_of(index * QB, QB), QB)
            dk = dk_ref[there, :]
            lane = lax.broadcasted_iota(jnp.int32, dk.shape, 1)
            dk = unrotate(jnp.where(lane < HD, dk, 0.0), *turn_at(table_ref, index))
            dv = dv_ref[there, :]
            outs[0][there, q_cols:] = jnp.concatenate([dk[:, :HD], dv[:, :HD]], 1).astype(bf16)
            return carry

        lax.fori_loop(0, dk_ref.shape[0] // QB, finish, 0)


def attend_back(first, queries, out_grads, attended, lse, keys, keys_t, values, table, carried):
    count, q_cols = queries.shape
    heads = q_cols // HD
    blocks = count // QB
    split = blocks * 5 // 8
    steps = blocks - split if first else split
    start = split if first else 0
    row = lambda i: (start + i, 0)
    whole = lambda i: (0, 0)
    total = pl.BlockSpec((count, 128), whole)
    total_shape = jax.ShapeDtypeStruct((count, 128), f32)
    early = (split * QB, q_cols)
    if first:
        out_specs = pl.BlockSpec((count, q_cols + 128), whole)
        out_shape = jax.ShapeDtypeStruct((count, q_cols + 128), bf16)
    else:
        out_specs = [pl.BlockSpec((QB, q_cols), row), total, total]
        out_shape = [jax.ShapeDtypeStruct(early, bf16), total_shape, total_shape]
    return pl.pallas_call(
        functools.partial(attend_back_kernel, heads, start),
        grid=(steps,),
        in_specs=[
            pl.BlockSpec((QB, q_cols), row),
            pl.BlockSpec((QB, q_cols), row),
            pl.BlockSpec((QB, q_cols), row),
            pl.BlockSpec((8, QB), lambda i: (0, start + i)),
            total,
            pl.BlockSpec((128, count), whole),
            total,
            pl.BlockSpec(table.shape, whole),
        ]
        + ([pl.BlockSpec(early, whole), total, total] if first else []),
        out_specs=out_specs,
        out_shape=out_shape,
        scratch_shapes=[
            pltpu.VMEM((heads, QB, 128), bf16),
            pltpu.VMEM((heads, QB, 128), bf16),
            pltpu.VMEM((8, QB), f32),
            pltpu.VMEM((heads, 128, QB), f32),
            pltpu.VMEM((count, 128), f32),
            pltpu.VMEM((count, 128), f32),
        ],
        cost_estimate=cost(heads * count * count * 640, 10 * count * q_cols),
        name="attend_back",
    )(queries, out_grads, attended, lse, keys, keys_t, values, table, *carried)


LENGTH, CORE, RING = 0, 1, 2


def out_norm_kernel(ids_ref, o_ref, mine_ref, other_ref, rows_ref, gain_ref, middle_ref, normed_ref):
    step = pl.program_id(0)
    steps = pl.num_programs(0)
    groups, _, q_cols = o_ref.shape
    cols = mine_ref.shape[1]

    def work(w_ref, core, index):
        total = None
        for place in range(groups):
            term = mm(
                o_ref[ids_ref[RING + place]], w_ref[place * q_cols : (place + 1) * q_cols, :], NN
            )
            total = term if total is None else total + term
        first = core * (steps // 2) + index
        here = pl.ds(pl.multiple_of(first * cols, cols), cols)
        middle_ref[:, here] = rows_ref[:, here].astype(f32) + RESID * total

    core = ids_ref[CORE]
    pl.when(step < steps // 2)(lambda: work(mine_ref, core, step))
    pl.when(step >= steps // 2)(lambda: work(other_ref, 1 - core, step - steps // 2))

    @pl.when(step == steps - 1)
    def _():
        middle = middle_ref[...]
        row_scale = lax.rsqrt(jnp.mean(middle * middle, axis=-1, keepdims=True) + EPSILON)
        normed_ref[...] = (middle * row_scale * gain_ref[...]).astype(bf16)


def out_norm(ids, attended, w_mine, w_other, hidden, gain):
    groups, share, q_cols = attended.shape
    width = hidden.shape[1]
    whole = lambda j, s: (0, 0)
    steps = 2
    return pl.pallas_call(
        out_norm_kernel,
        grid_spec=pltpu.PrefetchScalarGridSpec(
            num_scalar_prefetch=1,
            grid=(steps,),
            in_specs=[
                pl.BlockSpec((groups, share, q_cols), lambda j, s: (0, 0, 0)),
                pl.BlockSpec(
                    (groups * q_cols, width // steps), lambda j, s: (0, jnp.minimum(j, steps // 2 - 1))
                ),
                pl.BlockSpec(
                    (groups * q_cols, width // steps), lambda j, s: (0, jnp.maximum(j - steps // 2, 0))
                ),
                pl.BlockSpec((share, width), lambda j, s: (s[RING], 0)),
                pl.BlockSpec((1, width), whole),
            ],
            out_specs=[pl.BlockSpec((share, width), whole), pl.BlockSpec((share, width), whole)],
        ),
        out_shape=[
            jax.ShapeDtypeStruct((share, width), f32),
            jax.ShapeDtypeStruct((share, width), bf16),
        ],
        cost_estimate=cost(2 * groups * share * q_cols * width, 2 * groups * q_cols * width),
        name="out_project_and_norm",
    )(ids, attended, w_mine, w_other, hidden, gain)


def norm_back_kernel(
    ids_ref,
    own_ref,
    up_ref,
    down_ref,
    middle_ref,
    gain_ref,
    cotangent_ref,
    mine_ref,
    other_ref,
    dh_ref,
    da_ref,
    gain_grad_ref,
    do_ref,
):
    step = pl.program_id(0)

    @pl.when(step == 0)
    def _():
        incoming = own_ref[...].astype(f32) + up_ref[...].astype(f32) + down_ref[...].astype(f32)
        middle = middle_ref[...]
        row_scale = lax.rsqrt(jnp.mean(middle * middle, axis=-1, keepdims=True) + EPSILON)
        normed = middle * row_scale
        gain_grad_ref[...] = jnp.sum(incoming * normed, axis=0, keepdims=True)
        scaled = incoming * gain_ref[...]
        branch = row_scale * (scaled - normed * jnp.mean(scaled * normed, axis=-1, keepdims=True))
        share = middle.shape[0]
        position = ids_ref[RING] * share + lax.broadcasted_iota(jnp.int32, (share, 1), 0)
        direct = jnp.where(position < ids_ref[LENGTH], cotangent_ref[...].astype(f32), 0.0)
        dh = direct + branch
        dh_ref[...] = dh
        da_ref[...] = (RESID * dh).astype(bf16)

    rows, cols = mine_ref.shape
    q_cols = do_ref.shape[2]
    core = ids_ref[CORE]
    mine = da_ref[:, pl.ds(pl.multiple_of(core * cols, cols), cols)]
    other = da_ref[:, pl.ds(pl.multiple_of((1 - core) * cols, cols), cols)]
    per_step = rows // q_cols
    for index in range(per_step):
        here = slice(index * q_cols, (index + 1) * q_cols)
        grad = mm(mine, mine_ref[here, :], NT) + mm(other, other_ref[here, :], NT)
        do_ref[ids_ref[RING + step * per_step + index]] = grad.astype(bf16)


def norm_back(ids, parts, middle, gain, cotangent, w_mine, w_other, q_cols):
    share, width = middle.shape
    groups = w_mine.shape[0] // q_cols
    whole = lambda t, s: (0, 0)
    weight = pl.BlockSpec((groups * q_cols // 2, width // 2), lambda t, s: (t, 0))
    return pl.pallas_call(
        norm_back_kernel,
        grid_spec=pltpu.PrefetchScalarGridSpec(
            num_scalar_prefetch=1,
            grid=(2,),
            in_specs=[pl.BlockSpec((share, width), whole)] * 4
            + [
                pl.BlockSpec((1, width), whole),
                pl.BlockSpec((share, width), lambda t, s: (s[RING], 0)),
                weight,
                weight,
            ],
            out_specs=[
                pl.BlockSpec((share, width), whole),
                pl.BlockSpec((share, width), whole),
                pl.BlockSpec((1, width), whole),
                pl.BlockSpec((groups, share, q_cols), lambda t, s: (0, 0, 0)),
            ],
        ),
        out_shape=[
            jax.ShapeDtypeStruct((share, width), f32),
            jax.ShapeDtypeStruct((share, width), bf16),
            jax.ShapeDtypeStruct((1, width), f32),
            jax.ShapeDtypeStruct((groups, share, q_cols), bf16),
        ],
        cost_estimate=cost(2 * groups * share * q_cols * width, 2 * groups * q_cols * width),
        name="norm_back_and_project",
    )(ids, *parts, middle, gain, cotangent, w_mine, w_other)


def in_grad_kernel(ids_ref, own_ref, up_ref, down_ref, rows_ref, gain_ref, dh_ref, out_ref):
    incoming = own_ref[...].astype(f32) + up_ref[...].astype(f32) + down_ref[...].astype(f32)
    rows = rows_ref[...].astype(f32)
    row_scale = lax.rsqrt(jnp.mean(rows * rows, axis=-1, keepdims=True) + EPSILON)
    normed = rows * row_scale
    scaled = incoming * gain_ref[...]
    branch = row_scale * (scaled - normed * jnp.mean(scaled * normed, axis=-1, keepdims=True))
    out_ref[...] = dh_ref[...] + branch


def in_grad(ids, terms, got, hidden, gain, dh):
    share, width = dh.shape
    steps = 4
    rows = share // steps
    row = lambda j, s: (j, 0)
    own = lambda j, s: (steps * s[RING] + j, 0)
    return pl.pallas_call(
        in_grad_kernel,
        grid_spec=pltpu.PrefetchScalarGridSpec(
            num_scalar_prefetch=1,
            grid=(steps,),
            in_specs=[
                pl.BlockSpec((rows, width), own),
                pl.BlockSpec((rows, width), row),
                pl.BlockSpec((rows, width), row),
                pl.BlockSpec((rows, width), own),
                pl.BlockSpec((1, width), lambda j, s: (0, 0)),
                pl.BlockSpec((rows, width), row),
            ],
            out_specs=pl.BlockSpec((rows, width), row),
        ),
        out_shape=jax.ShapeDtypeStruct((share, width), f32),
        cost_estimate=cost(20 * share * width, 16 * share * width),
        name="input_grad",
    )(ids, terms, *got, hidden, gain, dh)


def core_halves(chips):
    piece = lambda i, s: jnp.where(i < chips, 2 * i + 1 - s[CORE], 2 * (i - chips) + s[CORE])
    sent = lambda i: jnp.minimum(i, chips - 1)
    kept = lambda i: jnp.maximum(i - chips, 0)
    return piece, sent, kept


def out_wgrad_kernel(ids_ref, o_ref, da_ref, send_ref, keep_ref):
    step = pl.program_id(0)
    groups, _, q_cols = o_ref.shape

    def store(ref):
        for group in range(groups):
            part = mm(o_ref[group], da_ref[...], TN)
            ref[0, group * q_cols : (group + 1) * q_cols, :] = part.astype(bf16)

    half = pl.num_programs(0) // 2
    pl.when(step < half)(lambda: store(send_ref))
    pl.when(step >= half)(lambda: store(keep_ref))


def out_wgrad_parts(ids, attended, branch_grad, replicas):
    groups, share, q_cols = attended.shape
    width = branch_grad.shape[1]
    cols = width // replicas
    chips = replicas // 2
    piece, sent, kept = core_halves(chips)
    out = jax.ShapeDtypeStruct((chips, groups * q_cols, cols), bf16)
    block = (1, groups * q_cols, cols)
    return pl.pallas_call(
        out_wgrad_kernel,
        grid_spec=pltpu.PrefetchScalarGridSpec(
            num_scalar_prefetch=1,
            grid=(replicas,),
            in_specs=[
                pl.BlockSpec((groups, share, q_cols), lambda i, s: (0, 0, 0)),
                pl.BlockSpec((share, cols), lambda i, s: (0, piece(i, s))),
            ],
            out_specs=[
                pl.BlockSpec(block, lambda i, s: (sent(i), 0, 0)),
                pl.BlockSpec(block, lambda i, s: (kept(i), 0, 0)),
            ],
        ),
        out_shape=[out, out],
        cost_estimate=cost(2 * groups * share * q_cols * width, 2 * groups * q_cols * width),
        name="out_weight_grad",
    )(ids, attended, branch_grad)


def qkv_wgrad_kernel(
    ids_ref,
    normed_ref,
    grad_ref,
    w_ref,
    gain_ref,
    other_gain_ref,
    q_send_ref,
    q_keep_ref,
    s_send_ref,
    s_keep_ref,
):
    step = pl.program_id(0)
    cols = normed_ref.shape[1]
    q_cols = q_send_ref.shape[2]

    def store(q_ref, s_ref):
        grad = mm(normed_ref[...], grad_ref[...], TN)
        q_ref[0] = grad[:, :q_cols].astype(bf16)
        s_ref[0, :, : 2 * HD] = grad[:, q_cols:]
        gain = jnp.sum(grad * w_ref[...].astype(f32), axis=1, keepdims=True)
        lane = lax.broadcasted_iota(jnp.int32, (cols, 128), 1)
        first = jnp.where(lane == 0, gain / gain_ref[...], 0.0)
        s_ref[0, :, 2 * HD :] = jnp.where(lane == 1, other_gain_ref[...], first)

    half = pl.num_programs(0) // 2
    pl.when(step < half)(lambda: store(q_send_ref, s_send_ref))
    pl.when(step >= half)(lambda: store(q_keep_ref, s_keep_ref))


def qkv_wgrad_parts(ids, normed, grads, w_qkv, gain, other_gain, replicas):
    count, width = normed.shape
    all_cols = grads.shape[1]
    q_cols = all_cols - 2 * HD
    chips = replicas // 2
    cols = width // replicas
    piece, sent, kept = core_halves(chips)
    down = lambda n: pl.BlockSpec((cols, n), lambda i, s: (piece(i, s), 0))
    out = lambda n, where: pl.BlockSpec((1, cols, n), lambda i, s: (where(i), 0, 0))
    shape = lambda n, kind: jax.ShapeDtypeStruct((chips, cols, n), kind)
    return pl.pallas_call(
        qkv_wgrad_kernel,
        grid_spec=pltpu.PrefetchScalarGridSpec(
            num_scalar_prefetch=1,
            grid=(replicas,),
            in_specs=[
                pl.BlockSpec((count, cols), lambda i, s: (0, piece(i, s))),
                pl.BlockSpec((count, all_cols), lambda i, s: (0, 0)),
                down(all_cols),
                down(1),
                down(1),
            ],
            out_specs=[out(q_cols, sent), out(q_cols, kept), out(256, sent), out(256, kept)],
        ),
        out_shape=[shape(q_cols, bf16)] * 2 + [shape(256, f32)] * 2,
        cost_estimate=cost(2 * count * width * all_cols, 3 * count * width),
        name="projection_weight_grads",
    )(ids, normed, grads, w_qkv, gain, other_gain)


def layer_out_kernel(middle_ref, own_ref, up_ref, down_ref, out_ref):
    total = own_ref[...].astype(f32) + up_ref[...].astype(f32) + down_ref[...].astype(f32)
    out_ref[...] = (middle_ref[...] + RESID * total).astype(bf16)


def layer_output(middle, own, own_row, got):
    share, width = middle.shape
    spec = lambda row: pl.BlockSpec((share, WIDE), lambda j: (row, j))
    return pl.pallas_call(
        layer_out_kernel,
        grid=(width // WIDE,),
        in_specs=[spec(0), spec(own_row), spec(0), spec(0)],
        out_specs=spec(0),
        out_shape=jax.ShapeDtypeStruct((share, width), bf16),
        cost_estimate=cost(5 * share * width, 12 * share * width),
        name="layer_output",
    )(middle, own, *got)


def ring_add_kernel(first, ids_ref, term_ref, got_ref, out_ref):
    rows = got_ref.shape[0]
    if rows < out_ref.shape[0]:
        out_ref[...] = term_ref[...]
    here = slice(first, first + rows)
    out_ref[here, :] = (term_ref[here, :].astype(f32) + got_ref[...].astype(f32)).astype(bf16)


def ring_add(ids, terms, block, place, got, first, share):
    width = terms.shape[1]
    cols = width // 2
    which = lambda j, s: (s[RING + place] if block is None else block, j)
    column = lambda j, s: (0, j)
    return pl.pallas_call(
        functools.partial(ring_add_kernel, first),
        grid_spec=pltpu.PrefetchScalarGridSpec(
            num_scalar_prefetch=1,
            grid=(2,),
            in_specs=[
                pl.BlockSpec((share, cols), which),
                pl.BlockSpec((got.shape[0], cols), column),
            ],
            out_specs=pl.BlockSpec((share, cols), column),
        ),
        out_shape=jax.ShapeDtypeStruct((share, width), bf16),
        cost_estimate=cost(2 * share * width, 6 * share * width),
        name="ring_add",
    )(ids, terms, got)


def swiglu_kernel(pieces, members, row, ids_ref, *refs):
    piece_refs = refs[:pieces]
    cot_ref, gate_ref, up_ref, down_ref = refs[pieces : pieces + 4]
    outs = refs[-19:-13]
    x, dm, wg, wu, wd, act, dgate, dup, in_sem, gate_sem, up_sem, down_sem, out_sem = refs[-13:]
    kept, dn_ref = outs[:5], outs[5]
    rows = x.shape[0]
    share = rows // len(members)
    width, units = wg.shape
    blocks = gate_sem.shape[0]
    block = units // blocks
    part = width // blocks
    arrivals = []
    at = 0
    for ref in piece_refs:
        count = ref.shape[0]
        arrivals.append((ref, x.at[at : at + count, :]))
        at += count
    for index, place in enumerate(members):
        first = pl.multiple_of(ids_ref[RING + place] * share, share)
        here = slice(index * share, (index + 1) * share)
        arrivals.append((cot_ref.at[pl.ds(first, share), :], dm.at[here, :]))
    arrivals = [pltpu.make_async_copy(*pair, in_sem.at[i]) for i, pair in enumerate(arrivals)]

    def weights(u):
        here = pl.ds(pl.multiple_of(u * block, block), block)
        return (
            pltpu.make_async_copy(gate_ref.at[:, here], wg.at[:, here], gate_sem.at[u]),
            pltpu.make_async_copy(up_ref.at[:, here], wu.at[:, here], up_sem.at[u]),
            pltpu.make_async_copy(down_ref.at[here, :], wd.at[here, :], down_sem.at[u]),
        )

    for copy in arrivals[:pieces]:
        copy.start()
    for copy in weights(0):
        copy.start()
    for copy in arrivals[pieces:]:
        copy.start()
    for u in range(1, blocks):
        for copy in weights(u):
            copy.start()
    for copy in arrivals:
        copy.wait()
    for index, place in enumerate(members):
        here = slice(index * share, (index + 1) * share)
        position = ids_ref[RING + place] * share + lax.broadcasted_iota(jnp.int32, (share, 1), 0)
        scaled = dm[here, :].astype(f32) * RESID
        dm[here, :] = jnp.where(position < ids_ref[LENGTH], scaled, 0.0).astype(bf16)

    def one_block(u, carry):
        for copy in weights(u):
            copy.wait()
        here = pl.ds(pl.multiple_of(u * block, block), block)
        gate = mm(x[...], wg[:, here], NN)
        up = mm(x[...], wu[:, here], NN)
        grad = mm(dm[...], wd[here, :], NT)
        sg = jax.nn.sigmoid(gate)
        silu = gate * sg
        act[:, here] = (silu * up).astype(bf16)
        dgate[:, here] = (grad * up * sg * (1.0 + gate * (1.0 - sg))).astype(bf16)
        dup[:, here] = (grad * silu).astype(bf16)
        return carry

    lax.fori_loop(0, blocks, one_block, 0)

    def one_part(n, carry):
        here = pl.ds(pl.multiple_of(n * part, part), part)
        grad = mm(dgate[...], wg[here, :], NT) + mm(dup[...], wu[here, :], NT)
        dn_ref[:, here] = grad.astype(bf16)
        return carry

    one_part(0, 0)
    leaving = [
        pltpu.make_async_copy(src, dst.at[pl.ds(row, rows), :], out_sem.at[i])
        for i, (src, dst) in enumerate(zip((x, dm, act, dgate, dup), kept))
    ]
    for copy in leaving:
        copy.start()
    lax.fori_loop(1, blocks, one_part, 0)
    for copy in leaving:
        copy.wait()


def swiglu(ids, pieces, members, cotangent, weights, row, buffers, total_rows):
    w_gate, w_up, w_down = weights
    width, units = w_gate.shape
    rows = sum(piece.shape[0] for piece in pieces)
    blocks = 2
    hbm = pl.BlockSpec(memory_space=pl.ANY)
    operands = [*pieces, cotangent, *weights, *buffers]
    aliases = {5 + len(pieces) + index: index for index in range(len(buffers))}
    collected = lambda n: jax.ShapeDtypeStruct((total_rows, n), bf16)
    held = lambda *shape: pltpu.VMEM(shape, bf16)
    copies = lambda n: pltpu.SemaphoreType.DMA((n,))
    return pl.pallas_call(
        functools.partial(swiglu_kernel, len(pieces), tuple(members), row),
        grid_spec=pltpu.PrefetchScalarGridSpec(
            num_scalar_prefetch=1,
            grid=(1,),
            in_specs=[hbm] * len(operands),
            out_specs=[hbm] * 5 + [pl.BlockSpec((rows, width), lambda i, s: (0, 0))],
            scratch_shapes=[held(rows, width)] * 2
            + [held(width, units), held(width, units), held(units, width)]
            + [held(rows, units)] * 3
            + [copies(len(pieces) + len(members)), *([copies(blocks)] * 3), copies(5)],
        ),
        out_shape=[collected(width)] * 2
        + [collected(units)] * 3
        + [jax.ShapeDtypeStruct((rows, width), bf16)],
        input_output_aliases=aliases,
        compiler_params=grant(58),
        cost_estimate=cost(12 * rows * width * units, 6 * width * units + 16 * rows * width),
        name="swiglu_rows",
    )(ids, *operands)


def ring_order(count):
    inner = 2 if count <= 8 else 4
    outer = count // inner
    cells = [(0, 0)]
    for row in range(outer):
        cells += [(row, c) for c in (range(1, inner) if row % 2 == 0 else range(inner - 1, 0, -1))]
    cells += [(row, 0) for row in range(outer - 1, 0, -1)]
    return [row * inner + c for row, c in cells]


def tie(*values):
    return lax.optimization_barrier(values)


def over_cores(send, keep):
    chips = send.shape[0]
    chip = lax.axis_index("dp") // 2
    take = lambda a, i: lax.dynamic_index_in_dim(a, i, 0, keepdims=False)
    got = lax.ppermute(send, "dp", [(i, i ^ 1) for i in range(2 * chips)])
    stay = [take(keep, chip), take(got, chip)]
    go = []
    for step in range(1, chips):
        there = (chip + step) % chips
        term = take(keep, there).astype(f32) + take(got, there).astype(f32)
        go.append(term.astype(send.dtype))
    return stay, go


def over_chips(stay, go):
    chips = len(go) + 1
    terms = list(stay)
    for step in range(1, chips):
        to = [(i, ((i // 2 + step) % chips) * 2 + i % 2) for i in range(2 * chips)]
        terms.append(lax.ppermute(go[step - 1], "dp", to))
    return terms


def total_of(terms):
    total = terms[0].astype(f32)
    for term in terms[1:]:
        total = total + term.astype(f32)
    return total


def local(
    hidden_in,
    seq_lengths,
    out_grad,
    attn_gain,
    mlp_gain,
    w_query,
    w_key,
    w_value,
    w_out,
    w_gate,
    w_up,
    w_down,
):
    rows_total, width = hidden_in.shape
    q_cols = w_query.shape[1]
    heads_here = q_cols // HD
    groups = lax.axis_size("tensor")
    replicas = lax.axis_size("dp")
    member = lax.axis_index("tensor")
    replica = lax.axis_index("dp")
    core = replica % 2
    share = rows_total // groups
    half = share // 2
    order = ring_order(groups)
    spot = [order.index(i) for i in range(groups)]
    ahead = [(order[i], order[(i + 1) % groups]) for i in range(groups)]
    behind = [(b, a) for a, b in ahead]
    half_way = groups // 2
    apart = [0]
    for d in range(1, half_way):
        apart += [-d, d]
    apart.append(half_way)
    ring = [[order[(spot[i] + d) % groups] for d in apart] for i in range(groups)]
    ids = jnp.concatenate(
        [seq_lengths, core[None].astype(jnp.int32), jnp.asarray(ring, jnp.int32)[member]]
    )
    table = rope_tables(rows_total)
    gain_one = attn_gain[None, :]
    gain_two = mlp_gain[None, :]

    def exchange(array):
        return lax.all_to_all(array, "tensor", 0, 0, tiled=True)

    def onward(array):
        return lax.ppermute(array, "tensor", ahead)

    def back(array):
        return lax.ppermute(array, "tensor", behind)

    w_own = lax.dynamic_slice_in_dim(w_out, core * (width // 2), width // 2, 1)
    w_hop = onward(w_own), back(w_own)
    w_mine = [w_own]

    def w_next():
        w_mine.extend(w_hop)
        if len(w_mine) < groups - 1:
            return onward(w_hop[0]), back(w_hop[1])
        return onward(w_hop[0][: q_cols // 2]), back(w_hop[1][q_cols // 2 :])

    kv_of = [i * heads_here // (H // KVH) for i in range(groups)]
    w_kv = pick_heads(w_key, w_value, kv_of)
    w_kv = exchange(w_kv).reshape(width, 2 * HD)
    normed_one, queries = front(hidden_in, gain_one, w_query, table)
    *w_hop, w_kv, normed_one, queries = tie(*w_hop, w_kv, normed_one, queries)
    for _ in range(half_way - 3):
        w_hop = w_next()
    keys, keys_t, values, values_t = keys_values(seq_lengths, normed_one, w_kv, table)
    *w_hop, keys = tie(*w_hop, keys)
    w_hop = w_next()
    attended, lse = attend(queries, keys, values_t)
    *w_hop, attended = tie(*w_hop, attended)
    attended_rows = exchange(attended.reshape(groups, share, q_cols))
    w_hop = w_next()
    w_mine = jnp.concatenate([*w_mine, *w_hop], 0)
    w_other = lax.ppermute(w_mine, "dp", [(i, i ^ 1) for i in range(replicas)])
    w_qkv = jnp.concatenate([w_query, w_kv], 1)
    middle, normed_two = out_norm(ids, attended_rows, w_mine, w_other, hidden_in, gain_two)

    weights = (w_gate, w_up, w_down)
    grads = []
    buffers = []

    def run(pieces, members, row):
        nonlocal buffers
        *buffers, grad = swiglu(
            ids, pieces, members, out_grad, weights, row, buffers, rows_total
        )
        grads.append(grad)

    pieces, members, row = [normed_two], [0], rows_total - 2 * share
    hop = [normed_two, normed_two]
    for d in range(1, half_way + 1):
        if d < half_way:
            hop = [onward(hop[0]), back(hop[1])]
        else:
            hop = [onward(hop[0][:half]), back(hop[1][half:])]
        run(pieces, members, row)
        hop, grads[-1], buffers = tie(hop, grads[-1], buffers)
        pieces = hop
        if d < half_way:
            members, row = [2 * d - 1, 2 * d], 2 * share * (d - 1)
        else:
            members, row = [groups - 1], rows_total - share
    run(pieces, members, row)
    normed_ring, down_ring, act, dgate, dup = buffers

    def first_hop(far):
        return onward(far[:half]), back(far[half:])

    def next_hop(terms, block, got):
        down = ring_add(ids, terms, block, None, got[1], share - got[1].shape[0], share)
        up = ring_add(ids, terms, block + 1, None, got[0], 0, share)
        return onward(up), back(down)

    def natural_hop(terms, distance, got):
        first = share - got[1].shape[0]
        down = ring_add(ids, terms, None, 2 * distance - 1, got[1], first, share)
        up = ring_add(ids, terms, None, 2 * distance, got[0], 0, share)
        return onward(up), back(down)

    got = first_hop(grads[-1])
    mlp = mm(act, w_down, NN).astype(bf16)
    *got, mlp = tie(*got, mlp)
    fillers = [
        lambda: mm(act, down_ring, TN).astype(bf16),
        lambda: mm(normed_ring, dgate, TN).astype(bf16),
        lambda: mm(normed_ring, dup, TN).astype(bf16),
    ]
    filled = []
    for d in range(half_way - 1, 0, -1):
        got = next_hop(grads[d], 0, got)
        if len(filled) < 3:
            *got, value = tie(*got, fillers[len(filled)]())
            filled.append(value)
    down_wgrad, gate_wgrad, up_wgrad = filled
    scatter = lambda a, d: lax.psum_scatter(a, "dp", scatter_dimension=d, tiled=True)
    down_wgrad = scatter(down_wgrad, 1)
    gate_wgrad = scatter(gate_wgrad, 0)
    up_wgrad = scatter(up_wgrad, 0)

    *got, mlp = tie(*got, mlp)
    out_got = first_hop(mlp[rows_total - share :])
    dh, da, gain_part, do_send = norm_back(
        ids, [grads[0], *got], middle, gain_two, out_grad, w_mine, w_other, q_cols
    )
    *out_got, do_send, da = tie(*out_got, do_send, da)
    do = exchange(do_send).reshape(rows_total, q_cols)
    out_parts = out_wgrad_parts(ids, attended_rows, da, replicas)
    do, out_parts = tie(do, out_parts)
    out_got = next_hop(mlp, 2 * half_way - 4, out_got)
    out_parts = over_cores(*out_parts)
    operands = [queries, do, attended, lse, keys, keys_t, values, table]
    carried = attend_back(0, *operands, [])
    out_got, carried, down_wgrad, out_parts = tie(out_got, carried, down_wgrad, out_parts)
    out_terms = over_chips(*out_parts)
    for d in range(half_way - 2, 1, -1):
        out_got = next_hop(mlp, 2 * d - 2, out_got)
    qkv_grad = attend_back(1, *operands, carried)
    out_got, qkv_grad = tie(out_got, qkv_grad)

    first_grad = mm(qkv_grad, w_qkv, NT).astype(bf16)
    far = lax.dynamic_slice_in_dim(first_grad, ids[RING + groups - 1] * share, share, 0)
    in_got = first_hop(far)
    out_got = next_hop(mlp, 0, out_got)
    q_send, q_keep, s_send, s_keep = qkv_wgrad_parts(
        ids,
        normed_one,
        qkv_grad,
        w_qkv,
        attn_gain[:, None],
        gain_part.reshape(width, 1),
        replicas,
    )
    in_got, out_got, q_send, s_send, gate_wgrad, out_terms = tie(
        in_got, out_got, q_send, s_send, gate_wgrad, out_terms
    )
    out_wgrad = total_of(out_terms).astype(bf16)
    out_wgrad = lax.psum_scatter(out_wgrad, "tensor", scatter_dimension=0, tiled=True)
    small = over_cores(s_send, s_keep)
    query_wgrad = over_cores(q_send, q_keep)
    for d in range(half_way - 1, 0, -1):
        in_got = natural_hop(first_grad, d, in_got)
        if d == half_way - 1:
            small = over_chips(*small)
            query_wgrad = over_chips(*query_wgrad)
            in_got, small, query_wgrad = tie(in_got, small, query_wgrad)
            small, query_wgrad = total_of(small), total_of(query_wgrad)
            layer_out = layer_output(middle, mlp, groups - 2, out_got)
        elif d == half_way - 2:
            in_got, layer_out, up_wgrad = tie(in_got, layer_out, up_wgrad)
    pieces = exchange(small.reshape(groups, small.shape[0] // groups, 256))
    input_grad = in_grad(ids, first_grad, in_got, hidden_in, gain_one, dh)
    gains = jnp.sum(pieces[:, :, 128:130], axis=0)
    kv = pieces[:, :, :128].reshape(KVH, groups // KVH, -1, 128).sum(axis=1)
    kv = jnp.swapaxes(kv, 0, 1)
    key_wgrad = kv[:, :, :HD].reshape(-1, KVH * HD)
    value_wgrad = kv[:, :, HD:].reshape(-1, KVH * HD)
    return (
        layer_out,
        input_grad,
        gains[:, 0],
        gains[:, 1],
        query_wgrad,
        key_wgrad,
        value_wgrad,
        out_wgrad.astype(f32),
        gate_wgrad.astype(f32),
        up_wgrad.astype(f32),
        down_wgrad.astype(f32),
    )


def solution(mesh):
    placed = (
        P("dp", None),
        P("dp"),
        P("dp", None),
        P(),
        P(),
        P(None, "tensor"),
        P("tensor", None),
        P("tensor", None),
        P("tensor", None),
        P(None, "tensor"),
        P(None, "tensor"),
        P("tensor", None),
    )
    return jax.shard_map(
        local,
        mesh=mesh,
        in_specs=placed,
        out_specs=(
            P(("dp", "tensor"), None),
            P(("dp", "tensor"), None),
            P(("dp", "tensor")),
            P(("dp", "tensor")),
            P("dp", "tensor"),
            P(("dp", "tensor"), None),
            P(("dp", "tensor"), None),
            P("tensor", "dp"),
            P("dp", "tensor"),
            P("dp", "tensor"),
            P("tensor", "dp"),
        ),
        check_vma=False,
    )
```

time: 663 us -> 641 us (0.967)
  Pallas kernels: 120 us -> 269 us
  matrix products: 157 us -> 62 us
  other arithmetic: 66.7 us -> 19.9 us
  waiting for transfers between devices: 181 us -> 163 us
  local copies, waits for them, and re-layouts: 49.9 us -> 35.2 us
    pallas_call x2 -> x28, Pallas kernels: 49.1 us -> 204 us  [the longest x5 80.6 us: swiglu(): pl.pallas_call(functools.partial(swiglu_kernel, len(pieces), tuple(member...]
    dot_general x30 -> x5, matrix products: 157 us -> 62 us  [mm(): return lax.dot_general(left, right, dims, preferred_element_type=f32)]
    reduce_scatter x1, waiting for transfers between devices: 39 us -> 0.01 us  [local(): lax.psum_scatter(out_wgrad, 'tensor', scatter_dimension=0, tiled=True)]
    convert_element_type x12 -> x4, other arithmetic: 40.9 us -> 11.1 us  [the longest x1 4.78 us: local(): out_wgrad = total_of(out_terms).astype(bf16)]
    ppermute x30 -> x47, waiting for transfers between devices: 108 us -> 129 us  [the longest x20 61.2 us: back(): return lax.ppermute(array, 'tensor', behind)]
    unnamed x106 -> x83, local copies, waits for them, and re-layouts: 31.1 us -> 16 us
    ppermute x30 -> x47, starting transfers between devices: 37 us -> 48.5 us  [the longest x20 28.1 us: onward(): return lax.ppermute(array, 'tensor', ahead)]
    all_to_all x5 -> x4, starting transfers between devices: 24 us -> 19 us  [exchange(): return lax.all_to_all(array, 'tensor', 0, 0, tiled=True)]
  transfers between devices with their start and end apart: 41 -> 55, of which waited for: 20 -> 27; matrix products, arithmetic and copies ran while one was open for 32% -> 17% of each run, Pallas kernels for 17% -> 38%
where the time goes in v3:
time: 641 us; the launch traced here: 633 us
  Pallas kernels  269 us (42%)
  waiting for transfers between devices  163 us (25%)
  starting transfers between devices  67.7 us (11%)
  matrix products  62 us (10%)
  local copies, waits for them, and re-layouts  35.2 us (5%)
  other arithmetic  19.9 us (3%)
  between operations  15.8 us (2%)
    pallas_call x5, Pallas kernels, swiglu(): pl.pallas_call(functools.partial(swiglu_kernel, len(pieces), tuple(member...  80.6 us
    dot_general x5, matrix products, mm(): return lax.dot_general(left, right, dims, preferred_element_type=f32)  62 us
    ppermute x20, waiting for transfers between devices, back(): return lax.ppermute(array, 'tensor', behind)  61.2 us
    pallas_call x18, Pallas kernels, ring_add(): pl.pallas_call(functools.partial(ring_add_kernel, first), grid_spec=pltpu...  55.4 us
    ppermute x20, waiting for transfers between devices, onward(): return lax.ppermute(array, 'tensor', ahead)  50.5 us
    pallas_call x2, Pallas kernels, attend_back(): pl.pallas_call(functools.partial(attend_back_kernel, heads, start), grid=...  40.9 us
    all_to_all x4, waiting for transfers between devices, exchange(): return lax.all_to_all(array, 'tensor', 0, 0, tiled=True)  33 us
    ppermute x20, starting transfers between devices, onward(): return lax.ppermute(array, 'tensor', ahead)  28.1 us
  transfers between devices with their start and end apart: 55, of which 27 were waited for; matrix products, arithmetic and copies ran while one was open for 17% of the time, Pallas kernels for 38%

profile of v3, /device:TPU:0, one launch (start us, length us, event | category | flops | bytes accessed | tf_op | source)
XLA Modules:
  0.0 632.9 jit_solution(17435161613884730409)
XLA Ops:
  9.2 7.3 %all-to-all-start = ((bf16[8,256,128]{2,1,0:T(8,128)(2,1)}), bf16[8,256,128]{2,1,0:T(8,128)(2,1)S(1)}, u32[]{:S(2)}, u32[]{:S(2)}) async-start(bf16[8,256,128]{2,1,0:T(8,128)(2,1)} %pick_heads.1), calls=%async_computation | async-start | bytes 1048576 | tf_op jit(solution)/shard_map/all_to_all | solution.py:955
  21.9 10.7 %norm_and_query.1 = (bf16[2048,2048]{1,0:T(8,128)(2,1)}, bf16[2048,256]{1,0:T(8,128)(2,1)}) custom-call(bf16[2048,2048]{1,0:T(8,128)(2,1)} %rows_ref.5, f32[1,2048]{1,0:T(1,128)} %bitcast.47, bf16[2048,256]{1,0:T(8,128)(2,1)} %wq_ref.1, f32[320,256]{1,0:T(8,128)} %pad_maximum_fusion.table_ref), custom_call_target="tpu_custom_call" | custom-call | flops 2147483648 | bytes 20971520 | tf_op jit(solution)/shard_map/norm_and_query/pallas_call | solution.py:102
  32.6 5.9 collective-permute-done
  40.0 2.9 collective-permute-start.3
  43.6 7.2 %keys_and_values.1 = (bf16[2048,128]{1,0:T(8,128)(2,1)}, bf16[128,2048]{1,0:T(8,128)(2,1)}, bf16[2048,128]{1,0:T(8,128)(2,1)}, bf16[128,2048]{1,0:T(8,128)(2,1)}) custom-call(s32[1]{0:T(128)S(6)} %copy.87.length_ref, bf16[2048,2048]{1,0:T(8,128)(2,1)} %get-tuple-element.167.normed_ref, bf16[2048,128]{1,0:T(8,128)(2,1)} %bitcast.42, ...), custom_call_target="tpu_custom_call" | custom-call | flops 1073741824 | bytes 8388608 | tf_op jit(solution)/shard_map/keys_and_values/pallas_call | solution.py:142
  58.0 22.6 %attend.1 = (bf16[2048,256]{1,0:T(8,128)(2,1)}, f32[8,2048]{1,0:T(8,128)}) custom-call(bf16[2048,256]{1,0:T(8,128)(2,1)} %get-tuple-element.172.q_ref, bf16[2048,128]{1,0:T(8,128)(2,1)} %get-tuple-element.173.k_ref, bf16[128,2048]{1,0:T(8,128)(2,1)} %get-tuple-element.174.vt_ref), custom_call_target="tpu_custom_call" | custom-call | flops 8589934592 | bytes 2097152 | tf_op jit(solution)/shard_map/attend/pallas_call | solution.py:244
  90.5 3.6 all-to-all-start.1
  96.0 24.7 %all-to-all-done.1.o_ref = bf16[8,256,256]{2,1,0:T(8,128)(2,1)S(1)} async-done(((bf16[8,256,256]{2,1,0:T(8,128)(2,1)}), bf16[8,256,256]{2,1,0:T(8,128)(2,1)S(1)}, u32[]{:S(2)}, u32[]{:S(2)}) %all-to-all-start.1) | async-done | bytes 1048608 | tf_op jit(solution)/shard_map/all_to_all | solution.py:955
  121.7 9.2 %out_project_and_norm.1 = (f32[256,2048]{1,0:T(8,128)}, bf16[256,2048]{1,0:T(8,128)(2,1)}) custom-call(s32[10]{0:T(128)} %pad_add_fusion.ids_ref, bf16[8,256,256]{2,1,0:T(8,128)(2,1)} %copy-done.5, bf16[2048,1024]{1,0:T(8,128)(2,1)} %constant_dynamic-update-slice_fusion.mine_ref, bf16[2048,1024]{1,0:T(8,128)(2,1)} %collective-permute-done.8.other_ref, ...), custom_call_target="tpu_custom_call" | custom-call | flops 2147483648 | bytes 8388608 | tf_op jit(solution)/shard_map/out_project_and_norm/pallas_call | solution.py:451
  133.1 12.2 %swiglu_rows.5 = (bf16[2048,2048]{1,0:T(8,128)(2,1)}, bf16[2048,2048]{1,0:T(8,128)(2,1)}, bf16[2048,1024]{1,0:T(8,128)(2,1)}, bf16[2048,1024]{1,0:T(8,128)(2,1)}...) custom-call(s32[10]{0:T(128)} %pad_add_fusion.ids_ref, bf16[256,2048]{1,0:T(8,128)(2,1)} %get-tuple-element.179.refs_0_, ...), custom_call_target="tpu_custom_call" | custom-call | flops 6442450944 | bytes 20971520 | tf_op jit(solution)/shard_map/swiglu_rows/pallas_call | solution.py:847
  145.3 10.6 %collective-permute-done.10.refs_1_ = bf16[256,2048]{1,0:T(8,128)(2,1)S(1)} collective-permute-done((bf16[256,2048]{1,0:T(8,128)(2,1)}, bf16[256,2048]{1,0:T(8,128)(2,1)S(1)}, u32[]{:S(2)}, u32[]{:S(2)}) %collective-permute-start.10) | collective-permute-done | bytes 1048608 | tf_op jit(solution)/shard_map/ppermute | solution.py:961
  158.1 18.4 %swiglu_rows.6 = (bf16[2048,2048]{1,0:T(8,128)(2,1)}, bf16[2048,2048]{1,0:T(8,128)(2,1)}, bf16[2048,1024]{1,0:T(8,128)(2,1)}, bf16[2048,1024]{1,0:T(8,128)(2,1)}...) custom-call(s32[10]{0:T(128)} %pad_add_fusion.ids_ref, ...), custom_call_target="tpu_custom_call", output_to_operand_aliasing={{0}: (7, {}), {1}: (8, {}), {2}: (9, {}), {3}: (10, {}), {4... | custom-call | flops 12884901888 | bytes 29360128 | tf_op jit(solution)/shard_map/swiglu_rows/pallas_call | solution.py:847
  176.5 3.8 collective-permute-done.11.refs_0_
  183.3 18.4 %swiglu_rows.7 = (bf16[2048,2048]{1,0:T(8,128)(2,1)}, bf16[2048,2048]{1,0:T(8,128)(2,1)}, bf16[2048,1024]{1,0:T(8,128)(2,1)}, bf16[2048,1024]{1,0:T(8,128)(2,1)}...) custom-call(s32[10]{0:T(128)} %pad_add_fusion.ids_ref, ...), custom_call_target="tpu_custom_call", output_to_operand_aliasing={{0}: (7, {}), {1}: (8, {}), {2}: (9, {}), {3}: (10, {}), {4... | custom-call | flops 12884901888 | bytes 29360128 | tf_op jit(solution)/shard_map/swiglu_rows/pallas_call | solution.py:847
  207.5 18.4 %swiglu_rows.8 = (bf16[2048,2048]{1,0:T(8,128)(2,1)}, bf16[2048,2048]{1,0:T(8,128)(2,1)}, bf16[2048,1024]{1,0:T(8,128)(2,1)}, bf16[2048,1024]{1,0:T(8,128)(2,1)}...) custom-call(s32[10]{0:T(128)} %pad_add_fusion.ids_ref, ...), custom_call_target="tpu_custom_call", output_to_operand_aliasing={{0}: (7, {}), {1}: (8, {}), {2}: (9, {}), {3}: (10, {}), {4... | custom-call | flops 12884901888 | bytes 29360128 | tf_op jit(solution)/shard_map/swiglu_rows/pallas_call | solution.py:847
  226.9 13.2 %swiglu_rows.9 = (bf16[2048,2048]{1,0:T(8,128)(2,1)}, bf16[2048,2048]{1,0:T(8,128)(2,1)}, bf16[2048,1024]{1,0:T(8,128)(2,1)}, bf16[2048,1024]{1,0:T(8,128)(2,1)}...) custom-call(s32[10]{0:T(128)} %pad_add_fusion.ids_ref, ...), custom_call_target="tpu_custom_call", output_to_operand_aliasing={{0}: (7, {}), {1}: (8, {}), {2}: (9, {}), {3}: (10, {}), {4... | custom-call | flops 6442450944 | bytes 20971520 | tf_op jit(solution)/shard_map/swiglu_rows/pallas_call | solution.py:847
  243.7 13.2 %convolution_convert_fusion.1.term_ref.own_ref = bf16[2048,2048]{1,0:T(8,128)(2,1)} fusion(bf16[2048,1024]{1,0:T(8,128)(2,1)} %get-tuple-element.236, bf16[1024,2048]{1,0:T(8,128)(2,1)S(1)} %copy-done.1), kind=kOutput, calls=%fused_computation.1 | convolution fusion | flops 8594128896 | bytes 16777216 | tf_op jit(solution)/shard_map/dot_general | solution.py:32
  257.7 2.9 ring_add.19
  261.7 2.9 ring_add.18
  265.6 14.0 %convolution_convert_fusion.2 = bf16[1024,2048]{1,0:T(8,128)(2,1)} fusion(bf16[2048,1024]{1,0:T(8,128)(2,1)} %get-tuple-element.236, bf16[2048,2048]{1,0:T(8,128)(2,1)} %get-tuple-element.239), kind=kOutput, calls=%fused_computation.4 | convolution fusion | flops 8592031744 | bytes 16777216 | tf_op jit(solution)/shard_map/dot_general | solution.py:32
  281.3 4.3 collective-permute-done.19.got_ref
  285.7 3.1 ring_add.21
  290.4 3.2 ring_add.20
  294.6 14.2 %convolution_convert_fusion.4 = bf16[2048,1024]{1,0:T(8,128)(2,1)} fusion(bf16[2048,2048]{1,0:T(8,128)(2,1)} %get-tuple-element.242, bf16[2048,1024]{1,0:T(8,128)(2,1)} %get-tuple-element.243), kind=kOutput, calls=%fused_computation.6 | convolution fusion | flops 8592031744 | bytes 16777216 | tf_op jit(solution)/shard_map/dot_general | solution.py:32
  308.9 4.7 collective-permute-done.21.got_ref
  313.6 3.1 ring_add.23
  317.5 3.1 ring_add.22
  321.9 14.1 %convolution_convert_fusion.3 = bf16[2048,1024]{1,0:T(8,128)(2,1)} fusion(bf16[2048,2048]{1,0:T(8,128)(2,1)} %get-tuple-element.242, bf16[2048,1024]{1,0:T(8,128)(2,1)} %get-tuple-element.246), kind=kOutput, calls=%fused_computation.5 | convolution fusion | flops 8592031744 | bytes 16777216 | tf_op jit(solution)/shard_map/dot_general | solution.py:32
  336.0 5.3 collective-permute-done.23.up_ref
  346.4 10.9 %norm_back_and_project.1 = (f32[256,2048]{1,0:T(8,128)}, bf16[256,2048]{1,0:T(8,128)(2,1)}, f32[1,2048]{1,0:T(1,128)}, bf16[8,256,256]{2,1,0:T(8,128)(2,1)}) custom-call(s32[10]{0:T(128)} %pad_add_fusion.ids_ref, bf16[256,2048]{1,0:T(8,128)(2,1)} %get-tuple-element.251.own_ref, bf16[256,2048]{1,0:T(8,128)(2,1)} %copy-done.16, bf16[256,2048]{1,0:T(8,128)(2,1)} %copy-done.15, ...), custom_call_target="tpu_custom_call" | custom-call | flops 2147483648 | bytes 8388608 | tf_op jit(solution)/shard_map/norm_back_and_project/pallas_call | solution.py:528
  357.4 3.6 all-to-all-start.2
  361.8 7.9 %out_weight_grad.1 = (bf16[2,2048,512]{2,1,0:T(8,128)(2,1)}, bf16[2,2048,512]{2,1,0:T(8,128)(2,1)}) custom-call(s32[10]{0:T(128)} %pad_add_fusion.ids_ref, bf16[8,256,256]{2,1,0:T(8,128)(2,1)} %copy-done.5, bf16[256,2048]{1,0:T(8,128)(2,1)} %get-tuple-element.260.da_ref), custom_call_target="tpu_custom_call" | custom-call | flops 2147483648 | bytes 8388608 | tf_op jit(solution)/shard_map/out_weight_grad/pallas_call | solution.py:624
  369.6 8.2 %all-to-all-done.2 = bf16[8,256,256]{2,1,0:T(8,128)(2,1)S(1)} async-done(((bf16[8,256,256]{2,1,0:T(8,128)(2,1)}), bf16[8,256,256]{2,1,0:T(8,128)(2,1)S(1)}, u32[]{:S(2)}, u32[]{:S(2)}) %all-to-all-start.2) | async-done | bytes 1048608 | tf_op jit(solution)/shard_map/all_to_all | solution.py:955
  380.3 3.0 ring_add.25
  383.4 3.2 ring_add.24
  388.4 17.7 %attend_back.2 = (bf16[1280,256]{1,0:T(8,128)(2,1)}, f32[2048,128]{1,0:T(8,128)}, f32[2048,128]{1,0:T(8,128)}) custom-call(bf16[2048,256]{1,0:T(8,128)(2,1)} %get-tuple-element.172.q_ref, bf16[2048,256]{1,0:T(8,128)(2,1)} %bitcast.45, bf16[2048,256]{1,0:T(8,128)(2,1)} %get-tuple-element.176.o_ref, f32[8,2048]{1,0:T(8,128)} %get-tuple-element.264.lse_ref, ...), custom_call_target="tpu_custom_call" | custom-call | flops 10737418240 | bytes 5242880 | tf_op jit(solution)/shard_map/attend_back/pallas_call | solution.py:386
  408.2 3.1 dynamic-slice_bitcast_fusion
  411.2 3.5 fusion
  415.7 3.1 ring_add.27
  419.5 3.1 ring_add.26
  426.5 23.2 %attend_back.3.grad_ref = bf16[2048,384]{1,0:T(8,128)(2,1)} custom-call(bf16[2048,256]{1,0:T(8,128)(2,1)} %get-tuple-element.172.q_ref, bf16[2048,256]{1,0:T(8,128)(2,1)} %bitcast.46, bf16[2048,256]{1,0:T(8,128)(2,1)} %get-tuple-element.176.o_ref, f32[8,2048]{1,0:T(8,128)} %get-tuple-element.264.lse_ref, bf16[2048,128]{1,0:T(8,128)(2,1)} %get-tuple-element.173.k_ref, ...), custom_call_target="tpu_custom_call" | custom-call | flops 10737418240 | bytes 5242880 | tf_op jit(solution)/shard_map/attend_back/pallas_call | solution.py:386
  449.7 3.1 ring_add.29
  453.1 3.1 ring_add.28
  457.9 6.4 %convolution_convert_fusion.term_ref.own_ref = bf16[2048,2048]{1,0:T(8,128)(2,1)S(1)} fusion(bf16[2048,384]{1,0:T(8,128)(2,1)} %attend_back.3.grad_ref, bf16[2048,384]{1,0:T(8,128)(2,1)} %constant_dynamic-update-slice_fusion.9.w_ref), kind=kOutput, calls=%fused_computation | convolution fusion | flops 3225419776 | bytes 11534336 | tf_op jit(solution)/shard_map/dot_general | solution.py:32
  464.4 3.3 copy-done
  473.6 11.7 %projection_weight_grads.1 = (bf16[2,512,256]{2,1,0:T(8,128)(2,1)}, bf16[2,512,256]{2,1,0:T(8,128)(2,1)}, f32[2,512,256]{2,1,0:T(8,128)}, f32[2,512,256]{2,1,0:T(8,128)}) custom-call(s32[10]{0:T(128)} %pad_add_fusion.ids_ref, bf16[2048,2048]{1,0:T(8,128)(2,1)} %get-tuple-element.167.normed_ref, bf16[2048,384]{1,0:T(8,128)(2,1)} %attend_back.3.grad_ref, ...), custom_call_target="tpu_custom_call" | custom-call | flops 3221225472 | bytes 12582912 | tf_op jit(solution)/shard_map/projection_weight_grads/pallas_call | solution.py:684
  485.3 6.7 %collective-permute-done.32.got_ref = bf16[128,2048]{1,0:T(8,128)(2,1)} collective-permute-done((bf16[128,2048]{1,0:T(8,128)(2,1)}, bf16[128,2048]{1,0:T(8,128)(2,1)}, u32[]{:S(2)}, u32[]{:S(2)}) %collective-permute-start.32) | collective-permute-done | bytes 524320 | tf_op jit(solution)/shard_map/ppermute | solution.py:958
  492.0 4.8 add_convert_fusion
  496.9 3.0 ring_add.31
  500.2 2.9 ring_add.30
  509.0 16.2 %collective-permute-done.42 = bf16[512,256]{1,0:T(8,128)(2,1)S(1)} collective-permute-done((bf16[512,256]{1,0:T(8,128)(2,1)S(1)}, bf16[512,256]{1,0:T(8,128)(2,1)S(1)}, u32[]{:S(2)}, u32[]{:S(2)}) %collective-permute-start.42) | collective-permute-done | bytes 262176 | tf_op jit(solution)/shard_map/ppermute | solution.py:902
  525.2 15.3 %collective-permute-done.38.got_ref = bf16[256,2048]{1,0:T(8,128)(2,1)} collective-permute-done((bf16[256,2048]{1,0:T(8,128)(2,1)}, bf16[256,2048]{1,0:T(8,128)(2,1)}, u32[]{:S(2)}, u32[]{:S(2)}) %collective-permute-start.38) | collective-permute-done | bytes 1048608 | tf_op jit(solution)/shard_map/ppermute | solution.py:961
  540.5 3.4 collective-permute-done.37.got_ref
  543.9 3.1 ring_add.33
  548.5 3.1 ring_add.32
  553.0 4.6 all-to-all-start.3
  557.6 4.4 layer_output.1
  562.0 18.8 %collective-permute-done.44.got_ref = bf16[256,2048]{1,0:T(8,128)(2,1)S(1)} collective-permute-done((bf16[256,2048]{1,0:T(8,128)(2,1)}, bf16[256,2048]{1,0:T(8,128)(2,1)S(1)}, u32[]{:S(2)}, u32[]{:S(2)}) %collective-permute-start.44) | collective-permute-done | bytes 1048608 | tf_op jit(solution)/shard_map/ppermute | solution.py:961
  580.8 5.6 collective-permute-done.43.got_ref
  586.4 3.1 ring_add.35
  591.7 3.1 ring_add.34
  603.3 9.4 %collective-permute-done.46.down_ref = bf16[256,2048]{1,0:T(8,128)(2,1)} collective-permute-done((bf16[256,2048]{1,0:T(8,128)(2,1)}, bf16[256,2048]{1,0:T(8,128)(2,1)}, u32[]{:S(2)}, u32[]{:S(2)}) %collective-permute-start.46) | collective-permute-done | bytes 1048608 | tf_op jit(solution)/shard_map/ppermute | solution.py:961
  612.6 5.8 collective-permute-done.45.up_ref
  618.5 5.9 input_grad.1
  (215 shorter events, 102.4 us)
Async XLA Ops:
  9.2 29.3 %all-to-all-start = ((bf16[8,256,128]{2,1,0:T(8,128)(2,1)}), bf16[8,256,128]{2,1,0:T(8,128)(2,1)S(1)}, u32[]{:S(2)}, u32[]{:S(2)}) async-start(bf16[8,256,128]{2,1,0:T(8,128)(2,1)} %pick_heads.1), calls=%async_computation | async-start | bytes 1048576 | tf_op jit(solution)/shard_map/all_to_all | solution.py:955
  18.4 20.1 %collective-permute-start = (bf16[256,1024]{1,0:T(8,128)(2,1)S(1)}, bf16[256,1024]{1,0:T(8,128)(2,1)S(1)}, u32[]{:S(2)}, u32[]{:S(2)}) collective-permute-start(bf16[256,1024]{1,0:T(8,128)(2,1)S(1)} %get-tuple-element.318), channel_id=1, source_target_pairs={{0,1},{1,3},{3,5},{5,7},{7,6},{6,4},{4,2},{2,0},{8,9},{9,11},{11,1... | collective-permute-start | bytes 1572872 | tf_op jit(solution)/shard_map/ppermute | solution.py:958
  20.4 18.1 %collective-permute-start.1 = (bf16[256,1024]{1,0:T(8,128)(2,1)S(1)}, bf16[256,1024]{1,0:T(8,128)(2,1)S(1)}, u32[]{:S(2)}, u32[]{:S(2)}) collective-permute-start(bf16[256,1024]{1,0:T(8,128)(2,1)S(1)} %get-tuple-element.318), channel_id=1, source_target_pairs={{1,0},{3,1},{5,3},{7,5},{6,7},{4,6},{2,4},{0,2},{9,8},{11,9},{13,1... | collective-permute-start | bytes 1572872 | tf_op jit(solution)/shard_map/ppermute | solution.py:961
  38.5 15.0 %collective-permute-start.2 = (bf16[256,1024]{1,0:T(8,128)(2,1)S(1)}, bf16[256,1024]{1,0:T(8,128)(2,1)S(1)}, u32[]{:S(2)}, u32[]{:S(2)}) collective-permute-start(bf16[256,1024]{1,0:T(8,128)(2,1)S(1)} %collective-permute-done), channel_id=1, source_target_pairs={{0,1},{1,3},{3,5},{5,7},{7,6},{6,4},{4,2},{2,0},{8,9},{9,11},{11,1... | collective-permute-start | bytes 1572872 | tf_op jit(solution)/shard_map/ppermute | solution.py:958
  40.0 15.1 %collective-permute-start.3 = (bf16[256,1024]{1,0:T(8,128)(2,1)S(1)}, bf16[256,1024]{1,0:T(8,128)(2,1)S(1)}, u32[]{:S(2)}, u32[]{:S(2)}) collective-permute-start(bf16[256,1024]{1,0:T(8,128)(2,1)S(1)} %collective-permute-done.1), channel_id=1, source_target_pairs={{1,0},{3,1},{5,3},{7,5},{6,7},{4,6},{2,4},{0,2},{9,8},{11,9},{13,1... | collective-permute-start | bytes 1572872 | tf_op jit(solution)/shard_map/ppermute | solution.py:961
  55.1 25.5 %collective-permute-start.4 = (bf16[256,1024]{1,0:T(8,128)(2,1)S(1)}, bf16[256,1024]{1,0:T(8,128)(2,1)S(1)}, u32[]{:S(2)}, u32[]{:S(2)}) collective-permute-start(bf16[256,1024]{1,0:T(8,128)(2,1)S(1)} %collective-permute-done.2), channel_id=1, source_target_pairs={{0,1},{1,3},{3,5},{5,7},{7,6},{6,4},{4,2},{2,0},{8,9},{9,11},{11,1... | collective-permute-start | bytes 1572872 | tf_op jit(solution)/shard_map/ppermute | solution.py:958
  57.7 22.9 %collective-permute-start.5 = (bf16[256,1024]{1,0:T(8,128)(2,1)S(1)}, bf16[256,1024]{1,0:T(8,128)(2,1)S(1)}, u32[]{:S(2)}, u32[]{:S(2)}) collective-permute-start(bf16[256,1024]{1,0:T(8,128)(2,1)S(1)} %collective-permute-done.3), channel_id=1, source_target_pairs={{1,0},{3,1},{5,3},{7,5},{6,7},{4,6},{2,4},{0,2},{9,8},{11,9},{13,1... | collective-permute-start | bytes 1572872 | tf_op jit(solution)/shard_map/ppermute | solution.py:961
  80.6 6.4 %collective-permute-start.6 = (bf16[128,1024]{1,0:T(8,128)(2,1)S(1)}, bf16[128,1024]{1,0:T(8,128)(2,1)S(1)}, u32[]{:S(2)}, u32[]{:S(2)}) collective-permute-start(bf16[128,1024]{1,0:T(8,128)(2,1)S(1)} %slice.55), channel_id=1, source_target_pairs={{0,1},{1,3},{3,5},{5,7},{7,6},{6,4},{4,2},{2,0},{8,9},{9,11},{11,1... | collective-permute-start | bytes 786440 | tf_op jit(solution)/shard_map/ppermute | solution.py:958
  83.3 6.4 %collective-permute-start.7 = (bf16[128,1024]{1,0:T(8,128)(2,1)S(1)}, bf16[128,1024]{1,0:T(8,128)(2,1)S(1)}, u32[]{:S(2)}, u32[]{:S(2)}) collective-permute-start(bf16[128,1024]{1,0:T(8,128)(2,1)S(1)} %slice.56), channel_id=1, source_target_pairs={{1,0},{3,1},{5,3},{7,5},{6,7},{4,6},{2,4},{0,2},{9,8},{11,9},{13,1... | collective-permute-start | bytes 786440 | tf_op jit(solution)/shard_map/ppermute | solution.py:961
  90.5 30.2 %collective-permute-start.8 = (bf16[2048,1024]{1,0:T(8,128)(2,1)}, bf16[2048,1024]{1,0:T(8,128)(2,1)}, u32[]{:S(2)}, u32[]{:S(2)}) collective-permute-start(bf16[2048,1024]{1,0:T(8,128)(2,1)} %constant_dynamic-update-slice_fusion.mine_ref), channel_id=1, source_target_pairs={{0,8},{8,0},{16,24},{24,16},{1,9},{9,1},{17,25},{25,17},{2,10},{10... | collective-permute-start | bytes 12582920 | tf_op jit(solution)/shard_map/ppermute | solution.py:988
  90.5 30.2 %all-to-all-start.1 = ((bf16[8,256,256]{2,1,0:T(8,128)(2,1)}), bf16[8,256,256]{2,1,0:T(8,128)(2,1)S(1)}, u32[]{:S(2)}, u32[]{:S(2)}) async-start(bf16[8,256,256]{2,1,0:T(8,128)(2,1)} %bitcast.44), calls=%async_computation.1 | async-start | bytes 2097152 | tf_op jit(solution)/shard_map/all_to_all | solution.py:955
  94.0 320.7 %reduce-scatter.5.cloned.1.call-start = ((), (), s32[]{:S(2)}) async-start(), calls=%async_computation.8 | async-start | bytes 5242880 | tf_op jit(solution)/shard_map/reduce_scatter | solution.py:1049
  130.9 25.0 %collective-permute-start.10 = (bf16[256,2048]{1,0:T(8,128)(2,1)}, bf16[256,2048]{1,0:T(8,128)(2,1)S(1)}, u32[]{:S(2)}, u32[]{:S(2)}) collective-permute-start(bf16[256,2048]{1,0:T(8,128)(2,1)} %get-tuple-element.179.refs_0_), channel_id=1, source_target_pairs={{1,0},{3,1},{5,3},{7,5},{6,7},{4,6},{2,4},{0,2},{9,8},{11,9},{13,1... | collective-permute-start | bytes 3145736 | tf_op jit(solution)/shard_map/ppermute | solution.py:961
  130.9 25.2 %collective-permute-start.9 = (bf16[256,2048]{1,0:T(8,128)(2,1)}, bf16[256,2048]{1,0:T(8,128)(2,1)S(1)}, u32[]{:S(2)}, u32[]{:S(2)}) collective-permute-start(bf16[256,2048]{1,0:T(8,128)(2,1)} %get-tuple-element.179.refs_0_), channel_id=1, source_target_pairs={{0,1},{1,3},{3,5},{5,7},{7,6},{6,4},{4,2},{2,0},{8,9},{9,11},{11,1... | collective-permute-start | bytes 3145736 | tf_op jit(solution)/shard_map/ppermute | solution.py:958
  156.1 24.3 %collective-permute-start.11 = (bf16[256,2048]{1,0:T(8,128)(2,1)S(1)}, bf16[256,2048]{1,0:T(8,128)(2,1)S(1)}, u32[]{:S(2)}, u32[]{:S(2)}) collective-permute-start(bf16[256,2048]{1,0:T(8,128)(2,1)S(1)} %collective-permute-done.9.refs_0_), channel_id=1, source_target_pairs={{0,1},{1,3},{3,5},{5,7},{7,6},{6,4},{4,2},{2,0},{8,9},{9,11},{11,1... | collective-permute-start | bytes 3145736 | tf_op jit(solution)/shard_map/ppermute | solution.py:958
  157.8 23.3 %collective-permute-start.12 = (bf16[256,2048]{1,0:T(8,128)(2,1)S(1)}, bf16[256,2048]{1,0:T(8,128)(2,1)S(1)}, u32[]{:S(2)}, u32[]{:S(2)}) collective-permute-start(bf16[256,2048]{1,0:T(8,128)(2,1)S(1)} %collective-permute-done.10.refs_1_), channel_id=1, source_target_pairs={{1,0},{3,1},{5,3},{7,5},{6,7},{4,6},{2,4},{0,2},{9,8},{11,9},{13,1... | collective-permute-start | bytes 3145736 | tf_op jit(solution)/shard_map/ppermute | solution.py:961
  181.1 22.7 %collective-permute-start.13 = (bf16[256,2048]{1,0:T(8,128)(2,1)S(1)}, bf16[256,2048]{1,0:T(8,128)(2,1)S(1)}, u32[]{:S(2)}, u32[]{:S(2)}) collective-permute-start(bf16[256,2048]{1,0:T(8,128)(2,1)S(1)} %collective-permute-done.11.refs_0_), channel_id=1, source_target_pairs={{0,1},{1,3},{3,5},{5,7},{7,6},{6,4},{4,2},{2,0},{8,9},{9,11},{11,1... | collective-permute-start | bytes 3145736 | tf_op jit(solution)/shard_map/ppermute | solution.py:958
  182.6 22.3 %collective-permute-start.14 = (bf16[256,2048]{1,0:T(8,128)(2,1)S(1)}, bf16[256,2048]{1,0:T(8,128)(2,1)S(1)}, u32[]{:S(2)}, u32[]{:S(2)}) collective-permute-start(bf16[256,2048]{1,0:T(8,128)(2,1)S(1)} %collective-permute-done.12.refs_1_), channel_id=1, source_target_pairs={{1,0},{3,1},{5,3},{7,5},{6,7},{4,6},{2,4},{0,2},{9,8},{11,9},{13,1... | collective-permute-start | bytes 3145736 | tf_op jit(solution)/shard_map/ppermute | solution.py:961
  204.9 21.0 %collective-permute-start.15 = (bf16[128,2048]{1,0:T(8,128)(2,1)S(1)}, bf16[128,2048]{1,0:T(8,128)(2,1)S(1)}, u32[]{:S(2)}, u32[]{:S(2)}) collective-permute-start(bf16[128,2048]{1,0:T(8,128)(2,1)S(1)} %slice.57), channel_id=1, source_target_pairs={{0,1},{1,3},{3,5},{5,7},{7,6},{6,4},{4,2},{2,0},{8,9},{9,11},{11,1... | collective-permute-start | bytes 1572872 | tf_op jit(solution)/shard_map/ppermute | solution.py:958
  205.9 20.0 %collective-permute-start.16 = (bf16[128,2048]{1,0:T(8,128)(2,1)S(1)}, bf16[128,2048]{1,0:T(8,128)(2,1)S(1)}, u32[]{:S(2)}, u32[]{:S(2)}) collective-permute-start(bf16[128,2048]{1,0:T(8,128)(2,1)S(1)} %slice.58), channel_id=1, source_target_pairs={{1,0},{3,1},{5,3},{7,5},{6,7},{4,6},{2,4},{0,2},{9,8},{11,9},{13,1... | collective-permute-start | bytes 1572872 | tf_op jit(solution)/shard_map/ppermute | solution.py:961
  226.9 16.8 %copy-start.1 = (bf16[1024,2048]{1,0:T(8,128)(2,1)S(1)}, bf16[1024,2048]{1,0:T(8,128)(2,1)}, u32[]{:S(2)}) copy-start(bf16[1024,2048]{1,0:T(8,128)(2,1)} %refs_5_.7) | copy-start | bytes 12582916
  241.4 15.5 %collective-permute-start.17 = (bf16[128,2048]{1,0:T(8,128)(2,1)S(1)}, bf16[128,2048]{1,0:T(8,128)(2,1)S(1)}, u32[]{:S(2)}, u32[]{:S(2)}) collective-permute-start(bf16[128,2048]{1,0:T(8,128)(2,1)S(1)} %get-tuple-element.327), channel_id=1, source_target_pairs={{0,1},{1,3},{3,5},{5,7},{7,6},{6,4},{4,2},{2,0},{8,9},{9,11},{11,1... | collective-permute-start | bytes 1572872 | tf_op jit(solution)/shard_map/ppermute | solution.py:958
  242.5 14.4 %collective-permute-start.18 = (bf16[128,2048]{1,0:T(8,128)(2,1)S(1)}, bf16[128,2048]{1,0:T(8,128)(2,1)S(1)}, u32[]{:S(2)}, u32[]{:S(2)}) collective-permute-start(bf16[128,2048]{1,0:T(8,128)(2,1)S(1)} %get-tuple-element.326), channel_id=1, source_target_pairs={{1,0},{3,1},{5,3},{7,5},{6,7},{4,6},{2,4},{0,2},{9,8},{11,9},{13,1... | collective-permute-start | bytes 1572872 | tf_op jit(solution)/shard_map/ppermute | solution.py:961
  260.7 20.6 %collective-permute-start.20 = (bf16[256,2048]{1,0:T(8,128)(2,1)}, bf16[256,2048]{1,0:T(8,128)(2,1)S(1)}, u32[]{:S(2)}, u32[]{:S(2)}) collective-permute-start(bf16[256,2048]{1,0:T(8,128)(2,1)} %ring_add.19), channel_id=1, source_target_pairs={{1,0},{3,1},{5,3},{7,5},{6,7},{4,6},{2,4},{0,2},{9,8},{11,9},{13,1... | collective-permute-start | bytes 3145736 | tf_op jit(solution)/shard_map/ppermute | solution.py:961
  264.6 21.0 %collective-permute-start.19 = (bf16[256,2048]{1,0:T(8,128)(2,1)}, bf16[256,2048]{1,0:T(8,128)(2,1)S(1)}, u32[]{:S(2)}, u32[]{:S(2)}) collective-permute-start(bf16[256,2048]{1,0:T(8,128)(2,1)} %ring_add.18), channel_id=1, source_target_pairs={{0,1},{1,3},{3,5},{5,7},{7,6},{6,4},{4,2},{2,0},{8,9},{9,11},{11,1... | collective-permute-start | bytes 3145736 | tf_op jit(solution)/shard_map/ppermute | solution.py:958
  285.6 199.7 %reduce-scatter.7.cloned.1.call-start = ((), (), s32[]{:S(2)}) async-start(), calls=%async_computation.9 | async-start | bytes 5242880 | tf_op jit(solution)/shard_map/reduce_scatter | solution.py:1049
  288.8 20.1 %collective-permute-start.22 = (bf16[256,2048]{1,0:T(8,128)(2,1)}, bf16[256,2048]{1,0:T(8,128)(2,1)S(1)}, u32[]{:S(2)}, u32[]{:S(2)}) collective-permute-start(bf16[256,2048]{1,0:T(8,128)(2,1)} %ring_add.21), channel_id=1, source_target_pairs={{1,0},{3,1},{5,3},{7,5},{6,7},{4,6},{2,4},{0,2},{9,8},{11,9},{13,1... | collective-permute-start | bytes 3145736 | tf_op jit(solution)/shard_map/ppermute | solution.py:961
  293.6 19.9 %collective-permute-start.21 = (bf16[256,2048]{1,0:T(8,128)(2,1)}, bf16[256,2048]{1,0:T(8,128)(2,1)S(1)}, u32[]{:S(2)}, u32[]{:S(2)}) collective-permute-start(bf16[256,2048]{1,0:T(8,128)(2,1)} %ring_add.20), channel_id=1, source_target_pairs={{0,1},{1,3},{3,5},{5,7},{7,6},{6,4},{4,2},{2,0},{8,9},{9,11},{11,1... | collective-permute-start | bytes 3145736 | tf_op jit(solution)/shard_map/ppermute | solution.py:958
  316.7 19.3 %collective-permute-start.24 = (bf16[256,2048]{1,0:T(8,128)(2,1)}, bf16[256,2048]{1,0:T(8,128)(2,1)S(1)}, u32[]{:S(2)}, u32[]{:S(2)}) collective-permute-start(bf16[256,2048]{1,0:T(8,128)(2,1)} %ring_add.23), channel_id=1, source_target_pairs={{1,0},{3,1},{5,3},{7,5},{6,7},{4,6},{2,4},{0,2},{9,8},{11,9},{13,1... | collective-permute-start | bytes 3145736 | tf_op jit(solution)/shard_map/ppermute | solution.py:961
  320.6 20.6 %collective-permute-start.23 = (bf16[256,2048]{1,0:T(8,128)(2,1)}, bf16[256,2048]{1,0:T(8,128)(2,1)S(1)}, u32[]{:S(2)}, u32[]{:S(2)}) collective-permute-start(bf16[256,2048]{1,0:T(8,128)(2,1)} %ring_add.22), channel_id=1, source_target_pairs={{0,1},{1,3},{3,5},{5,7},{7,6},{6,4},{4,2},{2,0},{8,9},{9,11},{11,1... | collective-permute-start | bytes 3145736 | tf_op jit(solution)/shard_map/ppermute | solution.py:958
  336.0 10.4 %copy-start.15 = (bf16[256,2048]{1,0:T(8,128)(2,1)}, bf16[256,2048]{1,0:T(8,128)(2,1)S(1)}, u32[]{:S(2)}) copy-start(bf16[256,2048]{1,0:T(8,128)(2,1)S(1)} %collective-permute-done.24.down_ref) | copy-start | bytes 3145732
  344.0 13.4 %collective-permute-start.25 = (bf16[128,2048]{1,0:T(8,128)(2,1)}, bf16[128,2048]{1,0:T(8,128)(2,1)S(1)}, u32[]{:S(2)}, u32[]{:S(2)}) collective-permute-start(bf16[128,2048]{1,0:T(8,128)(2,1)} %get-tuple-element.322), channel_id=1, source_target_pairs={{0,1},{1,3},{3,5},{5,7},{7,6},{6,4},{4,2},{2,0},{8,9},{9,11},{11,1... | collective-permute-start | bytes 1572872 | tf_op jit(solution)/shard_map/ppermute | solution.py:958
  345.3 12.1 %collective-permute-start.26 = (bf16[128,2048]{1,0:T(8,128)(2,1)}, bf16[128,2048]{1,0:T(8,128)(2,1)S(1)}, u32[]{:S(2)}, u32[]{:S(2)}) collective-permute-start(bf16[128,2048]{1,0:T(8,128)(2,1)} %get-tuple-element.321), channel_id=1, source_target_pairs={{1,0},{3,1},{5,3},{7,5},{6,7},{4,6},{2,4},{0,2},{9,8},{11,9},{13,1... | collective-permute-start | bytes 1572872 | tf_op jit(solution)/shard_map/ppermute | solution.py:961
  357.4 12.3 %copy-start.27 = (bf16[128,2048]{1,0:T(8,128)(2,1)}, bf16[128,2048]{1,0:T(8,128)(2,1)S(1)}, u32[]{:S(2)}) copy-start(bf16[128,2048]{1,0:T(8,128)(2,1)S(1)} %collective-permute-done.25.got_ref) | copy-start | bytes 1572868
  357.4 12.3 %copy-start.28 = (bf16[128,2048]{1,0:T(8,128)(2,1)}, bf16[128,2048]{1,0:T(8,128)(2,1)S(1)}, u32[]{:S(2)}) copy-start(bf16[128,2048]{1,0:T(8,128)(2,1)S(1)} %collective-permute-done.26.got_ref) | copy-start | bytes 1572868
  357.4 20.5 %all-to-all-start.2 = ((bf16[8,256,256]{2,1,0:T(8,128)(2,1)}), bf16[8,256,256]{2,1,0:T(8,128)(2,1)S(1)}, u32[]{:S(2)}, u32[]{:S(2)}) async-start(bf16[8,256,256]{2,1,0:T(8,128)(2,1)} %get-tuple-element.259), calls=%async_computation.2 | async-start | bytes 2097152 | tf_op jit(solution)/shard_map/all_to_all | solution.py:955
  361.0 201.0 %reduce-scatter.9.cloned.1.call-start = ((), (), s32[]{:S(2)}) async-start(), calls=%async_computation.10 | async-start | bytes 5242880 | tf_op jit(solution)/shard_map/reduce_scatter | solution.py:1049
  361.7 16.2 %copy-start.36 = (s32[1,8]{1,0:T(1,128)S(1)}, s32[1,8]{1,0:T(1,128)}, u32[]{:S(2)}) copy-start(s32[1,8]{1,0:T(1,128)} %get-tuple-element.330) | copy-start | bytes 100
  361.7 17.5 %copy-start.6 = (bf16[2048,256]{1,0:T(8,128)(2,1)S(1)}, bf16[2048,256]{1,0:T(8,128)(2,1)}, u32[]{:S(2)}) copy-start(bf16[2048,256]{1,0:T(8,128)(2,1)} %wq_ref.1) | copy-start | bytes 3145732
  361.7 262.6 %reduce-scatter.11.cloned.1.call-start = ((), (), s32[]{:S(2)}) async-start(), calls=%async_computation.11 | async-start | bytes 2359296 | tf_op jit(solution)/shard_map/reduce_scatter | solution.py:1091
  377.9 30.3 %collective-permute-start.29 = (bf16[2,2048,512]{2,1,0:T(8,128)(2,1)}, bf16[2,2048,512]{2,1,0:T(8,128)(2,1)}, u32[]{:S(2)}, u32[]{:S(2)}) collective-permute-start(bf16[2,2048,512]{2,1,0:T(8,128)(2,1)} %get-tuple-element.272), channel_id=1, source_target_pairs={{0,8},{8,0},{16,24},{24,16},{1,9},{9,1},{17,25},{25,17},{2,10},{10... | collective-permute-start | bytes 12582920 | tf_op jit(solution)/shard_map/ppermute | solution.py:887
  383.3 31.4 %collective-permute-start.28 = (bf16[256,2048]{1,0:T(8,128)(2,1)}, bf16[256,2048]{1,0:T(8,128)(2,1)S(1)}, u32[]{:S(2)}, u32[]{:S(2)}) collective-permute-start(bf16[256,2048]{1,0:T(8,128)(2,1)} %ring_add.25), channel_id=1, source_target_pairs={{1,0},{3,1},{5,3},{7,5},{6,7},{4,6},{2,4},{0,2},{9,8},{11,9},{13,1... | collective-permute-start | bytes 3145736 | tf_op jit(solution)/shard_map/ppermute | solution.py:961
  386.6 28.1 %collective-permute-start.27 = (bf16[256,2048]{1,0:T(8,128)(2,1)}, bf16[256,2048]{1,0:T(8,128)(2,1)}, u32[]{:S(2)}, u32[]{:S(2)}) collective-permute-start(bf16[256,2048]{1,0:T(8,128)(2,1)} %ring_add.24), channel_id=1, source_target_pairs={{0,1},{1,3},{3,5},{5,7},{7,6},{6,4},{4,2},{2,0},{8,9},{9,11},{11,1... | collective-permute-start | bytes 3145736 | tf_op jit(solution)/shard_map/ppermute | solution.py:958
  418.8 30.8 %collective-permute-start.31 = (bf16[256,2048]{1,0:T(8,128)(2,1)}, bf16[256,2048]{1,0:T(8,128)(2,1)}, u32[]{:S(2)}, u32[]{:S(2)}) collective-permute-start(bf16[256,2048]{1,0:T(8,128)(2,1)} %ring_add.27), channel_id=1, source_target_pairs={{1,0},{3,1},{5,3},{7,5},{6,7},{4,6},{2,4},{0,2},{9,8},{11,9},{13,1... | collective-permute-start | bytes 3145736 | tf_op jit(solution)/shard_map/ppermute | solution.py:961
  422.7 27.0 %collective-permute-start.30 = (bf16[256,2048]{1,0:T(8,128)(2,1)}, bf16[256,2048]{1,0:T(8,128)(2,1)}, u32[]{:S(2)}, u32[]{:S(2)}) collective-permute-start(bf16[256,2048]{1,0:T(8,128)(2,1)} %ring_add.26), channel_id=1, source_target_pairs={{0,1},{1,3},{3,5},{5,7},{7,6},{6,4},{4,2},{2,0},{8,9},{9,11},{11,1... | collective-permute-start | bytes 3145736 | tf_op jit(solution)/shard_map/ppermute | solution.py:958
  425.0 67.0 %collective-permute-start.36 = (bf16[2048,512]{1,0:T(8,128)(2,1)}, bf16[2048,512]{1,0:T(8,128)(2,1)}, u32[]{:S(2)}, u32[]{:S(2)}) collective-permute-start(bf16[2048,512]{1,0:T(8,128)(2,1)} %fusion), channel_id=1, source_target_pairs={{0,16},{8,24},{16,0},{24,8},{1,17},{9,25},{17,1},{25,9},{2,18},{10... | collective-permute-start | bytes 6291464 | tf_op jit(solution)/shard_map/ppermute | solution.py:902
  452.8 39.2 %collective-permute-start.35 = (bf16[256,2048]{1,0:T(8,128)(2,1)}, bf16[256,2048]{1,0:T(8,128)(2,1)S(1)}, u32[]{:S(2)}, u32[]{:S(2)}) collective-permute-start(bf16[256,2048]{1,0:T(8,128)(2,1)} %ring_add.29), channel_id=1, source_target_pairs={{1,0},{3,1},{5,3},{7,5},{6,7},{4,6},{2,4},{0,2},{9,8},{11,9},{13,1... | collective-permute-start | bytes 3145736 | tf_op jit(solution)/shard_map/ppermute | solution.py:961
  456.2 14.6 %copy-start.34 = (f32[2048]{0:T(1024)S(1)}, f32[2048]{0:T(1024)}, u32[]{:S(2)}) copy-start(f32[2048]{0:T(1024)} %param.16) | copy-start | bytes 24580
  456.2 16.0 %copy-start.35 = (f32[1,2048]{1,0:T(1,128)S(1)}, f32[1,2048]{1,0:T(1,128)}, u32[]{:S(2)}) copy-start(f32[1,2048]{1,0:T(1,128)} %get-tuple-element.281) | copy-start | bytes 24580
  456.2 35.8 %collective-permute-start.34 = (bf16[256,2048]{1,0:T(8,128)(2,1)}, bf16[256,2048]{1,0:T(8,128)(2,1)}, u32[]{:S(2)}, u32[]{:S(2)}) collective-permute-start(bf16[256,2048]{1,0:T(8,128)(2,1)} %ring_add.28), channel_id=1, source_target_pairs={{0,1},{1,3},{3,5},{5,7},{7,6},{6,4},{4,2},{2,0},{8,9},{9,11},{11,1... | collective-permute-start | bytes 3145736 | tf_op jit(solution)/shard_map/ppermute | solution.py:958
  468.8 23.2 %collective-permute-start.32 = (bf16[128,2048]{1,0:T(8,128)(2,1)}, bf16[128,2048]{1,0:T(8,128)(2,1)}, u32[]{:S(2)}, u32[]{:S(2)}) collective-permute-start(bf16[128,2048]{1,0:T(8,128)(2,1)} %get-tuple-element.320), channel_id=1, source_target_pairs={{0,1},{1,3},{3,5},{5,7},{7,6},{6,4},{4,2},{2,0},{8,9},{9,11},{11,1... | collective-permute-start | bytes 1572872 | tf_op jit(solution)/shard_map/ppermute | solution.py:958
  470.3 21.7 %collective-permute-start.33 = (bf16[128,2048]{1,0:T(8,128)(2,1)}, bf16[128,2048]{1,0:T(8,128)(2,1)}, u32[]{:S(2)}, u32[]{:S(2)}) collective-permute-start(bf16[128,2048]{1,0:T(8,128)(2,1)} %get-tuple-element.319), channel_id=1, source_target_pairs={{1,0},{3,1},{5,3},{7,5},{6,7},{4,6},{2,4},{0,2},{9,8},{11,9},{13,1... | collective-permute-start | bytes 1572872 | tf_op jit(solution)/shard_map/ppermute | solution.py:961
  496.8 8.2 %collective-permute-start.39 = (f32[2,512,256]{2,1,0:T(8,128)}, f32[2,512,256]{2,1,0:T(8,128)S(1)}, u32[]{:S(2)}, u32[]{:S(2)}) collective-permute-start(f32[2,512,256]{2,1,0:T(8,128)} %get-tuple-element.291), channel_id=1, source_target_pairs={{0,8},{8,0},{16,24},{24,16},{1,9},{9,1},{17,25},{25,17},{2,10},{10... | collective-permute-start | bytes 3145736 | tf_op jit(solution)/shard_map/ppermute | solution.py:887
  499.9 40.6 %collective-permute-start.38 = (bf16[256,2048]{1,0:T(8,128)(2,1)}, bf16[256,2048]{1,0:T(8,128)(2,1)}, u32[]{:S(2)}, u32[]{:S(2)}) collective-permute-start(bf16[256,2048]{1,0:T(8,128)(2,1)} %ring_add.31), channel_id=1, source_target_pairs={{1,0},{3,1},{5,3},{7,5},{6,7},{4,6},{2,4},{0,2},{9,8},{11,9},{13,1... | collective-permute-start | bytes 3145736 | tf_op jit(solution)/shard_map/ppermute | solution.py:961
  503.1 40.7 %collective-permute-start.37 = (bf16[256,2048]{1,0:T(8,128)(2,1)}, bf16[256,2048]{1,0:T(8,128)(2,1)}, u32[]{:S(2)}, u32[]{:S(2)}) collective-permute-start(bf16[256,2048]{1,0:T(8,128)(2,1)} %ring_add.30), channel_id=1, source_target_pairs={{0,1},{1,3},{3,5},{5,7},{7,6},{6,4},{4,2},{2,0},{8,9},{9,11},{11,1... | collective-permute-start | bytes 3145736 | tf_op jit(solution)/shard_map/ppermute | solution.py:958
  505.0 2.1 collective-permute-start.41
  505.2 38.7 %collective-permute-start.40 = (f32[512,256]{1,0:T(8,128)S(1)}, f32[512,256]{1,0:T(8,128)S(1)}, u32[]{:S(2)}, u32[]{:S(2)}) collective-permute-start(f32[512,256]{1,0:T(8,128)S(1)} %get-tuple-element.323), channel_id=1, source_target_pairs={{0,16},{8,24},{16,0},{24,8},{1,17},{9,25},{17,1},{25,9},{2,18},{10... | collective-permute-start | bytes 1572872 | tf_op jit(solution)/shard_map/ppermute | solution.py:902
  508.1 17.0 %collective-permute-start.42 = (bf16[512,256]{1,0:T(8,128)(2,1)S(1)}, bf16[512,256]{1,0:T(8,128)(2,1)S(1)}, u32[]{:S(2)}, u32[]{:S(2)}) collective-permute-start(bf16[512,256]{1,0:T(8,128)(2,1)S(1)} %fusion.1), channel_id=1, source_target_pairs={{0,16},{8,24},{16,0},{24,8},{1,17},{9,25},{17,1},{25,9},{2,18},{10... | collective-permute-start | bytes 786440 | tf_op jit(solution)/shard_map/ppermute | solution.py:902
  547.0 33.8 %collective-permute-start.44 = (bf16[256,2048]{1,0:T(8,128)(2,1)}, bf16[256,2048]{1,0:T(8,128)(2,1)S(1)}, u32[]{:S(2)}, u32[]{:S(2)}) collective-permute-start(bf16[256,2048]{1,0:T(8,128)(2,1)} %ring_add.33), channel_id=1, source_target_pairs={{1,0},{3,1},{5,3},{7,5},{6,7},{4,6},{2,4},{0,2},{9,8},{11,9},{13,1... | collective-permute-start | bytes 3145736 | tf_op jit(solution)/shard_map/ppermute | solution.py:961
  551.6 34.8 %collective-permute-start.43 = (bf16[256,2048]{1,0:T(8,128)(2,1)}, bf16[256,2048]{1,0:T(8,128)(2,1)}, u32[]{:S(2)}, u32[]{:S(2)}) collective-permute-start(bf16[256,2048]{1,0:T(8,128)(2,1)} %ring_add.32), channel_id=1, source_target_pairs={{0,1},{1,3},{3,5},{5,7},{7,6},{6,4},{4,2},{2,0},{8,9},{9,11},{11,1... | collective-permute-start | bytes 3145736 | tf_op jit(solution)/shard_map/ppermute | solution.py:958
  553.0 45.9 %all-to-all-start.3 = ((f32[8,64,256]{2,1,0:T(8,128)}), f32[8,64,256]{2,1,0:T(8,128)S(1)}, u32[]{:S(2)}, u32[]{:S(2)}) async-start(f32[8,64,256]{2,1,0:T(8,128)} %bitcast.19), calls=%async_computation.6 | async-start | bytes 1048576 | tf_op jit(solution)/shard_map/all_to_all | solution.py:955
  589.5 6.9 %copy-start.10 = (bf16[512,1024]{1,0:T(8,128)(2,1)S(1)}, bf16[512,1024]{1,0:T(8,128)(2,1)}, u32[]{:S(2)}) copy-start(bf16[512,1024]{1,0:T(8,128)(2,1)} %reduce-scatter.7.cloned.1.call-done) | copy-start | bytes 3145732
  589.5 23.1 %collective-permute-start.46 = (bf16[256,2048]{1,0:T(8,128)(2,1)}, bf16[256,2048]{1,0:T(8,128)(2,1)}, u32[]{:S(2)}, u32[]{:S(2)}) collective-permute-start(bf16[256,2048]{1,0:T(8,128)(2,1)} %ring_add.35), channel_id=1, source_target_pairs={{1,0},{3,1},{5,3},{7,5},{6,7},{4,6},{2,4},{0,2},{9,8},{11,9},{13,1... | collective-permute-start | bytes 3145736 | tf_op jit(solution)/shard_map/ppermute | solution.py:961
  594.9 23.6 %collective-permute-start.45 = (bf16[256,2048]{1,0:T(8,128)(2,1)}, bf16[256,2048]{1,0:T(8,128)(2,1)}, u32[]{:S(2)}, u32[]{:S(2)}) collective-permute-start(bf16[256,2048]{1,0:T(8,128)(2,1)} %ring_add.34), channel_id=1, source_target_pairs={{0,1},{1,3},{3,5},{5,7},{7,6},{6,4},{4,2},{2,0},{8,9},{9,11},{11,1... | collective-permute-start | bytes 3145736 | tf_op jit(solution)/shard_map/ppermute | solution.py:958
  (28 other events, 101.8 us)
Sparse Core Ops, SparseCore 0:
  285.7 43.7 reduce-scatter.4
  332.2 44.4 reduce-scatter.6
  379.2 44.4 reduce-scatter.8
  497.0 81.9 reduce-scatter.10

commit v4 on v3

--- a/solution.py
+++ b/solution.py
@@ -85,37 +85,42 @@
     return rows * widen(cosines, count) - turned
 
 
-def front_kernel(rows_ref, gain_ref, wq_ref, table_ref, normed_ref, q_ref):
+def front_kernel(start, rows_ref, gain_ref, wq_ref, table_ref, *refs):
+    normed_ref, q_ref = refs[-2:]
     rows = rows_ref[...].astype(f32)
     row_scale = lax.rsqrt(jnp.mean(rows * rows, axis=-1, keepdims=True) + EPSILON)
     normed_ref[...] = (rows * row_scale * gain_ref[...]).astype(bf16)
     q_raw = mm(normed_ref[...], wq_ref[...], NN)
-    turned = rotate(q_raw, *turn_at(table_ref, pl.program_id(0)))
+    turned = rotate(q_raw, *turn_at(table_ref, start + pl.program_id(0)))
     q_ref[...] = (turned.astype(bf16).astype(f32) * ATTN_SCALE).astype(bf16)
 
 
-def front(hidden, gain, w_query, table):
+def front(first, hidden, gain, w_query, table, carried):
     count, width = hidden.shape
     q_cols = w_query.shape[1]
-    row = lambda i: (i, 0)
+    steps = count // QB // 2
+    start = steps if first else 0
+    row = lambda i: (start + i, 0)
     whole = lambda i: (0, 0)
     return pl.pallas_call(
-        front_kernel,
-        grid=(count // QB,),
+        functools.partial(front_kernel, start),
+        grid=(steps,),
         in_specs=[
             pl.BlockSpec((QB, width), row),
             pl.BlockSpec((1, width), whole),
             pl.BlockSpec((width, q_cols), whole),
             pl.BlockSpec(table.shape, whole),
-        ],
+        ]
+        + [pl.BlockSpec(memory_space=pl.ANY)] * len(carried),
         out_specs=[pl.BlockSpec((QB, width), row), pl.BlockSpec((QB, q_cols), row)],
         out_shape=[
             jax.ShapeDtypeStruct((count, width), bf16),
             jax.ShapeDtypeStruct((count, q_cols), bf16),
         ],
-        cost_estimate=cost(2 * count * width * q_cols, 5 * count * width),
+        input_output_aliases={4 + index: index for index in range(len(carried))},
+        cost_estimate=cost(count * width * q_cols, 3 * count * width),
         name="norm_and_query",
-    )(hidden, gain, w_query, table)
+    )(hidden, gain, w_query, table, *carried)
 
 
 def keys_kernel(length_ref, normed_ref, wkv_ref, table_ref, k_ref, kt_ref, v_ref, vt_ref):
@@ -196,8 +201,9 @@
     return key <= lax.broadcasted_iota(jnp.int32, (keys_count, rows_count), 1)
 
 
-def attend_kernel(heads, q_ref, k_ref, vt_ref, o_ref, lse_ref, slab_ref, high_ref, total_ref):
-    block = pl.program_id(0)
+def attend_kernel(heads, start, q_ref, k_ref, vt_ref, *refs):
+    o_ref, lse_ref, slab_ref, high_ref, total_ref = refs[-5:]
+    block = start + pl.program_id(0)
     rows = q_ref[...]
     for head in range(heads):
         slab_ref[head] = head_slab(rows, head, 1.0)
@@ -238,20 +244,24 @@
     o_ref[...] = jnp.concatenate(outs, 0).T.astype(bf16)
 
 
-def attend(queries, keys, values_t):
+def attend(first, queries, keys, values_t, carried):
     count, q_cols = queries.shape
     heads = q_cols // HD
-    return pl.pallas_call(
-        functools.partial(attend_kernel, heads),
-        grid=(count // QB,),
+    blocks = count // QB
+    split = blocks * 5 // 8
+    start = split if first else 0
+    return pl.pallas_call(
+        functools.partial(attend_kernel, heads, start),
+        grid=(blocks - split if first else split,),
         in_specs=[
-            pl.BlockSpec((QB, q_cols), lambda i: (i, 0)),
+            pl.BlockSpec((QB, q_cols), lambda i: (start + i, 0)),
             pl.BlockSpec((count, 128), lambda i: (0, 0)),
             pl.BlockSpec((128, count), lambda i: (0, 0)),
-        ],
+        ]
+        + [pl.BlockSpec(memory_space=pl.ANY)] * len(carried),
         out_specs=[
-            pl.BlockSpec((QB, q_cols), lambda i: (i, 0)),
-            pl.BlockSpec((8, QB), lambda i: (0, i)),
+            pl.BlockSpec((QB, q_cols), lambda i: (start + i, 0)),
+            pl.BlockSpec((8, QB), lambda i: (0, start + i)),
         ],
         out_shape=[
             jax.ShapeDtypeStruct((count, q_cols), bf16),
@@ -262,9 +272,10 @@
             pltpu.VMEM((8, QB), f32),
             pltpu.VMEM((heads, 128, QB), f32),
         ],
-        cost_estimate=cost(heads * count * count * 512, 4 * count * q_cols),
+        input_output_aliases={3 + index: index for index in range(len(carried))},
+        cost_estimate=cost(heads * count * count * 256, 2 * count * q_cols),
         name="attend",
-    )(queries, keys, values_t)
+    )(queries, keys, values_t, *carried)
 
 
 def attend_back_kernel(
@@ -412,7 +423,7 @@
     )(queries, out_grads, attended, lse, keys, keys_t, values, table, *carried)
 
 
-LENGTH, CORE, RING = 0, 1, 2
+LENGTH, CORE, CHIP, RING = 0, 1, 2, 3
 
 
 def out_norm_kernel(ids_ref, o_ref, mine_ref, other_ref, rows_ref, gain_ref, middle_ref, normed_ref):
@@ -593,7 +604,10 @@
 
 
 def core_halves(chips):
-    piece = lambda i, s: jnp.where(i < chips, 2 * i + 1 - s[CORE], 2 * (i - chips) + s[CORE])
+    def piece(i, s):
+        chip = (s[CHIP] + i) % chips
+        return 2 * chip + jnp.where(i < chips, 1 - s[CORE], s[CORE])
+
     sent = lambda i: jnp.minimum(i, chips - 1)
     kept = lambda i: jnp.maximum(i - chips, 0)
     return piece, sent, kept
@@ -882,30 +896,26 @@
 
 def over_cores(send, keep):
     chips = send.shape[0]
-    chip = lax.axis_index("dp") // 2
-    take = lambda a, i: lax.dynamic_index_in_dim(a, i, 0, keepdims=False)
     got = lax.ppermute(send, "dp", [(i, i ^ 1) for i in range(2 * chips)])
-    stay = [take(keep, chip), take(got, chip)]
-    go = []
-    for step in range(1, chips):
-        there = (chip + step) % chips
-        term = take(keep, there).astype(f32) + take(got, there).astype(f32)
-        go.append(term.astype(send.dtype))
-    return stay, go
-
-
-def over_chips(stay, go):
+    go = [
+        (keep[step].astype(f32) + got[step].astype(f32)).astype(send.dtype)
+        for step in range(1, chips)
+    ]
+    return keep, got, go
+
+
+def over_chips(keep, got, go):
     chips = len(go) + 1
-    terms = list(stay)
+    arriving = []
     for step in range(1, chips):
         to = [(i, ((i // 2 + step) % chips) * 2 + i % 2) for i in range(2 * chips)]
-        terms.append(lax.ppermute(go[step - 1], "dp", to))
-    return terms
-
-
-def total_of(terms):
-    total = terms[0].astype(f32)
-    for term in terms[1:]:
+        arriving.append(lax.ppermute(go[step - 1], "dp", to))
+    return keep, got, arriving
+
+
+def total_of(keep, got, arriving):
+    total = keep[0].astype(f32) + got[0].astype(f32)
+    for term in arriving:
         total = total + term.astype(f32)
     return total
 
@@ -945,7 +955,11 @@
     apart.append(half_way)
     ring = [[order[(spot[i] + d) % groups] for d in apart] for i in range(groups)]
     ids = jnp.concatenate(
-        [seq_lengths, core[None].astype(jnp.int32), jnp.asarray(ring, jnp.int32)[member]]
+        [
+            seq_lengths,
+            jnp.stack([core, replica // 2]).astype(jnp.int32),
+            jnp.asarray(ring, jnp.int32)[member],
+        ]
     )
     table = rope_tables(rows_total)
     gain_one = attn_gain[None, :]
@@ -973,17 +987,20 @@
     kv_of = [i * heads_here // (H // KVH) for i in range(groups)]
     w_kv = pick_heads(w_key, w_value, kv_of)
     w_kv = exchange(w_kv).reshape(width, 2 * HD)
-    normed_one, queries = front(hidden_in, gain_one, w_query, table)
-    *w_hop, w_kv, normed_one, queries = tie(*w_hop, w_kv, normed_one, queries)
+    carried = front(0, hidden_in, gain_one, w_query, table, [])
+    w_hop, carried = tie(w_hop, carried)
     for _ in range(half_way - 3):
         w_hop = w_next()
+    normed_one, queries = front(1, hidden_in, gain_one, w_query, table, carried)
     keys, keys_t, values, values_t = keys_values(seq_lengths, normed_one, w_kv, table)
-    *w_hop, keys = tie(*w_hop, keys)
+    w_hop, keys = tie(w_hop, keys)
     w_hop = w_next()
-    attended, lse = attend(queries, keys, values_t)
-    *w_hop, attended = tie(*w_hop, attended)
+    carried = attend(0, queries, keys, values_t, [])
+    w_hop, carried = tie(w_hop, carried)
+    w_hop = w_next()
+    attended, lse = attend(1, queries, keys, values_t, carried)
+    w_hop, attended = tie(w_hop, attended)
     attended_rows = exchange(attended.reshape(groups, share, q_cols))
-    w_hop = w_next()
     w_mine = jnp.concatenate([*w_mine, *w_hop], 0)
     w_other = lax.ppermute(w_mine, "dp", [(i, i ^ 1) for i in range(replicas)])
     w_qkv = jnp.concatenate([w_query, w_kv], 1)
@@ -1020,20 +1037,27 @@
     def first_hop(far):
         return onward(far[:half]), back(far[half:])
 
-    def next_hop(terms, block, got):
+    def hop_sums(terms, block, got):
         down = ring_add(ids, terms, block, None, got[1], share - got[1].shape[0], share)
         up = ring_add(ids, terms, block + 1, None, got[0], 0, share)
-        return onward(up), back(down)
-
-    def natural_hop(terms, distance, got):
+        return up, down
+
+    def send_on(sums):
+        return onward(sums[0]), back(sums[1])
+
+    def next_hop(terms, block, got):
+        return send_on(hop_sums(terms, block, got))
+
+    def natural_sums(terms, distance, got):
         first = share - got[1].shape[0]
         down = ring_add(ids, terms, None, 2 * distance - 1, got[1], first, share)
         up = ring_add(ids, terms, None, 2 * distance, got[0], 0, share)
-        return onward(up), back(down)
+        return up, down
 
     got = first_hop(grads[-1])
     mlp = mm(act, w_down, NN).astype(bf16)
-    *got, mlp = tie(*got, mlp)
+    mlp_far = [mlp[rows_total - share : rows_total - half], mlp[rows_total - half :]]
+    got, mlp, mlp_far = tie(got, mlp, mlp_far)
     fillers = [
         lambda: mm(act, down_ring, TN).astype(bf16),
         lambda: mm(normed_ring, dgate, TN).astype(bf16),
@@ -1051,16 +1075,17 @@
     gate_wgrad = scatter(gate_wgrad, 0)
     up_wgrad = scatter(up_wgrad, 0)
 
-    *got, mlp = tie(*got, mlp)
-    out_got = first_hop(mlp[rows_total - share :])
+    got, mlp_far = tie(got, mlp_far)
+    out_got = send_on(mlp_far)
     dh, da, gain_part, do_send = norm_back(
         ids, [grads[0], *got], middle, gain_two, out_grad, w_mine, w_other, q_cols
     )
     *out_got, do_send, da = tie(*out_got, do_send, da)
     do = exchange(do_send).reshape(rows_total, q_cols)
     out_parts = out_wgrad_parts(ids, attended_rows, da, replicas)
-    do, out_parts = tie(do, out_parts)
-    out_got = next_hop(mlp, 2 * half_way - 4, out_got)
+    out_sums = hop_sums(mlp, 2 * half_way - 4, out_got)
+    do, out_parts, out_sums = tie(do, out_parts, out_sums)
+    out_got = send_on(out_sums)
     out_parts = over_cores(*out_parts)
     operands = [queries, do, attended, lse, keys, keys_t, values, table]
     carried = attend_back(0, *operands, [])
@@ -1071,10 +1096,12 @@
     qkv_grad = attend_back(1, *operands, carried)
     out_got, qkv_grad = tie(out_got, qkv_grad)
 
+    far = lax.dynamic_slice_in_dim(qkv_grad, ids[RING + groups - 1] * share, share, 0)
+    far = mm(far, w_qkv, NT).astype(bf16)
+    in_got = first_hop(far)
+    qkv_grad, far, out_got = tie(qkv_grad, far, out_got)
+    out_got = next_hop(mlp, 0, out_got)
     first_grad = mm(qkv_grad, w_qkv, NT).astype(bf16)
-    far = lax.dynamic_slice_in_dim(first_grad, ids[RING + groups - 1] * share, share, 0)
-    in_got = first_hop(far)
-    out_got = next_hop(mlp, 0, out_got)
     q_send, q_keep, s_send, s_keep = qkv_wgrad_parts(
         ids,
         normed_one,
@@ -1084,22 +1111,25 @@
         gain_part.reshape(width, 1),
         replicas,
     )
-    in_got, out_got, q_send, s_send, gate_wgrad, out_terms = tie(
-        in_got, out_got, q_send, s_send, gate_wgrad, out_terms
+    in_got, out_got, q_send, s_send, gate_wgrad, first_grad = tie(
+        in_got, out_got, q_send, s_send, gate_wgrad, first_grad
     )
-    out_wgrad = total_of(out_terms).astype(bf16)
-    out_wgrad = lax.psum_scatter(out_wgrad, "tensor", scatter_dimension=0, tiled=True)
     small = over_cores(s_send, s_keep)
     query_wgrad = over_cores(q_send, q_keep)
     for d in range(half_way - 1, 0, -1):
-        in_got = natural_hop(first_grad, d, in_got)
+        in_sums = natural_sums(first_grad, d, in_got)
         if d == half_way - 1:
+            in_got = send_on(in_sums)
             small = over_chips(*small)
             query_wgrad = over_chips(*query_wgrad)
-            in_got, small, query_wgrad = tie(in_got, small, query_wgrad)
-            small, query_wgrad = total_of(small), total_of(query_wgrad)
+            in_got, small, query_wgrad, out_terms = tie(in_got, small, query_wgrad, out_terms)
+            out_wgrad = total_of(*out_terms).astype(bf16)
+            out_wgrad = lax.psum_scatter(out_wgrad, "tensor", scatter_dimension=0, tiled=True)
+            small, query_wgrad = total_of(*small), total_of(*query_wgrad)
             layer_out = layer_output(middle, mlp, groups - 2, out_got)
-        elif d == half_way - 2:
+            continue
+        in_got = send_on(in_sums)
+        if d == half_way - 2:
             in_got, layer_out, up_wgrad = tie(in_got, layer_out, up_wgrad)
     pieces = exchange(small.reshape(groups, small.shape[0] // groups, 256))
     input_grad = in_grad(ids, first_grad, in_got, hidden_in, gain_one, dh)

time: 641 us -> 634 us (0.989)
  waiting for transfers between devices: 163 us -> 155 us
  local copies, waits for them, and re-layouts: 35.2 us -> 28.4 us
    pallas_call x2 -> x4, Pallas kernels: 33.4 us -> 37.1 us  [the longest x2 24.6 us: attend(): pl.pallas_call(functools.partial(attend_kernel, heads, start), grid=(bloc...]
    dot_general x5 -> x6, matrix products: 62 us -> 62.7 us  [mm(): return lax.dot_general(left, right, dims, preferred_element_type=f32)]
    unnamed x83 -> x90, local copies, waits for them, and re-layouts: 16 us -> 15.6 us
  transfers between devices with their start and end apart: 55 -> 55, of which waited for: 27 -> 26; matrix products, arithmetic and copies ran while one was open for 17% -> 16% of each run, Pallas kernels for 38% -> 40%
where the time goes in v4:
time: 634 us; the launch traced here: 624 us
  Pallas kernels  273 us (43%)
  waiting for transfers between devices  155 us (24%)
  starting transfers between devices  66.4 us (10%)
  matrix products  62.7 us (10%)
  local copies, waits for them, and re-layouts  28.4 us (4%)
  other arithmetic  23.2 us (4%)
  between operations  15.8 us (2%)
    pallas_call x5, Pallas kernels, swiglu(): pl.pallas_call(functools.partial(swiglu_kernel, len(pieces), tuple(member...  80.5 us
    dot_general x6, matrix products, mm(): return lax.dot_general(left, right, dims, preferred_element_type=f32)  62.7 us
    ppermute x20, waiting for transfers between devices, back(): return lax.ppermute(array, 'tensor', behind)  60.7 us
    pallas_call x18, Pallas kernels, ring_add(): pl.pallas_call(functools.partial(ring_add_kernel, first), grid_spec=pltpu...  55.1 us
    ppermute x20, waiting for transfers between devices, onward(): return lax.ppermute(array, 'tensor', ahead)  49.5 us
    pallas_call x2, Pallas kernels, attend_back(): pl.pallas_call(functools.partial(attend_back_kernel, heads, start), grid=...  40.9 us
    ppermute x20, starting transfers between devices, onward(): return lax.ppermute(array, 'tensor', ahead)  28.3 us
    all_to_all x4, waiting for transfers between devices, exchange(): return lax.all_to_all(array, 'tensor', 0, 0, tiled=True)  27.3 us
  transfers between devices with their start and end apart: 55, of which 26 were waited for; matrix products, arithmetic and copies ran while one was open for 16% of the time, Pallas kernels for 40%

profile of v4, /device:TPU:0, one launch (start us, length us, event | category | flops | bytes accessed | tf_op | source)
XLA Modules:
  0.0 624.3 jit_solution(3044765756880623460)
XLA Ops:
  9.2 3.0 collective-permute-start
  14.2 6.3 %all-to-all-start = ((bf16[8,256,128]{2,1,0:T(8,128)(2,1)}), bf16[8,256,128]{2,1,0:T(8,128)(2,1)S(1)}, u32[]{:S(2)}, u32[]{:S(2)}) async-start(bf16[8,256,128]{2,1,0:T(8,128)(2,1)} %pick_heads.1), calls=%async_computation | async-start | bytes 1048576 | tf_op jit(solution)/shard_map/all_to_all | solution.py:969
  21.9 6.3 %norm_and_query.2 = (bf16[2048,2048]{1,0:T(8,128)(2,1)}, bf16[2048,256]{1,0:T(8,128)(2,1)}) custom-call(bf16[2048,2048]{1,0:T(8,128)(2,1)} %rows_ref.7, f32[1,2048]{1,0:T(1,128)} %bitcast.45, bf16[2048,256]{1,0:T(8,128)(2,1)} %wq_ref.3, f32[320,256]{1,0:T(8,128)} %pad_maximum_fusion.1.table_ref), custom_call_target="tpu_custom_call" | custom-call | flops 1073741824 | bytes 12582912 | tf_op jit(solution)/shard_map/norm_and_query/pallas_call | solution.py:105
  31.0 6.3 %norm_and_query.3 = (bf16[2048,2048]{1,0:T(8,128)(2,1)}, bf16[2048,256]{1,0:T(8,128)(2,1)}) custom-call(bf16[2048,2048]{1,0:T(8,128)(2,1)} %rows_ref.7, f32[1,2048]{1,0:T(1,128)} %bitcast.46, bf16[2048,256]{1,0:T(8,128)(2,1)} %wq_ref.3, f32[320,256]{1,0:T(8,128)} %pad_maximum_fusion.1.table_ref, ...), custom_call_target="tpu_custom_call", output_to_operand_aliasing={{0}: (4, {}), {1}: (5, {})} | custom-call | flops 1073741824 | bytes 12582912 | tf_op jit(solution)/shard_map/norm_and_query/pallas_call | solution.py:105
  39.8 7.2 %keys_and_values.1 = (bf16[2048,128]{1,0:T(8,128)(2,1)}, bf16[128,2048]{1,0:T(8,128)(2,1)}, bf16[2048,128]{1,0:T(8,128)(2,1)}, bf16[128,2048]{1,0:T(8,128)(2,1)}) custom-call(s32[1]{0:T(128)S(6)} %copy.94.length_ref, bf16[2048,2048]{1,0:T(8,128)(2,1)} %get-tuple-element.185.normed_ref, bf16[2048,128]{1,0:T(8,128)(2,1)} %bitcast.38, ...), custom_call_target="tpu_custom_call" | custom-call | flops 1073741824 | bytes 8388608 | tf_op jit(solution)/shard_map/keys_and_values/pallas_call | solution.py:147
  50.7 11.3 %attend.2 = (bf16[2048,256]{1,0:T(8,128)(2,1)}, f32[8,2048]{1,0:T(8,128)}) custom-call(bf16[2048,256]{1,0:T(8,128)(2,1)} %get-tuple-element.189.q_ref, bf16[2048,128]{1,0:T(8,128)(2,1)} %get-tuple-element.190.k_ref, bf16[128,2048]{1,0:T(8,128)(2,1)} %get-tuple-element.191.vt_ref), custom_call_target="tpu_custom_call" | custom-call | flops 4294967296 | bytes 1048576 | tf_op jit(solution)/shard_map/attend/pallas_call | solution.py:253
  64.6 13.3 %attend.3 = (bf16[2048,256]{1,0:T(8,128)(2,1)}, f32[8,2048]{1,0:T(8,128)}) custom-call(bf16[2048,256]{1,0:T(8,128)(2,1)} %get-tuple-element.189.q_ref, bf16[2048,128]{1,0:T(8,128)(2,1)} %get-tuple-element.190.k_ref, bf16[128,2048]{1,0:T(8,128)(2,1)} %get-tuple-element.191.vt_ref, ...), custom_call_target="tpu_custom_call", output_to_operand_aliasing={{0}: (3, {}), {1}: (4, {})} | custom-call | flops 4294967296 | bytes 1048576 | tf_op jit(solution)/shard_map/attend/pallas_call | solution.py:253
  81.1 5.5 all-to-all-start.1
  88.5 24.6 %all-to-all-done.1.o_ref = bf16[8,256,256]{2,1,0:T(8,128)(2,1)S(1)} async-done(((bf16[8,256,256]{2,1,0:T(8,128)(2,1)}), bf16[8,256,256]{2,1,0:T(8,128)(2,1)S(1)}, u32[]{:S(2)}, u32[]{:S(2)}) %all-to-all-start.1) | async-done | bytes 1048608 | tf_op jit(solution)/shard_map/all_to_all | solution.py:969
  114.0 9.2 %out_project_and_norm.1 = (f32[256,2048]{1,0:T(8,128)}, bf16[256,2048]{1,0:T(8,128)(2,1)}) custom-call(s32[11]{0:T(128)} %pad_add_fusion.ids_ref, bf16[8,256,256]{2,1,0:T(8,128)(2,1)} %copy-done.5, bf16[2048,1024]{1,0:T(8,128)(2,1)} %constant_dynamic-update-slice_fusion.mine_ref, bf16[2048,1024]{1,0:T(8,128)(2,1)} %collective-permute-done.8.other_ref, ...), custom_call_target="tpu_custom_call" | custom-call | flops 2147483648 | bytes 8388608 | tf_op jit(solution)/shard_map/out_project_and_norm/pallas_call | solution.py:462
  125.4 12.2 %swiglu_rows.5 = (bf16[2048,2048]{1,0:T(8,128)(2,1)}, bf16[2048,2048]{1,0:T(8,128)(2,1)}, bf16[2048,1024]{1,0:T(8,128)(2,1)}, bf16[2048,1024]{1,0:T(8,128)(2,1)}...) custom-call(s32[11]{0:T(128)} %pad_add_fusion.ids_ref, bf16[256,2048]{1,0:T(8,128)(2,1)} %get-tuple-element.202.refs_0_, ...), custom_call_target="tpu_custom_call" | custom-call | flops 6442450944 | bytes 20971520 | tf_op jit(solution)/shard_map/swiglu_rows/pallas_call | solution.py:861
  137.6 10.3 %collective-permute-done.10.refs_1_ = bf16[256,2048]{1,0:T(8,128)(2,1)S(1)} collective-permute-done((bf16[256,2048]{1,0:T(8,128)(2,1)}, bf16[256,2048]{1,0:T(8,128)(2,1)S(1)}, u32[]{:S(2)}, u32[]{:S(2)}) %collective-permute-start.10) | collective-permute-done | bytes 1048608 | tf_op jit(solution)/shard_map/ppermute | solution.py:975
  150.1 18.4 %swiglu_rows.6 = (bf16[2048,2048]{1,0:T(8,128)(2,1)}, bf16[2048,2048]{1,0:T(8,128)(2,1)}, bf16[2048,1024]{1,0:T(8,128)(2,1)}, bf16[2048,1024]{1,0:T(8,128)(2,1)}...) custom-call(s32[11]{0:T(128)} %pad_add_fusion.ids_ref, ...), custom_call_target="tpu_custom_call", output_to_operand_aliasing={{0}: (7, {}), {1}: (8, {}), {2}: (9, {}), {3}: (10, {}), {4... | custom-call | flops 12884901888 | bytes 29360128 | tf_op jit(solution)/shard_map/swiglu_rows/pallas_call | solution.py:861
  168.5 4.1 collective-permute-done.11.refs_0_
  175.3 18.4 %swiglu_rows.7 = (bf16[2048,2048]{1,0:T(8,128)(2,1)}, bf16[2048,2048]{1,0:T(8,128)(2,1)}, bf16[2048,1024]{1,0:T(8,128)(2,1)}, bf16[2048,1024]{1,0:T(8,128)(2,1)}...) custom-call(s32[11]{0:T(128)} %pad_add_fusion.ids_ref, ...), custom_call_target="tpu_custom_call", output_to_operand_aliasing={{0}: (7, {}), {1}: (8, {}), {2}: (9, {}), {3}: (10, {}), {4... | custom-call | flops 12884901888 | bytes 29360128 | tf_op jit(solution)/shard_map/swiglu_rows/pallas_call | solution.py:861
  199.1 18.4 %swiglu_rows.8 = (bf16[2048,2048]{1,0:T(8,128)(2,1)}, bf16[2048,2048]{1,0:T(8,128)(2,1)}, bf16[2048,1024]{1,0:T(8,128)(2,1)}, bf16[2048,1024]{1,0:T(8,128)(2,1)}...) custom-call(s32[11]{0:T(128)} %pad_add_fusion.ids_ref, ...), custom_call_target="tpu_custom_call", output_to_operand_aliasing={{0}: (7, {}), {1}: (8, {}), {2}: (9, {}), {3}: (10, {}), {4... | custom-call | flops 12884901888 | bytes 29360128 | tf_op jit(solution)/shard_map/swiglu_rows/pallas_call | solution.py:861
  218.5 13.2 %swiglu_rows.9 = (bf16[2048,2048]{1,0:T(8,128)(2,1)}, bf16[2048,2048]{1,0:T(8,128)(2,1)}, bf16[2048,1024]{1,0:T(8,128)(2,1)}, bf16[2048,1024]{1,0:T(8,128)(2,1)}...) custom-call(s32[11]{0:T(128)} %pad_add_fusion.ids_ref, ...), custom_call_target="tpu_custom_call", output_to_operand_aliasing={{0}: (7, {}), {1}: (8, {}), {2}: (9, {}), {3}: (10, {}), {4... | custom-call | flops 6442450944 | bytes 20971520 | tf_op jit(solution)/shard_map/swiglu_rows/pallas_call | solution.py:861
  235.3 10.6 %convolution_convert_fusion.1.term_ref.own_ref = bf16[2048,2048]{1,0:T(8,128)(2,1)S(1)} fusion(bf16[2048,1024]{1,0:T(8,128)(2,1)} %get-tuple-element.256, bf16[1024,2048]{1,0:T(8,128)(2,1)S(1)} %copy-done.1), kind=kOutput, calls=%fused_computation.1 | convolution fusion | flops 8594128896 | bytes 16777216 | tf_op jit(solution)/shard_map/dot_general | solution.py:32
  245.9 3.3 copy-done
  251.2 2.9 ring_add.19
  255.8 2.9 ring_add.18
  259.0 14.1 %convolution_convert_fusion.2 = bf16[1024,2048]{1,0:T(8,128)(2,1)} fusion(bf16[2048,1024]{1,0:T(8,128)(2,1)} %get-tuple-element.256, bf16[2048,2048]{1,0:T(8,128)(2,1)} %get-tuple-element.263), kind=kOutput, calls=%fused_computation.5 | convolution fusion | flops 8592031744 | bytes 16777216 | tf_op jit(solution)/shard_map/dot_general | solution.py:32
  275.4 4.3 collective-permute-done.19.got_ref
  279.8 3.2 ring_add.21
  284.4 3.2 ring_add.20
  288.7 14.3 %convolution_convert_fusion.4 = bf16[2048,1024]{1,0:T(8,128)(2,1)} fusion(bf16[2048,2048]{1,0:T(8,128)(2,1)} %get-tuple-element.266, bf16[2048,1024]{1,0:T(8,128)(2,1)} %get-tuple-element.267), kind=kOutput, calls=%fused_computation.7 | convolution fusion | flops 8592031744 | bytes 16777216 | tf_op jit(solution)/shard_map/dot_general | solution.py:32
  303.0 4.6 collective-permute-done.21.got_ref
  307.6 3.1 ring_add.23
  311.6 3.1 ring_add.22
  315.9 14.1 %convolution_convert_fusion.3 = bf16[2048,1024]{1,0:T(8,128)(2,1)} fusion(bf16[2048,2048]{1,0:T(8,128)(2,1)} %get-tuple-element.266, bf16[2048,1024]{1,0:T(8,128)(2,1)} %get-tuple-element.270), kind=kOutput, calls=%fused_computation.6 | convolution fusion | flops 8592031744 | bytes 16777216 | tf_op jit(solution)/shard_map/dot_general | solution.py:32
  330.0 8.0 %collective-permute-done.23.up_ref = bf16[256,2048]{1,0:T(8,128)(2,1)S(1)} collective-permute-done((bf16[256,2048]{1,0:T(8,128)(2,1)}, bf16[256,2048]{1,0:T(8,128)(2,1)S(1)}, u32[]{:S(2)}, u32[]{:S(2)}) %collective-permute-start.23) | collective-permute-done | bytes 1048608 | tf_op jit(solution)/shard_map/ppermute | solution.py:972
  340.2 10.8 %norm_back_and_project.1 = (f32[256,2048]{1,0:T(8,128)}, bf16[256,2048]{1,0:T(8,128)(2,1)}, f32[1,2048]{1,0:T(1,128)}, bf16[8,256,256]{2,1,0:T(8,128)(2,1)}) custom-call(s32[11]{0:T(128)} %pad_add_fusion.ids_ref, bf16[256,2048]{1,0:T(8,128)(2,1)} %get-tuple-element.277.own_ref, bf16[256,2048]{1,0:T(8,128)(2,1)} %copy-done.19, bf16[256,2048]{1,0:T(8,128)(2,1)} %copy-done.17, ...), custom_call_target="tpu_custom_call" | custom-call | flops 2147483648 | bytes 8388608 | tf_op jit(solution)/shard_map/norm_back_and_project/pallas_call | solution.py:539
  352.9 4.1 all-to-all-start.2
  357.1 2.9 ring_add.25
  360.0 2.9 ring_add.24
  362.9 7.9 %out_weight_grad.1 = (bf16[2,2048,512]{2,1,0:T(8,128)(2,1)}, bf16[2,2048,512]{2,1,0:T(8,128)(2,1)}) custom-call(s32[11]{0:T(128)} %pad_add_fusion.ids_ref, bf16[8,256,256]{2,1,0:T(8,128)(2,1)} %copy-done.5, bf16[256,2048]{1,0:T(8,128)(2,1)} %get-tuple-element.284.da_ref), custom_call_target="tpu_custom_call" | custom-call | flops 2147483648 | bytes 8388608 | tf_op jit(solution)/shard_map/out_weight_grad/pallas_call | solution.py:638
  370.7 2.7 all-to-all-done.2
  378.3 17.7 %attend_back.2 = (bf16[1280,256]{1,0:T(8,128)(2,1)}, f32[2048,128]{1,0:T(8,128)}, f32[2048,128]{1,0:T(8,128)}) custom-call(bf16[2048,256]{1,0:T(8,128)(2,1)} %get-tuple-element.189.q_ref, bf16[2048,256]{1,0:T(8,128)(2,1)} %bitcast.42, bf16[2048,256]{1,0:T(8,128)(2,1)} %get-tuple-element.199.o_ref, f32[8,2048]{1,0:T(8,128)} %get-tuple-element.292.lse_ref, ...), custom_call_target="tpu_custom_call" | custom-call | flops 10737418240 | bytes 5242880 | tf_op jit(solution)/shard_map/attend_back/pallas_call | solution.py:397
  396.0 4.1 fusion.1
  402.5 3.1 ring_add.27
  406.7 3.1 ring_add.26
  415.2 23.2 %attend_back.3.grad_ref = bf16[2048,384]{1,0:T(8,128)(2,1)} custom-call(bf16[2048,256]{1,0:T(8,128)(2,1)} %get-tuple-element.189.q_ref, bf16[2048,256]{1,0:T(8,128)(2,1)} %bitcast.43, bf16[2048,256]{1,0:T(8,128)(2,1)} %get-tuple-element.199.o_ref, f32[8,2048]{1,0:T(8,128)} %get-tuple-element.292.lse_ref, bf16[2048,128]{1,0:T(8,128)(2,1)} %get-tuple-element.190.k_ref, ...), custom_call_target="tpu_custom_call" | custom-call | flops 10737418240 | bytes 5242880 | tf_op jit(solution)/shard_map/attend_back/pallas_call | solution.py:397
  438.4 2.9 convolution_convert_fusion.5
  441.3 3.1 ring_add.29
  445.5 3.1 ring_add.28
  453.9 6.8 %convolution_convert_fusion.term_ref.own_ref = bf16[2048,2048]{1,0:T(8,128)(2,1)} fusion(bf16[2048,384]{1,0:T(8,128)(2,1)S(1)} %copy-done.8, bf16[2048,128]{1,0:T(8,128)(2,1)S(1)} %bitcast.41, bf16[2048,256]{1,0:T(8,128)(2,1)S(1)} %copy-done.2), kind=kOutput, calls=%fused_computation | convolution fusion | flops 3228565504 | bytes 11534336 | tf_op jit(solution)/shard_map/dot_general | solution.py:32
  460.7 11.8 %projection_weight_grads.1 = (bf16[2,512,256]{2,1,0:T(8,128)(2,1)}, bf16[2,512,256]{2,1,0:T(8,128)(2,1)}, f32[2,512,256]{2,1,0:T(8,128)}, f32[2,512,256]{2,1,0:T(8,128)}) custom-call(s32[11]{0:T(128)} %pad_add_fusion.ids_ref, bf16[2048,2048]{1,0:T(8,128)(2,1)} %get-tuple-element.185.normed_ref, bf16[2048,384]{1,0:T(8,128)(2,1)} %attend_back.3.grad_ref, ...), custom_call_target="tpu_custom_call" | custom-call | flops 3221225472 | bytes 12582912 | tf_op jit(solution)/shard_map/projection_weight_grads/pallas_call | solution.py:698
  472.5 10.8 %collective-permute-done.32.got_ref = bf16[128,2048]{1,0:T(8,128)(2,1)} collective-permute-done((bf16[128,2048]{1,0:T(8,128)(2,1)}, bf16[128,2048]{1,0:T(8,128)(2,1)}, u32[]{:S(2)}, u32[]{:S(2)}) %collective-permute-start.32) | collective-permute-done | bytes 524320 | tf_op jit(solution)/shard_map/ppermute | solution.py:972
  483.4 2.9 ring_add.31
  487.2 2.9 ring_add.30
  495.2 16.2 %collective-permute-done.41 = bf16[512,256]{1,0:T(8,128)(2,1)S(1)} collective-permute-done((bf16[512,256]{1,0:T(8,128)(2,1)S(1)}, bf16[512,256]{1,0:T(8,128)(2,1)S(1)}, u32[]{:S(2)}, u32[]{:S(2)}) %collective-permute-start.41) | collective-permute-done | bytes 262176 | tf_op jit(solution)/shard_map/ppermute | solution.py:912
  512.1 3.6 collective-permute-done.36.got_ref
  515.7 5.1 fusion
  520.8 3.1 ring_add.33
  524.5 3.2 ring_add.32
  531.1 3.5 all-to-all-start.3
  534.6 4.4 layer_output.1
  539.0 26.2 %collective-permute-done.44.got_ref = bf16[256,2048]{1,0:T(8,128)(2,1)S(1)} collective-permute-done((bf16[256,2048]{1,0:T(8,128)(2,1)}, bf16[256,2048]{1,0:T(8,128)(2,1)S(1)}, u32[]{:S(2)}, u32[]{:S(2)}) %collective-permute-start.44) | collective-permute-done | bytes 1048608 | tf_op jit(solution)/shard_map/ppermute | solution.py:975
  565.1 3.0 collective-permute-done.43.got_ref
  568.1 3.2 ring_add.35
  572.7 3.1 ring_add.34
  585.0 18.2 %collective-permute-done.46.down_ref = bf16[256,2048]{1,0:T(8,128)(2,1)} collective-permute-done((bf16[256,2048]{1,0:T(8,128)(2,1)}, bf16[256,2048]{1,0:T(8,128)(2,1)}, u32[]{:S(2)}, u32[]{:S(2)}) %collective-permute-start.46) | collective-permute-done | bytes 1048608 | tf_op jit(solution)/shard_map/ppermute | solution.py:975
  603.2 6.7 %collective-permute-done.45.up_ref = bf16[256,2048]{1,0:T(8,128)(2,1)} collective-permute-done((bf16[256,2048]{1,0:T(8,128)(2,1)}, bf16[256,2048]{1,0:T(8,128)(2,1)}, u32[]{:S(2)}, u32[]{:S(2)}) %collective-permute-start.45) | collective-permute-done | bytes 1048608 | tf_op jit(solution)/shard_map/ppermute | solution.py:972
  609.9 5.9 input_grad.1
  (221 shorter events, 97.2 us)
Async XLA Ops:
  9.2 19.1 %collective-permute-start = (bf16[256,1024]{1,0:T(8,128)(2,1)S(1)}, bf16[256,1024]{1,0:T(8,128)(2,1)S(1)}, u32[]{:S(2)}, u32[]{:S(2)}) collective-permute-start(bf16[256,1024]{1,0:T(8,128)(2,1)S(1)} %get-tuple-element.350), channel_id=1, source_target_pairs={{0,1},{1,3},{3,5},{5,7},{7,6},{6,4},{4,2},{2,0},{8,9},{9,11},{11,1... | collective-permute-start | bytes 1572872 | tf_op jit(solution)/shard_map/ppermute | solution.py:972
  12.1 16.1 %collective-permute-start.1 = (bf16[256,1024]{1,0:T(8,128)(2,1)S(1)}, bf16[256,1024]{1,0:T(8,128)(2,1)S(1)}, u32[]{:S(2)}, u32[]{:S(2)}) collective-permute-start(bf16[256,1024]{1,0:T(8,128)(2,1)S(1)} %get-tuple-element.350), channel_id=1, source_target_pairs={{1,0},{3,1},{5,3},{7,5},{6,7},{4,6},{2,4},{0,2},{9,8},{11,9},{13,1... | collective-permute-start | bytes 1572872 | tf_op jit(solution)/shard_map/ppermute | solution.py:975
  14.2 24.8 %all-to-all-start = ((bf16[8,256,128]{2,1,0:T(8,128)(2,1)}), bf16[8,256,128]{2,1,0:T(8,128)(2,1)S(1)}, u32[]{:S(2)}, u32[]{:S(2)}) async-start(bf16[8,256,128]{2,1,0:T(8,128)(2,1)} %pick_heads.1), calls=%async_computation | async-start | bytes 1048576 | tf_op jit(solution)/shard_map/all_to_all | solution.py:969
  28.2 18.8 %collective-permute-start.2 = (bf16[256,1024]{1,0:T(8,128)(2,1)S(1)}, bf16[256,1024]{1,0:T(8,128)(2,1)S(1)}, u32[]{:S(2)}, u32[]{:S(2)}) collective-permute-start(bf16[256,1024]{1,0:T(8,128)(2,1)S(1)} %collective-permute-done), channel_id=1, source_target_pairs={{0,1},{1,3},{3,5},{5,7},{7,6},{6,4},{4,2},{2,0},{8,9},{9,11},{11,1... | collective-permute-start | bytes 1572872 | tf_op jit(solution)/shard_map/ppermute | solution.py:972
  30.3 16.7 %collective-permute-start.3 = (bf16[256,1024]{1,0:T(8,128)(2,1)S(1)}, bf16[256,1024]{1,0:T(8,128)(2,1)S(1)}, u32[]{:S(2)}, u32[]{:S(2)}) collective-permute-start(bf16[256,1024]{1,0:T(8,128)(2,1)S(1)} %collective-permute-done.1), channel_id=1, source_target_pairs={{1,0},{3,1},{5,3},{7,5},{6,7},{4,6},{2,4},{0,2},{9,8},{11,9},{13,1... | collective-permute-start | bytes 1572872 | tf_op jit(solution)/shard_map/ppermute | solution.py:975
  47.0 15.0 %collective-permute-start.4 = (bf16[256,1024]{1,0:T(8,128)(2,1)S(1)}, bf16[256,1024]{1,0:T(8,128)(2,1)S(1)}, u32[]{:S(2)}, u32[]{:S(2)}) collective-permute-start(bf16[256,1024]{1,0:T(8,128)(2,1)S(1)} %collective-permute-done.2), channel_id=1, source_target_pairs={{0,1},{1,3},{3,5},{5,7},{7,6},{6,4},{4,2},{2,0},{8,9},{9,11},{11,1... | collective-permute-start | bytes 1572872 | tf_op jit(solution)/shard_map/ppermute | solution.py:972
  49.8 12.6 %collective-permute-start.5 = (bf16[256,1024]{1,0:T(8,128)(2,1)S(1)}, bf16[256,1024]{1,0:T(8,128)(2,1)S(1)}, u32[]{:S(2)}, u32[]{:S(2)}) collective-permute-start(bf16[256,1024]{1,0:T(8,128)(2,1)S(1)} %collective-permute-done.3), channel_id=1, source_target_pairs={{1,0},{3,1},{5,3},{7,5},{6,7},{4,6},{2,4},{0,2},{9,8},{11,9},{13,1... | collective-permute-start | bytes 1572872 | tf_op jit(solution)/shard_map/ppermute | solution.py:975
  62.4 17.1 %collective-permute-start.6 = (bf16[128,1024]{1,0:T(8,128)(2,1)S(1)}, bf16[128,1024]{1,0:T(8,128)(2,1)S(1)}, u32[]{:S(2)}, u32[]{:S(2)}) collective-permute-start(bf16[128,1024]{1,0:T(8,128)(2,1)S(1)} %slice.88), channel_id=1, source_target_pairs={{0,1},{1,3},{3,5},{5,7},{7,6},{6,4},{4,2},{2,0},{8,9},{9,11},{11,1... | collective-permute-start | bytes 786440 | tf_op jit(solution)/shard_map/ppermute | solution.py:972
  64.3 15.3 %collective-permute-start.7 = (bf16[128,1024]{1,0:T(8,128)(2,1)S(1)}, bf16[128,1024]{1,0:T(8,128)(2,1)S(1)}, u32[]{:S(2)}, u32[]{:S(2)}) collective-permute-start(bf16[128,1024]{1,0:T(8,128)(2,1)S(1)} %slice.89), channel_id=1, source_target_pairs={{1,0},{3,1},{5,3},{7,5},{6,7},{4,6},{2,4},{0,2},{9,8},{11,9},{13,1... | collective-permute-start | bytes 786440 | tf_op jit(solution)/shard_map/ppermute | solution.py:975
  81.1 32.0 %collective-permute-start.8 = (bf16[2048,1024]{1,0:T(8,128)(2,1)}, bf16[2048,1024]{1,0:T(8,128)(2,1)}, u32[]{:S(2)}, u32[]{:S(2)}) collective-permute-start(bf16[2048,1024]{1,0:T(8,128)(2,1)} %constant_dynamic-update-slice_fusion.mine_ref), channel_id=1, source_target_pairs={{0,8},{8,0},{16,24},{24,16},{1,9},{9,1},{17,25},{25,17},{2,10},{10... | collective-permute-start | bytes 12582920 | tf_op jit(solution)/shard_map/ppermute | solution.py:1005
  81.1 32.0 %all-to-all-start.1 = ((bf16[8,256,256]{2,1,0:T(8,128)(2,1)}), bf16[8,256,256]{2,1,0:T(8,128)(2,1)S(1)}, u32[]{:S(2)}, u32[]{:S(2)}) async-start(bf16[8,256,256]{2,1,0:T(8,128)(2,1)} %bitcast.44), calls=%async_computation.1 | async-start | bytes 2097152 | tf_op jit(solution)/shard_map/all_to_all | solution.py:969
  86.6 315.9 %reduce-scatter.5.cloned.1.call-start = ((), (), s32[]{:S(2)}) async-start(), calls=%async_computation.8 | async-start | bytes 5242880 | tf_op jit(solution)/shard_map/reduce_scatter | solution.py:1073
  123.2 24.7 %collective-permute-start.10 = (bf16[256,2048]{1,0:T(8,128)(2,1)}, bf16[256,2048]{1,0:T(8,128)(2,1)S(1)}, u32[]{:S(2)}, u32[]{:S(2)}) collective-permute-start(bf16[256,2048]{1,0:T(8,128)(2,1)} %get-tuple-element.202.refs_0_), channel_id=1, source_target_pairs={{1,0},{3,1},{5,3},{7,5},{6,7},{4,6},{2,4},{0,2},{9,8},{11,9},{13,1... | collective-permute-start | bytes 3145736 | tf_op jit(solution)/shard_map/ppermute | solution.py:975
  123.2 24.9 %collective-permute-start.9 = (bf16[256,2048]{1,0:T(8,128)(2,1)}, bf16[256,2048]{1,0:T(8,128)(2,1)S(1)}, u32[]{:S(2)}, u32[]{:S(2)}) collective-permute-start(bf16[256,2048]{1,0:T(8,128)(2,1)} %get-tuple-element.202.refs_0_), channel_id=1, source_target_pairs={{0,1},{1,3},{3,5},{5,7},{7,6},{6,4},{4,2},{2,0},{8,9},{9,11},{11,1... | collective-permute-start | bytes 3145736 | tf_op jit(solution)/shard_map/ppermute | solution.py:972
  148.1 24.5 %collective-permute-start.11 = (bf16[256,2048]{1,0:T(8,128)(2,1)S(1)}, bf16[256,2048]{1,0:T(8,128)(2,1)S(1)}, u32[]{:S(2)}, u32[]{:S(2)}) collective-permute-start(bf16[256,2048]{1,0:T(8,128)(2,1)S(1)} %collective-permute-done.9.refs_0_), channel_id=1, source_target_pairs={{0,1},{1,3},{3,5},{5,7},{7,6},{6,4},{4,2},{2,0},{8,9},{9,11},{11,1... | collective-permute-start | bytes 3145736 | tf_op jit(solution)/shard_map/ppermute | solution.py:972
  149.8 23.0 %collective-permute-start.12 = (bf16[256,2048]{1,0:T(8,128)(2,1)S(1)}, bf16[256,2048]{1,0:T(8,128)(2,1)S(1)}, u32[]{:S(2)}, u32[]{:S(2)}) collective-permute-start(bf16[256,2048]{1,0:T(8,128)(2,1)S(1)} %collective-permute-done.10.refs_1_), channel_id=1, source_target_pairs={{1,0},{3,1},{5,3},{7,5},{6,7},{4,6},{2,4},{0,2},{9,8},{11,9},{13,1... | collective-permute-start | bytes 3145736 | tf_op jit(solution)/shard_map/ppermute | solution.py:975
  172.8 23.4 %collective-permute-start.13 = (bf16[256,2048]{1,0:T(8,128)(2,1)S(1)}, bf16[256,2048]{1,0:T(8,128)(2,1)S(1)}, u32[]{:S(2)}, u32[]{:S(2)}) collective-permute-start(bf16[256,2048]{1,0:T(8,128)(2,1)S(1)} %collective-permute-done.11.refs_0_), channel_id=1, source_target_pairs={{0,1},{1,3},{3,5},{5,7},{7,6},{6,4},{4,2},{2,0},{8,9},{9,11},{11,1... | collective-permute-start | bytes 3145736 | tf_op jit(solution)/shard_map/ppermute | solution.py:972
  174.3 22.5 %collective-permute-start.14 = (bf16[256,2048]{1,0:T(8,128)(2,1)S(1)}, bf16[256,2048]{1,0:T(8,128)(2,1)S(1)}, u32[]{:S(2)}, u32[]{:S(2)}) collective-permute-start(bf16[256,2048]{1,0:T(8,128)(2,1)S(1)} %collective-permute-done.12.refs_1_), channel_id=1, source_target_pairs={{1,0},{3,1},{5,3},{7,5},{6,7},{4,6},{2,4},{0,2},{9,8},{11,9},{13,1... | collective-permute-start | bytes 3145736 | tf_op jit(solution)/shard_map/ppermute | solution.py:975
  196.8 20.7 %collective-permute-start.15 = (bf16[128,2048]{1,0:T(8,128)(2,1)S(1)}, bf16[128,2048]{1,0:T(8,128)(2,1)S(1)}, u32[]{:S(2)}, u32[]{:S(2)}) collective-permute-start(bf16[128,2048]{1,0:T(8,128)(2,1)S(1)} %slice.90), channel_id=1, source_target_pairs={{0,1},{1,3},{3,5},{5,7},{7,6},{6,4},{4,2},{2,0},{8,9},{9,11},{11,1... | collective-permute-start | bytes 1572872 | tf_op jit(solution)/shard_map/ppermute | solution.py:972
  198.4 19.2 %collective-permute-start.16 = (bf16[128,2048]{1,0:T(8,128)(2,1)S(1)}, bf16[128,2048]{1,0:T(8,128)(2,1)S(1)}, u32[]{:S(2)}, u32[]{:S(2)}) collective-permute-start(bf16[128,2048]{1,0:T(8,128)(2,1)S(1)} %slice.91), channel_id=1, source_target_pairs={{1,0},{3,1},{5,3},{7,5},{6,7},{4,6},{2,4},{0,2},{9,8},{11,9},{13,1... | collective-permute-start | bytes 1572872 | tf_op jit(solution)/shard_map/ppermute | solution.py:975
  218.5 16.8 %copy-start.1 = (bf16[1024,2048]{1,0:T(8,128)(2,1)S(1)}, bf16[1024,2048]{1,0:T(8,128)(2,1)}, u32[]{:S(2)}) copy-start(bf16[1024,2048]{1,0:T(8,128)(2,1)} %refs_5_.7) | copy-start | bytes 12582916
  233.0 17.3 %collective-permute-start.17 = (bf16[128,2048]{1,0:T(8,128)(2,1)S(1)}, bf16[128,2048]{1,0:T(8,128)(2,1)S(1)}, u32[]{:S(2)}, u32[]{:S(2)}) collective-permute-start(bf16[128,2048]{1,0:T(8,128)(2,1)S(1)} %get-tuple-element.356), channel_id=1, source_target_pairs={{0,1},{1,3},{3,5},{5,7},{7,6},{6,4},{4,2},{2,0},{8,9},{9,11},{11,1... | collective-permute-start | bytes 1572872 | tf_op jit(solution)/shard_map/ppermute | solution.py:972
  234.7 15.7 %collective-permute-start.18 = (bf16[128,2048]{1,0:T(8,128)(2,1)S(1)}, bf16[128,2048]{1,0:T(8,128)(2,1)S(1)}, u32[]{:S(2)}, u32[]{:S(2)}) collective-permute-start(bf16[128,2048]{1,0:T(8,128)(2,1)S(1)} %get-tuple-element.355), channel_id=1, source_target_pairs={{1,0},{3,1},{5,3},{7,5},{6,7},{4,6},{2,4},{0,2},{9,8},{11,9},{13,1... | collective-permute-start | bytes 1572872 | tf_op jit(solution)/shard_map/ppermute | solution.py:975
  254.1 21.3 %collective-permute-start.20 = (bf16[256,2048]{1,0:T(8,128)(2,1)}, bf16[256,2048]{1,0:T(8,128)(2,1)S(1)}, u32[]{:S(2)}, u32[]{:S(2)}) collective-permute-start(bf16[256,2048]{1,0:T(8,128)(2,1)} %ring_add.19), channel_id=1, source_target_pairs={{1,0},{3,1},{5,3},{7,5},{6,7},{4,6},{2,4},{0,2},{9,8},{11,9},{13,1... | collective-permute-start | bytes 3145736 | tf_op jit(solution)/shard_map/ppermute | solution.py:975
  258.7 21.0 %collective-permute-start.19 = (bf16[256,2048]{1,0:T(8,128)(2,1)}, bf16[256,2048]{1,0:T(8,128)(2,1)S(1)}, u32[]{:S(2)}, u32[]{:S(2)}) collective-permute-start(bf16[256,2048]{1,0:T(8,128)(2,1)} %ring_add.18), channel_id=1, source_target_pairs={{0,1},{1,3},{3,5},{5,7},{7,6},{6,4},{4,2},{2,0},{8,9},{9,11},{11,1... | collective-permute-start | bytes 3145736 | tf_op jit(solution)/shard_map/ppermute | solution.py:972
  279.7 192.8 %reduce-scatter.7.cloned.1.call-start = ((), (), s32[]{:S(2)}) async-start(), calls=%async_computation.9 | async-start | bytes 5242880 | tf_op jit(solution)/shard_map/reduce_scatter | solution.py:1073
  282.9 20.1 %collective-permute-start.22 = (bf16[256,2048]{1,0:T(8,128)(2,1)}, bf16[256,2048]{1,0:T(8,128)(2,1)S(1)}, u32[]{:S(2)}, u32[]{:S(2)}) collective-permute-start(bf16[256,2048]{1,0:T(8,128)(2,1)} %ring_add.21), channel_id=1, source_target_pairs={{1,0},{3,1},{5,3},{7,5},{6,7},{4,6},{2,4},{0,2},{9,8},{11,9},{13,1... | collective-permute-start | bytes 3145736 | tf_op jit(solution)/shard_map/ppermute | solution.py:975
  287.5 20.1 %collective-permute-start.21 = (bf16[256,2048]{1,0:T(8,128)(2,1)}, bf16[256,2048]{1,0:T(8,128)(2,1)S(1)}, u32[]{:S(2)}, u32[]{:S(2)}) collective-permute-start(bf16[256,2048]{1,0:T(8,128)(2,1)} %ring_add.20), channel_id=1, source_target_pairs={{0,1},{1,3},{3,5},{5,7},{7,6},{6,4},{4,2},{2,0},{8,9},{9,11},{11,1... | collective-permute-start | bytes 3145736 | tf_op jit(solution)/shard_map/ppermute | solution.py:972
  310.8 19.3 %collective-permute-start.24 = (bf16[256,2048]{1,0:T(8,128)(2,1)}, bf16[256,2048]{1,0:T(8,128)(2,1)S(1)}, u32[]{:S(2)}, u32[]{:S(2)}) collective-permute-start(bf16[256,2048]{1,0:T(8,128)(2,1)} %ring_add.23), channel_id=1, source_target_pairs={{1,0},{3,1},{5,3},{7,5},{6,7},{4,6},{2,4},{0,2},{9,8},{11,9},{13,1... | collective-permute-start | bytes 3145736 | tf_op jit(solution)/shard_map/ppermute | solution.py:975
  314.7 23.3 %collective-permute-start.23 = (bf16[256,2048]{1,0:T(8,128)(2,1)}, bf16[256,2048]{1,0:T(8,128)(2,1)S(1)}, u32[]{:S(2)}, u32[]{:S(2)}) collective-permute-start(bf16[256,2048]{1,0:T(8,128)(2,1)} %ring_add.22), channel_id=1, source_target_pairs={{0,1},{1,3},{3,5},{5,7},{7,6},{6,4},{4,2},{2,0},{8,9},{9,11},{11,1... | collective-permute-start | bytes 3145736 | tf_op jit(solution)/shard_map/ppermute | solution.py:972
  330.0 10.2 %copy-start.17 = (bf16[256,2048]{1,0:T(8,128)(2,1)}, bf16[256,2048]{1,0:T(8,128)(2,1)S(1)}, u32[]{:S(2)}) copy-start(bf16[256,2048]{1,0:T(8,128)(2,1)S(1)} %collective-permute-done.24.down_ref) | copy-start | bytes 3145732
  338.1 12.9 %collective-permute-start.25 = (bf16[128,2048]{1,0:T(8,128)(2,1)}, bf16[128,2048]{1,0:T(8,128)(2,1)S(1)}, u32[]{:S(2)}, u32[]{:S(2)}) collective-permute-start(bf16[128,2048]{1,0:T(8,128)(2,1)} %get-tuple-element.275), channel_id=1, source_target_pairs={{0,1},{1,3},{3,5},{5,7},{7,6},{6,4},{4,2},{2,0},{8,9},{9,11},{11,1... | collective-permute-start | bytes 1572872 | tf_op jit(solution)/shard_map/ppermute | solution.py:972
  339.3 12.9 %collective-permute-start.26 = (bf16[128,2048]{1,0:T(8,128)(2,1)}, bf16[128,2048]{1,0:T(8,128)(2,1)S(1)}, u32[]{:S(2)}, u32[]{:S(2)}) collective-permute-start(bf16[128,2048]{1,0:T(8,128)(2,1)} %get-tuple-element.276), channel_id=1, source_target_pairs={{1,0},{3,1},{5,3},{7,5},{6,7},{4,6},{2,4},{0,2},{9,8},{11,9},{13,1... | collective-permute-start | bytes 1572872 | tf_op jit(solution)/shard_map/ppermute | solution.py:975
  352.9 20.5 %all-to-all-start.2 = ((bf16[8,256,256]{2,1,0:T(8,128)(2,1)}), bf16[8,256,256]{2,1,0:T(8,128)(2,1)S(1)}, u32[]{:S(2)}, u32[]{:S(2)}) async-start(bf16[8,256,256]{2,1,0:T(8,128)(2,1)} %get-tuple-element.283), calls=%async_computation.2 | async-start | bytes 2097152 | tf_op jit(solution)/shard_map/all_to_all | solution.py:969
  357.0 182.0 %reduce-scatter.9.cloned.1.call-start = ((), (), s32[]{:S(2)}) async-start(), calls=%async_computation.10 | async-start | bytes 5242880 | tf_op jit(solution)/shard_map/reduce_scatter | solution.py:1073
  362.9 10.6 %copy-start.40 = (s32[1,8]{1,0:T(1,128)S(1)}, s32[1,8]{1,0:T(1,128)}, u32[]{:S(2)}) copy-start(s32[1,8]{1,0:T(1,128)} %get-tuple-element.359) | copy-start | bytes 100
  362.9 12.0 %copy-start.38 = (f32[2048]{0:T(1024)S(1)}, f32[2048]{0:T(1024)}, u32[]{:S(2)}) copy-start(f32[2048]{0:T(1024)} %param.16) | copy-start | bytes 24580
  373.4 22.6 %collective-permute-start.29 = (bf16[2,2048,512]{2,1,0:T(8,128)(2,1)}, bf16[2,2048,512]{2,1,0:T(8,128)(2,1)}, u32[]{:S(2)}, u32[]{:S(2)}) collective-permute-start(bf16[2,2048,512]{2,1,0:T(8,128)(2,1)} %get-tuple-element.300), channel_id=1, source_target_pairs={{0,8},{8,0},{16,24},{24,16},{1,9},{9,1},{17,25},{25,17},{2,10},{10... | collective-permute-start | bytes 12582920 | tf_op jit(solution)/shard_map/ppermute | solution.py:899
  373.4 242.3 %reduce-scatter.11.cloned.1.call-start = ((), (), s32[]{:S(2)}) async-start(), calls=%async_computation.11 | async-start | bytes 2359296 | tf_op jit(solution)/shard_map/reduce_scatter | solution.py:1127
  376.2 25.5 %collective-permute-start.27 = (bf16[256,2048]{1,0:T(8,128)(2,1)S(1)}, bf16[256,2048]{1,0:T(8,128)(2,1)}, u32[]{:S(2)}, u32[]{:S(2)}) collective-permute-start(bf16[256,2048]{1,0:T(8,128)(2,1)S(1)} %copy-done.13), channel_id=1, source_target_pairs={{0,1},{1,3},{3,5},{5,7},{7,6},{6,4},{4,2},{2,0},{8,9},{9,11},{11,1... | collective-permute-start | bytes 3145736 | tf_op jit(solution)/shard_map/ppermute | solution.py:972
  377.2 25.2 %collective-permute-start.28 = (bf16[256,2048]{1,0:T(8,128)(2,1)S(1)}, bf16[256,2048]{1,0:T(8,128)(2,1)}, u32[]{:S(2)}, u32[]{:S(2)}) collective-permute-start(bf16[256,2048]{1,0:T(8,128)(2,1)S(1)} %copy-done.12), channel_id=1, source_target_pairs={{1,0},{3,1},{5,3},{7,5},{6,7},{4,6},{2,4},{0,2},{9,8},{11,9},{13,1... | collective-permute-start | bytes 3145736 | tf_op jit(solution)/shard_map/ppermute | solution.py:975
  405.6 6.7 %copy-start.39 = (f32[1,2048]{1,0:T(1,128)S(1)}, f32[1,2048]{1,0:T(1,128)}, u32[]{:S(2)}) copy-start(f32[1,2048]{1,0:T(1,128)} %get-tuple-element.312) | copy-start | bytes 24580
  405.6 32.8 %collective-permute-start.31 = (bf16[256,2048]{1,0:T(8,128)(2,1)}, bf16[256,2048]{1,0:T(8,128)(2,1)S(1)}, u32[]{:S(2)}, u32[]{:S(2)}) collective-permute-start(bf16[256,2048]{1,0:T(8,128)(2,1)} %ring_add.27), channel_id=1, source_target_pairs={{1,0},{3,1},{5,3},{7,5},{6,7},{4,6},{2,4},{0,2},{9,8},{11,9},{13,1... | collective-permute-start | bytes 3145736 | tf_op jit(solution)/shard_map/ppermute | solution.py:975
  409.8 28.6 %collective-permute-start.30 = (bf16[256,2048]{1,0:T(8,128)(2,1)}, bf16[256,2048]{1,0:T(8,128)(2,1)}, u32[]{:S(2)}, u32[]{:S(2)}) collective-permute-start(bf16[256,2048]{1,0:T(8,128)(2,1)} %ring_add.26), channel_id=1, source_target_pairs={{0,1},{1,3},{3,5},{5,7},{7,6},{6,4},{4,2},{2,0},{8,9},{9,11},{11,1... | collective-permute-start | bytes 3145736 | tf_op jit(solution)/shard_map/ppermute | solution.py:972
  413.7 81.5 %collective-permute-start.42 = (bf16[2048,512]{1,0:T(8,128)(2,1)}, bf16[2048,512]{1,0:T(8,128)(2,1)}, u32[]{:S(2)}, u32[]{:S(2)}) collective-permute-start(bf16[2048,512]{1,0:T(8,128)(2,1)} %fusion.1), channel_id=1, source_target_pairs={{0,16},{8,24},{16,0},{24,8},{1,17},{9,25},{17,1},{25,9},{2,18},{10... | collective-permute-start | bytes 6291464 | tf_op jit(solution)/shard_map/ppermute | solution.py:912
  444.4 9.4 %copy-start.8 = (bf16[2048,384]{1,0:T(8,128)(2,1)S(1)}, bf16[2048,384]{1,0:T(8,128)(2,1)}, u32[]{:S(2)}) copy-start(bf16[2048,384]{1,0:T(8,128)(2,1)} %attend_back.3.grad_ref) | copy-start | bytes 4718596
  444.4 38.9 %collective-permute-start.35 = (bf16[256,2048]{1,0:T(8,128)(2,1)}, bf16[256,2048]{1,0:T(8,128)(2,1)}, u32[]{:S(2)}, u32[]{:S(2)}) collective-permute-start(bf16[256,2048]{1,0:T(8,128)(2,1)} %ring_add.29), channel_id=1, source_target_pairs={{1,0},{3,1},{5,3},{7,5},{6,7},{4,6},{2,4},{0,2},{9,8},{11,9},{13,1... | collective-permute-start | bytes 3145736 | tf_op jit(solution)/shard_map/ppermute | solution.py:975
  448.6 34.8 %collective-permute-start.34 = (bf16[256,2048]{1,0:T(8,128)(2,1)}, bf16[256,2048]{1,0:T(8,128)(2,1)}, u32[]{:S(2)}, u32[]{:S(2)}) collective-permute-start(bf16[256,2048]{1,0:T(8,128)(2,1)} %ring_add.28), channel_id=1, source_target_pairs={{0,1},{1,3},{3,5},{5,7},{7,6},{6,4},{4,2},{2,0},{8,9},{9,11},{11,1... | collective-permute-start | bytes 3145736 | tf_op jit(solution)/shard_map/ppermute | solution.py:972
  451.9 31.5 %collective-permute-start.32 = (bf16[128,2048]{1,0:T(8,128)(2,1)}, bf16[128,2048]{1,0:T(8,128)(2,1)}, u32[]{:S(2)}, u32[]{:S(2)}) collective-permute-start(bf16[128,2048]{1,0:T(8,128)(2,1)} %get-tuple-element.354), channel_id=1, source_target_pairs={{0,1},{1,3},{3,5},{5,7},{7,6},{6,4},{4,2},{2,0},{8,9},{9,11},{11,1... | collective-permute-start | bytes 1572872 | tf_op jit(solution)/shard_map/ppermute | solution.py:972
  452.2 31.1 %collective-permute-start.33 = (bf16[128,2048]{1,0:T(8,128)(2,1)}, bf16[128,2048]{1,0:T(8,128)(2,1)}, u32[]{:S(2)}, u32[]{:S(2)}) collective-permute-start(bf16[128,2048]{1,0:T(8,128)(2,1)} %get-tuple-element.353), channel_id=1, source_target_pairs={{1,0},{3,1},{5,3},{7,5},{6,7},{4,6},{2,4},{0,2},{9,8},{11,9},{13,1... | collective-permute-start | bytes 1572872 | tf_op jit(solution)/shard_map/ppermute | solution.py:975
  483.4 7.9 %collective-permute-start.38 = (f32[2,512,256]{2,1,0:T(8,128)}, f32[2,512,256]{2,1,0:T(8,128)S(1)}, u32[]{:S(2)}, u32[]{:S(2)}) collective-permute-start(f32[2,512,256]{2,1,0:T(8,128)} %get-tuple-element.320), channel_id=1, source_target_pairs={{0,8},{8,0},{16,24},{24,16},{1,9},{9,1},{17,25},{25,17},{2,10},{10... | collective-permute-start | bytes 3145736 | tf_op jit(solution)/shard_map/ppermute | solution.py:899
  486.3 25.8 %collective-permute-start.37 = (bf16[256,2048]{1,0:T(8,128)(2,1)}, bf16[256,2048]{1,0:T(8,128)(2,1)S(1)}, u32[]{:S(2)}, u32[]{:S(2)}) collective-permute-start(bf16[256,2048]{1,0:T(8,128)(2,1)} %ring_add.31), channel_id=1, source_target_pairs={{1,0},{3,1},{5,3},{7,5},{6,7},{4,6},{2,4},{0,2},{9,8},{11,9},{13,1... | collective-permute-start | bytes 3145736 | tf_op jit(solution)/shard_map/ppermute | solution.py:975
  490.1 25.6 %collective-permute-start.36 = (bf16[256,2048]{1,0:T(8,128)(2,1)}, bf16[256,2048]{1,0:T(8,128)(2,1)}, u32[]{:S(2)}, u32[]{:S(2)}) collective-permute-start(bf16[256,2048]{1,0:T(8,128)(2,1)} %ring_add.30), channel_id=1, source_target_pairs={{0,1},{1,3},{3,5},{5,7},{7,6},{6,4},{4,2},{2,0},{8,9},{9,11},{11,1... | collective-permute-start | bytes 3145736 | tf_op jit(solution)/shard_map/ppermute | solution.py:972
  491.3 2.1 collective-permute-start.40
  491.4 24.3 %collective-permute-start.39 = (f32[512,256]{1,0:T(8,128)S(1)}, f32[512,256]{1,0:T(8,128)}, u32[]{:S(2)}, u32[]{:S(2)}) collective-permute-start(f32[512,256]{1,0:T(8,128)S(1)} %fusion.2), channel_id=1, source_target_pairs={{0,16},{8,24},{16,0},{24,8},{1,17},{9,25},{17,1},{25,9},{2,18},{10... | collective-permute-start | bytes 1572872 | tf_op jit(solution)/shard_map/ppermute | solution.py:912
  493.4 18.7 %copy-start.30 = (bf16[2,512,256]{2,1,0:T(8,128)(2,1)}, bf16[2,512,256]{2,1,0:T(8,128)(2,1)S(1)}, u32[]{:S(2)}) copy-start(bf16[2,512,256]{2,1,0:T(8,128)(2,1)S(1)} %collective-permute-done.40) | copy-start | bytes 1572868
  494.6 16.8 %collective-permute-start.41 = (bf16[512,256]{1,0:T(8,128)(2,1)S(1)}, bf16[512,256]{1,0:T(8,128)(2,1)S(1)}, u32[]{:S(2)}, u32[]{:S(2)}) collective-permute-start(bf16[512,256]{1,0:T(8,128)(2,1)S(1)} %fusion.3), channel_id=1, source_target_pairs={{0,16},{8,24},{16,0},{24,8},{1,17},{9,25},{17,1},{25,9},{2,18},{10... | collective-permute-start | bytes 786440 | tf_op jit(solution)/shard_map/ppermute | solution.py:912
  512.1 8.6 %copy-start.26 = (bf16[256,2048]{1,0:T(8,128)(2,1)}, bf16[256,2048]{1,0:T(8,128)(2,1)S(1)}, u32[]{:S(2)}) copy-start(bf16[256,2048]{1,0:T(8,128)(2,1)S(1)} %collective-permute-done.37.got_ref) | copy-start | bytes 3145732
  523.9 41.3 %collective-permute-start.44 = (bf16[256,2048]{1,0:T(8,128)(2,1)}, bf16[256,2048]{1,0:T(8,128)(2,1)S(1)}, u32[]{:S(2)}, u32[]{:S(2)}) collective-permute-start(bf16[256,2048]{1,0:T(8,128)(2,1)} %ring_add.33), channel_id=1, source_target_pairs={{1,0},{3,1},{5,3},{7,5},{6,7},{4,6},{2,4},{0,2},{9,8},{11,9},{13,1... | collective-permute-start | bytes 3145736 | tf_op jit(solution)/shard_map/ppermute | solution.py:975
  527.7 40.5 %collective-permute-start.43 = (bf16[256,2048]{1,0:T(8,128)(2,1)}, bf16[256,2048]{1,0:T(8,128)(2,1)}, u32[]{:S(2)}, u32[]{:S(2)}) collective-permute-start(bf16[256,2048]{1,0:T(8,128)(2,1)} %ring_add.32), channel_id=1, source_target_pairs={{0,1},{1,3},{3,5},{5,7},{7,6},{6,4},{4,2},{2,0},{8,9},{9,11},{11,1... | collective-permute-start | bytes 3145736 | tf_op jit(solution)/shard_map/ppermute | solution.py:972
  531.1 49.6 %all-to-all-start.3 = ((f32[8,64,256]{2,1,0:T(8,128)}), f32[8,64,256]{2,1,0:T(8,128)S(1)}, u32[]{:S(2)}, u32[]{:S(2)}) async-start(f32[8,64,256]{2,1,0:T(8,128)} %bitcast.15), calls=%async_computation.6 | async-start | bytes 1048576 | tf_op jit(solution)/shard_map/all_to_all | solution.py:969
  571.3 6.9 %copy-start.10 = (bf16[512,1024]{1,0:T(8,128)(2,1)S(1)}, bf16[512,1024]{1,0:T(8,128)(2,1)}, u32[]{:S(2)}) copy-start(bf16[512,1024]{1,0:T(8,128)(2,1)} %reduce-scatter.7.cloned.1.call-done) | copy-start | bytes 3145732
  571.3 31.8 %collective-permute-start.46 = (bf16[256,2048]{1,0:T(8,128)(2,1)}, bf16[256,2048]{1,0:T(8,128)(2,1)}, u32[]{:S(2)}, u32[]{:S(2)}) collective-permute-start(bf16[256,2048]{1,0:T(8,128)(2,1)} %ring_add.35), channel_id=1, source_target_pairs={{1,0},{3,1},{5,3},{7,5},{6,7},{4,6},{2,4},{0,2},{9,8},{11,9},{13,1... | collective-permute-start | bytes 3145736 | tf_op jit(solution)/shard_map/ppermute | solution.py:975
  575.8 34.0 %collective-permute-start.45 = (bf16[256,2048]{1,0:T(8,128)(2,1)}, bf16[256,2048]{1,0:T(8,128)(2,1)}, u32[]{:S(2)}, u32[]{:S(2)}) collective-permute-start(bf16[256,2048]{1,0:T(8,128)(2,1)} %ring_add.34), channel_id=1, source_target_pairs={{0,1},{1,3},{3,5},{5,7},{7,6},{6,4},{4,2},{2,0},{8,9},{9,11},{11,1... | collective-permute-start | bytes 3145736 | tf_op jit(solution)/shard_map/ppermute | solution.py:972
  (32 other events, 104.1 us)
Sparse Core Ops, SparseCore 0:
  279.8 43.5 reduce-scatter.4
  326.1 44.5 reduce-scatter.6
  373.6 44.8 reduce-scatter.8
  520.9 83.9 reduce-scatter.10

commit v5 on v4

--- a/solution.py
+++ b/solution.py
@@ -894,22 +894,18 @@
     return lax.optimization_barrier(values)
 
 
-def over_cores(send, keep):
-    chips = send.shape[0]
-    got = lax.ppermute(send, "dp", [(i, i ^ 1) for i in range(2 * chips)])
-    go = [
-        (keep[step].astype(f32) + got[step].astype(f32)).astype(send.dtype)
-        for step in range(1, chips)
-    ]
-    return keep, got, go
-
-
-def over_chips(keep, got, go):
-    chips = len(go) + 1
+def other_core(array):
+    replicas = lax.axis_size("dp")
+    return lax.ppermute(array, "dp", [(i, i ^ 1) for i in range(replicas)])
+
+
+def over_chips(keep, got):
+    chips = keep.shape[0]
     arriving = []
     for step in range(1, chips):
         to = [(i, ((i // 2 + step) % chips) * 2 + i % 2) for i in range(2 * chips)]
-        arriving.append(lax.ppermute(go[step - 1], "dp", to))
+        go = (keep[step].astype(f32) + got[step].astype(f32)).astype(keep.dtype)
+        arriving.append(lax.ppermute(go, "dp", to))
     return keep, got, arriving
 
 
@@ -1086,21 +1082,22 @@
     out_sums = hop_sums(mlp, 2 * half_way - 4, out_got)
     do, out_parts, out_sums = tie(do, out_parts, out_sums)
     out_got = send_on(out_sums)
-    out_parts = over_cores(*out_parts)
+    out_send, out_keep = out_parts
+    out_swapped = other_core(out_send)
     operands = [queries, do, attended, lse, keys, keys_t, values, table]
     carried = attend_back(0, *operands, [])
-    out_got, carried, down_wgrad, out_parts = tie(out_got, carried, down_wgrad, out_parts)
-    out_terms = over_chips(*out_parts)
+    out_got, carried, down_wgrad, out_swapped = tie(out_got, carried, down_wgrad, out_swapped)
     for d in range(half_way - 2, 1, -1):
         out_got = next_hop(mlp, 2 * d - 2, out_got)
     qkv_grad = attend_back(1, *operands, carried)
-    out_got, qkv_grad = tie(out_got, qkv_grad)
+    out_got, qkv_grad, out_keep = tie(out_got, qkv_grad, out_keep)
 
     far = lax.dynamic_slice_in_dim(qkv_grad, ids[RING + groups - 1] * share, share, 0)
     far = mm(far, w_qkv, NT).astype(bf16)
     in_got = first_hop(far)
-    qkv_grad, far, out_got = tie(qkv_grad, far, out_got)
+    qkv_grad, far, out_got, out_keep = tie(qkv_grad, far, out_got, out_keep)
     out_got = next_hop(mlp, 0, out_got)
+    out_terms = over_chips(out_keep, out_swapped)
     first_grad = mm(qkv_grad, w_qkv, NT).astype(bf16)
     q_send, q_keep, s_send, s_keep = qkv_wgrad_parts(
         ids,
@@ -1114,14 +1111,13 @@
     in_got, out_got, q_send, s_send, gate_wgrad, first_grad = tie(
         in_got, out_got, q_send, s_send, gate_wgrad, first_grad
     )
-    small = over_cores(s_send, s_keep)
-    query_wgrad = over_cores(q_send, q_keep)
+    s_swapped, q_swapped = other_core(s_send), other_core(q_send)
     for d in range(half_way - 1, 0, -1):
         in_sums = natural_sums(first_grad, d, in_got)
         if d == half_way - 1:
             in_got = send_on(in_sums)
-            small = over_chips(*small)
-            query_wgrad = over_chips(*query_wgrad)
+            small = over_chips(s_keep, s_swapped)
+            query_wgrad = over_chips(q_keep, q_swapped)
             in_got, small, query_wgrad, out_terms = tie(in_got, small, query_wgrad, out_terms)
             out_wgrad = total_of(*out_terms).astype(bf16)
             out_wgrad = lax.psum_scatter(out_wgrad, "tensor", scatter_dimension=0, tiled=True)

time: 634 us -> 631 us (level)
    unnamed x90 -> x92, local copies, waits for them, and re-layouts: 15.6 us -> 15.5 us
  transfers between devices with their start and end apart: 55 -> 55, of which waited for: 26 -> 23; matrix products, arithmetic and copies ran while one was open for 16% -> 16% of each run, Pallas kernels for 40% -> 40%
where the time goes in v5:
time: 631 us; the launch traced here: 621 us
  Pallas kernels  273 us (43%)
  waiting for transfers between devices  151 us (24%)
  starting transfers between devices  68.1 us (11%)
  matrix products  62.7 us (10%)
  local copies, waits for them, and re-layouts  26.9 us (4%)
  other arithmetic  23.5 us (4%)
  between operations  15.8 us (3%)
    pallas_call x5, Pallas kernels, swiglu(): pl.pallas_call(functools.partial(swiglu_kernel, len(pieces), tuple(member...  80.5 us
    dot_general x6, matrix products, mm(): return lax.dot_general(left, right, dims, preferred_element_type=f32)  62.7 us
    ppermute x20, waiting for transfers between devices, back(): return lax.ppermute(array, 'tensor', behind)  57.6 us
    pallas_call x18, Pallas kernels, ring_add(): pl.pallas_call(functools.partial(ring_add_kernel, first), grid_spec=pltpu...  55.2 us
    ppermute x20, waiting for transfers between devices, onward(): return lax.ppermute(array, 'tensor', ahead)  45 us
    pallas_call x2, Pallas kernels, attend_back(): pl.pallas_call(functools.partial(attend_back_kernel, heads, start), grid=...  41 us
    ppermute x20, starting transfers between devices, onward(): return lax.ppermute(array, 'tensor', ahead)  27.9 us
    all_to_all x4, waiting for transfers between devices, exchange(): return lax.all_to_all(array, 'tensor', 0, 0, tiled=True)  27.2 us
  transfers between devices with their start and end apart: 55, of which 23 were waited for; matrix products, arithmetic and copies ran while one was open for 16% of the time, Pallas kernels for 40%

profile of v5, /device:TPU:0, one launch (start us, length us, event | category | flops | bytes accessed | tf_op | source)
XLA Modules:
  0.0 621.2 jit_solution(13034856389448513356)
XLA Ops:
  9.2 3.0 collective-permute-start
  14.2 6.3 %all-to-all-start = ((bf16[8,256,128]{2,1,0:T(8,128)(2,1)}), bf16[8,256,128]{2,1,0:T(8,128)(2,1)S(1)}, u32[]{:S(2)}, u32[]{:S(2)}) async-start(bf16[8,256,128]{2,1,0:T(8,128)(2,1)} %pick_heads.1), calls=%async_computation | async-start | bytes 1048576 | tf_op jit(solution)/shard_map/all_to_all | solution.py:965
  21.9 6.3 %norm_and_query.2 = (bf16[2048,2048]{1,0:T(8,128)(2,1)}, bf16[2048,256]{1,0:T(8,128)(2,1)}) custom-call(bf16[2048,2048]{1,0:T(8,128)(2,1)} %rows_ref.7, f32[1,2048]{1,0:T(1,128)} %bitcast.45, bf16[2048,256]{1,0:T(8,128)(2,1)} %wq_ref.3, f32[320,256]{1,0:T(8,128)} %pad_maximum_fusion.1.table_ref), custom_call_target="tpu_custom_call" | custom-call | flops 1073741824 | bytes 12582912 | tf_op jit(solution)/shard_map/norm_and_query/pallas_call | solution.py:105
  31.0 6.3 %norm_and_query.3 = (bf16[2048,2048]{1,0:T(8,128)(2,1)}, bf16[2048,256]{1,0:T(8,128)(2,1)}) custom-call(bf16[2048,2048]{1,0:T(8,128)(2,1)} %rows_ref.7, f32[1,2048]{1,0:T(1,128)} %bitcast.46, bf16[2048,256]{1,0:T(8,128)(2,1)} %wq_ref.3, f32[320,256]{1,0:T(8,128)} %pad_maximum_fusion.1.table_ref, ...), custom_call_target="tpu_custom_call", output_to_operand_aliasing={{0}: (4, {}), {1}: (5, {})} | custom-call | flops 1073741824 | bytes 12582912 | tf_op jit(solution)/shard_map/norm_and_query/pallas_call | solution.py:105
  39.8 7.2 %keys_and_values.1 = (bf16[2048,128]{1,0:T(8,128)(2,1)}, bf16[128,2048]{1,0:T(8,128)(2,1)}, bf16[2048,128]{1,0:T(8,128)(2,1)}, bf16[128,2048]{1,0:T(8,128)(2,1)}) custom-call(s32[1]{0:T(128)S(6)} %copy.94.length_ref, bf16[2048,2048]{1,0:T(8,128)(2,1)} %get-tuple-element.185.normed_ref, bf16[2048,128]{1,0:T(8,128)(2,1)} %bitcast.38, ...), custom_call_target="tpu_custom_call" | custom-call | flops 1073741824 | bytes 8388608 | tf_op jit(solution)/shard_map/keys_and_values/pallas_call | solution.py:147
  50.7 11.3 %attend.2 = (bf16[2048,256]{1,0:T(8,128)(2,1)}, f32[8,2048]{1,0:T(8,128)}) custom-call(bf16[2048,256]{1,0:T(8,128)(2,1)} %get-tuple-element.189.q_ref, bf16[2048,128]{1,0:T(8,128)(2,1)} %get-tuple-element.190.k_ref, bf16[128,2048]{1,0:T(8,128)(2,1)} %get-tuple-element.191.vt_ref), custom_call_target="tpu_custom_call" | custom-call | flops 4294967296 | bytes 1048576 | tf_op jit(solution)/shard_map/attend/pallas_call | solution.py:253
  64.6 13.3 %attend.3 = (bf16[2048,256]{1,0:T(8,128)(2,1)}, f32[8,2048]{1,0:T(8,128)}) custom-call(bf16[2048,256]{1,0:T(8,128)(2,1)} %get-tuple-element.189.q_ref, bf16[2048,128]{1,0:T(8,128)(2,1)} %get-tuple-element.190.k_ref, bf16[128,2048]{1,0:T(8,128)(2,1)} %get-tuple-element.191.vt_ref, ...), custom_call_target="tpu_custom_call", output_to_operand_aliasing={{0}: (3, {}), {1}: (4, {})} | custom-call | flops 4294967296 | bytes 1048576 | tf_op jit(solution)/shard_map/attend/pallas_call | solution.py:253
  81.0 5.5 all-to-all-start.1
  88.4 24.5 %all-to-all-done.1.o_ref = bf16[8,256,256]{2,1,0:T(8,128)(2,1)S(1)} async-done(((bf16[8,256,256]{2,1,0:T(8,128)(2,1)}), bf16[8,256,256]{2,1,0:T(8,128)(2,1)S(1)}, u32[]{:S(2)}, u32[]{:S(2)}) %all-to-all-start.1) | async-done | bytes 1048608 | tf_op jit(solution)/shard_map/all_to_all | solution.py:965
  113.9 9.2 %out_project_and_norm.1 = (f32[256,2048]{1,0:T(8,128)}, bf16[256,2048]{1,0:T(8,128)(2,1)}) custom-call(s32[11]{0:T(128)} %pad_add_fusion.ids_ref, bf16[8,256,256]{2,1,0:T(8,128)(2,1)} %copy-done.5, bf16[2048,1024]{1,0:T(8,128)(2,1)} %constant_dynamic-update-slice_fusion.mine_ref, bf16[2048,1024]{1,0:T(8,128)(2,1)} %collective-permute-done.8.other_ref, ...), custom_call_target="tpu_custom_call" | custom-call | flops 2147483648 | bytes 8388608 | tf_op jit(solution)/shard_map/out_project_and_norm/pallas_call | solution.py:462
  125.3 12.2 %swiglu_rows.5 = (bf16[2048,2048]{1,0:T(8,128)(2,1)}, bf16[2048,2048]{1,0:T(8,128)(2,1)}, bf16[2048,1024]{1,0:T(8,128)(2,1)}, bf16[2048,1024]{1,0:T(8,128)(2,1)}...) custom-call(s32[11]{0:T(128)} %pad_add_fusion.ids_ref, bf16[256,2048]{1,0:T(8,128)(2,1)} %get-tuple-element.202.refs_0_, ...), custom_call_target="tpu_custom_call" | custom-call | flops 6442450944 | bytes 20971520 | tf_op jit(solution)/shard_map/swiglu_rows/pallas_call | solution.py:861
  137.5 10.3 %collective-permute-done.10.refs_1_ = bf16[256,2048]{1,0:T(8,128)(2,1)S(1)} collective-permute-done((bf16[256,2048]{1,0:T(8,128)(2,1)}, bf16[256,2048]{1,0:T(8,128)(2,1)S(1)}, u32[]{:S(2)}, u32[]{:S(2)}) %collective-permute-start.10) | collective-permute-done | bytes 1048608 | tf_op jit(solution)/shard_map/ppermute | solution.py:971
  150.0 18.4 %swiglu_rows.6 = (bf16[2048,2048]{1,0:T(8,128)(2,1)}, bf16[2048,2048]{1,0:T(8,128)(2,1)}, bf16[2048,1024]{1,0:T(8,128)(2,1)}, bf16[2048,1024]{1,0:T(8,128)(2,1)}...) custom-call(s32[11]{0:T(128)} %pad_add_fusion.ids_ref, ...), custom_call_target="tpu_custom_call", output_to_operand_aliasing={{0}: (7, {}), {1}: (8, {}), {2}: (9, {}), {3}: (10, {}), {4... | custom-call | flops 12884901888 | bytes 29360128 | tf_op jit(solution)/shard_map/swiglu_rows/pallas_call | solution.py:861
  168.4 4.1 collective-permute-done.11.refs_0_
  175.1 18.4 %swiglu_rows.7 = (bf16[2048,2048]{1,0:T(8,128)(2,1)}, bf16[2048,2048]{1,0:T(8,128)(2,1)}, bf16[2048,1024]{1,0:T(8,128)(2,1)}, bf16[2048,1024]{1,0:T(8,128)(2,1)}...) custom-call(s32[11]{0:T(128)} %pad_add_fusion.ids_ref, ...), custom_call_target="tpu_custom_call", output_to_operand_aliasing={{0}: (7, {}), {1}: (8, {}), {2}: (9, {}), {3}: (10, {}), {4... | custom-call | flops 12884901888 | bytes 29360128 | tf_op jit(solution)/shard_map/swiglu_rows/pallas_call | solution.py:861
  199.0 18.4 %swiglu_rows.8 = (bf16[2048,2048]{1,0:T(8,128)(2,1)}, bf16[2048,2048]{1,0:T(8,128)(2,1)}, bf16[2048,1024]{1,0:T(8,128)(2,1)}, bf16[2048,1024]{1,0:T(8,128)(2,1)}...) custom-call(s32[11]{0:T(128)} %pad_add_fusion.ids_ref, ...), custom_call_target="tpu_custom_call", output_to_operand_aliasing={{0}: (7, {}), {1}: (8, {}), {2}: (9, {}), {3}: (10, {}), {4... | custom-call | flops 12884901888 | bytes 29360128 | tf_op jit(solution)/shard_map/swiglu_rows/pallas_call | solution.py:861
  218.4 13.2 %swiglu_rows.9 = (bf16[2048,2048]{1,0:T(8,128)(2,1)}, bf16[2048,2048]{1,0:T(8,128)(2,1)}, bf16[2048,1024]{1,0:T(8,128)(2,1)}, bf16[2048,1024]{1,0:T(8,128)(2,1)}...) custom-call(s32[11]{0:T(128)} %pad_add_fusion.ids_ref, ...), custom_call_target="tpu_custom_call", output_to_operand_aliasing={{0}: (7, {}), {1}: (8, {}), {2}: (9, {}), {3}: (10, {}), {4... | custom-call | flops 6442450944 | bytes 20971520 | tf_op jit(solution)/shard_map/swiglu_rows/pallas_call | solution.py:861
  235.2 10.6 %convolution_convert_fusion.1.term_ref.own_ref = bf16[2048,2048]{1,0:T(8,128)(2,1)S(1)} fusion(bf16[2048,1024]{1,0:T(8,128)(2,1)} %get-tuple-element.256, bf16[1024,2048]{1,0:T(8,128)(2,1)S(1)} %copy-done.1), kind=kOutput, calls=%fused_computation.1 | convolution fusion | flops 8594128896 | bytes 16777216 | tf_op jit(solution)/shard_map/dot_general | solution.py:32
  245.8 3.3 copy-done
  251.0 2.9 ring_add.19
  255.6 2.9 ring_add.18
  258.9 14.1 %convolution_convert_fusion.2 = bf16[1024,2048]{1,0:T(8,128)(2,1)} fusion(bf16[2048,1024]{1,0:T(8,128)(2,1)} %get-tuple-element.256, bf16[2048,2048]{1,0:T(8,128)(2,1)} %get-tuple-element.263), kind=kOutput, calls=%fused_computation.5 | convolution fusion | flops 8592031744 | bytes 16777216 | tf_op jit(solution)/shard_map/dot_general | solution.py:32
  275.3 4.3 collective-permute-done.19.got_ref
  279.7 3.1 ring_add.21
  284.2 3.2 ring_add.20
  288.6 14.3 %convolution_convert_fusion.4 = bf16[2048,1024]{1,0:T(8,128)(2,1)} fusion(bf16[2048,2048]{1,0:T(8,128)(2,1)} %get-tuple-element.266, bf16[2048,1024]{1,0:T(8,128)(2,1)} %get-tuple-element.267), kind=kOutput, calls=%fused_computation.7 | convolution fusion | flops 8592031744 | bytes 16777216 | tf_op jit(solution)/shard_map/dot_general | solution.py:32
  302.9 4.6 collective-permute-done.21.got_ref
  307.5 3.2 ring_add.23
  311.6 3.1 ring_add.22
  315.9 14.1 %convolution_convert_fusion.3 = bf16[2048,1024]{1,0:T(8,128)(2,1)} fusion(bf16[2048,2048]{1,0:T(8,128)(2,1)} %get-tuple-element.266, bf16[2048,1024]{1,0:T(8,128)(2,1)} %get-tuple-element.270), kind=kOutput, calls=%fused_computation.6 | convolution fusion | flops 8592031744 | bytes 16777216 | tf_op jit(solution)/shard_map/dot_general | solution.py:32
  330.0 8.1 %collective-permute-done.23.up_ref = bf16[256,2048]{1,0:T(8,128)(2,1)S(1)} collective-permute-done((bf16[256,2048]{1,0:T(8,128)(2,1)}, bf16[256,2048]{1,0:T(8,128)(2,1)S(1)}, u32[]{:S(2)}, u32[]{:S(2)}) %collective-permute-start.23) | collective-permute-done | bytes 1048608 | tf_op jit(solution)/shard_map/ppermute | solution.py:968
  340.2 10.8 %norm_back_and_project.1 = (f32[256,2048]{1,0:T(8,128)}, bf16[256,2048]{1,0:T(8,128)(2,1)}, f32[1,2048]{1,0:T(1,128)}, bf16[8,256,256]{2,1,0:T(8,128)(2,1)}) custom-call(s32[11]{0:T(128)} %pad_add_fusion.ids_ref, bf16[256,2048]{1,0:T(8,128)(2,1)} %get-tuple-element.277.own_ref, bf16[256,2048]{1,0:T(8,128)(2,1)} %copy-done.19, bf16[256,2048]{1,0:T(8,128)(2,1)} %copy-done.17, ...), custom_call_target="tpu_custom_call" | custom-call | flops 2147483648 | bytes 8388608 | tf_op jit(solution)/shard_map/norm_back_and_project/pallas_call | solution.py:539
  352.9 4.1 all-to-all-start.2
  357.0 2.9 ring_add.25
  359.9 2.9 ring_add.24
  362.8 7.9 %out_weight_grad.1 = (bf16[2,2048,512]{2,1,0:T(8,128)(2,1)}, bf16[2,2048,512]{2,1,0:T(8,128)(2,1)}) custom-call(s32[11]{0:T(128)} %pad_add_fusion.ids_ref, bf16[8,256,256]{2,1,0:T(8,128)(2,1)} %copy-done.5, bf16[256,2048]{1,0:T(8,128)(2,1)} %get-tuple-element.284.da_ref), custom_call_target="tpu_custom_call" | custom-call | flops 2147483648 | bytes 8388608 | tf_op jit(solution)/shard_map/out_weight_grad/pallas_call | solution.py:638
  370.7 2.7 all-to-all-done.2
  378.1 17.7 %attend_back.2 = (bf16[1280,256]{1,0:T(8,128)(2,1)}, f32[2048,128]{1,0:T(8,128)}, f32[2048,128]{1,0:T(8,128)}) custom-call(bf16[2048,256]{1,0:T(8,128)(2,1)} %get-tuple-element.189.q_ref, bf16[2048,256]{1,0:T(8,128)(2,1)} %bitcast.42, bf16[2048,256]{1,0:T(8,128)(2,1)} %get-tuple-element.199.o_ref, f32[8,2048]{1,0:T(8,128)} %get-tuple-element.292.lse_ref, ...), custom_call_target="tpu_custom_call" | custom-call | flops 10737418240 | bytes 5242880 | tf_op jit(solution)/shard_map/attend_back/pallas_call | solution.py:397
  395.8 3.4 collective-permute-done.27.got_ref
  399.9 3.2 ring_add.27
  404.2 3.1 ring_add.26
  410.9 23.3 %attend_back.3.grad_ref = bf16[2048,384]{1,0:T(8,128)(2,1)} custom-call(bf16[2048,256]{1,0:T(8,128)(2,1)} %get-tuple-element.189.q_ref, bf16[2048,256]{1,0:T(8,128)(2,1)} %bitcast.43, bf16[2048,256]{1,0:T(8,128)(2,1)} %get-tuple-element.199.o_ref, f32[8,2048]{1,0:T(8,128)} %get-tuple-element.292.lse_ref, bf16[2048,128]{1,0:T(8,128)(2,1)} %get-tuple-element.190.k_ref, ...), custom_call_target="tpu_custom_call" | custom-call | flops 10737418240 | bytes 5242880 | tf_op jit(solution)/shard_map/attend_back/pallas_call | solution.py:397
  434.2 2.9 convolution_convert_fusion.5
  437.1 3.1 ring_add.29
  441.5 3.1 ring_add.28
  445.6 4.1 fusion.1
  454.2 6.8 %convolution_convert_fusion.term_ref.own_ref = bf16[2048,2048]{1,0:T(8,128)(2,1)} fusion(bf16[2048,384]{1,0:T(8,128)(2,1)S(1)} %copy-done.8, bf16[2048,128]{1,0:T(8,128)(2,1)S(1)} %bitcast.41, bf16[2048,256]{1,0:T(8,128)(2,1)S(1)} %copy-done.2), kind=kOutput, calls=%fused_computation | convolution fusion | flops 3228565504 | bytes 11534336 | tf_op jit(solution)/shard_map/dot_general | solution.py:32
  460.9 11.8 %projection_weight_grads.1 = (bf16[2,512,256]{2,1,0:T(8,128)(2,1)}, bf16[2,512,256]{2,1,0:T(8,128)(2,1)}, f32[2,512,256]{2,1,0:T(8,128)}, f32[2,512,256]{2,1,0:T(8,128)}) custom-call(s32[11]{0:T(128)} %pad_add_fusion.ids_ref, bf16[2048,2048]{1,0:T(8,128)(2,1)} %get-tuple-element.185.normed_ref, bf16[2048,384]{1,0:T(8,128)(2,1)} %attend_back.3.grad_ref, ...), custom_call_target="tpu_custom_call" | custom-call | flops 3221225472 | bytes 12582912 | tf_op jit(solution)/shard_map/projection_weight_grads/pallas_call | solution.py:698
  472.7 7.0 %collective-permute-done.32.got_ref = bf16[128,2048]{1,0:T(8,128)(2,1)} collective-permute-done((bf16[128,2048]{1,0:T(8,128)(2,1)}, bf16[128,2048]{1,0:T(8,128)(2,1)}, u32[]{:S(2)}, u32[]{:S(2)}) %collective-permute-start.32) | collective-permute-done | bytes 524320 | tf_op jit(solution)/shard_map/ppermute | solution.py:968
  479.8 2.9 ring_add.31
  483.4 2.9 ring_add.30
  492.6 21.1 %collective-permute-done.41 = bf16[512,256]{1,0:T(8,128)(2,1)S(1)} collective-permute-done((bf16[512,256]{1,0:T(8,128)(2,1)S(1)}, bf16[512,256]{1,0:T(8,128)(2,1)S(1)}, u32[]{:S(2)}, u32[]{:S(2)}) %collective-permute-start.41) | collective-permute-done | bytes 262176 | tf_op jit(solution)/shard_map/ppermute | solution.py:908
  513.7 5.4 fusion
  519.1 3.1 ring_add.33
  523.2 3.3 ring_add.32
  529.3 3.5 all-to-all-start.3
  532.8 4.3 layer_output.1
  537.1 26.8 %collective-permute-done.44.got_ref = bf16[256,2048]{1,0:T(8,128)(2,1)S(1)} collective-permute-done((bf16[256,2048]{1,0:T(8,128)(2,1)}, bf16[256,2048]{1,0:T(8,128)(2,1)S(1)}, u32[]{:S(2)}, u32[]{:S(2)}) %collective-permute-start.44) | collective-permute-done | bytes 1048608 | tf_op jit(solution)/shard_map/ppermute | solution.py:971
  564.0 3.8 collective-permute-done.43.got_ref
  567.7 3.1 ring_add.35
  572.2 3.1 ring_add.34
  584.4 15.3 %collective-permute-done.46.down_ref = bf16[256,2048]{1,0:T(8,128)(2,1)} collective-permute-done((bf16[256,2048]{1,0:T(8,128)(2,1)}, bf16[256,2048]{1,0:T(8,128)(2,1)}, u32[]{:S(2)}, u32[]{:S(2)}) %collective-permute-start.46) | collective-permute-done | bytes 1048608 | tf_op jit(solution)/shard_map/ppermute | solution.py:971
  599.7 7.1 %collective-permute-done.45.up_ref = bf16[256,2048]{1,0:T(8,128)(2,1)} collective-permute-done((bf16[256,2048]{1,0:T(8,128)(2,1)}, bf16[256,2048]{1,0:T(8,128)(2,1)}, u32[]{:S(2)}, u32[]{:S(2)}) %collective-permute-start.45) | collective-permute-done | bytes 1048608 | tf_op jit(solution)/shard_map/ppermute | solution.py:968
  606.8 5.9 input_grad.1
  (223 shorter events, 94.0 us)
Async XLA Ops:
  9.2 19.0 %collective-permute-start = (bf16[256,1024]{1,0:T(8,128)(2,1)S(1)}, bf16[256,1024]{1,0:T(8,128)(2,1)S(1)}, u32[]{:S(2)}, u32[]{:S(2)}) collective-permute-start(bf16[256,1024]{1,0:T(8,128)(2,1)S(1)} %get-tuple-element.350), channel_id=1, source_target_pairs={{0,1},{1,3},{3,5},{5,7},{7,6},{6,4},{4,2},{2,0},{8,9},{9,11},{11,1... | collective-permute-start | bytes 1572872 | tf_op jit(solution)/shard_map/ppermute | solution.py:968
  12.1 16.1 %collective-permute-start.1 = (bf16[256,1024]{1,0:T(8,128)(2,1)S(1)}, bf16[256,1024]{1,0:T(8,128)(2,1)S(1)}, u32[]{:S(2)}, u32[]{:S(2)}) collective-permute-start(bf16[256,1024]{1,0:T(8,128)(2,1)S(1)} %get-tuple-element.350), channel_id=1, source_target_pairs={{1,0},{3,1},{5,3},{7,5},{6,7},{4,6},{2,4},{0,2},{9,8},{11,9},{13,1... | collective-permute-start | bytes 1572872 | tf_op jit(solution)/shard_map/ppermute | solution.py:971
  14.2 24.8 %all-to-all-start = ((bf16[8,256,128]{2,1,0:T(8,128)(2,1)}), bf16[8,256,128]{2,1,0:T(8,128)(2,1)S(1)}, u32[]{:S(2)}, u32[]{:S(2)}) async-start(bf16[8,256,128]{2,1,0:T(8,128)(2,1)} %pick_heads.1), calls=%async_computation | async-start | bytes 1048576 | tf_op jit(solution)/shard_map/all_to_all | solution.py:965
  28.2 18.7 %collective-permute-start.2 = (bf16[256,1024]{1,0:T(8,128)(2,1)S(1)}, bf16[256,1024]{1,0:T(8,128)(2,1)S(1)}, u32[]{:S(2)}, u32[]{:S(2)}) collective-permute-start(bf16[256,1024]{1,0:T(8,128)(2,1)S(1)} %collective-permute-done), channel_id=1, source_target_pairs={{0,1},{1,3},{3,5},{5,7},{7,6},{6,4},{4,2},{2,0},{8,9},{9,11},{11,1... | collective-permute-start | bytes 1572872 | tf_op jit(solution)/shard_map/ppermute | solution.py:968
  30.3 16.7 %collective-permute-start.3 = (bf16[256,1024]{1,0:T(8,128)(2,1)S(1)}, bf16[256,1024]{1,0:T(8,128)(2,1)S(1)}, u32[]{:S(2)}, u32[]{:S(2)}) collective-permute-start(bf16[256,1024]{1,0:T(8,128)(2,1)S(1)} %collective-permute-done.1), channel_id=1, source_target_pairs={{1,0},{3,1},{5,3},{7,5},{6,7},{4,6},{2,4},{0,2},{9,8},{11,9},{13,1... | collective-permute-start | bytes 1572872 | tf_op jit(solution)/shard_map/ppermute | solution.py:971
  46.9 15.0 %collective-permute-start.4 = (bf16[256,1024]{1,0:T(8,128)(2,1)S(1)}, bf16[256,1024]{1,0:T(8,128)(2,1)S(1)}, u32[]{:S(2)}, u32[]{:S(2)}) collective-permute-start(bf16[256,1024]{1,0:T(8,128)(2,1)S(1)} %collective-permute-done.2), channel_id=1, source_target_pairs={{0,1},{1,3},{3,5},{5,7},{7,6},{6,4},{4,2},{2,0},{8,9},{9,11},{11,1... | collective-permute-start | bytes 1572872 | tf_op jit(solution)/shard_map/ppermute | solution.py:968
  49.8 12.6 %collective-permute-start.5 = (bf16[256,1024]{1,0:T(8,128)(2,1)S(1)}, bf16[256,1024]{1,0:T(8,128)(2,1)S(1)}, u32[]{:S(2)}, u32[]{:S(2)}) collective-permute-start(bf16[256,1024]{1,0:T(8,128)(2,1)S(1)} %collective-permute-done.3), channel_id=1, source_target_pairs={{1,0},{3,1},{5,3},{7,5},{6,7},{4,6},{2,4},{0,2},{9,8},{11,9},{13,1... | collective-permute-start | bytes 1572872 | tf_op jit(solution)/shard_map/ppermute | solution.py:971
  62.4 17.1 %collective-permute-start.6 = (bf16[128,1024]{1,0:T(8,128)(2,1)S(1)}, bf16[128,1024]{1,0:T(8,128)(2,1)S(1)}, u32[]{:S(2)}, u32[]{:S(2)}) collective-permute-start(bf16[128,1024]{1,0:T(8,128)(2,1)S(1)} %slice.88), channel_id=1, source_target_pairs={{0,1},{1,3},{3,5},{5,7},{7,6},{6,4},{4,2},{2,0},{8,9},{9,11},{11,1... | collective-permute-start | bytes 786440 | tf_op jit(solution)/shard_map/ppermute | solution.py:968
  64.3 15.3 %collective-permute-start.7 = (bf16[128,1024]{1,0:T(8,128)(2,1)S(1)}, bf16[128,1024]{1,0:T(8,128)(2,1)S(1)}, u32[]{:S(2)}, u32[]{:S(2)}) collective-permute-start(bf16[128,1024]{1,0:T(8,128)(2,1)S(1)} %slice.89), channel_id=1, source_target_pairs={{1,0},{3,1},{5,3},{7,5},{6,7},{4,6},{2,4},{0,2},{9,8},{11,9},{13,1... | collective-permute-start | bytes 786440 | tf_op jit(solution)/shard_map/ppermute | solution.py:971
  81.0 31.9 %collective-permute-start.8 = (bf16[2048,1024]{1,0:T(8,128)(2,1)}, bf16[2048,1024]{1,0:T(8,128)(2,1)}, u32[]{:S(2)}, u32[]{:S(2)}) collective-permute-start(bf16[2048,1024]{1,0:T(8,128)(2,1)} %constant_dynamic-update-slice_fusion.mine_ref), channel_id=1, source_target_pairs={{0,8},{8,0},{16,24},{24,16},{1,9},{9,1},{17,25},{25,17},{2,10},{10... | collective-permute-start | bytes 12582920 | tf_op jit(solution)/shard_map/ppermute | solution.py:1001
  81.0 31.9 %all-to-all-start.1 = ((bf16[8,256,256]{2,1,0:T(8,128)(2,1)}), bf16[8,256,256]{2,1,0:T(8,128)(2,1)S(1)}, u32[]{:S(2)}, u32[]{:S(2)}) async-start(bf16[8,256,256]{2,1,0:T(8,128)(2,1)} %bitcast.44), calls=%async_computation.1 | async-start | bytes 2097152 | tf_op jit(solution)/shard_map/all_to_all | solution.py:965
  86.5 313.4 %reduce-scatter.5.cloned.1.call-start = ((), (), s32[]{:S(2)}) async-start(), calls=%async_computation.8 | async-start | bytes 5242880 | tf_op jit(solution)/shard_map/reduce_scatter | solution.py:1069
  123.1 24.7 %collective-permute-start.10 = (bf16[256,2048]{1,0:T(8,128)(2,1)}, bf16[256,2048]{1,0:T(8,128)(2,1)S(1)}, u32[]{:S(2)}, u32[]{:S(2)}) collective-permute-start(bf16[256,2048]{1,0:T(8,128)(2,1)} %get-tuple-element.202.refs_0_), channel_id=1, source_target_pairs={{1,0},{3,1},{5,3},{7,5},{6,7},{4,6},{2,4},{0,2},{9,8},{11,9},{13,1... | collective-permute-start | bytes 3145736 | tf_op jit(solution)/shard_map/ppermute | solution.py:971
  123.1 24.9 %collective-permute-start.9 = (bf16[256,2048]{1,0:T(8,128)(2,1)}, bf16[256,2048]{1,0:T(8,128)(2,1)S(1)}, u32[]{:S(2)}, u32[]{:S(2)}) collective-permute-start(bf16[256,2048]{1,0:T(8,128)(2,1)} %get-tuple-element.202.refs_0_), channel_id=1, source_target_pairs={{0,1},{1,3},{3,5},{5,7},{7,6},{6,4},{4,2},{2,0},{8,9},{9,11},{11,1... | collective-permute-start | bytes 3145736 | tf_op jit(solution)/shard_map/ppermute | solution.py:968
  148.0 24.5 %collective-permute-start.11 = (bf16[256,2048]{1,0:T(8,128)(2,1)S(1)}, bf16[256,2048]{1,0:T(8,128)(2,1)S(1)}, u32[]{:S(2)}, u32[]{:S(2)}) collective-permute-start(bf16[256,2048]{1,0:T(8,128)(2,1)S(1)} %collective-permute-done.9.refs_0_), channel_id=1, source_target_pairs={{0,1},{1,3},{3,5},{5,7},{7,6},{6,4},{4,2},{2,0},{8,9},{9,11},{11,1... | collective-permute-start | bytes 3145736 | tf_op jit(solution)/shard_map/ppermute | solution.py:968
  149.7 23.0 %collective-permute-start.12 = (bf16[256,2048]{1,0:T(8,128)(2,1)S(1)}, bf16[256,2048]{1,0:T(8,128)(2,1)S(1)}, u32[]{:S(2)}, u32[]{:S(2)}) collective-permute-start(bf16[256,2048]{1,0:T(8,128)(2,1)S(1)} %collective-permute-done.10.refs_1_), channel_id=1, source_target_pairs={{1,0},{3,1},{5,3},{7,5},{6,7},{4,6},{2,4},{0,2},{9,8},{11,9},{13,1... | collective-permute-start | bytes 3145736 | tf_op jit(solution)/shard_map/ppermute | solution.py:971
  172.7 23.4 %collective-permute-start.13 = (bf16[256,2048]{1,0:T(8,128)(2,1)S(1)}, bf16[256,2048]{1,0:T(8,128)(2,1)S(1)}, u32[]{:S(2)}, u32[]{:S(2)}) collective-permute-start(bf16[256,2048]{1,0:T(8,128)(2,1)S(1)} %collective-permute-done.11.refs_0_), channel_id=1, source_target_pairs={{0,1},{1,3},{3,5},{5,7},{7,6},{6,4},{4,2},{2,0},{8,9},{9,11},{11,1... | collective-permute-start | bytes 3145736 | tf_op jit(solution)/shard_map/ppermute | solution.py:968
  174.1 22.5 %collective-permute-start.14 = (bf16[256,2048]{1,0:T(8,128)(2,1)S(1)}, bf16[256,2048]{1,0:T(8,128)(2,1)S(1)}, u32[]{:S(2)}, u32[]{:S(2)}) collective-permute-start(bf16[256,2048]{1,0:T(8,128)(2,1)S(1)} %collective-permute-done.12.refs_1_), channel_id=1, source_target_pairs={{1,0},{3,1},{5,3},{7,5},{6,7},{4,6},{2,4},{0,2},{9,8},{11,9},{13,1... | collective-permute-start | bytes 3145736 | tf_op jit(solution)/shard_map/ppermute | solution.py:971
  196.7 20.7 %collective-permute-start.15 = (bf16[128,2048]{1,0:T(8,128)(2,1)S(1)}, bf16[128,2048]{1,0:T(8,128)(2,1)S(1)}, u32[]{:S(2)}, u32[]{:S(2)}) collective-permute-start(bf16[128,2048]{1,0:T(8,128)(2,1)S(1)} %slice.90), channel_id=1, source_target_pairs={{0,1},{1,3},{3,5},{5,7},{7,6},{6,4},{4,2},{2,0},{8,9},{9,11},{11,1... | collective-permute-start | bytes 1572872 | tf_op jit(solution)/shard_map/ppermute | solution.py:968
  198.3 19.2 %collective-permute-start.16 = (bf16[128,2048]{1,0:T(8,128)(2,1)S(1)}, bf16[128,2048]{1,0:T(8,128)(2,1)S(1)}, u32[]{:S(2)}, u32[]{:S(2)}) collective-permute-start(bf16[128,2048]{1,0:T(8,128)(2,1)S(1)} %slice.91), channel_id=1, source_target_pairs={{1,0},{3,1},{5,3},{7,5},{6,7},{4,6},{2,4},{0,2},{9,8},{11,9},{13,1... | collective-permute-start | bytes 1572872 | tf_op jit(solution)/shard_map/ppermute | solution.py:971
  218.4 16.8 %copy-start.1 = (bf16[1024,2048]{1,0:T(8,128)(2,1)S(1)}, bf16[1024,2048]{1,0:T(8,128)(2,1)}, u32[]{:S(2)}) copy-start(bf16[1024,2048]{1,0:T(8,128)(2,1)} %refs_5_.7) | copy-start | bytes 12582916
  232.9 17.3 %collective-permute-start.17 = (bf16[128,2048]{1,0:T(8,128)(2,1)S(1)}, bf16[128,2048]{1,0:T(8,128)(2,1)S(1)}, u32[]{:S(2)}, u32[]{:S(2)}) collective-permute-start(bf16[128,2048]{1,0:T(8,128)(2,1)S(1)} %get-tuple-element.356), channel_id=1, source_target_pairs={{0,1},{1,3},{3,5},{5,7},{7,6},{6,4},{4,2},{2,0},{8,9},{9,11},{11,1... | collective-permute-start | bytes 1572872 | tf_op jit(solution)/shard_map/ppermute | solution.py:968
  234.5 15.7 %collective-permute-start.18 = (bf16[128,2048]{1,0:T(8,128)(2,1)S(1)}, bf16[128,2048]{1,0:T(8,128)(2,1)S(1)}, u32[]{:S(2)}, u32[]{:S(2)}) collective-permute-start(bf16[128,2048]{1,0:T(8,128)(2,1)S(1)} %get-tuple-element.355), channel_id=1, source_target_pairs={{1,0},{3,1},{5,3},{7,5},{6,7},{4,6},{2,4},{0,2},{9,8},{11,9},{13,1... | collective-permute-start | bytes 1572872 | tf_op jit(solution)/shard_map/ppermute | solution.py:971
  254.0 21.3 %collective-permute-start.20 = (bf16[256,2048]{1,0:T(8,128)(2,1)}, bf16[256,2048]{1,0:T(8,128)(2,1)S(1)}, u32[]{:S(2)}, u32[]{:S(2)}) collective-permute-start(bf16[256,2048]{1,0:T(8,128)(2,1)} %ring_add.19), channel_id=1, source_target_pairs={{1,0},{3,1},{5,3},{7,5},{6,7},{4,6},{2,4},{0,2},{9,8},{11,9},{13,1... | collective-permute-start | bytes 3145736 | tf_op jit(solution)/shard_map/ppermute | solution.py:971
  258.5 21.0 %collective-permute-start.19 = (bf16[256,2048]{1,0:T(8,128)(2,1)}, bf16[256,2048]{1,0:T(8,128)(2,1)S(1)}, u32[]{:S(2)}, u32[]{:S(2)}) collective-permute-start(bf16[256,2048]{1,0:T(8,128)(2,1)} %ring_add.18), channel_id=1, source_target_pairs={{0,1},{1,3},{3,5},{5,7},{7,6},{6,4},{4,2},{2,0},{8,9},{9,11},{11,1... | collective-permute-start | bytes 3145736 | tf_op jit(solution)/shard_map/ppermute | solution.py:968
  279.6 193.1 %reduce-scatter.7.cloned.1.call-start = ((), (), s32[]{:S(2)}) async-start(), calls=%async_computation.9 | async-start | bytes 5242880 | tf_op jit(solution)/shard_map/reduce_scatter | solution.py:1069
  282.8 20.1 %collective-permute-start.22 = (bf16[256,2048]{1,0:T(8,128)(2,1)}, bf16[256,2048]{1,0:T(8,128)(2,1)S(1)}, u32[]{:S(2)}, u32[]{:S(2)}) collective-permute-start(bf16[256,2048]{1,0:T(8,128)(2,1)} %ring_add.21), channel_id=1, source_target_pairs={{1,0},{3,1},{5,3},{7,5},{6,7},{4,6},{2,4},{0,2},{9,8},{11,9},{13,1... | collective-permute-start | bytes 3145736 | tf_op jit(solution)/shard_map/ppermute | solution.py:971
  287.4 20.1 %collective-permute-start.21 = (bf16[256,2048]{1,0:T(8,128)(2,1)}, bf16[256,2048]{1,0:T(8,128)(2,1)S(1)}, u32[]{:S(2)}, u32[]{:S(2)}) collective-permute-start(bf16[256,2048]{1,0:T(8,128)(2,1)} %ring_add.20), channel_id=1, source_target_pairs={{0,1},{1,3},{3,5},{5,7},{7,6},{6,4},{4,2},{2,0},{8,9},{9,11},{11,1... | collective-permute-start | bytes 3145736 | tf_op jit(solution)/shard_map/ppermute | solution.py:968
  310.7 19.2 %collective-permute-start.24 = (bf16[256,2048]{1,0:T(8,128)(2,1)}, bf16[256,2048]{1,0:T(8,128)(2,1)S(1)}, u32[]{:S(2)}, u32[]{:S(2)}) collective-permute-start(bf16[256,2048]{1,0:T(8,128)(2,1)} %ring_add.23), channel_id=1, source_target_pairs={{1,0},{3,1},{5,3},{7,5},{6,7},{4,6},{2,4},{0,2},{9,8},{11,9},{13,1... | collective-permute-start | bytes 3145736 | tf_op jit(solution)/shard_map/ppermute | solution.py:971
  314.7 23.3 %collective-permute-start.23 = (bf16[256,2048]{1,0:T(8,128)(2,1)}, bf16[256,2048]{1,0:T(8,128)(2,1)S(1)}, u32[]{:S(2)}, u32[]{:S(2)}) collective-permute-start(bf16[256,2048]{1,0:T(8,128)(2,1)} %ring_add.22), channel_id=1, source_target_pairs={{0,1},{1,3},{3,5},{5,7},{7,6},{6,4},{4,2},{2,0},{8,9},{9,11},{11,1... | collective-permute-start | bytes 3145736 | tf_op jit(solution)/shard_map/ppermute | solution.py:968
  330.0 10.2 %copy-start.17 = (bf16[256,2048]{1,0:T(8,128)(2,1)}, bf16[256,2048]{1,0:T(8,128)(2,1)S(1)}, u32[]{:S(2)}) copy-start(bf16[256,2048]{1,0:T(8,128)(2,1)S(1)} %collective-permute-done.24.down_ref) | copy-start | bytes 3145732
  338.0 13.0 %collective-permute-start.25 = (bf16[128,2048]{1,0:T(8,128)(2,1)}, bf16[128,2048]{1,0:T(8,128)(2,1)S(1)}, u32[]{:S(2)}, u32[]{:S(2)}) collective-permute-start(bf16[128,2048]{1,0:T(8,128)(2,1)} %get-tuple-element.275), channel_id=1, source_target_pairs={{0,1},{1,3},{3,5},{5,7},{7,6},{6,4},{4,2},{2,0},{8,9},{9,11},{11,1... | collective-permute-start | bytes 1572872 | tf_op jit(solution)/shard_map/ppermute | solution.py:968
  339.2 12.9 %collective-permute-start.26 = (bf16[128,2048]{1,0:T(8,128)(2,1)}, bf16[128,2048]{1,0:T(8,128)(2,1)S(1)}, u32[]{:S(2)}, u32[]{:S(2)}) collective-permute-start(bf16[128,2048]{1,0:T(8,128)(2,1)} %get-tuple-element.276), channel_id=1, source_target_pairs={{1,0},{3,1},{5,3},{7,5},{6,7},{4,6},{2,4},{0,2},{9,8},{11,9},{13,1... | collective-permute-start | bytes 1572872 | tf_op jit(solution)/shard_map/ppermute | solution.py:971
  352.9 20.5 %all-to-all-start.2 = ((bf16[8,256,256]{2,1,0:T(8,128)(2,1)}), bf16[8,256,256]{2,1,0:T(8,128)(2,1)S(1)}, u32[]{:S(2)}, u32[]{:S(2)}) async-start(bf16[8,256,256]{2,1,0:T(8,128)(2,1)} %get-tuple-element.283), calls=%async_computation.2 | async-start | bytes 2097152 | tf_op jit(solution)/shard_map/all_to_all | solution.py:965
  357.0 180.2 %reduce-scatter.9.cloned.1.call-start = ((), (), s32[]{:S(2)}) async-start(), calls=%async_computation.10 | async-start | bytes 5242880 | tf_op jit(solution)/shard_map/reduce_scatter | solution.py:1069
  362.8 10.6 %copy-start.13 = (bf16[256,2048]{1,0:T(8,128)(2,1)S(1)}, bf16[256,2048]{1,0:T(8,128)(2,1)}, u32[]{:S(2)}) copy-start(bf16[256,2048]{1,0:T(8,128)(2,1)} %ring_add.24) | copy-start | bytes 3145732
  362.8 11.7 %copy-start.12 = (bf16[256,2048]{1,0:T(8,128)(2,1)S(1)}, bf16[256,2048]{1,0:T(8,128)(2,1)}, u32[]{:S(2)}) copy-start(bf16[256,2048]{1,0:T(8,128)(2,1)} %ring_add.25) | copy-start | bytes 3145732
  362.8 12.7 %copy-start.41 = (s32[1,8]{1,0:T(1,128)S(1)}, s32[1,8]{1,0:T(1,128)}, u32[]{:S(2)}) copy-start(s32[1,8]{1,0:T(1,128)} %get-tuple-element.359) | copy-start | bytes 100
  362.8 14.0 %copy-start.39 = (f32[2048]{0:T(1024)S(1)}, f32[2048]{0:T(1024)}, u32[]{:S(2)}) copy-start(f32[2048]{0:T(1024)} %param.16) | copy-start | bytes 24580
  373.4 26.5 %collective-permute-start.29 = (bf16[2,2048,512]{2,1,0:T(8,128)(2,1)}, bf16[2,2048,512]{2,1,0:T(8,128)(2,1)}, u32[]{:S(2)}, u32[]{:S(2)}) collective-permute-start(bf16[2,2048,512]{2,1,0:T(8,128)(2,1)} %get-tuple-element.299), channel_id=1, source_target_pairs={{0,8},{8,0},{16,24},{24,16},{1,9},{9,1},{17,25},{25,17},{2,10},{10... | collective-permute-start | bytes 12582920 | tf_op jit(solution)/shard_map/ppermute | solution.py:899
  373.4 239.3 %reduce-scatter.11.cloned.1.call-start = ((), (), s32[]{:S(2)}) async-start(), calls=%async_computation.11 | async-start | bytes 2359296 | tf_op jit(solution)/shard_map/reduce_scatter | solution.py:1123
  373.4 25.7 %collective-permute-start.27 = (bf16[256,2048]{1,0:T(8,128)(2,1)S(1)}, bf16[256,2048]{1,0:T(8,128)(2,1)}, u32[]{:S(2)}, u32[]{:S(2)}) collective-permute-start(bf16[256,2048]{1,0:T(8,128)(2,1)S(1)} %copy-done.13), channel_id=1, source_target_pairs={{0,1},{1,3},{3,5},{5,7},{7,6},{6,4},{4,2},{2,0},{8,9},{9,11},{11,1... | collective-permute-start | bytes 3145736 | tf_op jit(solution)/shard_map/ppermute | solution.py:968
  374.5 25.4 %collective-permute-start.28 = (bf16[256,2048]{1,0:T(8,128)(2,1)S(1)}, bf16[256,2048]{1,0:T(8,128)(2,1)}, u32[]{:S(2)}, u32[]{:S(2)}) collective-permute-start(bf16[256,2048]{1,0:T(8,128)(2,1)S(1)} %copy-done.12), channel_id=1, source_target_pairs={{1,0},{3,1},{5,3},{7,5},{6,7},{4,6},{2,4},{0,2},{9,8},{11,9},{13,1... | collective-permute-start | bytes 3145736 | tf_op jit(solution)/shard_map/ppermute | solution.py:971
  403.0 31.1 %collective-permute-start.31 = (bf16[256,2048]{1,0:T(8,128)(2,1)}, bf16[256,2048]{1,0:T(8,128)(2,1)S(1)}, u32[]{:S(2)}, u32[]{:S(2)}) collective-permute-start(bf16[256,2048]{1,0:T(8,128)(2,1)} %ring_add.27), channel_id=1, source_target_pairs={{1,0},{3,1},{5,3},{7,5},{6,7},{4,6},{2,4},{0,2},{9,8},{11,9},{13,1... | collective-permute-start | bytes 3145736 | tf_op jit(solution)/shard_map/ppermute | solution.py:971
  407.3 26.9 %collective-permute-start.30 = (bf16[256,2048]{1,0:T(8,128)(2,1)}, bf16[256,2048]{1,0:T(8,128)(2,1)}, u32[]{:S(2)}, u32[]{:S(2)}) collective-permute-start(bf16[256,2048]{1,0:T(8,128)(2,1)} %ring_add.26), channel_id=1, source_target_pairs={{0,1},{1,3},{3,5},{5,7},{7,6},{6,4},{4,2},{2,0},{8,9},{9,11},{11,1... | collective-permute-start | bytes 3145736 | tf_op jit(solution)/shard_map/ppermute | solution.py:968
  440.2 39.5 %collective-permute-start.35 = (bf16[256,2048]{1,0:T(8,128)(2,1)}, bf16[256,2048]{1,0:T(8,128)(2,1)}, u32[]{:S(2)}, u32[]{:S(2)}) collective-permute-start(bf16[256,2048]{1,0:T(8,128)(2,1)} %ring_add.29), channel_id=1, source_target_pairs={{1,0},{3,1},{5,3},{7,5},{6,7},{4,6},{2,4},{0,2},{9,8},{11,9},{13,1... | collective-permute-start | bytes 3145736 | tf_op jit(solution)/shard_map/ppermute | solution.py:971
  444.7 9.5 %copy-start.8 = (bf16[2048,384]{1,0:T(8,128)(2,1)S(1)}, bf16[2048,384]{1,0:T(8,128)(2,1)}, u32[]{:S(2)}) copy-start(bf16[2048,384]{1,0:T(8,128)(2,1)} %attend_back.3.grad_ref) | copy-start | bytes 4718596
  444.7 35.1 %collective-permute-start.34 = (bf16[256,2048]{1,0:T(8,128)(2,1)}, bf16[256,2048]{1,0:T(8,128)(2,1)}, u32[]{:S(2)}, u32[]{:S(2)}) collective-permute-start(bf16[256,2048]{1,0:T(8,128)(2,1)} %ring_add.28), channel_id=1, source_target_pairs={{0,1},{1,3},{3,5},{5,7},{7,6},{6,4},{4,2},{2,0},{8,9},{9,11},{11,1... | collective-permute-start | bytes 3145736 | tf_op jit(solution)/shard_map/ppermute | solution.py:968
  450.7 62.9 %collective-permute-start.42 = (bf16[2048,512]{1,0:T(8,128)(2,1)}, bf16[2048,512]{1,0:T(8,128)(2,1)}, u32[]{:S(2)}, u32[]{:S(2)}) collective-permute-start(bf16[2048,512]{1,0:T(8,128)(2,1)} %fusion.1), channel_id=1, source_target_pairs={{0,16},{8,24},{16,0},{24,8},{1,17},{9,25},{17,1},{25,9},{2,18},{10... | collective-permute-start | bytes 6291464 | tf_op jit(solution)/shard_map/ppermute | solution.py:908
  452.1 27.6 %collective-permute-start.32 = (bf16[128,2048]{1,0:T(8,128)(2,1)}, bf16[128,2048]{1,0:T(8,128)(2,1)}, u32[]{:S(2)}, u32[]{:S(2)}) collective-permute-start(bf16[128,2048]{1,0:T(8,128)(2,1)} %get-tuple-element.354), channel_id=1, source_target_pairs={{0,1},{1,3},{3,5},{5,7},{7,6},{6,4},{4,2},{2,0},{8,9},{9,11},{11,1... | collective-permute-start | bytes 1572872 | tf_op jit(solution)/shard_map/ppermute | solution.py:968
  452.9 26.9 %collective-permute-start.33 = (bf16[128,2048]{1,0:T(8,128)(2,1)}, bf16[128,2048]{1,0:T(8,128)(2,1)}, u32[]{:S(2)}, u32[]{:S(2)}) collective-permute-start(bf16[128,2048]{1,0:T(8,128)(2,1)} %get-tuple-element.353), channel_id=1, source_target_pairs={{1,0},{3,1},{5,3},{7,5},{6,7},{4,6},{2,4},{0,2},{9,8},{11,9},{13,1... | collective-permute-start | bytes 1572872 | tf_op jit(solution)/shard_map/ppermute | solution.py:971
  479.8 7.9 %collective-permute-start.38 = (f32[2,512,256]{2,1,0:T(8,128)}, f32[2,512,256]{2,1,0:T(8,128)S(1)}, u32[]{:S(2)}, u32[]{:S(2)}) collective-permute-start(f32[2,512,256]{2,1,0:T(8,128)} %get-tuple-element.321), channel_id=1, source_target_pairs={{0,8},{8,0},{16,24},{24,16},{1,9},{9,1},{17,25},{25,17},{2,10},{10... | collective-permute-start | bytes 3145736 | tf_op jit(solution)/shard_map/ppermute | solution.py:899
  482.7 30.9 %collective-permute-start.37 = (bf16[256,2048]{1,0:T(8,128)(2,1)}, bf16[256,2048]{1,0:T(8,128)(2,1)S(1)}, u32[]{:S(2)}, u32[]{:S(2)}) collective-permute-start(bf16[256,2048]{1,0:T(8,128)(2,1)} %ring_add.31), channel_id=1, source_target_pairs={{1,0},{3,1},{5,3},{7,5},{6,7},{4,6},{2,4},{0,2},{9,8},{11,9},{13,1... | collective-permute-start | bytes 3145736 | tf_op jit(solution)/shard_map/ppermute | solution.py:971
  486.3 27.4 %collective-permute-start.36 = (bf16[256,2048]{1,0:T(8,128)(2,1)}, bf16[256,2048]{1,0:T(8,128)(2,1)}, u32[]{:S(2)}, u32[]{:S(2)}) collective-permute-start(bf16[256,2048]{1,0:T(8,128)(2,1)} %ring_add.30), channel_id=1, source_target_pairs={{0,1},{1,3},{3,5},{5,7},{7,6},{6,4},{4,2},{2,0},{8,9},{9,11},{11,1... | collective-permute-start | bytes 3145736 | tf_op jit(solution)/shard_map/ppermute | solution.py:968
  487.7 2.1 collective-permute-start.40
  487.7 26.0 %collective-permute-start.39 = (f32[512,256]{1,0:T(8,128)S(1)}, f32[512,256]{1,0:T(8,128)}, u32[]{:S(2)}, u32[]{:S(2)}) collective-permute-start(f32[512,256]{1,0:T(8,128)S(1)} %fusion.2), channel_id=1, source_target_pairs={{0,16},{8,24},{16,0},{24,8},{1,17},{9,25},{17,1},{25,9},{2,18},{10... | collective-permute-start | bytes 1572872 | tf_op jit(solution)/shard_map/ppermute | solution.py:908
  489.8 23.9 %copy-start.31 = (bf16[2,512,256]{2,1,0:T(8,128)(2,1)}, bf16[2,512,256]{2,1,0:T(8,128)(2,1)S(1)}, u32[]{:S(2)}) copy-start(bf16[2,512,256]{2,1,0:T(8,128)(2,1)S(1)} %collective-permute-done.40) | copy-start | bytes 1572868
  491.0 22.7 %collective-permute-start.41 = (bf16[512,256]{1,0:T(8,128)(2,1)S(1)}, bf16[512,256]{1,0:T(8,128)(2,1)S(1)}, u32[]{:S(2)}, u32[]{:S(2)}) collective-permute-start(bf16[512,256]{1,0:T(8,128)(2,1)S(1)} %fusion.3), channel_id=1, source_target_pairs={{0,16},{8,24},{16,0},{24,8},{1,17},{9,25},{17,1},{25,9},{2,18},{10... | collective-permute-start | bytes 786440 | tf_op jit(solution)/shard_map/ppermute | solution.py:908
  522.2 41.7 %collective-permute-start.44 = (bf16[256,2048]{1,0:T(8,128)(2,1)}, bf16[256,2048]{1,0:T(8,128)(2,1)S(1)}, u32[]{:S(2)}, u32[]{:S(2)}) collective-permute-start(bf16[256,2048]{1,0:T(8,128)(2,1)} %ring_add.33), channel_id=1, source_target_pairs={{1,0},{3,1},{5,3},{7,5},{6,7},{4,6},{2,4},{0,2},{9,8},{11,9},{13,1... | collective-permute-start | bytes 3145736 | tf_op jit(solution)/shard_map/ppermute | solution.py:971
  526.5 41.3 %collective-permute-start.43 = (bf16[256,2048]{1,0:T(8,128)(2,1)}, bf16[256,2048]{1,0:T(8,128)(2,1)}, u32[]{:S(2)}, u32[]{:S(2)}) collective-permute-start(bf16[256,2048]{1,0:T(8,128)(2,1)} %ring_add.32), channel_id=1, source_target_pairs={{0,1},{1,3},{3,5},{5,7},{7,6},{6,4},{4,2},{2,0},{8,9},{9,11},{11,1... | collective-permute-start | bytes 3145736 | tf_op jit(solution)/shard_map/ppermute | solution.py:968
  529.3 50.8 %all-to-all-start.3 = ((f32[8,64,256]{2,1,0:T(8,128)}), f32[8,64,256]{2,1,0:T(8,128)S(1)}, u32[]{:S(2)}, u32[]{:S(2)}) async-start(f32[8,64,256]{2,1,0:T(8,128)} %bitcast.15), calls=%async_computation.6 | async-start | bytes 1048576 | tf_op jit(solution)/shard_map/all_to_all | solution.py:965
  570.9 6.8 %copy-start.10 = (bf16[512,1024]{1,0:T(8,128)(2,1)S(1)}, bf16[512,1024]{1,0:T(8,128)(2,1)}, u32[]{:S(2)}) copy-start(bf16[512,1024]{1,0:T(8,128)(2,1)} %reduce-scatter.7.cloned.1.call-done) | copy-start | bytes 3145732
  570.9 28.8 %collective-permute-start.46 = (bf16[256,2048]{1,0:T(8,128)(2,1)}, bf16[256,2048]{1,0:T(8,128)(2,1)}, u32[]{:S(2)}, u32[]{:S(2)}) collective-permute-start(bf16[256,2048]{1,0:T(8,128)(2,1)} %ring_add.35), channel_id=1, source_target_pairs={{1,0},{3,1},{5,3},{7,5},{6,7},{4,6},{2,4},{0,2},{9,8},{11,9},{13,1... | collective-permute-start | bytes 3145736 | tf_op jit(solution)/shard_map/ppermute | solution.py:971
  575.3 31.5 %collective-permute-start.45 = (bf16[256,2048]{1,0:T(8,128)(2,1)}, bf16[256,2048]{1,0:T(8,128)(2,1)}, u32[]{:S(2)}, u32[]{:S(2)}) collective-permute-start(bf16[256,2048]{1,0:T(8,128)(2,1)} %ring_add.34), channel_id=1, source_target_pairs={{0,1},{1,3},{3,5},{5,7},{7,6},{6,4},{4,2},{2,0},{8,9},{9,11},{11,1... | collective-permute-start | bytes 3145736 | tf_op jit(solution)/shard_map/ppermute | solution.py:968
  (33 other events, 109.1 us)
Sparse Core Ops, SparseCore 0:
  279.7 43.5 reduce-scatter.4
  326.0 44.5 reduce-scatter.6
  373.5 44.1 reduce-scatter.8
  519.2 82.5 reduce-scatter.10

commit v6 on v5

--- a/solution.py
+++ b/solution.py
@@ -1015,20 +1015,25 @@
 
     pieces, members, row = [normed_two], [0], rows_total - 2 * share
     hop = [normed_two, normed_two]
+    split = 2 * share * (half_way - 2)
     for d in range(1, half_way + 1):
         if d < half_way:
             hop = [onward(hop[0]), back(hop[1])]
         else:
             hop = [onward(hop[0][:half]), back(hop[1][half:])]
-        run(pieces, members, row)
-        hop, grads[-1], buffers = tie(hop, grads[-1], buffers)
+        if d < half_way:
+            run(pieces, members, row)
+            hop, grads[-1], buffers = tie(hop, grads[-1], buffers)
+        else:
+            last_pair = pieces, members, row
+            early = mm(buffers[2][:split], w_down, NN).astype(bf16)
+            hop, early, buffers = tie(hop, early, buffers)
         pieces = hop
         if d < half_way:
             members, row = [2 * d - 1, 2 * d], 2 * share * (d - 1)
         else:
             members, row = [groups - 1], rows_total - share
     run(pieces, members, row)
-    normed_ring, down_ring, act, dgate, dup = buffers
 
     def first_hop(far):
         return onward(far[:half]), back(far[half:])
@@ -1050,10 +1055,11 @@
         up = ring_add(ids, terms, None, 2 * distance, got[0], 0, share)
         return up, down
 
-    got = first_hop(grads[-1])
-    mlp = mm(act, w_down, NN).astype(bf16)
-    mlp_far = [mlp[rows_total - share : rows_total - half], mlp[rows_total - half :]]
-    got, mlp, mlp_far = tie(got, mlp, mlp_far)
+    got = first_hop(grads.pop())
+    run(*last_pair)
+    got, grads[-1], buffers = tie(got, grads[-1], buffers)
+    normed_ring, down_ring, act, dgate, dup = buffers
+    late_act = act[split:]
     fillers = [
         lambda: mm(act, down_ring, TN).astype(bf16),
         lambda: mm(normed_ring, dgate, TN).astype(bf16),
@@ -1061,10 +1067,17 @@
     ]
     filled = []
     for d in range(half_way - 1, 0, -1):
-        got = next_hop(grads[d], 0, got)
-        if len(filled) < 3:
-            *got, value = tie(*got, fillers[len(filled)]())
-            filled.append(value)
+        hop = hop_sums(grads[d], 0, got)
+        hop, normed_ring, act, late_act = tie(hop, normed_ring, act, late_act)
+        got = send_on(hop)
+        work = [fillers[len(filled)]()] if len(filled) < 3 else []
+        if d == half_way - 2:
+            late = mm(late_act, w_down, NN).astype(bf16)
+            mlp_far = [late[-share:-half], late[-half:]]
+            got, work, late, mlp_far = tie(got, work, late, mlp_far)
+        else:
+            got, work = tie(got, work)
+        filled += work
     down_wgrad, gate_wgrad, up_wgrad = filled
     scatter = lambda a, d: lax.psum_scatter(a, "dp", scatter_dimension=d, tiled=True)
     down_wgrad = scatter(down_wgrad, 1)
@@ -1079,7 +1092,7 @@
     *out_got, do_send, da = tie(*out_got, do_send, da)
     do = exchange(do_send).reshape(rows_total, q_cols)
     out_parts = out_wgrad_parts(ids, attended_rows, da, replicas)
-    out_sums = hop_sums(mlp, 2 * half_way - 4, out_got)
+    out_sums = hop_sums(late, 0, out_got)
     do, out_parts, out_sums = tie(do, out_parts, out_sums)
     out_got = send_on(out_sums)
     out_send, out_keep = out_parts
@@ -1088,7 +1101,7 @@
     carried = attend_back(0, *operands, [])
     out_got, carried, down_wgrad, out_swapped = tie(out_got, carried, down_wgrad, out_swapped)
     for d in range(half_way - 2, 1, -1):
-        out_got = next_hop(mlp, 2 * d - 2, out_got)
+        out_got = next_hop(early, 2 * d - 2, out_got)
     qkv_grad = attend_back(1, *operands, carried)
     out_got, qkv_grad, out_keep = tie(out_got, qkv_grad, out_keep)
 
@@ -1096,7 +1109,7 @@
     far = mm(far, w_qkv, NT).astype(bf16)
     in_got = first_hop(far)
     qkv_grad, far, out_got, out_keep = tie(qkv_grad, far, out_got, out_keep)
-    out_got = next_hop(mlp, 0, out_got)
+    out_got = next_hop(early, 0, out_got)
     out_terms = over_chips(out_keep, out_swapped)
     first_grad = mm(qkv_grad, w_qkv, NT).astype(bf16)
     q_send, q_keep, s_send, s_keep = qkv_wgrad_parts(
@@ -1122,7 +1135,7 @@
             out_wgrad = total_of(*out_terms).astype(bf16)
             out_wgrad = lax.psum_scatter(out_wgrad, "tensor", scatter_dimension=0, tiled=True)
             small, query_wgrad = total_of(*small), total_of(*query_wgrad)
-            layer_out = layer_output(middle, mlp, groups - 2, out_got)
+            layer_out = layer_output(middle, late, 2, out_got)
             continue
         in_got = send_on(in_sums)
         if d == half_way - 2:

time: 631 us -> 638 us (1.011)
  starting transfers between devices: 68.1 us -> 74.8 us
    ppermute x20, waiting for transfers between devices: 57.6 us -> 12.6 us  [back(): return lax.ppermute(array, 'tensor', behind)]
    ppermute x20, waiting for transfers between devices: 45 us -> 72.8 us  [onward(): return lax.ppermute(array, 'tensor', ahead)]
    ppermute x3, waiting for transfers between devices: 21.1 us -> 34.5 us  [over_chips(): arriving.append(lax.ppermute(go, 'dp', to))]
    dot_general x6 -> x7, matrix products: 62.7 us -> 65 us  [mm(): return lax.dot_general(left, right, dims, preferred_element_type=f32)]
    unnamed x92 -> x86, local copies, waits for them, and re-layouts: 15.5 us -> 15.7 us
  transfers between devices with their start and end apart: 55 -> 55, of which waited for: 23 -> 23; matrix products, arithmetic and copies ran while one was open for 16% -> 16% of each run, Pallas kernels for 40% -> 39%
where the time goes in v6:
time: 638 us; the launch traced here: 628 us
  Pallas kernels  271 us (42%)
  waiting for transfers between devices  147 us (23%)
  starting transfers between devices  74.8 us (12%)
  matrix products  65 us (10%)
  local copies, waits for them, and re-layouts  30.1 us (5%)
  other arithmetic  23.7 us (4%)
  between operations  16 us (3%)
    pallas_call x5, Pallas kernels, swiglu(): pl.pallas_call(functools.partial(swiglu_kernel, len(pieces), tuple(member...  78.9 us
    ppermute x20, waiting for transfers between devices, onward(): return lax.ppermute(array, 'tensor', ahead)  72.8 us
    dot_general x7, matrix products, mm(): return lax.dot_general(left, right, dims, preferred_element_type=f32)  65 us
    pallas_call x18, Pallas kernels, ring_add(): pl.pallas_call(functools.partial(ring_add_kernel, first), grid_spec=pltpu...  55.5 us
    pallas_call x2, Pallas kernels, attend_back(): pl.pallas_call(functools.partial(attend_back_kernel, heads, start), grid=...  40.8 us
    ppermute x3, waiting for transfers between devices, over_chips(): arriving.append(lax.ppermute(go, 'dp', to))  34.5 us
    ppermute x20, starting transfers between devices, onward(): return lax.ppermute(array, 'tensor', ahead)  31.2 us
    all_to_all x4, waiting for transfers between devices, exchange(): return lax.all_to_all(array, 'tensor', 0, 0, tiled=True)  27.2 us
  transfers between devices with their start and end apart: 55, of which 23 were waited for; matrix products, arithmetic and copies ran while one was open for 16% of the time, Pallas kernels for 39%

profile of v6, /device:TPU:0, one launch (start us, length us, event | category | flops | bytes accessed | tf_op | source)
XLA Modules:
  0.0 628.1 jit_solution(15822557313587600033)
XLA Ops:
  9.2 3.0 collective-permute-start
  14.3 6.3 all-to-all-start
  22.0 6.3 norm_and_query.2
  31.0 6.3 norm_and_query.3
  39.8 7.2 %keys_and_values.1 = (bf16[2048,128]{1,0:T(8,128)(2,1)}, bf16[128,2048]{1,0:T(8,128)(2,1)}, bf16[2048,128]{1,0:T(8,128)(2,1)}, bf16[128,2048]{1,0:T(8,128)(2,1)}) custom-call(s32[1]{0:T(128)S(6)} %copy.94.length_ref, bf16[2048,2048]{1,0:T(8,128)(2,1)} %get-tuple-element.203.normed_ref, bf16[2048,128]{1,0:T(8,128)(2,1)} %bitcast.39, ...), custom_call_target="tpu_custom_call" | custom-call | flops 1073741824 | bytes 8388608 | tf_op jit(solution)/shard_map/keys_and_values/pallas_call | solution.py:147
  50.7 11.3 %attend.2 = (bf16[2048,256]{1,0:T(8,128)(2,1)}, f32[8,2048]{1,0:T(8,128)}) custom-call(bf16[2048,256]{1,0:T(8,128)(2,1)} %get-tuple-element.207.q_ref, bf16[2048,128]{1,0:T(8,128)(2,1)} %get-tuple-element.208.k_ref, bf16[128,2048]{1,0:T(8,128)(2,1)} %get-tuple-element.209.vt_ref), custom_call_target="tpu_custom_call" | custom-call | flops 4294967296 | bytes 1048576 | tf_op jit(solution)/shard_map/attend/pallas_call | solution.py:253
  62.0 2.2 collective-permute-start.6
  64.3 13.3 %attend.3 = (bf16[2048,256]{1,0:T(8,128)(2,1)}, f32[8,2048]{1,0:T(8,128)}) custom-call(bf16[2048,256]{1,0:T(8,128)(2,1)} %get-tuple-element.207.q_ref, bf16[2048,128]{1,0:T(8,128)(2,1)} %get-tuple-element.208.k_ref, bf16[128,2048]{1,0:T(8,128)(2,1)} %get-tuple-element.209.vt_ref, ...), custom_call_target="tpu_custom_call", output_to_operand_aliasing={{0}: (3, {}), {1}: (4, {})} | custom-call | flops 4294967296 | bytes 1048576 | tf_op jit(solution)/shard_map/attend/pallas_call | solution.py:253
  80.8 5.8 all-to-all-start.1
  88.4 24.5 %all-to-all-done.1.o_ref = bf16[8,256,256]{2,1,0:T(8,128)(2,1)S(1)} async-done(((bf16[8,256,256]{2,1,0:T(8,128)(2,1)}), bf16[8,256,256]{2,1,0:T(8,128)(2,1)S(1)}, u32[]{:S(2)}, u32[]{:S(2)}) %all-to-all-start.1) | async-done | bytes 1048608 | tf_op jit(solution)/shard_map/all_to_all | solution.py:965
  114.0 9.2 %out_project_and_norm.1 = (f32[256,2048]{1,0:T(8,128)}, bf16[256,2048]{1,0:T(8,128)(2,1)}) custom-call(s32[11]{0:T(128)} %pad_add_fusion.ids_ref, bf16[8,256,256]{2,1,0:T(8,128)(2,1)} %copy-done.6, bf16[2048,1024]{1,0:T(8,128)(2,1)} %constant_dynamic-update-slice_fusion.mine_ref, bf16[2048,1024]{1,0:T(8,128)(2,1)} %collective-permute-done.8.other_ref, ...), custom_call_target="tpu_custom_call" | custom-call | flops 2147483648 | bytes 8388608 | tf_op jit(solution)/shard_map/out_project_and_norm/pallas_call | solution.py:462
  125.4 12.1 %swiglu_rows.5 = (bf16[2048,2048]{1,0:T(8,128)(2,1)}, bf16[2048,2048]{1,0:T(8,128)(2,1)}, bf16[2048,1024]{1,0:T(8,128)(2,1)}, bf16[2048,1024]{1,0:T(8,128)(2,1)}...) custom-call(s32[11]{0:T(128)} %pad_add_fusion.ids_ref, bf16[256,2048]{1,0:T(8,128)(2,1)} %get-tuple-element.220.refs_0_, ...), custom_call_target="tpu_custom_call" | custom-call | flops 6442450944 | bytes 20971520 | tf_op jit(solution)/shard_map/swiglu_rows/pallas_call | solution.py:861
  137.5 10.3 %collective-permute-done.9.refs_0_ = bf16[256,2048]{1,0:T(8,128)(2,1)S(1)} collective-permute-done((bf16[256,2048]{1,0:T(8,128)(2,1)}, bf16[256,2048]{1,0:T(8,128)(2,1)S(1)}, u32[]{:S(2)}, u32[]{:S(2)}) %collective-permute-start.9) | collective-permute-done | bytes 1048608 | tf_op jit(solution)/shard_map/ppermute | solution.py:968
  151.2 18.4 %swiglu_rows.6 = (bf16[2048,2048]{1,0:T(8,128)(2,1)}, bf16[2048,2048]{1,0:T(8,128)(2,1)}, bf16[2048,1024]{1,0:T(8,128)(2,1)}, bf16[2048,1024]{1,0:T(8,128)(2,1)}...) custom-call(s32[11]{0:T(128)} %pad_add_fusion.ids_ref, ...), custom_call_target="tpu_custom_call", output_to_operand_aliasing={{0}: (7, {}), {1}: (8, {}), {2}: (9, {}), {3}: (10, {}), {4... | custom-call | flops 12884901888 | bytes 29360128 | tf_op jit(solution)/shard_map/swiglu_rows/pallas_call | solution.py:861
  169.6 2.8 collective-permute-done.11.refs_0_
  176.2 18.4 %swiglu_rows.7 = (bf16[2048,2048]{1,0:T(8,128)(2,1)}, bf16[2048,2048]{1,0:T(8,128)(2,1)}, bf16[2048,1024]{1,0:T(8,128)(2,1)}, bf16[2048,1024]{1,0:T(8,128)(2,1)}...) custom-call(s32[11]{0:T(128)} %pad_add_fusion.ids_ref, ...), custom_call_target="tpu_custom_call", output_to_operand_aliasing={{0}: (7, {}), {1}: (8, {}), {2}: (9, {}), {3}: (10, {}), {4... | custom-call | flops 12884901888 | bytes 29360128 | tf_op jit(solution)/shard_map/swiglu_rows/pallas_call | solution.py:861
  194.6 2.2 collective-permute-done.13.refs_0_
  196.7 2.3 collective-permute-done.14.refs_1_
  202.3 7.7 %convolution_convert_fusion.3.term_ref = bf16[1024,2048]{1,0:T(8,128)(2,1)} fusion(bf16[1024,2048]{1,0:T(8,128)(2,1)S(1)} %copy-done.1, bf16[2048,1024]{1,0:T(8,128)(2,1)} %get-tuple-element.267.refs_8_), kind=kOutput, calls=%fused_computation.6 | convolution fusion | flops 4297064448 | bytes 10485760 | tf_op jit(solution)/shard_map/dot_general | solution.py:32
  211.5 11.6 %swiglu_rows.8 = (bf16[2048,2048]{1,0:T(8,128)(2,1)}, bf16[2048,2048]{1,0:T(8,128)(2,1)}, bf16[2048,1024]{1,0:T(8,128)(2,1)}, bf16[2048,1024]{1,0:T(8,128)(2,1)}...) custom-call(s32[11]{0:T(128)} %pad_add_fusion.ids_ref, ...), custom_call_target="tpu_custom_call", output_to_operand_aliasing={{0}: (7, {}), {1}: (8, {}), {2}: (9, {}), {3}: (10, {}), {4... | custom-call | flops 6442450944 | bytes 20971520 | tf_op jit(solution)/shard_map/swiglu_rows/pallas_call | solution.py:861
  226.9 18.4 %swiglu_rows.9 = (bf16[2048,2048]{1,0:T(8,128)(2,1)}, bf16[2048,2048]{1,0:T(8,128)(2,1)}, bf16[2048,1024]{1,0:T(8,128)(2,1)}, bf16[2048,1024]{1,0:T(8,128)(2,1)}...) custom-call(s32[11]{0:T(128)} %pad_add_fusion.ids_ref, ...), custom_call_target="tpu_custom_call", output_to_operand_aliasing={{0}: (7, {}), {1}: (8, {}), {2}: (9, {}), {3}: (10, {}), {4... | custom-call | flops 12884901888 | bytes 29360128 | tf_op jit(solution)/shard_map/swiglu_rows/pallas_call | solution.py:861
  246.1 2.9 ring_add.18
  249.0 3.0 ring_add.19
  256.0 13.1 %convolution_convert_fusion.1 = bf16[1024,2048]{1,0:T(8,128)(2,1)} fusion(bf16[2048,1024]{1,0:T(8,128)(2,1)S(1)} %copy-done, bf16[2048,2048]{1,0:T(8,128)(2,1)} %get-tuple-element.290), kind=kOutput, calls=%fused_computation.4 | convolution fusion | flops 8592031744 | bytes 16777216 | tf_op jit(solution)/shard_map/dot_general | solution.py:32
  269.1 5.1 collective-permute-done.19.got_ref
  275.3 3.2 ring_add.20
  278.5 3.1 ring_add.21
  283.8 14.6 %convolution_convert_fusion.5 = bf16[2048,1024]{1,0:T(8,128)(2,1)} fusion(bf16[2048,2048]{1,0:T(8,128)(2,1)} %get-tuple-element.304, bf16[2048,1024]{1,0:T(8,128)(2,1)} %get-tuple-element.298), kind=kOutput, calls=%fused_computation.8 | convolution fusion | flops 8592031744 | bytes 16777216 | tf_op jit(solution)/shard_map/dot_general | solution.py:32
  298.4 6.9 %convolution_convert_fusion.2.term_ref.own_ref = bf16[1024,2048]{1,0:T(8,128)(2,1)S(1)} fusion(bf16[1024,1024]{1,0:T(8,128)(2,1)S(1)} %slice.101, bf16[1024,2048]{1,0:T(8,128)(2,1)} %refs_5_.7), kind=kOutput, calls=%fused_computation.5 | convolution fusion | flops 4297064448 | bytes 10485760 | tf_op jit(solution)/shard_map/dot_general | solution.py:32
  309.2 3.1 ring_add.22
  312.3 3.3 ring_add.23
  317.6 14.1 %convolution_convert_fusion.4 = bf16[2048,1024]{1,0:T(8,128)(2,1)} fusion(bf16[2048,2048]{1,0:T(8,128)(2,1)} %get-tuple-element.304, bf16[2048,1024]{1,0:T(8,128)(2,1)} %get-tuple-element.305), kind=kOutput, calls=%fused_computation.7 | convolution fusion | flops 8592031744 | bytes 16777216 | tf_op jit(solution)/shard_map/dot_general | solution.py:32
  331.7 6.0 collective-permute-done.23.up_ref
  340.6 10.7 %norm_back_and_project.1 = (f32[256,2048]{1,0:T(8,128)}, bf16[256,2048]{1,0:T(8,128)(2,1)}, f32[1,2048]{1,0:T(1,128)}, bf16[8,256,256]{2,1,0:T(8,128)(2,1)}) custom-call(s32[11]{0:T(128)} %pad_add_fusion.ids_ref, bf16[256,2048]{1,0:T(8,128)(2,1)} %get-tuple-element.312.own_ref, bf16[256,2048]{1,0:T(8,128)(2,1)} %copy-done.20, bf16[256,2048]{1,0:T(8,128)(2,1)} %copy-done.21, ...), custom_call_target="tpu_custom_call" | custom-call | flops 2147483648 | bytes 8388608 | tf_op jit(solution)/shard_map/norm_back_and_project/pallas_call | solution.py:539
  351.9 9.8 %all-to-all-start.2 = ((bf16[8,256,256]{2,1,0:T(8,128)(2,1)}), bf16[8,256,256]{2,1,0:T(8,128)(2,1)S(1)}, u32[]{:S(2)}, u32[]{:S(2)}) async-start(bf16[8,256,256]{2,1,0:T(8,128)(2,1)} %get-tuple-element.318), calls=%async_computation.2 | async-start | bytes 2097152 | tf_op jit(solution)/shard_map/all_to_all | solution.py:965
  361.7 2.9 ring_add.24
  364.6 2.9 ring_add.25
  367.5 7.9 %out_weight_grad.1 = (bf16[2,2048,512]{2,1,0:T(8,128)(2,1)}, bf16[2,2048,512]{2,1,0:T(8,128)(2,1)}) custom-call(s32[11]{0:T(128)} %pad_add_fusion.ids_ref, bf16[8,256,256]{2,1,0:T(8,128)(2,1)} %copy-done.6, bf16[256,2048]{1,0:T(8,128)(2,1)} %get-tuple-element.319.da_ref), custom_call_target="tpu_custom_call" | custom-call | flops 2147483648 | bytes 8388608 | tf_op jit(solution)/shard_map/out_weight_grad/pallas_call | solution.py:638
  375.4 2.6 all-to-all-done.2
  383.7 17.6 %attend_back.2 = (bf16[1280,256]{1,0:T(8,128)(2,1)}, f32[2048,128]{1,0:T(8,128)}, f32[2048,128]{1,0:T(8,128)}) custom-call(bf16[2048,256]{1,0:T(8,128)(2,1)} %get-tuple-element.207.q_ref, bf16[2048,256]{1,0:T(8,128)(2,1)} %bitcast.43, bf16[2048,256]{1,0:T(8,128)(2,1)} %get-tuple-element.217.o_ref, f32[8,2048]{1,0:T(8,128)} %get-tuple-element.328.lse_ref, ...), custom_call_target="tpu_custom_call" | custom-call | flops 10737418240 | bytes 5242880 | tf_op jit(solution)/shard_map/attend_back/pallas_call | solution.py:397
  401.2 2.8 collective-permute-done.27.got_ref
  405.0 3.1 ring_add.26
  409.1 3.2 ring_add.27
  416.0 23.2 %attend_back.3.grad_ref = bf16[2048,384]{1,0:T(8,128)(2,1)} custom-call(bf16[2048,256]{1,0:T(8,128)(2,1)} %get-tuple-element.207.q_ref, bf16[2048,256]{1,0:T(8,128)(2,1)} %bitcast.44, bf16[2048,256]{1,0:T(8,128)(2,1)} %get-tuple-element.217.o_ref, f32[8,2048]{1,0:T(8,128)} %get-tuple-element.328.lse_ref, bf16[2048,128]{1,0:T(8,128)(2,1)} %get-tuple-element.208.k_ref, ...), custom_call_target="tpu_custom_call" | custom-call | flops 10737418240 | bytes 5242880 | tf_op jit(solution)/shard_map/attend_back/pallas_call | solution.py:397
  444.5 3.1 ring_add.28
  448.6 3.2 ring_add.29
  452.8 4.1 fusion.1
  456.9 6.8 %convolution_convert_fusion.term_ref.own_ref = bf16[2048,2048]{1,0:T(8,128)(2,1)} fusion(bf16[2048,384]{1,0:T(8,128)(2,1)S(1)} %copy-done.8, bf16[2048,128]{1,0:T(8,128)(2,1)S(1)} %bitcast.42, bf16[2048,256]{1,0:T(8,128)(2,1)S(1)} %copy-done.3), kind=kOutput, calls=%fused_computation | convolution fusion | flops 3228565504 | bytes 11534336 | tf_op jit(solution)/shard_map/dot_general | solution.py:32
  465.2 11.8 %projection_weight_grads.1 = (bf16[2,512,256]{2,1,0:T(8,128)(2,1)}, bf16[2,512,256]{2,1,0:T(8,128)(2,1)}, f32[2,512,256]{2,1,0:T(8,128)}, f32[2,512,256]{2,1,0:T(8,128)}) custom-call(s32[11]{0:T(128)} %pad_add_fusion.ids_ref, bf16[2048,2048]{1,0:T(8,128)(2,1)} %get-tuple-element.203.normed_ref, bf16[2048,384]{1,0:T(8,128)(2,1)} %attend_back.3.grad_ref, ...), custom_call_target="tpu_custom_call" | custom-call | flops 3221225472 | bytes 12582912 | tf_op jit(solution)/shard_map/projection_weight_grads/pallas_call | solution.py:698
  478.1 2.9 ring_add.30
  481.7 3.0 ring_add.31
  491.0 34.5 %collective-permute-done.41 = bf16[512,256]{1,0:T(8,128)(2,1)S(1)} collective-permute-done((bf16[512,256]{1,0:T(8,128)(2,1)S(1)}, bf16[512,256]{1,0:T(8,128)(2,1)S(1)}, u32[]{:S(2)}, u32[]{:S(2)}) %collective-permute-start.41) | collective-permute-done | bytes 262176 | tf_op jit(solution)/shard_map/ppermute | solution.py:908
  525.5 4.4 fusion
  530.0 3.1 ring_add.32
  534.1 3.2 ring_add.33
  540.3 3.5 all-to-all-start.3
  543.8 4.3 layer_output.1
  548.1 27.7 %collective-permute-done.43.got_ref = bf16[256,2048]{1,0:T(8,128)(2,1)S(1)} collective-permute-done((bf16[256,2048]{1,0:T(8,128)(2,1)}, bf16[256,2048]{1,0:T(8,128)(2,1)S(1)}, u32[]{:S(2)}, u32[]{:S(2)}) %collective-permute-start.43) | collective-permute-done | bytes 1048608 | tf_op jit(solution)/shard_map/ppermute | solution.py:968
  576.8 3.1 ring_add.34
  580.0 3.8 collective-permute-start.45
  583.7 3.2 ring_add.35
  595.3 15.8 %collective-permute-done.45.up_ref = bf16[256,2048]{1,0:T(8,128)(2,1)} collective-permute-done((bf16[256,2048]{1,0:T(8,128)(2,1)}, bf16[256,2048]{1,0:T(8,128)(2,1)}, u32[]{:S(2)}, u32[]{:S(2)}) %collective-permute-start.45) | collective-permute-done | bytes 1048608 | tf_op jit(solution)/shard_map/ppermute | solution.py:968
  611.1 2.4 collective-permute-done.46.down_ref
  613.4 5.9 input_grad.1
  (219 shorter events, 97.9 us)
Async XLA Ops:
  9.2 19.0 %collective-permute-start = (bf16[256,1024]{1,0:T(8,128)(2,1)S(1)}, bf16[256,1024]{1,0:T(8,128)(2,1)S(1)}, u32[]{:S(2)}, u32[]{:S(2)}) collective-permute-start(bf16[256,1024]{1,0:T(8,128)(2,1)S(1)} %get-tuple-element.386), channel_id=1, source_target_pairs={{0,1},{1,3},{3,5},{5,7},{7,6},{6,4},{4,2},{2,0},{8,9},{9,11},{11,1... | collective-permute-start | bytes 1572872 | tf_op jit(solution)/shard_map/ppermute | solution.py:968
  12.2 16.1 %collective-permute-start.1 = (bf16[256,1024]{1,0:T(8,128)(2,1)S(1)}, bf16[256,1024]{1,0:T(8,128)(2,1)S(1)}, u32[]{:S(2)}, u32[]{:S(2)}) collective-permute-start(bf16[256,1024]{1,0:T(8,128)(2,1)S(1)} %get-tuple-element.386), channel_id=1, source_target_pairs={{1,0},{3,1},{5,3},{7,5},{6,7},{4,6},{2,4},{0,2},{9,8},{11,9},{13,1... | collective-permute-start | bytes 1572872 | tf_op jit(solution)/shard_map/ppermute | solution.py:971
  14.3 24.7 %all-to-all-start = ((bf16[8,256,128]{2,1,0:T(8,128)(2,1)}), bf16[8,256,128]{2,1,0:T(8,128)(2,1)S(1)}, u32[]{:S(2)}, u32[]{:S(2)}) async-start(bf16[8,256,128]{2,1,0:T(8,128)(2,1)} %pick_heads.1), calls=%async_computation | async-start | bytes 1048576 | tf_op jit(solution)/shard_map/all_to_all | solution.py:965
  28.2 18.7 %collective-permute-start.2 = (bf16[256,1024]{1,0:T(8,128)(2,1)S(1)}, bf16[256,1024]{1,0:T(8,128)(2,1)S(1)}, u32[]{:S(2)}, u32[]{:S(2)}) collective-permute-start(bf16[256,1024]{1,0:T(8,128)(2,1)S(1)} %collective-permute-done), channel_id=1, source_target_pairs={{0,1},{1,3},{3,5},{5,7},{7,6},{6,4},{4,2},{2,0},{8,9},{9,11},{11,1... | collective-permute-start | bytes 1572872 | tf_op jit(solution)/shard_map/ppermute | solution.py:968
  30.3 16.6 %collective-permute-start.3 = (bf16[256,1024]{1,0:T(8,128)(2,1)S(1)}, bf16[256,1024]{1,0:T(8,128)(2,1)S(1)}, u32[]{:S(2)}, u32[]{:S(2)}) collective-permute-start(bf16[256,1024]{1,0:T(8,128)(2,1)S(1)} %collective-permute-done.1), channel_id=1, source_target_pairs={{1,0},{3,1},{5,3},{7,5},{6,7},{4,6},{2,4},{0,2},{9,8},{11,9},{13,1... | collective-permute-start | bytes 1572872 | tf_op jit(solution)/shard_map/ppermute | solution.py:971
  47.0 15.0 %collective-permute-start.4 = (bf16[256,1024]{1,0:T(8,128)(2,1)S(1)}, bf16[256,1024]{1,0:T(8,128)(2,1)S(1)}, u32[]{:S(2)}, u32[]{:S(2)}) collective-permute-start(bf16[256,1024]{1,0:T(8,128)(2,1)S(1)} %collective-permute-done.2), channel_id=1, source_target_pairs={{0,1},{1,3},{3,5},{5,7},{7,6},{6,4},{4,2},{2,0},{8,9},{9,11},{11,1... | collective-permute-start | bytes 1572872 | tf_op jit(solution)/shard_map/ppermute | solution.py:968
  49.0 13.0 %collective-permute-start.5 = (bf16[256,1024]{1,0:T(8,128)(2,1)S(1)}, bf16[256,1024]{1,0:T(8,128)(2,1)S(1)}, u32[]{:S(2)}, u32[]{:S(2)}) collective-permute-start(bf16[256,1024]{1,0:T(8,128)(2,1)S(1)} %collective-permute-done.3), channel_id=1, source_target_pairs={{1,0},{3,1},{5,3},{7,5},{6,7},{4,6},{2,4},{0,2},{9,8},{11,9},{13,1... | collective-permute-start | bytes 1572872 | tf_op jit(solution)/shard_map/ppermute | solution.py:971
  62.0 17.3 %collective-permute-start.6 = (bf16[128,1024]{1,0:T(8,128)(2,1)S(1)}, bf16[128,1024]{1,0:T(8,128)(2,1)S(1)}, u32[]{:S(2)}, u32[]{:S(2)}) collective-permute-start(bf16[128,1024]{1,0:T(8,128)(2,1)S(1)} %slice.94), channel_id=1, source_target_pairs={{0,1},{1,3},{3,5},{5,7},{7,6},{6,4},{4,2},{2,0},{8,9},{9,11},{11,1... | collective-permute-start | bytes 786440 | tf_op jit(solution)/shard_map/ppermute | solution.py:968
  64.2 15.1 %collective-permute-start.7 = (bf16[128,1024]{1,0:T(8,128)(2,1)S(1)}, bf16[128,1024]{1,0:T(8,128)(2,1)S(1)}, u32[]{:S(2)}, u32[]{:S(2)}) collective-permute-start(bf16[128,1024]{1,0:T(8,128)(2,1)S(1)} %slice.95), channel_id=1, source_target_pairs={{1,0},{3,1},{5,3},{7,5},{6,7},{4,6},{2,4},{0,2},{9,8},{11,9},{13,1... | collective-permute-start | bytes 786440 | tf_op jit(solution)/shard_map/ppermute | solution.py:971
  80.8 32.2 %collective-permute-start.8 = (bf16[2048,1024]{1,0:T(8,128)(2,1)}, bf16[2048,1024]{1,0:T(8,128)(2,1)}, u32[]{:S(2)}, u32[]{:S(2)}) collective-permute-start(bf16[2048,1024]{1,0:T(8,128)(2,1)} %constant_dynamic-update-slice_fusion.mine_ref), channel_id=1, source_target_pairs={{0,8},{8,0},{16,24},{24,16},{1,9},{9,1},{17,25},{25,17},{2,10},{10... | collective-permute-start | bytes 12582920 | tf_op jit(solution)/shard_map/ppermute | solution.py:1001
  80.8 32.2 %all-to-all-start.1 = ((bf16[8,256,256]{2,1,0:T(8,128)(2,1)}), bf16[8,256,256]{2,1,0:T(8,128)(2,1)S(1)}, u32[]{:S(2)}, u32[]{:S(2)}) async-start(bf16[8,256,256]{2,1,0:T(8,128)(2,1)} %bitcast.45), calls=%async_computation.1 | async-start | bytes 2097152 | tf_op jit(solution)/shard_map/all_to_all | solution.py:965
  86.5 318.1 %reduce-scatter.5.cloned.1.call-start = ((), (), s32[]{:S(2)}) async-start(), calls=%async_computation.8 | async-start | bytes 5242880 | tf_op jit(solution)/shard_map/reduce_scatter | solution.py:1082
  123.2 24.7 %collective-permute-start.9 = (bf16[256,2048]{1,0:T(8,128)(2,1)}, bf16[256,2048]{1,0:T(8,128)(2,1)S(1)}, u32[]{:S(2)}, u32[]{:S(2)}) collective-permute-start(bf16[256,2048]{1,0:T(8,128)(2,1)} %get-tuple-element.220.refs_0_), channel_id=1, source_target_pairs={{0,1},{1,3},{3,5},{5,7},{7,6},{6,4},{4,2},{2,0},{8,9},{9,11},{11,1... | collective-permute-start | bytes 3145736 | tf_op jit(solution)/shard_map/ppermute | solution.py:968
  124.6 24.6 %collective-permute-start.10 = (bf16[256,2048]{1,0:T(8,128)(2,1)}, bf16[256,2048]{1,0:T(8,128)(2,1)S(1)}, u32[]{:S(2)}, u32[]{:S(2)}) collective-permute-start(bf16[256,2048]{1,0:T(8,128)(2,1)} %get-tuple-element.220.refs_0_), channel_id=1, source_target_pairs={{1,0},{3,1},{5,3},{7,5},{6,7},{4,6},{2,4},{0,2},{9,8},{11,9},{13,1... | collective-permute-start | bytes 3145736 | tf_op jit(solution)/shard_map/ppermute | solution.py:971
  149.2 23.3 %collective-permute-start.11 = (bf16[256,2048]{1,0:T(8,128)(2,1)S(1)}, bf16[256,2048]{1,0:T(8,128)(2,1)S(1)}, u32[]{:S(2)}, u32[]{:S(2)}) collective-permute-start(bf16[256,2048]{1,0:T(8,128)(2,1)S(1)} %collective-permute-done.9.refs_0_), channel_id=1, source_target_pairs={{0,1},{1,3},{3,5},{5,7},{7,6},{6,4},{4,2},{2,0},{8,9},{9,11},{11,1... | collective-permute-start | bytes 3145736 | tf_op jit(solution)/shard_map/ppermute | solution.py:968
  149.4 23.5 %collective-permute-start.12 = (bf16[256,2048]{1,0:T(8,128)(2,1)S(1)}, bf16[256,2048]{1,0:T(8,128)(2,1)S(1)}, u32[]{:S(2)}, u32[]{:S(2)}) collective-permute-start(bf16[256,2048]{1,0:T(8,128)(2,1)S(1)} %collective-permute-done.10.refs_1_), channel_id=1, source_target_pairs={{1,0},{3,1},{5,3},{7,5},{6,7},{4,6},{2,4},{0,2},{9,8},{11,9},{13,1... | collective-permute-start | bytes 3145736 | tf_op jit(solution)/shard_map/ppermute | solution.py:971
  174.0 28.3 %copy-start.1 = (bf16[1024,2048]{1,0:T(8,128)(2,1)S(1)}, bf16[1024,2048]{1,0:T(8,128)(2,1)}, u32[]{:S(2)}) copy-start(bf16[1024,2048]{1,0:T(8,128)(2,1)} %refs_5_.7) | copy-start | bytes 12582916
  174.0 22.8 %collective-permute-start.13 = (bf16[256,2048]{1,0:T(8,128)(2,1)}, bf16[256,2048]{1,0:T(8,128)(2,1)S(1)}, u32[]{:S(2)}, u32[]{:S(2)}) collective-permute-start(bf16[256,2048]{1,0:T(8,128)(2,1)} %copy-done.14), channel_id=1, source_target_pairs={{0,1},{1,3},{3,5},{5,7},{7,6},{6,4},{4,2},{2,0},{8,9},{9,11},{11,1... | collective-permute-start | bytes 3145736 | tf_op jit(solution)/shard_map/ppermute | solution.py:968
  175.7 23.3 %collective-permute-start.14 = (bf16[256,2048]{1,0:T(8,128)(2,1)}, bf16[256,2048]{1,0:T(8,128)(2,1)}, u32[]{:S(2)}, u32[]{:S(2)}) collective-permute-start(bf16[256,2048]{1,0:T(8,128)(2,1)} %copy-done.15), channel_id=1, source_target_pairs={{1,0},{3,1},{5,3},{7,5},{6,7},{4,6},{2,4},{0,2},{9,8},{11,9},{13,1... | collective-permute-start | bytes 3145736 | tf_op jit(solution)/shard_map/ppermute | solution.py:971
  196.7 13.2 %copy-start.7 = (bf16[256,2048]{1,0:T(8,128)(2,1)}, bf16[256,2048]{1,0:T(8,128)(2,1)S(1)}, u32[]{:S(2)}) copy-start(bf16[256,2048]{1,0:T(8,128)(2,1)S(1)} %collective-permute-done.13.refs_0_) | copy-start | bytes 3145732
  199.0 10.9 %collective-permute-start.15 = (bf16[128,2048]{1,0:T(8,128)(2,1)S(1)}, bf16[128,2048]{1,0:T(8,128)(2,1)S(1)}, u32[]{:S(2)}, u32[]{:S(2)}) collective-permute-start(bf16[128,2048]{1,0:T(8,128)(2,1)S(1)} %slice.96), channel_id=1, source_target_pairs={{0,1},{1,3},{3,5},{5,7},{7,6},{6,4},{4,2},{2,0},{8,9},{9,11},{11,1... | collective-permute-start | bytes 1572872 | tf_op jit(solution)/shard_map/ppermute | solution.py:968
  201.3 10.2 %collective-permute-start.16 = (bf16[128,2048]{1,0:T(8,128)(2,1)S(1)}, bf16[128,2048]{1,0:T(8,128)(2,1)}, u32[]{:S(2)}, u32[]{:S(2)}) collective-permute-start(bf16[128,2048]{1,0:T(8,128)(2,1)S(1)} %slice.97), channel_id=1, source_target_pairs={{1,0},{3,1},{5,3},{7,5},{6,7},{4,6},{2,4},{0,2},{9,8},{11,9},{13,1... | collective-permute-start | bytes 1572872 | tf_op jit(solution)/shard_map/ppermute | solution.py:971
  224.4 20.9 %collective-permute-start.17 = (bf16[128,2048]{1,0:T(8,128)(2,1)S(1)}, bf16[128,2048]{1,0:T(8,128)(2,1)S(1)}, u32[]{:S(2)}, u32[]{:S(2)}) collective-permute-start(bf16[128,2048]{1,0:T(8,128)(2,1)S(1)} %get-tuple-element.392), channel_id=1, source_target_pairs={{0,1},{1,3},{3,5},{5,7},{7,6},{6,4},{4,2},{2,0},{8,9},{9,11},{11,1... | collective-permute-start | bytes 1572872 | tf_op jit(solution)/shard_map/ppermute | solution.py:968
  226.1 19.2 %collective-permute-start.18 = (bf16[128,2048]{1,0:T(8,128)(2,1)S(1)}, bf16[128,2048]{1,0:T(8,128)(2,1)S(1)}, u32[]{:S(2)}, u32[]{:S(2)}) collective-permute-start(bf16[128,2048]{1,0:T(8,128)(2,1)S(1)} %get-tuple-element.391), channel_id=1, source_target_pairs={{1,0},{3,1},{5,3},{7,5},{6,7},{4,6},{2,4},{0,2},{9,8},{11,9},{13,1... | collective-permute-start | bytes 1572872 | tf_op jit(solution)/shard_map/ppermute | solution.py:971
  253.9 20.3 %collective-permute-start.19 = (bf16[256,2048]{1,0:T(8,128)(2,1)}, bf16[256,2048]{1,0:T(8,128)(2,1)S(1)}, u32[]{:S(2)}, u32[]{:S(2)}) collective-permute-start(bf16[256,2048]{1,0:T(8,128)(2,1)} %ring_add.18), channel_id=1, source_target_pairs={{0,1},{1,3},{3,5},{5,7},{7,6},{6,4},{4,2},{2,0},{8,9},{9,11},{11,1... | collective-permute-start | bytes 3145736 | tf_op jit(solution)/shard_map/ppermute | solution.py:968
  255.4 19.8 %collective-permute-start.20 = (bf16[256,2048]{1,0:T(8,128)(2,1)}, bf16[256,2048]{1,0:T(8,128)(2,1)}, u32[]{:S(2)}, u32[]{:S(2)}) collective-permute-start(bf16[256,2048]{1,0:T(8,128)(2,1)} %ring_add.19), channel_id=1, source_target_pairs={{1,0},{3,1},{5,3},{7,5},{6,7},{4,6},{2,4},{0,2},{9,8},{11,9},{13,1... | collective-permute-start | bytes 3145736 | tf_op jit(solution)/shard_map/ppermute | solution.py:971
  275.2 201.7 %reduce-scatter.7.cloned.1.call-start = ((), (), s32[]{:S(2)}) async-start(), calls=%async_computation.9 | async-start | bytes 5242880 | tf_op jit(solution)/shard_map/reduce_scatter | solution.py:1082
  281.6 26.6 %collective-permute-start.21 = (bf16[256,2048]{1,0:T(8,128)(2,1)}, bf16[256,2048]{1,0:T(8,128)(2,1)S(1)}, u32[]{:S(2)}, u32[]{:S(2)}) collective-permute-start(bf16[256,2048]{1,0:T(8,128)(2,1)} %ring_add.20), channel_id=1, source_target_pairs={{0,1},{1,3},{3,5},{5,7},{7,6},{6,4},{4,2},{2,0},{8,9},{9,11},{11,1... | collective-permute-start | bytes 3145736 | tf_op jit(solution)/shard_map/ppermute | solution.py:968
  283.0 25.3 %collective-permute-start.22 = (bf16[256,2048]{1,0:T(8,128)(2,1)}, bf16[256,2048]{1,0:T(8,128)(2,1)}, u32[]{:S(2)}, u32[]{:S(2)}) collective-permute-start(bf16[256,2048]{1,0:T(8,128)(2,1)} %ring_add.21), channel_id=1, source_target_pairs={{1,0},{3,1},{5,3},{7,5},{6,7},{4,6},{2,4},{0,2},{9,8},{11,9},{13,1... | collective-permute-start | bytes 3145736 | tf_op jit(solution)/shard_map/ppermute | solution.py:971
  315.6 22.1 %collective-permute-start.23 = (bf16[256,2048]{1,0:T(8,128)(2,1)S(1)}, bf16[256,2048]{1,0:T(8,128)(2,1)S(1)}, u32[]{:S(2)}, u32[]{:S(2)}) collective-permute-start(bf16[256,2048]{1,0:T(8,128)(2,1)S(1)} %copy-done.24), channel_id=1, source_target_pairs={{0,1},{1,3},{3,5},{5,7},{7,6},{6,4},{4,2},{2,0},{8,9},{9,11},{11,1... | collective-permute-start | bytes 3145736 | tf_op jit(solution)/shard_map/ppermute | solution.py:968
  317.2 21.3 %collective-permute-start.24 = (bf16[256,2048]{1,0:T(8,128)(2,1)}, bf16[256,2048]{1,0:T(8,128)(2,1)S(1)}, u32[]{:S(2)}, u32[]{:S(2)}) collective-permute-start(bf16[256,2048]{1,0:T(8,128)(2,1)} %ring_add.23), channel_id=1, source_target_pairs={{1,0},{3,1},{5,3},{7,5},{6,7},{4,6},{2,4},{0,2},{9,8},{11,9},{13,1... | collective-permute-start | bytes 3145736 | tf_op jit(solution)/shard_map/ppermute | solution.py:971
  338.4 13.0 %collective-permute-start.25 = (bf16[128,2048]{1,0:T(8,128)(2,1)}, bf16[128,2048]{1,0:T(8,128)(2,1)S(1)}, u32[]{:S(2)}, u32[]{:S(2)}) collective-permute-start(bf16[128,2048]{1,0:T(8,128)(2,1)} %get-tuple-element.310), channel_id=1, source_target_pairs={{0,1},{1,3},{3,5},{5,7},{7,6},{6,4},{4,2},{2,0},{8,9},{9,11},{11,1... | collective-permute-start | bytes 1572872 | tf_op jit(solution)/shard_map/ppermute | solution.py:968
  340.2 11.7 %collective-permute-start.26 = (bf16[128,2048]{1,0:T(8,128)(2,1)}, bf16[128,2048]{1,0:T(8,128)(2,1)S(1)}, u32[]{:S(2)}, u32[]{:S(2)}) collective-permute-start(bf16[128,2048]{1,0:T(8,128)(2,1)} %get-tuple-element.311), channel_id=1, source_target_pairs={{1,0},{3,1},{5,3},{7,5},{6,7},{4,6},{2,4},{0,2},{9,8},{11,9},{13,1... | collective-permute-start | bytes 1572872 | tf_op jit(solution)/shard_map/ppermute | solution.py:971
  351.4 10.3 %copy-start.31 = (bf16[128,2048]{1,0:T(8,128)(2,1)}, bf16[128,2048]{1,0:T(8,128)(2,1)S(1)}, u32[]{:S(2)}) copy-start(bf16[128,2048]{1,0:T(8,128)(2,1)S(1)} %collective-permute-done.25.got_ref) | copy-start | bytes 1572868
  351.9 12.8 %copy-start.32 = (bf16[128,2048]{1,0:T(8,128)(2,1)}, bf16[128,2048]{1,0:T(8,128)(2,1)S(1)}, u32[]{:S(2)}) copy-start(bf16[128,2048]{1,0:T(8,128)(2,1)S(1)} %collective-permute-done.26.got_ref) | copy-start | bytes 1572868
  351.9 26.2 %all-to-all-start.2 = ((bf16[8,256,256]{2,1,0:T(8,128)(2,1)}), bf16[8,256,256]{2,1,0:T(8,128)(2,1)S(1)}, u32[]{:S(2)}, u32[]{:S(2)}) async-start(bf16[8,256,256]{2,1,0:T(8,128)(2,1)} %get-tuple-element.318), calls=%async_computation.2 | async-start | bytes 2097152 | tf_op jit(solution)/shard_map/all_to_all | solution.py:965
  361.7 186.5 %reduce-scatter.9.cloned.1.call-start = ((), (), s32[]{:S(2)}) async-start(), calls=%async_computation.10 | async-start | bytes 5242880 | tf_op jit(solution)/shard_map/reduce_scatter | solution.py:1082
  367.5 13.5 %copy-start.38 = (s32[1,8]{1,0:T(1,128)S(1)}, s32[1,8]{1,0:T(1,128)}, u32[]{:S(2)}) copy-start(s32[1,8]{1,0:T(1,128)} %get-tuple-element.395) | copy-start | bytes 100
  367.5 14.8 %copy-start.36 = (f32[2048]{0:T(1024)S(1)}, f32[2048]{0:T(1024)}, u32[]{:S(2)}) copy-start(f32[2048]{0:T(1024)} %param.16) | copy-start | bytes 24580
  378.1 26.6 %collective-permute-start.29 = (bf16[2,2048,512]{2,1,0:T(8,128)(2,1)}, bf16[2,2048,512]{2,1,0:T(8,128)(2,1)}, u32[]{:S(2)}, u32[]{:S(2)}) collective-permute-start(bf16[2,2048,512]{2,1,0:T(8,128)(2,1)} %get-tuple-element.335), channel_id=1, source_target_pairs={{0,8},{8,0},{16,24},{24,16},{1,9},{9,1},{17,25},{25,17},{2,10},{10... | collective-permute-start | bytes 12582920 | tf_op jit(solution)/shard_map/ppermute | solution.py:899
  379.0 240.3 %reduce-scatter.11.cloned.1.call-start = ((), (), s32[]{:S(2)}) async-start(), calls=%async_computation.11 | async-start | bytes 2359296 | tf_op jit(solution)/shard_map/reduce_scatter | solution.py:1136
  379.0 25.0 %collective-permute-start.27 = (bf16[256,2048]{1,0:T(8,128)(2,1)}, bf16[256,2048]{1,0:T(8,128)(2,1)S(1)}, u32[]{:S(2)}, u32[]{:S(2)}) collective-permute-start(bf16[256,2048]{1,0:T(8,128)(2,1)} %ring_add.24), channel_id=1, source_target_pairs={{0,1},{1,3},{3,5},{5,7},{7,6},{6,4},{4,2},{2,0},{8,9},{9,11},{11,1... | collective-permute-start | bytes 3145736 | tf_op jit(solution)/shard_map/ppermute | solution.py:968
  380.0 24.7 %collective-permute-start.28 = (bf16[256,2048]{1,0:T(8,128)(2,1)}, bf16[256,2048]{1,0:T(8,128)(2,1)S(1)}, u32[]{:S(2)}, u32[]{:S(2)}) collective-permute-start(bf16[256,2048]{1,0:T(8,128)(2,1)} %ring_add.25), channel_id=1, source_target_pairs={{1,0},{3,1},{5,3},{7,5},{6,7},{4,6},{2,4},{0,2},{9,8},{11,9},{13,1... | collective-permute-start | bytes 3145736 | tf_op jit(solution)/shard_map/ppermute | solution.py:971
  408.1 31.1 %collective-permute-start.30 = (bf16[256,2048]{1,0:T(8,128)(2,1)}, bf16[256,2048]{1,0:T(8,128)(2,1)}, u32[]{:S(2)}, u32[]{:S(2)}) collective-permute-start(bf16[256,2048]{1,0:T(8,128)(2,1)} %ring_add.26), channel_id=1, source_target_pairs={{0,1},{1,3},{3,5},{5,7},{7,6},{6,4},{4,2},{2,0},{8,9},{9,11},{11,1... | collective-permute-start | bytes 3145736 | tf_op jit(solution)/shard_map/ppermute | solution.py:968
  412.3 26.9 %collective-permute-start.31 = (bf16[256,2048]{1,0:T(8,128)(2,1)}, bf16[256,2048]{1,0:T(8,128)(2,1)S(1)}, u32[]{:S(2)}, u32[]{:S(2)}) collective-permute-start(bf16[256,2048]{1,0:T(8,128)(2,1)} %ring_add.27), channel_id=1, source_target_pairs={{1,0},{3,1},{5,3},{7,5},{6,7},{4,6},{2,4},{0,2},{9,8},{11,9},{13,1... | collective-permute-start | bytes 3145736 | tf_op jit(solution)/shard_map/ppermute | solution.py:971
  442.2 34.8 %collective-permute-start.32 = (bf16[128,2048]{1,0:T(8,128)(2,1)}, bf16[128,2048]{1,0:T(8,128)(2,1)}, u32[]{:S(2)}, u32[]{:S(2)}) collective-permute-start(bf16[128,2048]{1,0:T(8,128)(2,1)} %get-tuple-element.390), channel_id=1, source_target_pairs={{0,1},{1,3},{3,5},{5,7},{7,6},{6,4},{4,2},{2,0},{8,9},{9,11},{11,1... | collective-permute-start | bytes 1572872 | tf_op jit(solution)/shard_map/ppermute | solution.py:968
  443.2 33.7 %collective-permute-start.33 = (bf16[128,2048]{1,0:T(8,128)(2,1)}, bf16[128,2048]{1,0:T(8,128)(2,1)}, u32[]{:S(2)}, u32[]{:S(2)}) collective-permute-start(bf16[128,2048]{1,0:T(8,128)(2,1)} %get-tuple-element.389), channel_id=1, source_target_pairs={{1,0},{3,1},{5,3},{7,5},{6,7},{4,6},{2,4},{0,2},{9,8},{11,9},{13,1... | collective-permute-start | bytes 1572872 | tf_op jit(solution)/shard_map/ppermute | solution.py:971
  447.6 29.5 %collective-permute-start.34 = (bf16[256,2048]{1,0:T(8,128)(2,1)}, bf16[256,2048]{1,0:T(8,128)(2,1)S(1)}, u32[]{:S(2)}, u32[]{:S(2)}) collective-permute-start(bf16[256,2048]{1,0:T(8,128)(2,1)} %ring_add.28), channel_id=1, source_target_pairs={{0,1},{1,3},{3,5},{5,7},{7,6},{6,4},{4,2},{2,0},{8,9},{9,11},{11,1... | collective-permute-start | bytes 3145736 | tf_op jit(solution)/shard_map/ppermute | solution.py:968
  451.8 26.4 %collective-permute-start.35 = (bf16[256,2048]{1,0:T(8,128)(2,1)}, bf16[256,2048]{1,0:T(8,128)(2,1)}, u32[]{:S(2)}, u32[]{:S(2)}) collective-permute-start(bf16[256,2048]{1,0:T(8,128)(2,1)} %ring_add.29), channel_id=1, source_target_pairs={{1,0},{3,1},{5,3},{7,5},{6,7},{4,6},{2,4},{0,2},{9,8},{11,9},{13,1... | collective-permute-start | bytes 3145736 | tf_op jit(solution)/shard_map/ppermute | solution.py:971
  463.7 61.9 %collective-permute-start.42 = (bf16[2048,512]{1,0:T(8,128)(2,1)}, bf16[2048,512]{1,0:T(8,128)(2,1)S(1)}, u32[]{:S(2)}, u32[]{:S(2)}) collective-permute-start(bf16[2048,512]{1,0:T(8,128)(2,1)} %fusion.1), channel_id=1, source_target_pairs={{0,16},{8,24},{16,0},{24,8},{1,17},{9,25},{17,1},{25,9},{2,18},{10... | collective-permute-start | bytes 6291464 | tf_op jit(solution)/shard_map/ppermute | solution.py:908
  478.1 8.0 %collective-permute-start.38 = (f32[2,512,256]{2,1,0:T(8,128)}, f32[2,512,256]{2,1,0:T(8,128)}, u32[]{:S(2)}, u32[]{:S(2)}) collective-permute-start(f32[2,512,256]{2,1,0:T(8,128)} %get-tuple-element.357), channel_id=1, source_target_pairs={{0,8},{8,0},{16,24},{24,16},{1,9},{9,1},{17,25},{25,17},{2,10},{10... | collective-permute-start | bytes 3145736 | tf_op jit(solution)/shard_map/ppermute | solution.py:899
  481.0 44.5 %collective-permute-start.36 = (bf16[256,2048]{1,0:T(8,128)(2,1)}, bf16[256,2048]{1,0:T(8,128)(2,1)}, u32[]{:S(2)}, u32[]{:S(2)}) collective-permute-start(bf16[256,2048]{1,0:T(8,128)(2,1)} %ring_add.30), channel_id=1, source_target_pairs={{0,1},{1,3},{3,5},{5,7},{7,6},{6,4},{4,2},{2,0},{8,9},{9,11},{11,1... | collective-permute-start | bytes 3145736 | tf_op jit(solution)/shard_map/ppermute | solution.py:968
  484.7 40.8 %collective-permute-start.37 = (bf16[256,2048]{1,0:T(8,128)(2,1)}, bf16[256,2048]{1,0:T(8,128)(2,1)}, u32[]{:S(2)}, u32[]{:S(2)}) collective-permute-start(bf16[256,2048]{1,0:T(8,128)(2,1)} %ring_add.31), channel_id=1, source_target_pairs={{1,0},{3,1},{5,3},{7,5},{6,7},{4,6},{2,4},{0,2},{9,8},{11,9},{13,1... | collective-permute-start | bytes 3145736 | tf_op jit(solution)/shard_map/ppermute | solution.py:971
  486.1 2.8 collective-permute-start.40
  487.2 38.3 %collective-permute-start.39 = (f32[512,256]{1,0:T(8,128)S(1)}, f32[512,256]{1,0:T(8,128)}, u32[]{:S(2)}, u32[]{:S(2)}) collective-permute-start(f32[512,256]{1,0:T(8,128)S(1)} %fusion.3), channel_id=1, source_target_pairs={{0,16},{8,24},{16,0},{24,8},{1,17},{9,25},{17,1},{25,9},{2,18},{10... | collective-permute-start | bytes 1572872 | tf_op jit(solution)/shard_map/ppermute | solution.py:908
  488.9 36.7 %copy-start.29 = (bf16[2,512,256]{2,1,0:T(8,128)(2,1)}, bf16[2,512,256]{2,1,0:T(8,128)(2,1)S(1)}, u32[]{:S(2)}) copy-start(bf16[2,512,256]{2,1,0:T(8,128)(2,1)S(1)} %collective-permute-done.40) | copy-start | bytes 1572868
  490.1 35.5 %collective-permute-start.41 = (bf16[512,256]{1,0:T(8,128)(2,1)S(1)}, bf16[512,256]{1,0:T(8,128)(2,1)S(1)}, u32[]{:S(2)}, u32[]{:S(2)}) collective-permute-start(bf16[512,256]{1,0:T(8,128)(2,1)S(1)} %fusion.4), channel_id=1, source_target_pairs={{0,16},{8,24},{16,0},{24,8},{1,17},{9,25},{17,1},{25,9},{2,18},{10... | collective-permute-start | bytes 786440 | tf_op jit(solution)/shard_map/ppermute | solution.py:908
  533.1 42.8 %collective-permute-start.43 = (bf16[256,2048]{1,0:T(8,128)(2,1)}, bf16[256,2048]{1,0:T(8,128)(2,1)S(1)}, u32[]{:S(2)}, u32[]{:S(2)}) collective-permute-start(bf16[256,2048]{1,0:T(8,128)(2,1)} %ring_add.32), channel_id=1, source_target_pairs={{0,1},{1,3},{3,5},{5,7},{7,6},{6,4},{4,2},{2,0},{8,9},{9,11},{11,1... | collective-permute-start | bytes 3145736 | tf_op jit(solution)/shard_map/ppermute | solution.py:968
  537.3 39.3 %collective-permute-start.44 = (bf16[256,2048]{1,0:T(8,128)(2,1)}, bf16[256,2048]{1,0:T(8,128)(2,1)}, u32[]{:S(2)}, u32[]{:S(2)}) collective-permute-start(bf16[256,2048]{1,0:T(8,128)(2,1)} %ring_add.33), channel_id=1, source_target_pairs={{1,0},{3,1},{5,3},{7,5},{6,7},{4,6},{2,4},{0,2},{9,8},{11,9},{13,1... | collective-permute-start | bytes 3145736 | tf_op jit(solution)/shard_map/ppermute | solution.py:971
  540.3 50.7 %all-to-all-start.3 = ((f32[8,64,256]{2,1,0:T(8,128)}), f32[8,64,256]{2,1,0:T(8,128)S(1)}, u32[]{:S(2)}, u32[]{:S(2)}) async-start(f32[8,64,256]{2,1,0:T(8,128)} %bitcast.15), calls=%async_computation.6 | async-start | bytes 1048576 | tf_op jit(solution)/shard_map/all_to_all | solution.py:965
  580.0 6.9 %copy-start.9 = (bf16[1024,512]{1,0:T(8,128)(2,1)S(1)}, bf16[1024,512]{1,0:T(8,128)(2,1)}, u32[]{:S(2)}) copy-start(bf16[1024,512]{1,0:T(8,128)(2,1)} %reduce-scatter.5.cloned.1.call-done) | copy-start | bytes 3145732
  580.0 8.6 %copy-start.10 = (bf16[512,1024]{1,0:T(8,128)(2,1)S(1)}, bf16[512,1024]{1,0:T(8,128)(2,1)}, u32[]{:S(2)}) copy-start(bf16[512,1024]{1,0:T(8,128)(2,1)} %reduce-scatter.7.cloned.1.call-done) | copy-start | bytes 3145732
  580.0 31.1 %collective-permute-start.45 = (bf16[256,2048]{1,0:T(8,128)(2,1)}, bf16[256,2048]{1,0:T(8,128)(2,1)}, u32[]{:S(2)}, u32[]{:S(2)}) collective-permute-start(bf16[256,2048]{1,0:T(8,128)(2,1)} %ring_add.34), channel_id=1, source_target_pairs={{0,1},{1,3},{3,5},{5,7},{7,6},{6,4},{4,2},{2,0},{8,9},{9,11},{11,1... | collective-permute-start | bytes 3145736 | tf_op jit(solution)/shard_map/ppermute | solution.py:968
  586.9 26.6 %collective-permute-start.46 = (bf16[256,2048]{1,0:T(8,128)(2,1)}, bf16[256,2048]{1,0:T(8,128)(2,1)}, u32[]{:S(2)}, u32[]{:S(2)}) collective-permute-start(bf16[256,2048]{1,0:T(8,128)(2,1)} %ring_add.35), channel_id=1, source_target_pairs={{1,0},{3,1},{5,3},{7,5},{6,7},{4,6},{2,4},{0,2},{9,8},{11,9},{13,1... | collective-permute-start | bytes 3145736 | tf_op jit(solution)/shard_map/ppermute | solution.py:971
  (30 other events, 86.3 us)
Sparse Core Ops, SparseCore 0:
  275.3 44.4 reduce-scatter.4
  322.6 44.5 reduce-scatter.6
  378.2 43.5 reduce-scatter.8
  530.1 82.1 reduce-scatter.10
